TPU v7x, 128 devices: a whole 4x4x4 slice. The times are simulated.
128 devices in a mesh: dp: 4 (over x), gx: 4 (over y_lo, core), gy: 8 (over z, y_hi).
Axes of the slice: x: 4, y: 4 (y_hi: 2, y_lo: 2; y = y_hi * 2 + y_lo), z: 4, core: 2. Of those that a mesh axis runs over, the one named last changes fastest.
Arguments:
- field: bfloat16 [4, 20, 256, 16384], P('dp', None, 'gx', 'gy'), may hold values from -6 to 6
- spectral_weight: bfloat16 [12, 20, 20, 2, 4096], P('dp', None, None, None, ('gx', 'gy')), may hold values from -6 to 6
- bypass_weight: bfloat16 [20, 20], replicated, may hold values from -1.25 to 1.25
- bias: float32 [20], replicated, may hold values from -3 to 3
- cotangent: bfloat16 [4, 20, 256, 16384], P('dp', None, 'gx', 'gy'), may hold values from -6 to 6
Outputs:
- activation: bfloat16 [4, 20, 256, 16384], P('dp', None, 'gx', 'gy')
- field_grad: bfloat16 [4, 20, 256, 16384], P('dp', None, 'gx', 'gy')
- weight_grad: float32 [12, 20, 20, 2, 4096], P('dp', None, None, None, ('gx', 'gy'))
All inputs are finite; a program needn't handle non-finite values.
Results may differ from a plain program's by a relative error of at most 0.024.
Values may be sent and summed in bfloat16 or wider, within the bound.
No kernel may reach another device: no remote copies, remote signals or barrier semaphores. Data moves between devices by JAX's collectives and lax.ppermute only.
A program may use at most 192 MiB of HBM per device.

v0:
```python
import functools
import math

import jax
import jax.numpy as jnp
import ml_dtypes
import numpy as np
from jax import lax
from jax.experimental import pallas as pl
from jax.experimental.pallas import tpu as pltpu
from jax.sharding import PartitionSpec as P

CH = 20
NX = 256
NY = 256
NZ = 64
KX = 64
KY = 64
KZ = 12
GX = 4
GY = 8
DP = 4
XL = NX // GX
YL = NY // GY
YB = 8
STEPS = YL // YB
LANES = YB * NZ
KB = KZ // GX
ROWS = 2 * KB * YB
GROUP = 4
GROUPS = CH // GROUP
GL = GROUP * KX
WIDE = CH * KX
XB = 16
ORDER = (0, 2, 1, 3)

BF = jnp.bfloat16
F32 = jnp.float32


def wave(freqs, points, length):
    offsets = np.mod(freqs[:, None] * points[None, :], length)
    angle = offsets.astype(np.float32) * np.float32(2.0 * math.pi / length)
    return np.cos(angle), np.sin(angle)


def kept(count):
    index = np.arange(count)
    return np.where(index < count // 2, index, index - count)


def depth_tables():
    out = np.zeros((GX, 2, GX, KB, YB, YB, NZ), np.float32)
    for b in range(GX):
        for pos, delta in enumerate(ORDER):
            freqs = (b ^ delta) * KB + np.arange(KB)
            cosine, sine = wave(freqs, np.arange(NZ), NZ)
            for y in range(YB):
                out[b, 0, pos, :, y, y] = cosine
                out[b, 1, pos, :, y, y] = -sine
    return out.reshape(GX, 2 * KZ * YB, LANES).astype(ml_dtypes.bfloat16)


def width_tables():
    out = np.zeros((GX, 2, XL, GL), np.float32)
    for b in range(GX):
        cosine, sine = wave(kept(KX), b * XL + np.arange(XL), NX)
        out[b, 0] = np.tile(cosine.T, (1, GROUP))
        out[b, 1] = np.tile(sine.T, (1, GROUP))
    return out.astype(ml_dtypes.bfloat16)


def line_tables():
    out = np.zeros((GY, GY, 2, 2, GX, KB, STEPS, 2, KB, YB), np.float32)
    fy = kept(KY)
    for g in range(GY):
        cosine, sine = wave(fy, g * YL + np.arange(YL), NY)
        cosine = cosine.reshape(GX, GY, 2, STEPS, YB)
        sine = sine.reshape(GX, GY, 2, STEPS, YB)
        for i in range(KB):
            for owner in range(GY):
                for q in range(2):
                    c = cosine[:, owner, q]
                    s = sine[:, owner, q]
                    out[g, owner, q, 0, :, i, :, 0, i] = c
                    out[g, owner, q, 0, :, i, :, 1, i] = s
                    out[g, owner, q, 1, :, i, :, 0, i] = -s
                    out[g, owner, q, 1, :, i, :, 1, i] = c
    return out.reshape(GY, GY * 48, STEPS * ROWS).astype(ml_dtypes.bfloat16)


DEPTH = depth_tables()
WIDTH = width_tables()
LINE = line_tables()
SPREAD = np.kron(np.eye(CH), np.ones((XB, 1))).astype(ml_dtypes.bfloat16)
SAME = np.kron(np.ones((CH, CH)), np.eye(XB)).astype(ml_dtypes.bfloat16)


def dot(left, right, left_dim=1, right_dim=0):
    return lax.dot_general(
        left, right, (((left_dim,), (right_dim,)), ((), ())), preferred_element_type=F32
    )


def fill_width(wide_ref, blocks_ref):
    rows = lax.broadcasted_iota(jnp.int32, (GL, GL), 0) // XL
    columns = lax.broadcasted_iota(jnp.int32, (GL, GL), 1) // KX
    for part in range(2):
        strip = wide_ref[0, part].astype(F32)
        full = jnp.concatenate([strip] * GROUP, axis=0)
        blocks_ref[part] = jnp.where(rows == columns, full, 0.0).astype(BF)


def forward_columns(source_ref, depth_ref, blocks_ref, outs):
    half = KZ * YB
    for j in range(GROUPS):
        rows = source_ref[GROUP * j : GROUP * (j + 1)].reshape(GROUP * XL, LANES)
        planes = dot(depth_ref[0], rows, 1, 1).astype(BF)
        by_cos = dot(planes, blocks_ref[0])
        by_sin = dot(planes, blocks_ref[1])
        real = by_cos[:half] + by_sin[half:]
        imag = by_cos[half:] - by_sin[:half]
        for pos in range(GX):
            lo = pos * KB * YB
            piece = jnp.concatenate([real[lo : lo + KB * YB], imag[lo : lo + KB * YB]], axis=0)
            outs[pos][0, :, GL * j : GL * (j + 1)] = piece.astype(BF)


def inverse_columns(ins, depth_ref, blocks_ref, total_ref):
    half = KZ * YB
    part = KB * YB
    for j in range(GROUPS):
        pieces = [ref[0, :, GL * j : GL * (j + 1)].astype(F32) for ref in ins]
        stacked = jnp.concatenate(
            [piece[:part] for piece in pieces] + [piece[part:] for piece in pieces], axis=0
        ).astype(BF)
        by_cos = dot(stacked, blocks_ref[0], 1, 1)
        by_sin = dot(stacked, blocks_ref[1], 1, 1)
        real = by_cos[:half] - by_sin[half:]
        imag = by_sin[:half] + by_cos[half:]
        planes = jnp.concatenate([real, imag], axis=0).astype(BF)
        values = dot(planes, depth_ref[0], 0, 0)
        total_ref[GROUP * j : GROUP * (j + 1)] = values.reshape(GROUP, XL, LANES)


def add_bypass(source_ref, mixer_ref, total_ref):
    @pl.loop(0, XL // XB)
    def _(i):
        span = pl.ds(pl.multiple_of(i * XB, XB), XB)
        rows = source_ref[:, span, :].reshape(CH * XB, LANES)
        mixed = dot(mixer_ref[...], rows).reshape(CH, XB, LANES)
        total_ref[:, span, :] = total_ref[:, span, :] + mixed


def start_kernel(where_ref, field_ref, depth_ref, wide_ref, o0, o1, o2, o3, blocks_ref):
    @pl.when(pl.program_id(0) == 0)
    def _():
        fill_width(wide_ref, blocks_ref)

    forward_columns(field_ref, depth_ref, blocks_ref, (o0, o1, o2, o3))


ROOT = math.sqrt(2.0 / math.pi)
CUBE = 0.044715


def middle_kernel(
    where_ref, bias_ref, i0, i1, i2, i3, field_ref, upstream_ref, mixer_ref, depth_ref, wide_ref,
    act_ref, grad_ref, o0, o1, o2, o3, blocks_ref, total_ref,
):
    @pl.when(pl.program_id(0) == 0)
    def _():
        fill_width(wide_ref, blocks_ref)

    inverse_columns((i0, i1, i2, i3), depth_ref, blocks_ref, total_ref)
    add_bypass(field_ref, mixer_ref, total_ref)

    @pl.loop(0, CH)
    def _(channel):
        shift = bias_ref[channel]
        for i in range(XL // XB):
            span = slice(i * XB, (i + 1) * XB)
            x = total_ref[channel, span, :] + shift
            square = x * x
            t = jnp.tanh(x * (ROOT + (ROOT * CUBE) * square))
            h = 0.5 * t + 0.5
            act = x * h
            slope = h + act * (1.0 - h) * (2.0 * ROOT + (6.0 * ROOT * CUBE) * square)
            act_ref[channel, span, :] = act.astype(BF)
            up = upstream_ref[channel, span, :].astype(F32)
            grad_ref[channel, span, :] = (up * slope).astype(BF)

    forward_columns(grad_ref, depth_ref, blocks_ref, (o0, o1, o2, o3))


def end_kernel(
    where_ref, i0, i1, i2, i3, grad_ref, mixer_ref, depth_ref, wide_ref, out_ref,
    blocks_ref, total_ref,
):
    @pl.when(pl.program_id(0) == 0)
    def _():
        fill_width(wide_ref, blocks_ref)

    inverse_columns((i0, i1, i2, i3), depth_ref, blocks_ref, total_ref)
    add_bypass(grad_ref, mixer_ref, total_ref)

    @pl.loop(0, CH)
    def _(channel):
        out_ref[channel] = total_ref[channel].astype(BF)


def column_specs():
    columns = pl.BlockSpec((CH, XL, LANES), lambda i, w: (0, 0, i))
    coeffs = pl.BlockSpec((1, ROWS, WIDE), lambda i, w: (i, 0, 0))
    depth = pl.BlockSpec((1, 2 * KZ * YB, LANES), lambda i, w: (w[1], 0, 0))
    wide = pl.BlockSpec((1, 2, XL, GL), lambda i, w: (w[1], 0, 0, 0))
    mixer = pl.BlockSpec((CH * XB, CH * XB), lambda i, w: (0, 0))
    return columns, coeffs, depth, wide, mixer


COEFFS = jax.ShapeDtypeStruct((STEPS, ROWS, WIDE), BF)
COLUMNS = jax.ShapeDtypeStruct((CH, XL, YL * NZ), BF)
BLOCKS = pltpu.VMEM((2, GL, GL), BF)
TOTAL = pltpu.VMEM((CH, XL, LANES), F32)
PARAMS = pltpu.CompilerParams(vmem_limit_bytes=56 * 1024 * 1024)


def start_columns(where, field):
    columns, coeffs, depth, wide, _ = column_specs()
    return pl.pallas_call(
        start_kernel,
        grid_spec=pltpu.PrefetchScalarGridSpec(
            num_scalar_prefetch=1,
            grid=(STEPS,),
            in_specs=[columns, depth, wide],
            out_specs=[coeffs] * 4,
            scratch_shapes=[BLOCKS],
        ),
        out_shape=[COEFFS] * 4,
        compiler_params=PARAMS,
        name="start_columns",
    )(where, field, jnp.asarray(DEPTH), jnp.asarray(WIDTH))


def middle_columns(where, bias, coeffs_in, field, upstream, mixer):
    columns, coeffs, depth, wide, mix = column_specs()
    return pl.pallas_call(
        middle_kernel,
        grid_spec=pltpu.PrefetchScalarGridSpec(
            num_scalar_prefetch=1,
            grid=(STEPS,),
            in_specs=[pl.BlockSpec(memory_space=pltpu.SMEM)]
            + [coeffs] * 4
            + [columns, columns, mix, depth, wide],
            out_specs=[columns, columns] + [coeffs] * 4,
            scratch_shapes=[BLOCKS, TOTAL],
        ),
        out_shape=[COLUMNS, COLUMNS] + [COEFFS] * 4,
        compiler_params=PARAMS,
        name="middle_columns",
    )(where, bias, *coeffs_in, field, upstream, mixer, jnp.asarray(DEPTH), jnp.asarray(WIDTH))


def end_columns(where, coeffs_in, grad, mixer):
    columns, coeffs, depth, wide, mix = column_specs()
    return pl.pallas_call(
        end_kernel,
        grid_spec=pltpu.PrefetchScalarGridSpec(
            num_scalar_prefetch=1,
            grid=(STEPS,),
            in_specs=[coeffs] * 4 + [columns, mix, depth, wide],
            out_specs=columns,
            scratch_shapes=[BLOCKS, TOTAL],
        ),
        out_shape=COLUMNS,
        compiler_params=PARAMS,
        name="end_columns",
    )(where, *coeffs_in, grad, mixer, jnp.asarray(DEPTH), jnp.asarray(WIDTH))


def line_kernel(where_ref, a_ref, b_ref, c_ref, table_ref, out_ref):
    total = a_ref[...].astype(F32) + b_ref[...].astype(F32) + c_ref[...].astype(F32)
    rows = total.astype(BF).reshape(STEPS * ROWS, GL)
    out_ref[...] = dot(table_ref[0], rows).astype(BF).reshape(GY, 48, GL)


def to_lines(where, own, from_core, from_chip):
    piece = pl.BlockSpec((STEPS, ROWS, GL), lambda i, w: (0, 0, i))
    table = pl.BlockSpec((1, GY * 48, STEPS * ROWS), lambda i, w: (w[2], 0, 0))
    return pl.pallas_call(
        line_kernel,
        grid_spec=pltpu.PrefetchScalarGridSpec(
            num_scalar_prefetch=1,
            grid=(GROUPS,),
            in_specs=[piece] * 3 + [table],
            out_specs=pl.BlockSpec((GY, 48, GL), lambda i, w: (0, 0, i)),
        ),
        out_shape=jax.ShapeDtypeStruct((GY, 48, WIDE), BF),
        name="to_lines",
    )(where, own, from_core, from_chip, jnp.asarray(LINE))


def unline_kernel(where_ref, modes_ref, table_ref, out_ref):
    rows = modes_ref[...].reshape(GY * 48, GL)
    out_ref[...] = dot(table_ref[0], rows, 0, 0).astype(BF).reshape(STEPS, ROWS, GL)


def from_lines(where, modes):
    table = pl.BlockSpec((1, GY * 48, STEPS * ROWS), lambda i, w: (w[2], 0, 0))
    return pl.pallas_call(
        unline_kernel,
        grid_spec=pltpu.PrefetchScalarGridSpec(
            num_scalar_prefetch=1,
            grid=(GROUPS,),
            in_specs=[pl.BlockSpec((GY, 48, GL), lambda i, w: (0, 0, i)), table],
            out_specs=pl.BlockSpec((STEPS, ROWS, GL), lambda i, w: (0, 0, i)),
        ),
        out_shape=COEFFS,
        name="from_lines",
    )(where, modes, jnp.asarray(LINE))


SETS = GX * KB
PAIR = 2 * CH
HALF = KX


def low_lanes():
    return lax.broadcasted_iota(jnp.int32, (SETS, 2 * HALF), 1) < HALF


def gather_modes(arrived_ref, sum_ref, modes_ref, scale=None):
    total = arrived_ref[0].astype(F32)
    for i in range(1, GY):
        total = total + arrived_ref[i].astype(F32)
    sum_ref[...] = total.astype(BF).astype(F32)
    low = low_lanes()
    for j in range(CH // 2):
        lanes = slice(2 * HALF * j, 2 * HALF * (j + 1))
        for part in range(2):
            first = sum_ref[part * SETS : (part + 1) * SETS, lanes]
            second = sum_ref[(2 + part) * SETS : (3 + part) * SETS, lanes]
            if scale is not None:
                first = first * scale
                second = second * scale
            even = jnp.where(low, first, pltpu.roll(second, HALF, 1))
            odd = jnp.where(low, pltpu.roll(first, HALF, 1), second)
            modes_ref[pl.ds(4 * j + part, SETS, stride=PAIR), :] = even
            modes_ref[pl.ds(4 * j + 2 + part, SETS, stride=PAIR), :] = odd


def spread_modes(modes_ref, sum_ref, out_ref, scale=None):
    low = low_lanes()
    for j in range(CH // 2):
        lanes = slice(2 * HALF * j, 2 * HALF * (j + 1))
        for part in range(2):
            even = modes_ref[pl.ds(4 * j + part, SETS, stride=PAIR), :]
            odd = modes_ref[pl.ds(4 * j + 2 + part, SETS, stride=PAIR), :]
            if scale is not None:
                even = even * scale
                odd = odd * scale
            sum_ref[part * SETS : (part + 1) * SETS, lanes] = jnp.where(
                low, even, pltpu.roll(odd, HALF, 1)
            )
            sum_ref[(2 + part) * SETS : (3 + part) * SETS, lanes] = jnp.where(
                low, pltpu.roll(even, HALF, 1), odd
            )
    out_ref[...] = sum_ref[...].astype(BF)


def fold_scale(where_ref):
    kz = where_ref[1] * KB + lax.broadcasted_iota(jnp.int32, (SETS, 2 * HALF), 0) % KB
    return jnp.where(kz == 0, 1.0, 2.0).astype(F32) / float(NX * NY * NZ)


def turned(rows):
    even = lax.broadcasted_iota(jnp.int32, rows.shape, 0) % 2 == 0
    up = pltpu.roll(rows, PAIR - 1, 0)
    down = pltpu.roll(rows, 1, 0)
    return jnp.where(even, -up, down)


def hand_out(where_ref, modes_ref, outs):
    for k in range(DP):
        chunk = lax.rem(where_ref[0] + k, DP)
        start = pl.multiple_of(chunk * KB * PAIR, 8)
        outs[k][...] = modes_ref[pl.ds(start, KB * PAIR), :].astype(BF)


def mix_kernel(where_ref, arrived_ref, weight_ref, out_ref, u0, u1, u2, u3, sum_ref, in_ref, mix_ref):
    step = pl.program_id(0)

    @pl.when(step == 0)
    def _():
        gather_modes(arrived_ref, sum_ref, in_ref)
        hand_out(where_ref, in_ref, (u0, u1, u2, u3))

    @pl.loop(0, KB)
    def _(i):
        base = pl.multiple_of((step * KB + i) * PAIR, 8)
        by_real = jnp.zeros((PAIR, 2 * HALF), F32)
        by_imag = jnp.zeros((PAIR, 2 * HALF), F32)
        for c in range(CH):
            weight = weight_ref[i, c].astype(F32)
            by_real = by_real + weight * in_ref[pl.ds(base + 2 * c, 1), :]
            by_imag = by_imag + weight * in_ref[pl.ds(base + 2 * c + 1, 1), :]
        mix_ref[pl.ds(base, PAIR), :] = (by_real + turned(by_imag)).astype(BF).astype(F32)

    @pl.when(step == DP - 1)
    def _():
        spread_modes(mix_ref, sum_ref, out_ref, fold_scale(where_ref))


def back_kernel(where_ref, arrived_ref, weight_ref, out_ref, u0, u1, u2, u3, sum_ref, in_ref, mix_ref):
    step = pl.program_id(0)

    @pl.when(step == 0)
    def _():
        gather_modes(arrived_ref, sum_ref, in_ref, fold_scale(where_ref))
        hand_out(where_ref, in_ref, (u0, u1, u2, u3))

    @pl.loop(0, KB)
    def _(i):
        base = pl.multiple_of((step * KB + i) * PAIR, 8)
        grad = in_ref[pl.ds(base, PAIR), :]
        other = -turned(grad)
        for c in range(CH):
            weight = weight_ref[i, c].astype(F32)
            mix_ref[pl.ds(base + 2 * c, 1), :] = jnp.sum(weight * grad, axis=0, keepdims=True)
            mix_ref[pl.ds(base + 2 * c + 1, 1), :] = jnp.sum(weight * other, axis=0, keepdims=True)

    @pl.when(step == DP - 1)
    def _():
        spread_modes(mix_ref, sum_ref, out_ref)


def mode_call(kernel, name, where, arrived, weight):
    chunk = pl.BlockSpec((KB * PAIR, 2 * HALF), lambda i, w: (0, 0))
    return pl.pallas_call(
        kernel,
        grid_spec=pltpu.PrefetchScalarGridSpec(
            num_scalar_prefetch=1,
            grid=(DP,),
            in_specs=[
                pl.BlockSpec((GY, 48, WIDE), lambda i, w: (0, 0, 0)),
                pl.BlockSpec((KB, CH, PAIR, 2 * HALF), lambda i, w: (i, 0, 0, 0)),
            ],
            out_specs=[pl.BlockSpec((48, WIDE), lambda i, w: (0, 0))] + [chunk] * 4,
            scratch_shapes=[
                pltpu.VMEM((48, WIDE), F32),
                pltpu.VMEM((SETS * PAIR, 2 * HALF), F32),
                pltpu.VMEM((SETS * PAIR, 2 * HALF), F32),
            ],
        ),
        out_shape=[jax.ShapeDtypeStruct((48, WIDE), BF)]
        + [jax.ShapeDtypeStruct((KB * PAIR, 2 * HALF), BF)] * 4,
        name=name,
    )(where, arrived, weight)


def outer_kernel(s0, s1, s2, s3, g0, g1, g2, g3, out_ref, spec_ref):
    for k, ref in enumerate((s0, s1, s2, s3)):
        spec_ref[k] = ref[...].astype(F32)
    for i in range(KB):
        grads = []
        others = []
        for ref in (g0, g1, g2, g3):
            grad = ref[...].astype(F32)[i * PAIR : (i + 1) * PAIR]
            grads.append(grad)
            others.append(-turned(grad))

        @pl.loop(0, CH)
        def _(c):
            row = i * PAIR + 2 * c
            total = jnp.zeros((PAIR, 2 * HALF), F32)
            for k in range(DP):
                total = total + spec_ref[k, pl.ds(row, 1), :] * grads[k]
                total = total + spec_ref[k, pl.ds(row + 1, 1), :] * others[k]
            out_ref[i, c] = total


def outer_sum(spectra, grads):
    return pl.pallas_call(
        outer_kernel,
        out_shape=jax.ShapeDtypeStruct((KB, CH, PAIR, 2 * HALF), F32),
        scratch_shapes=[pltpu.VMEM((DP, KB * PAIR, 2 * HALF), F32)],
        name="outer_sum",
    )(*spectra, *grads)


def swap(values, bit):
    return lax.ppermute(values, "gx", [(i, i ^ bit) for i in range(GX)])


def reduce_slabs(where, pieces):
    own, far, near, across = pieces
    far_sum = (far.astype(F32) + swap(across, 1).astype(F32)).astype(BF)
    return to_lines(where, own, swap(near, 1), swap(far_sum, 2))


def share_slabs(own):
    far = swap(own, 2)
    return own, far, swap(own, 1), swap(far, 1)


def exchange_lines(parts):
    return lax.all_to_all(parts, "gy", split_axis=0, concat_axis=0, tiled=True)


def to_owners(chunks):
    moved = []
    for k, chunk in enumerate(chunks):
        pairs = [
            (a * GX + b, b * GX + (a + k) % DP) for a in range(DP) for b in range(GX)
        ]
        moved.append(lax.ppermute(chunk, ("dp", "gx"), pairs))
    return moved


def per_device(field, spectral_weight, bypass_weight, bias, cotangent):
    where = jnp.stack(
        [lax.axis_index("dp"), lax.axis_index("gx"), lax.axis_index("gy")]
    ).astype(jnp.int32)
    turn = [(a * GX + b, b * GX + a) for a in range(DP) for b in range(GX)]
    weight = lax.ppermute(spectral_weight, ("dp", "gx"), turn)
    weight = lax.all_gather(weight, "dp", axis=0, tiled=True)
    weight = weight.reshape(KZ, CH, PAIR, 2 * HALF)
    spread = jnp.asarray(SPREAD)

    def mixer_of(matrix):
        wide = dot(dot(spread, matrix).astype(BF), spread, 1, 1)
        return wide.astype(BF) * jnp.asarray(SAME)

    values = field[0]
    lines = reduce_slabs(where, start_columns(where, values))
    mode_out, *spectra = mode_call(mix_kernel, "mix_modes", where, exchange_lines(lines), weight)
    coeffs = share_slabs(from_lines(where, lax.all_gather(mode_out, "gy", axis=0)))
    spectra = to_owners(spectra)
    activation, grad, *pieces = middle_columns(
        where, bias, coeffs, values, cotangent[0], mixer_of(bypass_weight)
    )
    lines = reduce_slabs(where, pieces)
    mode_back, *grads = mode_call(back_kernel, "back_modes", where, exchange_lines(lines), weight)
    coeffs = share_slabs(from_lines(where, lax.all_gather(mode_back, "gy", axis=0)))
    weight_grad = outer_sum(spectra, to_owners(grads))
    field_grad = end_columns(where, coeffs, grad, mixer_of(bypass_weight.T))
    return (
        activation[None],
        field_grad[None],
        weight_grad.reshape(KB, CH, CH, 2, 2 * HALF),
    )


def solution(mesh):
    placed = (
        P("dp", None, "gx", "gy"),
        P("dp", None, None, None, ("gx", "gy")),
        P(),
        P(),
        P("dp", None, "gx", "gy"),
    )
    return jax.shard_map(
        per_device,
        mesh=mesh,
        in_specs=placed,
        out_specs=(
            P("dp", None, "gx", "gy"),
            P("dp", None, "gx", "gy"),
            P("dp", None, None, None, ("gx", "gy")),
        ),
        check_vma=False,
    )
```

profile of v0, /device:TPU:1, one launch (start us, length us, event | category | flops | bytes accessed | tf_op | source)
XLA Modules:
  0.0 327.2 jit_solution(10678169221650516433)
XLA Ops:
  7.2 4.5 %collective-permute-start.3 = (bf16[3,20,20,2,128]{4,3,2,1,0:T(2,128)(2,1)}, bf16[3,20,20,2,128]{4,3,2,1,0:T(2,128)(2,1)S(1)}, u32[]{:S(2)}, u32[]{:S(2)}) collective-permute-start(bf16[3,20,20,2,128]{4,3,2,1,0:T(2,128)(2,1)} %param.11), channel_id=1, source_target_pairs={{0,0},{8,32},{16,64},{24,96},{32,8},{40,40},{48,72},{56,104},{64,1... | collective-permute-start | bytes 1843208 | tf_op jit(solution)/shard_map/ppermute | solution.py:525
  11.7 8.0 %collective-permute-done.3 = bf16[3,20,20,2,128]{4,3,2,1,0:T(2,128)(2,1)S(1)} collective-permute-done((bf16[3,20,20,2,128]{4,3,2,1,0:T(2,128)(2,1)}, bf16[3,20,20,2,128]{4,3,2,1,0:T(2,128)(2,1)S(1)}, u32[]{:S(2)}, u32[]{:S(2)}) %collective-permute-start.3) | collective-permute-done | bytes 614432 | tf_op jit(solution)/shard_map/ppermute | solution.py:525
  19.8 0.8 copy-done.3
  20.6 0.6 pad_add_fusion.where_ref
  21.2 9.1 %start_columns.1 = (bf16[4,48,1280]{2,1,0:T(8,128)(2,1)}, bf16[4,48,1280]{2,1,0:T(8,128)(2,1)}, bf16[4,48,1280]{2,1,0:T(8,128)(2,1)}, bf16[4,48,1280]{2,1,0:T(8,128)(2,1)}) custom-call(s32[3]{0:T(128)} %pad_add_fusion.where_ref, bf16[20,64,2048]{2,1,0:T(8,128)(2,1)} %bitcast.17, bf16[4,192,512]{2,1,0:T(8,128)(2,1)} %constant.23.clone.depth_ref, ...), custom_call_target="tpu_custom_call" | custom-call | tf_op jit(solution)/shard_map/start_columns/pallas_call | solution.py:230
  30.3 0.5 collective-permute-start
  30.8 1.6 collective-permute-done.1
  32.4 1.2 add_convert_fusion.1
  33.6 10.1 %collective-permute-start.2 = (bf16[4,48,1280]{2,1,0:T(8,128)(2,1)S(1)}, bf16[4,48,1280]{2,1,0:T(8,128)(2,1)S(1)}, u32[]{:S(2)}, u32[]{:S(2)}) collective-permute-start(bf16[4,48,1280]{2,1,0:T(8,128)(2,1)S(1)} %add_convert_fusion.1), channel_id=1, source_target_pairs={{0,16},{8,24},{16,0},{24,8},{1,17},{9,25},{17,1},{25,9},{2,18},{10... | collective-permute-start | bytes 1474568 | tf_op jit(solution)/shard_map/ppermute | solution.py:492
  43.6 11.6 %collective-permute-done.2.c_ref = bf16[4,48,1280]{2,1,0:T(8,128)(2,1)S(1)} collective-permute-done((bf16[4,48,1280]{2,1,0:T(8,128)(2,1)S(1)}, bf16[4,48,1280]{2,1,0:T(8,128)(2,1)S(1)}, u32[]{:S(2)}, u32[]{:S(2)}) %collective-permute-start.2) | collective-permute-done | bytes 491552 | tf_op jit(solution)/shard_map/ppermute | solution.py:492
  55.2 0.8 copy-done.9
  56.0 5.3 %to_lines.2 = bf16[8,48,1280]{2,1,0:T(8,128)(2,1)} custom-call(s32[3]{0:T(128)} %pad_add_fusion.where_ref, bf16[4,48,1280]{2,1,0:T(8,128)(2,1)} %get-tuple-element.23.a_ref, bf16[4,48,1280]{2,1,0:T(8,128)(2,1)} %copy-done.6, bf16[4,48,1280]{2,1,0:T(8,128)(2,1)} %copy-done.9, bf16[8,384,192]{2,1,0:T(8,128)(2,1)} %constant.25.clone.table_ref), custom_call_target="tpu_custom_call" | custom-call | tf_op jit(solution)/shard_map/to_lines/pallas_call | solution.py:290
  61.3 22.9 %all_to_all.10.arrived_ref = bf16[8,48,1280]{2,1,0:T(8,128)(2,1)} all-to-all(bf16[8,48,1280]{2,1,0:T(8,128)(2,1)} %to_lines.2), channel_id=1, replica_groups=mesh['dp'=4,'gx'=4,'gy'=8] {'gy'}, dimensions={0} | all-to-all | bytes 1966080 | tf_op jit(solution)/shard_map/all_to_all | solution.py:507
  84.3 5.2 %mix_modes.1 = (bf16[48,1280]{1,0:T(8,128)(2,1)}, bf16[120,128]{1,0:T(8,128)(2,1)}, bf16[120,128]{1,0:T(8,128)(2,1)}, bf16[120,128]{1,0:T(8,128)(2,1)}, bf16[120,128]{1,0:T(8,128)(2,1)}) custom-call(s32[3]{0:T(128)} %pad_add_fusion.where_ref, bf16[8,48,1280]{2,1,0:T(8,128)(2,1)} %all_to_all.10.arrived_ref, bf16[12,20,40,128]{3,2,1,0:T(8,128)(2,1)} %bitcast.19), custom_call_target="tpu_custom_call" | custom-call | tf_op jit(solution)/shard_map/mix_modes/pallas_call | solution.py:439
  89.5 35.2 %all-gather = bf16[384,1280]{1,0:T(8,128)(2,1)} all-gather(bf16[48,1280]{1,0:T(8,128)(2,1)} %get-tuple-element.27), channel_id=2, replica_groups=mesh['dp'=4,'gx'=4,'gy'=8] {'gy'}, dimensions={0}, use_global_device_ids=true | all-gather | bytes 1105920 | tf_op jit(solution)/shard_map/all_gather | solution.py:537
  124.6 5.1 %from_lines.2.i0 = bf16[4,48,1280]{2,1,0:T(8,128)(2,1)} custom-call(s32[3]{0:T(128)} %pad_add_fusion.where_ref, bf16[8,48,1280]{2,1,0:T(8,128)(2,1)} %bitcast.24, bf16[8,384,192]{2,1,0:T(8,128)(2,1)} %constant.25.clone.table_ref), custom_call_target="tpu_custom_call" | custom-call | tf_op jit(solution)/shard_map/from_lines/pallas_call | solution.py:310
  129.7 0.9 collective-permute-start.4
  130.6 7.1 %collective-permute-start.5 = (bf16[4,48,1280]{2,1,0:T(8,128)(2,1)}, bf16[4,48,1280]{2,1,0:T(8,128)(2,1)S(1)}, u32[]{:S(2)}, u32[]{:S(2)}) collective-permute-start(bf16[4,48,1280]{2,1,0:T(8,128)(2,1)} %from_lines.2.i0), channel_id=1, source_target_pairs={{0,8},{8,0},{16,24},{24,16},{1,9},{9,1},{17,25},{25,17},{2,10},{10... | collective-permute-start | bytes 1474568 | tf_op jit(solution)/shard_map/ppermute | solution.py:492
  137.6 8.1 %collective-permute-start.6 = (bf16[4,48,1280]{2,1,0:T(8,128)(2,1)S(1)}, bf16[4,48,1280]{2,1,0:T(8,128)(2,1)S(1)}, u32[]{:S(2)}, u32[]{:S(2)}) collective-permute-start(bf16[4,48,1280]{2,1,0:T(8,128)(2,1)S(1)} %collective-permute-done.4.i1), channel_id=1, source_target_pairs={{0,8},{8,0},{16,24},{24,16},{1,9},{9,1},{17,25},{25,17},{2,10},{10... | collective-permute-start | bytes 1474568 | tf_op jit(solution)/shard_map/ppermute | solution.py:492
  145.7 1.0 fusion.mixer_ref
  148.0 27.9 %middle_columns.1 = (bf16[20,64,2048]{2,1,0:T(8,128)(2,1)}, bf16[20,64,2048]{2,1,0:T(8,128)(2,1)}, bf16[4,48,1280]{2,1,0:T(8,128)(2,1)}, bf16[4,48,1280]{2,1,0:T...) custom-call(s32[3]{0:T(128)} %pad_add_fusion.where_ref, f32[20]{0:T(128)} %bias_ref.1, ...), custom_call_target="tpu_custom_call" | custom-call | tf_op jit(solution)/shard_map/middle_columns/pallas_call | solution.py:247
  176.5 1.6 collective-permute-done.8
  178.1 1.2 add_convert_fusion
  179.2 0.8 collective-permute-start.9
  180.0 11.8 %collective-permute-done.9.c_ref = bf16[4,48,1280]{2,1,0:T(8,128)(2,1)S(1)} collective-permute-done((bf16[4,48,1280]{2,1,0:T(8,128)(2,1)S(1)}, bf16[4,48,1280]{2,1,0:T(8,128)(2,1)S(1)}, u32[]{:S(2)}, u32[]{:S(2)}) %collective-permute-start.9) | collective-permute-done | bytes 491552 | tf_op jit(solution)/shard_map/ppermute | solution.py:492
  191.8 0.8 copy-done.10
  192.6 5.3 %to_lines.3 = bf16[8,48,1280]{2,1,0:T(8,128)(2,1)} custom-call(s32[3]{0:T(128)} %pad_add_fusion.where_ref, bf16[4,48,1280]{2,1,0:T(8,128)(2,1)} %get-tuple-element.29.a_ref, bf16[4,48,1280]{2,1,0:T(8,128)(2,1)} %copy-done.7, bf16[4,48,1280]{2,1,0:T(8,128)(2,1)} %copy-done.10, bf16[8,384,192]{2,1,0:T(8,128)(2,1)} %constant.25.clone.table_ref), custom_call_target="tpu_custom_call" | custom-call | tf_op jit(solution)/shard_map/to_lines/pallas_call | solution.py:290
  197.9 19.7 %all_to_all.11.arrived_ref = bf16[8,48,1280]{2,1,0:T(8,128)(2,1)} all-to-all(bf16[8,48,1280]{2,1,0:T(8,128)(2,1)} %to_lines.3), channel_id=1, replica_groups=mesh['dp'=4,'gx'=4,'gy'=8] {'gy'}, dimensions={0} | all-to-all | bytes 1966080 | tf_op jit(solution)/shard_map/all_to_all | solution.py:507
  217.6 5.4 %back_modes.1 = (bf16[48,1280]{1,0:T(8,128)(2,1)}, bf16[120,128]{1,0:T(8,128)(2,1)}, bf16[120,128]{1,0:T(8,128)(2,1)}, bf16[120,128]{1,0:T(8,128)(2,1)}, bf16[120,128]{1,0:T(8,128)(2,1)}) custom-call(s32[3]{0:T(128)} %pad_add_fusion.where_ref, bf16[8,48,1280]{2,1,0:T(8,128)(2,1)} %all_to_all.11.arrived_ref, bf16[12,20,40,128]{3,2,1,0:T(8,128)(2,1)} %bitcast.20), custom_call_target="tpu_custom_call" | custom-call | tf_op jit(solution)/shard_map/back_modes/pallas_call | solution.py:439
  223.0 35.0 %all-gather.1 = bf16[384,1280]{1,0:T(8,128)(2,1)} all-gather(bf16[48,1280]{1,0:T(8,128)(2,1)} %get-tuple-element.33), channel_id=3, replica_groups=mesh['dp'=4,'gx'=4,'gy'=8] {'gy'}, dimensions={0}, use_global_device_ids=true | all-gather | bytes 1105920 | tf_op jit(solution)/shard_map/all_gather | solution.py:544
  258.0 5.1 %from_lines.3.i0 = bf16[4,48,1280]{2,1,0:T(8,128)(2,1)} custom-call(s32[3]{0:T(128)} %pad_add_fusion.where_ref, bf16[8,48,1280]{2,1,0:T(8,128)(2,1)} %bitcast.23, bf16[8,384,192]{2,1,0:T(8,128)(2,1)} %constant.25.clone.table_ref), custom_call_target="tpu_custom_call" | custom-call | tf_op jit(solution)/shard_map/from_lines/pallas_call | solution.py:310
  263.1 0.7 collective-permute-start.10
  263.7 7.4 %collective-permute-start.11 = (bf16[4,48,1280]{2,1,0:T(8,128)(2,1)}, bf16[4,48,1280]{2,1,0:T(8,128)(2,1)S(1)}, u32[]{:S(2)}, u32[]{:S(2)}) collective-permute-start(bf16[4,48,1280]{2,1,0:T(8,128)(2,1)} %from_lines.3.i0), channel_id=1, source_target_pairs={{0,8},{8,0},{16,24},{24,16},{1,9},{9,1},{17,25},{25,17},{2,10},{10... | collective-permute-start | bytes 1474568 | tf_op jit(solution)/shard_map/ppermute | solution.py:492
  271.1 8.1 %collective-permute-start.12 = (bf16[4,48,1280]{2,1,0:T(8,128)(2,1)S(1)}, bf16[4,48,1280]{2,1,0:T(8,128)(2,1)S(1)}, u32[]{:S(2)}, u32[]{:S(2)}) collective-permute-start(bf16[4,48,1280]{2,1,0:T(8,128)(2,1)S(1)} %collective-permute-done.10.i1), channel_id=1, source_target_pairs={{0,8},{8,0},{16,24},{24,16},{1,9},{9,1},{17,25},{25,17},{2,10},{10... | collective-permute-start | bytes 1474568 | tf_op jit(solution)/shard_map/ppermute | solution.py:492
  279.2 1.9 collective-permute-start.13
  281.3 2.7 collective-permute-start.15
  284.0 0.5 collective-permute-done.13.s0
  284.4 2.1 collective-permute-start.16
  286.6 3.1 collective-permute-start.17
  289.8 0.9 collective-permute-done.16.s3
  290.7 1.5 collective-permute-start.19
  292.2 5.4 %collective-permute-start.20 = (bf16[120,128]{1,0:T(8,128)(2,1)}, bf16[120,128]{1,0:T(8,128)(2,1)S(1)}, u32[]{:S(2)}, u32[]{:S(2)}) collective-permute-start(bf16[120,128]{1,0:T(8,128)(2,1)} %get-tuple-element.42), channel_id=1, source_target_pairs={{0,24},{8,56},{16,88},{24,120},{32,0},{40,32},{48,64},{56,96},{64,... | collective-permute-start | bytes 92168 | tf_op jit(solution)/shard_map/ppermute | solution.py:516
  297.5 1.0 fusion.1.mixer_ref
  298.6 1.4 collective-permute-done.20.g3
  300.1 0.6 copy-done.21
  300.7 3.1 outer_sum.1
  303.8 0.8 copy-done.12
  304.7 15.7 %end_columns.1 = bf16[20,64,2048]{2,1,0:T(8,128)(2,1)} custom-call(s32[3]{0:T(128)} %pad_add_fusion.where_ref, bf16[4,48,1280]{2,1,0:T(8,128)(2,1)} %from_lines.3.i0, bf16[4,48,1280]{2,1,0:T(8,128)(2,1)} %copy-done.11, bf16[4,48,1280]{2,1,0:T(8,128)(2,1)} %copy-done.12, bf16[4,48,1280]{2,1,0:T(8,128)(2,1)} %copy-done.13, ...), custom_call_target="tpu_custom_call" | custom-call | tf_op jit(solution)/shard_map/end_columns/pallas_call | solution.py:266
  (68 shorter events, 2.3 us)
Async XLA Ops:
  7.2 138.6 %copy-start = (bf16[20,20]{1,0:T(8,128)(2,1)S(1)}, bf16[20,20]{1,0:T(8,128)(2,1)}, u32[]{:S(2)}) copy-start(bf16[20,20]{1,0:T(8,128)(2,1)} %param.12) | copy-start | bytes 2404
  7.2 77.1 %all-gather.4.cloned.1.call-start = ((), (), s32[]{:S(2)}) async-start(), calls=%async_computation.2 | async-start | bytes 3072000 | tf_op jit(solution)/shard_map/all_gather | solution.py:526
  7.2 12.5 %collective-permute-start.3 = (bf16[3,20,20,2,128]{4,3,2,1,0:T(2,128)(2,1)}, bf16[3,20,20,2,128]{4,3,2,1,0:T(2,128)(2,1)S(1)}, u32[]{:S(2)}, u32[]{:S(2)}) collective-permute-start(bf16[3,20,20,2,128]{4,3,2,1,0:T(2,128)(2,1)} %param.11), channel_id=1, source_target_pairs={{0,0},{8,32},{16,64},{24,96},{32,8},{40,40},{48,72},{56,104},{64,1... | collective-permute-start | bytes 1843208 | tf_op jit(solution)/shard_map/ppermute | solution.py:525
  19.8 0.8 copy-start.3
  30.3 2.1 collective-permute-start.1
  30.3 13.3 %collective-permute-start = (bf16[4,48,1280]{2,1,0:T(8,128)(2,1)}, bf16[4,48,1280]{2,1,0:T(8,128)(2,1)S(1)}, u32[]{:S(2)}, u32[]{:S(2)}) collective-permute-start(bf16[4,48,1280]{2,1,0:T(8,128)(2,1)} %get-tuple-element.24), channel_id=1, source_target_pairs={{0,8},{8,0},{16,24},{24,16},{1,9},{9,1},{17,25},{25,17},{2,10},{10... | collective-permute-start | bytes 1474568 | tf_op jit(solution)/shard_map/ppermute | solution.py:492
  33.6 21.6 %collective-permute-start.2 = (bf16[4,48,1280]{2,1,0:T(8,128)(2,1)S(1)}, bf16[4,48,1280]{2,1,0:T(8,128)(2,1)S(1)}, u32[]{:S(2)}, u32[]{:S(2)}) collective-permute-start(bf16[4,48,1280]{2,1,0:T(8,128)(2,1)S(1)} %add_convert_fusion.1), channel_id=1, source_target_pairs={{0,16},{8,24},{16,0},{24,8},{1,17},{9,25},{17,1},{25,9},{2,18},{10... | collective-permute-start | bytes 1474568 | tf_op jit(solution)/shard_map/ppermute | solution.py:492
  43.6 11.6 %copy-start.6 = (bf16[4,48,1280]{2,1,0:T(8,128)(2,1)}, bf16[4,48,1280]{2,1,0:T(8,128)(2,1)S(1)}, u32[]{:S(2)}) copy-start(bf16[4,48,1280]{2,1,0:T(8,128)(2,1)S(1)} %collective-permute-done.b_ref) | copy-start | bytes 1474564
  55.2 0.8 copy-start.9
  61.3 84.4 %copy-start.1 = (bf16[320,20]{1,0:T(8,128)(2,1)S(1)}, bf16[320,20]{1,0:T(8,128)(2,1)}, u32[]{:S(2)}) copy-start(bf16[320,20]{1,0:T(8,128)(2,1)} %constant.22.clone) | copy-start | bytes 38404
  61.3 84.4 %copy-start.2 = (bf16[320,320]{1,0:T(8,128)(2,1)S(1)}, bf16[320,320]{1,0:T(8,128)(2,1)}, u32[]{:S(2)}) copy-start(bf16[320,320]{1,0:T(8,128)(2,1)} %constant.26.clone) | copy-start | bytes 614404
  129.7 7.9 %collective-permute-start.4 = (bf16[4,48,1280]{2,1,0:T(8,128)(2,1)}, bf16[4,48,1280]{2,1,0:T(8,128)(2,1)S(1)}, u32[]{:S(2)}, u32[]{:S(2)}) collective-permute-start(bf16[4,48,1280]{2,1,0:T(8,128)(2,1)} %from_lines.2.i0), channel_id=1, source_target_pairs={{0,16},{8,24},{16,0},{24,8},{1,17},{9,25},{17,1},{25,9},{2,18},{10... | collective-permute-start | bytes 1474568 | tf_op jit(solution)/shard_map/ppermute | solution.py:492
  130.6 16.2 %collective-permute-start.5 = (bf16[4,48,1280]{2,1,0:T(8,128)(2,1)}, bf16[4,48,1280]{2,1,0:T(8,128)(2,1)S(1)}, u32[]{:S(2)}, u32[]{:S(2)}) collective-permute-start(bf16[4,48,1280]{2,1,0:T(8,128)(2,1)} %from_lines.2.i0), channel_id=1, source_target_pairs={{0,8},{8,0},{16,24},{24,16},{1,9},{9,1},{17,25},{25,17},{2,10},{10... | collective-permute-start | bytes 1474568 | tf_op jit(solution)/shard_map/ppermute | solution.py:492
  137.6 9.6 %copy-start.4 = (bf16[4,48,1280]{2,1,0:T(8,128)(2,1)}, bf16[4,48,1280]{2,1,0:T(8,128)(2,1)S(1)}, u32[]{:S(2)}) copy-start(bf16[4,48,1280]{2,1,0:T(8,128)(2,1)S(1)} %collective-permute-done.4.i1) | copy-start | bytes 1474564
  137.6 9.6 %collective-permute-start.6 = (bf16[4,48,1280]{2,1,0:T(8,128)(2,1)S(1)}, bf16[4,48,1280]{2,1,0:T(8,128)(2,1)S(1)}, u32[]{:S(2)}, u32[]{:S(2)}) collective-permute-start(bf16[4,48,1280]{2,1,0:T(8,128)(2,1)S(1)} %collective-permute-done.4.i1), channel_id=1, source_target_pairs={{0,8},{8,0},{16,24},{24,16},{1,9},{9,1},{17,25},{25,17},{2,10},{10... | collective-permute-start | bytes 1474568 | tf_op jit(solution)/shard_map/ppermute | solution.py:492
  146.8 0.8 copy-start.5
  147.2 0.8 copy-start.8
  175.9 2.2 collective-permute-start.8
  176.4 3.6 %collective-permute-start.7 = (bf16[4,48,1280]{2,1,0:T(8,128)(2,1)}, bf16[4,48,1280]{2,1,0:T(8,128)(2,1)S(1)}, u32[]{:S(2)}, u32[]{:S(2)}) collective-permute-start(bf16[4,48,1280]{2,1,0:T(8,128)(2,1)} %get-tuple-element.30), channel_id=1, source_target_pairs={{0,8},{8,0},{16,24},{24,16},{1,9},{9,1},{17,25},{25,17},{2,10},{10... | collective-permute-start | bytes 1474568 | tf_op jit(solution)/shard_map/ppermute | solution.py:492
  179.2 12.5 %collective-permute-start.9 = (bf16[4,48,1280]{2,1,0:T(8,128)(2,1)S(1)}, bf16[4,48,1280]{2,1,0:T(8,128)(2,1)S(1)}, u32[]{:S(2)}, u32[]{:S(2)}) collective-permute-start(bf16[4,48,1280]{2,1,0:T(8,128)(2,1)S(1)} %add_convert_fusion), channel_id=1, source_target_pairs={{0,16},{8,24},{16,0},{24,8},{1,17},{9,25},{17,1},{25,9},{2,18},{10... | collective-permute-start | bytes 1474568 | tf_op jit(solution)/shard_map/ppermute | solution.py:492
  180.0 11.8 %copy-start.7 = (bf16[4,48,1280]{2,1,0:T(8,128)(2,1)}, bf16[4,48,1280]{2,1,0:T(8,128)(2,1)S(1)}, u32[]{:S(2)}) copy-start(bf16[4,48,1280]{2,1,0:T(8,128)(2,1)S(1)} %collective-permute-done.7.b_ref) | copy-start | bytes 1474564
  191.8 0.8 copy-start.10
  197.9 81.4 %copy-start.25 = (bf16[120,128]{1,0:T(8,128)(2,1)S(1)}, bf16[120,128]{1,0:T(8,128)(2,1)}, u32[]{:S(2)}) copy-start(bf16[120,128]{1,0:T(8,128)(2,1)} %get-tuple-element.35) | copy-start | bytes 92164
  197.9 83.3 %copy-start.24 = (bf16[120,128]{1,0:T(8,128)(2,1)S(1)}, bf16[120,128]{1,0:T(8,128)(2,1)}, u32[]{:S(2)}) copy-start(bf16[120,128]{1,0:T(8,128)(2,1)} %get-tuple-element.36) | copy-start | bytes 92164
  197.9 83.4 %copy-start.23 = (bf16[120,128]{1,0:T(8,128)(2,1)S(1)}, bf16[120,128]{1,0:T(8,128)(2,1)}, u32[]{:S(2)}) copy-start(bf16[120,128]{1,0:T(8,128)(2,1)} %get-tuple-element.37) | copy-start | bytes 92164
  197.9 86.6 %copy-start.22 = (bf16[120,128]{1,0:T(8,128)(2,1)S(1)}, bf16[120,128]{1,0:T(8,128)(2,1)}, u32[]{:S(2)}) copy-start(bf16[120,128]{1,0:T(8,128)(2,1)} %get-tuple-element.38) | copy-start | bytes 92164
  263.1 8.1 %collective-permute-start.10 = (bf16[4,48,1280]{2,1,0:T(8,128)(2,1)}, bf16[4,48,1280]{2,1,0:T(8,128)(2,1)S(1)}, u32[]{:S(2)}, u32[]{:S(2)}) collective-permute-start(bf16[4,48,1280]{2,1,0:T(8,128)(2,1)} %from_lines.3.i0), channel_id=1, source_target_pairs={{0,16},{8,24},{16,0},{24,8},{1,17},{9,25},{17,1},{25,9},{2,18},{10... | collective-permute-start | bytes 1474568 | tf_op jit(solution)/shard_map/ppermute | solution.py:492
  263.7 40.0 %collective-permute-start.11 = (bf16[4,48,1280]{2,1,0:T(8,128)(2,1)}, bf16[4,48,1280]{2,1,0:T(8,128)(2,1)S(1)}, u32[]{:S(2)}, u32[]{:S(2)}) collective-permute-start(bf16[4,48,1280]{2,1,0:T(8,128)(2,1)} %from_lines.3.i0), channel_id=1, source_target_pairs={{0,8},{8,0},{16,24},{24,16},{1,9},{9,1},{17,25},{25,17},{2,10},{10... | collective-permute-start | bytes 1474568 | tf_op jit(solution)/shard_map/ppermute | solution.py:492
  271.1 32.6 %copy-start.11 = (bf16[4,48,1280]{2,1,0:T(8,128)(2,1)}, bf16[4,48,1280]{2,1,0:T(8,128)(2,1)S(1)}, u32[]{:S(2)}) copy-start(bf16[4,48,1280]{2,1,0:T(8,128)(2,1)S(1)} %collective-permute-done.10.i1) | copy-start | bytes 1474564
  271.1 32.6 %collective-permute-start.12 = (bf16[4,48,1280]{2,1,0:T(8,128)(2,1)S(1)}, bf16[4,48,1280]{2,1,0:T(8,128)(2,1)S(1)}, u32[]{:S(2)}, u32[]{:S(2)}) collective-permute-start(bf16[4,48,1280]{2,1,0:T(8,128)(2,1)S(1)} %collective-permute-done.10.i1), channel_id=1, source_target_pairs={{0,8},{8,0},{16,24},{24,16},{1,9},{9,1},{17,25},{25,17},{2,10},{10... | collective-permute-start | bytes 1474568 | tf_op jit(solution)/shard_map/ppermute | solution.py:492
  279.2 5.2 %collective-permute-start.13 = (bf16[120,128]{1,0:T(8,128)(2,1)S(1)}, bf16[120,128]{1,0:T(8,128)(2,1)S(1)}, u32[]{:S(2)}, u32[]{:S(2)}) collective-permute-start(bf16[120,128]{1,0:T(8,128)(2,1)S(1)} %copy-done.25), channel_id=1, source_target_pairs={{0,0},{8,32},{16,64},{24,96},{32,8},{40,40},{48,72},{56,104},{64,1... | collective-permute-start | bytes 92168 | tf_op jit(solution)/shard_map/ppermute | solution.py:516
  281.2 5.4 %collective-permute-start.14 = (bf16[120,128]{1,0:T(8,128)(2,1)S(1)}, bf16[120,128]{1,0:T(8,128)(2,1)S(1)}, u32[]{:S(2)}, u32[]{:S(2)}) collective-permute-start(bf16[120,128]{1,0:T(8,128)(2,1)S(1)} %copy-done.24), channel_id=1, source_target_pairs={{0,8},{8,40},{16,72},{24,104},{32,16},{40,48},{48,80},{56,112},{64... | collective-permute-start | bytes 92168 | tf_op jit(solution)/shard_map/ppermute | solution.py:516
  281.3 8.4 %collective-permute-start.15 = (bf16[120,128]{1,0:T(8,128)(2,1)S(1)}, bf16[120,128]{1,0:T(8,128)(2,1)S(1)}, u32[]{:S(2)}, u32[]{:S(2)}) collective-permute-start(bf16[120,128]{1,0:T(8,128)(2,1)S(1)} %copy-done.23), channel_id=1, source_target_pairs={{0,16},{8,48},{16,80},{24,112},{32,24},{40,56},{48,88},{56,120},{6... | collective-permute-start | bytes 92168 | tf_op jit(solution)/shard_map/ppermute | solution.py:516
  284.4 15.6 %copy-start.14 = (bf16[120,128]{1,0:T(8,128)(2,1)}, bf16[120,128]{1,0:T(8,128)(2,1)S(1)}, u32[]{:S(2)}) copy-start(bf16[120,128]{1,0:T(8,128)(2,1)S(1)} %collective-permute-done.13.s0) | copy-start | bytes 92164
  284.4 6.3 %collective-permute-start.16 = (bf16[120,128]{1,0:T(8,128)(2,1)S(1)}, bf16[120,128]{1,0:T(8,128)(2,1)S(1)}, u32[]{:S(2)}, u32[]{:S(2)}) collective-permute-start(bf16[120,128]{1,0:T(8,128)(2,1)S(1)} %copy-done.22), channel_id=1, source_target_pairs={{0,24},{8,56},{16,88},{24,120},{32,0},{40,32},{48,64},{56,96},{64,... | collective-permute-start | bytes 92168 | tf_op jit(solution)/shard_map/ppermute | solution.py:516
  286.6 13.4 %copy-start.15 = (bf16[120,128]{1,0:T(8,128)(2,1)}, bf16[120,128]{1,0:T(8,128)(2,1)S(1)}, u32[]{:S(2)}) copy-start(bf16[120,128]{1,0:T(8,128)(2,1)S(1)} %collective-permute-done.14.s1) | copy-start | bytes 92164
  286.6 5.6 %collective-permute-start.17 = (bf16[120,128]{1,0:T(8,128)(2,1)}, bf16[120,128]{1,0:T(8,128)(2,1)S(1)}, u32[]{:S(2)}, u32[]{:S(2)}) collective-permute-start(bf16[120,128]{1,0:T(8,128)(2,1)} %get-tuple-element.39), channel_id=1, source_target_pairs={{0,0},{8,32},{16,64},{24,96},{32,8},{40,40},{48,72},{56,104},{64,1... | collective-permute-start | bytes 92168 | tf_op jit(solution)/shard_map/ppermute | solution.py:516
  289.7 10.3 %copy-start.16 = (bf16[120,128]{1,0:T(8,128)(2,1)}, bf16[120,128]{1,0:T(8,128)(2,1)S(1)}, u32[]{:S(2)}) copy-start(bf16[120,128]{1,0:T(8,128)(2,1)S(1)} %collective-permute-done.15.s2) | copy-start | bytes 92164
  289.7 8.9 %collective-permute-start.18 = (bf16[120,128]{1,0:T(8,128)(2,1)}, bf16[120,128]{1,0:T(8,128)(2,1)S(1)}, u32[]{:S(2)}, u32[]{:S(2)}) collective-permute-start(bf16[120,128]{1,0:T(8,128)(2,1)} %get-tuple-element.40), channel_id=1, source_target_pairs={{0,8},{8,40},{16,72},{24,104},{32,16},{40,48},{48,80},{56,112},{64... | collective-permute-start | bytes 92168 | tf_op jit(solution)/shard_map/ppermute | solution.py:516
  290.7 9.3 %copy-start.17 = (bf16[120,128]{1,0:T(8,128)(2,1)}, bf16[120,128]{1,0:T(8,128)(2,1)S(1)}, u32[]{:S(2)}) copy-start(bf16[120,128]{1,0:T(8,128)(2,1)S(1)} %collective-permute-done.16.s3) | copy-start | bytes 92164
  290.7 7.9 %collective-permute-start.19 = (bf16[120,128]{1,0:T(8,128)(2,1)}, bf16[120,128]{1,0:T(8,128)(2,1)S(1)}, u32[]{:S(2)}, u32[]{:S(2)}) collective-permute-start(bf16[120,128]{1,0:T(8,128)(2,1)} %get-tuple-element.41), channel_id=1, source_target_pairs={{0,16},{8,48},{16,80},{24,112},{32,24},{40,56},{48,88},{56,120},{6... | collective-permute-start | bytes 92168 | tf_op jit(solution)/shard_map/ppermute | solution.py:516
  292.2 7.8 %copy-start.18 = (bf16[120,128]{1,0:T(8,128)(2,1)}, bf16[120,128]{1,0:T(8,128)(2,1)S(1)}, u32[]{:S(2)}) copy-start(bf16[120,128]{1,0:T(8,128)(2,1)S(1)} %collective-permute-done.17.g0) | copy-start | bytes 92164
  292.2 7.8 %collective-permute-start.20 = (bf16[120,128]{1,0:T(8,128)(2,1)}, bf16[120,128]{1,0:T(8,128)(2,1)S(1)}, u32[]{:S(2)}, u32[]{:S(2)}) collective-permute-start(bf16[120,128]{1,0:T(8,128)(2,1)} %get-tuple-element.42), channel_id=1, source_target_pairs={{0,24},{8,56},{16,88},{24,120},{32,0},{40,32},{48,64},{56,96},{64,... | collective-permute-start | bytes 92168 | tf_op jit(solution)/shard_map/ppermute | solution.py:516
  298.6 1.4 copy-start.19
  298.6 1.4 copy-start.20
  300.1 0.6 copy-start.21
  303.7 0.8 copy-start.12
  303.8 0.9 copy-start.13
Sparse Core Ops, SparseCore 0:
  20.7 44.2 all-gather.3
where the time goes:
time: 330 us; the launch traced here: 327 us
  blocking collectives  113 us (34%)
  Pallas kernels  87.1 us (26%)
  starting transfers between devices  65.5 us (20%)
  waiting for transfers between devices  37.7 us (11%)
  between operations  14.2 us (4%)
  local copies, waits for them, and re-layouts  4.79 us (1%)
    ppermute x12, starting transfers between devices, swap(): return lax.ppermute(values, 'gx', [(i, i ^ bit) for i in range(GX)])  44.1 us
    all_to_all x2, blocking collectives, exchange_lines(): return lax.all_to_all(parts, 'gy', split_axis=0, concat_axis=0, tiled=True)  42.7 us
    all_gather x1, blocking collectives, per_device(): lax.all_gather(mode_out, 'gy', axis=0)  35.2 us
    all_gather x1, blocking collectives, per_device(): lax.all_gather(mode_back, 'gy', axis=0)  35 us
    pallas_call x1, Pallas kernels, middle_columns(): pl.pallas_call(middle_kernel, grid_spec=pltpu.PrefetchScalarGridSpec(num_...  27.9 us
    ppermute x12, waiting for transfers between devices, swap(): return lax.ppermute(values, 'gx', [(i, i ^ bit) for i in range(GX)])  26.9 us
    ppermute x8, starting transfers between devices, to_owners(): moved.append(lax.ppermute(chunk, ('dp', 'gx'), pairs))  16.9 us
    pallas_call x1, Pallas kernels, end_columns(): pl.pallas_call(end_kernel, grid_spec=pltpu.PrefetchScalarGridSpec(num_sca...  15.7 us
  transfers between devices with their start and end apart: 22, of which 9 were waited for; matrix products, arithmetic and copies ran while one was open for 2% of the time, Pallas kernels for 5%

commit v1 on v0

--- a/solution.py
+++ b/solution.py
@@ -365,7 +365,9 @@
             sum_ref[(2 + part) * SETS : (3 + part) * SETS, lanes] = jnp.where(
                 low, pltpu.roll(even, HALF, 1), odd
             )
-    out_ref[...] = sum_ref[...].astype(BF)
+    modes = sum_ref[...].astype(BF)
+    for owner in range(GY):
+        out_ref[owner] = modes
 
 
 def fold_scale(where_ref):
@@ -387,7 +389,14 @@
         outs[k][...] = modes_ref[pl.ds(start, KB * PAIR), :].astype(BF)
 
 
-def mix_kernel(where_ref, arrived_ref, weight_ref, out_ref, u0, u1, u2, u3, sum_ref, in_ref, mix_ref):
+def set_row(where_ref, k):
+    block = lax.rem(where_ref[0] + k, DP) * KB + pl.program_id(0)
+    return pl.multiple_of(block * PAIR, 8)
+
+
+def mix_kernel(
+    where_ref, arrived_ref, w0, w1, w2, w3, out_ref, u0, u1, u2, u3, sum_ref, in_ref, mix_ref
+):
     step = pl.program_id(0)
 
     @pl.when(step == 0)
@@ -395,23 +404,24 @@
         gather_modes(arrived_ref, sum_ref, in_ref)
         hand_out(where_ref, in_ref, (u0, u1, u2, u3))
 
-    @pl.loop(0, KB)
-    def _(i):
-        base = pl.multiple_of((step * KB + i) * PAIR, 8)
+    for k, weight_ref in enumerate((w0, w1, w2, w3)):
+        base = set_row(where_ref, k)
         by_real = jnp.zeros((PAIR, 2 * HALF), F32)
         by_imag = jnp.zeros((PAIR, 2 * HALF), F32)
         for c in range(CH):
-            weight = weight_ref[i, c].astype(F32)
+            weight = weight_ref[0, c].astype(F32)
             by_real = by_real + weight * in_ref[pl.ds(base + 2 * c, 1), :]
             by_imag = by_imag + weight * in_ref[pl.ds(base + 2 * c + 1, 1), :]
         mix_ref[pl.ds(base, PAIR), :] = (by_real + turned(by_imag)).astype(BF).astype(F32)
 
-    @pl.when(step == DP - 1)
+    @pl.when(step == KB - 1)
     def _():
         spread_modes(mix_ref, sum_ref, out_ref, fold_scale(where_ref))
 
 
-def back_kernel(where_ref, arrived_ref, weight_ref, out_ref, u0, u1, u2, u3, sum_ref, in_ref, mix_ref):
+def back_kernel(
+    where_ref, arrived_ref, w0, w1, w2, w3, out_ref, u0, u1, u2, u3, sum_ref, in_ref, mix_ref
+):
     step = pl.program_id(0)
 
     @pl.when(step == 0)
@@ -419,43 +429,40 @@
         gather_modes(arrived_ref, sum_ref, in_ref, fold_scale(where_ref))
         hand_out(where_ref, in_ref, (u0, u1, u2, u3))
 
-    @pl.loop(0, KB)
-    def _(i):
-        base = pl.multiple_of((step * KB + i) * PAIR, 8)
+    for k, weight_ref in enumerate((w0, w1, w2, w3)):
+        base = set_row(where_ref, k)
         grad = in_ref[pl.ds(base, PAIR), :]
         other = -turned(grad)
         for c in range(CH):
-            weight = weight_ref[i, c].astype(F32)
+            weight = weight_ref[0, c].astype(F32)
             mix_ref[pl.ds(base + 2 * c, 1), :] = jnp.sum(weight * grad, axis=0, keepdims=True)
             mix_ref[pl.ds(base + 2 * c + 1, 1), :] = jnp.sum(weight * other, axis=0, keepdims=True)
 
-    @pl.when(step == DP - 1)
+    @pl.when(step == KB - 1)
     def _():
         spread_modes(mix_ref, sum_ref, out_ref)
 
 
-def mode_call(kernel, name, where, arrived, weight):
+def mode_call(kernel, name, where, arrived, weights):
     chunk = pl.BlockSpec((KB * PAIR, 2 * HALF), lambda i, w: (0, 0))
     return pl.pallas_call(
         kernel,
         grid_spec=pltpu.PrefetchScalarGridSpec(
             num_scalar_prefetch=1,
-            grid=(DP,),
-            in_specs=[
-                pl.BlockSpec((GY, 48, WIDE), lambda i, w: (0, 0, 0)),
-                pl.BlockSpec((KB, CH, PAIR, 2 * HALF), lambda i, w: (i, 0, 0, 0)),
-            ],
-            out_specs=[pl.BlockSpec((48, WIDE), lambda i, w: (0, 0))] + [chunk] * 4,
+            grid=(KB,),
+            in_specs=[pl.BlockSpec((GY, 48, WIDE), lambda i, w: (0, 0, 0))]
+            + [pl.BlockSpec((1, CH, PAIR, 2 * HALF), lambda i, w: (i, 0, 0, 0))] * 4,
+            out_specs=[pl.BlockSpec((GY, 48, WIDE), lambda i, w: (0, 0, 0))] + [chunk] * 4,
             scratch_shapes=[
                 pltpu.VMEM((48, WIDE), F32),
                 pltpu.VMEM((SETS * PAIR, 2 * HALF), F32),
                 pltpu.VMEM((SETS * PAIR, 2 * HALF), F32),
             ],
         ),
-        out_shape=[jax.ShapeDtypeStruct((48, WIDE), BF)]
+        out_shape=[jax.ShapeDtypeStruct((GY, 48, WIDE), BF)]
         + [jax.ShapeDtypeStruct((KB * PAIR, 2 * HALF), BF)] * 4,
         name=name,
-    )(where, arrived, weight)
+    )(where, arrived, *weights)
 
 
 def outer_kernel(s0, s1, s2, s3, g0, g1, g2, g3, out_ref, spec_ref):
@@ -492,10 +499,17 @@
     return lax.ppermute(values, "gx", [(i, i ^ bit) for i in range(GX)])
 
 
-def reduce_slabs(where, pieces):
+def start_slabs(pieces):
     own, far, near, across = pieces
     far_sum = (far.astype(F32) + swap(across, 1).astype(F32)).astype(BF)
-    return to_lines(where, own, swap(near, 1), swap(far_sum, 2))
+    return own, swap(near, 1), swap(far_sum, 2)
+
+
+def gather_weights(weight):
+    held = [weight]
+    for k in range(1, DP):
+        held.append(lax.ppermute(weight, "dp", [((a + k) % DP, a) for a in range(DP)]))
+    return [part.reshape(KB, CH, PAIR, 2 * HALF) for part in held]
 
 
 def share_slabs(own):
@@ -523,8 +537,6 @@
     ).astype(jnp.int32)
     turn = [(a * GX + b, b * GX + a) for a in range(DP) for b in range(GX)]
     weight = lax.ppermute(spectral_weight, ("dp", "gx"), turn)
-    weight = lax.all_gather(weight, "dp", axis=0, tiled=True)
-    weight = weight.reshape(KZ, CH, PAIR, 2 * HALF)
     spread = jnp.asarray(SPREAD)
 
     def mixer_of(matrix):
@@ -532,17 +544,21 @@
         return wide.astype(BF) * jnp.asarray(SAME)
 
     values = field[0]
-    lines = reduce_slabs(where, start_columns(where, values))
-    mode_out, *spectra = mode_call(mix_kernel, "mix_modes", where, exchange_lines(lines), weight)
-    coeffs = share_slabs(from_lines(where, lax.all_gather(mode_out, "gy", axis=0)))
-    spectra = to_owners(spectra)
+    own, *others = start_slabs(start_columns(where, values))
+    weight, *others = lax.optimization_barrier((weight, *others))
+    weights = gather_weights(weight)
+    arrived = exchange_lines(to_lines(where, own, *others))
+    modes, *spectra = mode_call(mix_kernel, "mix_modes", where, arrived, weights)
+    modes, *spectra = lax.optimization_barrier((exchange_lines(modes), *to_owners(spectra)))
+    coeffs = share_slabs(from_lines(where, modes))
     activation, grad, *pieces = middle_columns(
         where, bias, coeffs, values, cotangent[0], mixer_of(bypass_weight)
     )
-    lines = reduce_slabs(where, pieces)
-    mode_back, *grads = mode_call(back_kernel, "back_modes", where, exchange_lines(lines), weight)
-    coeffs = share_slabs(from_lines(where, lax.all_gather(mode_back, "gy", axis=0)))
-    weight_grad = outer_sum(spectra, to_owners(grads))
+    arrived = exchange_lines(to_lines(where, *start_slabs(pieces)))
+    modes, *grads = mode_call(back_kernel, "back_modes", where, arrived, weights)
+    modes, *grads = lax.optimization_barrier((exchange_lines(modes), *to_owners(grads)))
+    coeffs = share_slabs(from_lines(where, modes))
+    weight_grad = outer_sum(spectra, grads)
     field_grad = end_columns(where, coeffs, grad, mixer_of(bypass_weight.T))
     return (
         activation[None],

time: 330 us -> 276 us (0.84)
  blocking collectives: 113 us -> 21.8 us
  waiting for transfers between devices: 37.7 us -> 83.3 us
  between operations: 14.2 us -> 0.9 us
    all_gather x2 -> x0, blocking collectives: 70.2 us -> none  [the longest x1 35.2 us: per_device(): lax.all_gather(mode_out, 'gy', axis=0)]
    ppermute x0 -> x3, waiting for transfers between devices: none -> 25.6 us  [gather_weights(): lax.ppermute(weight, 'dp', [((a + k) % DP, a) for a in range(DP)])]
    all_to_all x2 -> x1, blocking collectives: 42.7 us -> 21.8 us  [exchange_lines(): return lax.all_to_all(parts, 'gy', split_axis=0, concat_axis=0, tiled=True)]
    ppermute x12, starting transfers between devices: 44.1 us -> 24.5 us  [swap(): return lax.ppermute(values, 'gx', [(i, i ^ bit) for i in range(GX)])]
    all_to_all x0 -> x3, starting transfers between devices: none -> 17.4 us  [exchange_lines(): return lax.all_to_all(parts, 'gy', split_axis=0, concat_axis=0, tiled=True)]
    ppermute x12, waiting for transfers between devices: 26.9 us -> 41.2 us  [swap(): return lax.ppermute(values, 'gx', [(i, i ^ bit) for i in range(GX)])]
    ppermute x8, waiting for transfers between devices: 2.74 us -> 10.2 us  [to_owners(): moved.append(lax.ppermute(chunk, ('dp', 'gx'), pairs))]
    ppermute x0 -> x3, starting transfers between devices: none -> 4.78 us  [gather_weights(): lax.ppermute(weight, 'dp', [((a + k) % DP, a) for a in range(DP)])]
  transfers between devices with their start and end apart: 22 -> 27, of which waited for: 9 -> 13; matrix products, arithmetic and copies ran while one was open for 2% -> 2% of each run, Pallas kernels for 5% -> 1%
where the time goes in v1:
time: 276 us; the launch traced here: 274 us
  Pallas kernels  88.1 us (32%)
  waiting for transfers between devices  83.3 us (30%)
  starting transfers between devices  66.6 us (24%)
  blocking collectives  21.8 us (8%)
  local copies, waits for them, and re-layouts  6.73 us (2%)
  matrix products  3.07 us (1%)
  other arithmetic  3.02 us (1%)
    ppermute x12, waiting for transfers between devices, swap(): return lax.ppermute(values, 'gx', [(i, i ^ bit) for i in range(GX)])  41.2 us
    pallas_call x1, Pallas kernels, middle_columns(): pl.pallas_call(middle_kernel, grid_spec=pltpu.PrefetchScalarGridSpec(num_...  27.9 us
    ppermute x3, waiting for transfers between devices, gather_weights(): lax.ppermute(weight, 'dp', [((a + k) % DP, a) for a in range(DP)])  25.6 us
    ppermute x12, starting transfers between devices, swap(): return lax.ppermute(values, 'gx', [(i, i ^ bit) for i in range(GX)])  24.5 us
    all_to_all x1, blocking collectives, exchange_lines(): return lax.all_to_all(parts, 'gy', split_axis=0, concat_axis=0, tiled=True)  21.8 us
    all_to_all x3, starting transfers between devices, exchange_lines(): return lax.all_to_all(parts, 'gy', split_axis=0, concat_axis=0, tiled=True)  17.4 us
    ppermute x8, starting transfers between devices, to_owners(): moved.append(lax.ppermute(chunk, ('dp', 'gx'), pairs))  16.9 us
    pallas_call x1, Pallas kernels, end_columns(): pl.pallas_call(end_kernel, grid_spec=pltpu.PrefetchScalarGridSpec(num_sca...  15.7 us
  transfers between devices with their start and end apart: 27, of which 13 were waited for; matrix products, arithmetic and copies ran while one was open for 2% of the time, Pallas kernels for 1%

profile of v1, /device:TPU:1, one launch (start us, length us, event | category | flops | bytes accessed | tf_op | source)
XLA Modules:
  0.0 273.6 jit_solution(10636219179291578285)
XLA Ops:
  1.3 9.1 %start_columns.1 = (bf16[4,48,1280]{2,1,0:T(8,128)(2,1)}, bf16[4,48,1280]{2,1,0:T(8,128)(2,1)}, bf16[4,48,1280]{2,1,0:T(8,128)(2,1)}, bf16[4,48,1280]{2,1,0:T(8,128)(2,1)}) custom-call(s32[3]{0:T(128)} %pad_add_fusion.where_ref, bf16[20,64,2048]{2,1,0:T(8,128)(2,1)} %bitcast.18, bf16[4,192,512]{2,1,0:T(8,128)(2,1)} %constant.23.clone.depth_ref, ...), custom_call_target="tpu_custom_call" | custom-call | tf_op jit(solution)/shard_map/start_columns/pallas_call | solution.py:230
  10.5 1.4 collective-permute-start.2
  11.9 3.1 %collective-permute-start = (bf16[3,20,20,2,128]{4,3,2,1,0:T(2,128)(2,1)S(1)}, bf16[3,20,20,2,128]{4,3,2,1,0:T(2,128)(2,1)S(1)}, u32[]{:S(2)}, u32[]{:S(2)}) collective-permute-start(bf16[3,20,20,2,128]{4,3,2,1,0:T(2,128)(2,1)S(1)} %copy-done.28), channel_id=1, source_target_pairs={{0,0},{8,32},{16,64},{24,96},{32,8},{40,40},{48,72},{56,104},{64,1... | collective-permute-start | bytes 1843208 | tf_op jit(solution)/shard_map/ppermute | solution.py:539
  15.1 1.2 add_convert_fusion.1
  16.3 3.2 %collective-permute-start.3 = (bf16[4,48,1280]{2,1,0:T(8,128)(2,1)S(1)}, bf16[4,48,1280]{2,1,0:T(8,128)(2,1)S(1)}, u32[]{:S(2)}, u32[]{:S(2)}) collective-permute-start(bf16[4,48,1280]{2,1,0:T(8,128)(2,1)S(1)} %add_convert_fusion.1), channel_id=1, source_target_pairs={{0,16},{8,24},{16,0},{24,8},{1,17},{9,25},{17,1},{25,9},{2,18},{10... | collective-permute-start | bytes 1474568 | tf_op jit(solution)/shard_map/ppermute | solution.py:499
  19.4 4.2 %collective-permute-done = bf16[3,20,20,2,128]{4,3,2,1,0:T(2,128)(2,1)S(1)} collective-permute-done((bf16[3,20,20,2,128]{4,3,2,1,0:T(2,128)(2,1)S(1)}, bf16[3,20,20,2,128]{4,3,2,1,0:T(2,128)(2,1)S(1)}, u32[]{:S(2)}, u32[]{:S(2)}) %collective-permute-start) | collective-permute-done | bytes 614432 | tf_op jit(solution)/shard_map/ppermute | solution.py:539
  23.6 18.4 %collective-permute-done.3.c_ref = bf16[4,48,1280]{2,1,0:T(8,128)(2,1)S(1)} collective-permute-done((bf16[4,48,1280]{2,1,0:T(8,128)(2,1)S(1)}, bf16[4,48,1280]{2,1,0:T(8,128)(2,1)S(1)}, u32[]{:S(2)}, u32[]{:S(2)}) %collective-permute-start.3) | collective-permute-done | bytes 491552 | tf_op jit(solution)/shard_map/ppermute | solution.py:499
  42.8 5.3 %to_lines.2 = bf16[8,48,1280]{2,1,0:T(8,128)(2,1)} custom-call(s32[3]{0:T(128)} %pad_add_fusion.where_ref, bf16[4,48,1280]{2,1,0:T(8,128)(2,1)} %get-tuple-element.36.a_ref, bf16[4,48,1280]{2,1,0:T(8,128)(2,1)} %copy-done.11, bf16[4,48,1280]{2,1,0:T(8,128)(2,1)} %copy-done.15, bf16[8,384,192]{2,1,0:T(8,128)(2,1)} %constant.25.clone.table_ref), custom_call_target="tpu_custom_call" | custom-call | tf_op jit(solution)/shard_map/to_lines/pallas_call | solution.py:290
  48.1 7.5 %all-to-all-start = ((bf16[8,48,1280]{2,1,0:T(8,128)(2,1)}), bf16[8,48,1280]{2,1,0:T(8,128)(2,1)S(1)}, u32[]{:S(2)}, u32[]{:S(2)}) async-start(bf16[8,48,1280]{2,1,0:T(8,128)(2,1)} %to_lines.2), calls=%async_computation | async-start | bytes 1966080 | tf_op jit(solution)/shard_map/all_to_all | solution.py:521
  55.6 4.1 %collective-permute-start.5 = (bf16[3,20,20,2,128]{4,3,2,1,0:T(2,128)(2,1)S(1)}, bf16[3,20,20,2,128]{4,3,2,1,0:T(2,128)(2,1)S(1)}, u32[]{:S(2)}, u32[]{:S(2)}) collective-permute-start(bf16[3,20,20,2,128]{4,3,2,1,0:T(2,128)(2,1)S(1)} %collective-permute-done), channel_id=1, source_target_pairs={{64,0},{96,32},{0,64},{32,96},{65,1},{97,33},{1,65},{33,97},{66,2}... | collective-permute-start | bytes 1843208 | tf_op jit(solution)/shard_map/ppermute | solution.py:511
  60.4 11.6 %collective-permute-done.6 = bf16[3,20,20,2,128]{4,3,2,1,0:T(2,128)(2,1)S(1)} collective-permute-done((bf16[3,20,20,2,128]{4,3,2,1,0:T(2,128)(2,1)S(1)}, bf16[3,20,20,2,128]{4,3,2,1,0:T(2,128)(2,1)S(1)}, u32[]{:S(2)}, u32[]{:S(2)}) %collective-permute-start.6) | collective-permute-done | bytes 614432 | tf_op jit(solution)/shard_map/ppermute | solution.py:511
  72.0 14.0 %collective-permute-done.5 = bf16[3,20,20,2,128]{4,3,2,1,0:T(2,128)(2,1)S(1)} collective-permute-done((bf16[3,20,20,2,128]{4,3,2,1,0:T(2,128)(2,1)S(1)}, bf16[3,20,20,2,128]{4,3,2,1,0:T(2,128)(2,1)S(1)}, u32[]{:S(2)}, u32[]{:S(2)}) %collective-permute-start.5) | collective-permute-done | bytes 614432 | tf_op jit(solution)/shard_map/ppermute | solution.py:511
  87.4 5.7 %mix_modes.1 = (bf16[8,48,1280]{2,1,0:T(8,128)(2,1)}, bf16[120,128]{1,0:T(8,128)(2,1)}, bf16[120,128]{1,0:T(8,128)(2,1)}, bf16[120,128]{1,0:T(8,128)(2,1)}, bf16[120,128]{1,0:T(8,128)(2,1)}) custom-call(s32[3]{0:T(128)} %pad_add_fusion.where_ref, bf16[8,48,1280]{2,1,0:T(8,128)(2,1)} %copy-done.3, bf16[3,20,40,128]{3,2,1,0:T(8,128)(2,1)} %bitcast.22, ...), custom_call_target="tpu_custom_call" | custom-call | tf_op jit(solution)/shard_map/mix_modes/pallas_call | solution.py:448
  93.1 6.3 %all-to-all-start.1 = ((bf16[8,48,1280]{2,1,0:T(8,128)(2,1)}), bf16[8,48,1280]{2,1,0:T(8,128)(2,1)S(1)}, u32[]{:S(2)}, u32[]{:S(2)}) async-start(bf16[8,48,1280]{2,1,0:T(8,128)(2,1)} %get-tuple-element.43), calls=%async_computation.1 | async-start | bytes 1966080 | tf_op jit(solution)/shard_map/all_to_all | solution.py:521
  99.4 4.7 %collective-permute-start.7 = (bf16[120,128]{1,0:T(8,128)(2,1)}, bf16[120,128]{1,0:T(8,128)(2,1)S(1)}, u32[]{:S(2)}, u32[]{:S(2)}) collective-permute-start(bf16[120,128]{1,0:T(8,128)(2,1)} %get-tuple-element.44), channel_id=1, source_target_pairs={{0,0},{8,32},{16,64},{24,96},{32,8},{40,40},{48,72},{56,104},{64,1... | collective-permute-start | bytes 92168 | tf_op jit(solution)/shard_map/ppermute | solution.py:530
  104.3 2.6 collective-permute-start.10
  106.9 2.5 collective-permute-done.9.s2
  109.4 2.6 collective-permute-done.10.s3
  112.0 2.0 all-to-all-done.1.modes_ref
  114.0 0.9 copy-done.2
  115.0 5.0 %from_lines.2.i0 = bf16[4,48,1280]{2,1,0:T(8,128)(2,1)} custom-call(s32[3]{0:T(128)} %pad_add_fusion.where_ref, bf16[8,48,1280]{2,1,0:T(8,128)(2,1)} %copy-done.2, bf16[8,384,192]{2,1,0:T(8,128)(2,1)} %constant.25.clone.table_ref), custom_call_target="tpu_custom_call" | custom-call | tf_op jit(solution)/shard_map/from_lines/pallas_call | solution.py:310
  120.0 1.5 collective-permute-start.11
  121.5 3.0 %collective-permute-start.12 = (bf16[4,48,1280]{2,1,0:T(8,128)(2,1)}, bf16[4,48,1280]{2,1,0:T(8,128)(2,1)S(1)}, u32[]{:S(2)}, u32[]{:S(2)}) collective-permute-start(bf16[4,48,1280]{2,1,0:T(8,128)(2,1)} %from_lines.2.i0), channel_id=1, source_target_pairs={{0,8},{8,0},{16,24},{24,16},{1,9},{9,1},{17,25},{25,17},{2,10},{10... | collective-permute-start | bytes 1474568 | tf_op jit(solution)/shard_map/ppermute | solution.py:499
  124.5 5.1 %collective-permute-done.11.i1 = bf16[4,48,1280]{2,1,0:T(8,128)(2,1)S(1)} collective-permute-done((bf16[4,48,1280]{2,1,0:T(8,128)(2,1)}, bf16[4,48,1280]{2,1,0:T(8,128)(2,1)S(1)}, u32[]{:S(2)}, u32[]{:S(2)}) %collective-permute-start.11) | collective-permute-done | bytes 491552 | tf_op jit(solution)/shard_map/ppermute | solution.py:499
  129.6 4.3 %collective-permute-start.13 = (bf16[4,48,1280]{2,1,0:T(8,128)(2,1)S(1)}, bf16[4,48,1280]{2,1,0:T(8,128)(2,1)S(1)}, u32[]{:S(2)}, u32[]{:S(2)}) collective-permute-start(bf16[4,48,1280]{2,1,0:T(8,128)(2,1)S(1)} %collective-permute-done.11.i1), channel_id=1, source_target_pairs={{0,8},{8,0},{16,24},{24,16},{1,9},{9,1},{17,25},{25,17},{2,10},{10... | collective-permute-start | bytes 1474568 | tf_op jit(solution)/shard_map/ppermute | solution.py:499
  133.9 2.0 fusion.mixer_ref
  136.9 27.9 %middle_columns.1 = (bf16[20,64,2048]{2,1,0:T(8,128)(2,1)}, bf16[20,64,2048]{2,1,0:T(8,128)(2,1)}, bf16[4,48,1280]{2,1,0:T(8,128)(2,1)}, bf16[4,48,1280]{2,1,0:T...) custom-call(s32[3]{0:T(128)} %pad_add_fusion.where_ref, f32[20]{0:T(128)} %bias_ref.1, ...), custom_call_target="tpu_custom_call" | custom-call | tf_op jit(solution)/shard_map/middle_columns/pallas_call | solution.py:247
  165.4 1.6 collective-permute-done.15
  167.0 1.2 add_convert_fusion
  168.1 1.5 collective-permute-start.16
  169.7 11.2 %collective-permute-done.16.c_ref = bf16[4,48,1280]{2,1,0:T(8,128)(2,1)S(1)} collective-permute-done((bf16[4,48,1280]{2,1,0:T(8,128)(2,1)S(1)}, bf16[4,48,1280]{2,1,0:T(8,128)(2,1)S(1)}, u32[]{:S(2)}, u32[]{:S(2)}) %collective-permute-start.16) | collective-permute-done | bytes 491552 | tf_op jit(solution)/shard_map/ppermute | solution.py:499
  181.6 5.3 %to_lines.3 = bf16[8,48,1280]{2,1,0:T(8,128)(2,1)} custom-call(s32[3]{0:T(128)} %pad_add_fusion.where_ref, bf16[4,48,1280]{2,1,0:T(8,128)(2,1)} %get-tuple-element.50.a_ref, bf16[4,48,1280]{2,1,0:T(8,128)(2,1)} %copy-done.13, bf16[4,48,1280]{2,1,0:T(8,128)(2,1)} %copy-done.16, bf16[8,384,192]{2,1,0:T(8,128)(2,1)} %constant.25.clone.table_ref), custom_call_target="tpu_custom_call" | custom-call | tf_op jit(solution)/shard_map/to_lines/pallas_call | solution.py:290
  186.9 21.8 %all_to_all.20.arrived_ref = bf16[8,48,1280]{2,1,0:T(8,128)(2,1)} all-to-all(bf16[8,48,1280]{2,1,0:T(8,128)(2,1)} %to_lines.3), channel_id=1, replica_groups=mesh['dp'=4,'gx'=4,'gy'=8] {'gy'}, dimensions={0} | all-to-all | bytes 1966080 | tf_op jit(solution)/shard_map/all_to_all | solution.py:521
  208.8 5.9 %back_modes.1 = (bf16[8,48,1280]{2,1,0:T(8,128)(2,1)}, bf16[120,128]{1,0:T(8,128)(2,1)}, bf16[120,128]{1,0:T(8,128)(2,1)}, bf16[120,128]{1,0:T(8,128)(2,1)}, bf16[120,128]{1,0:T(8,128)(2,1)}) custom-call(s32[3]{0:T(128)} %pad_add_fusion.where_ref, bf16[8,48,1280]{2,1,0:T(8,128)(2,1)} %all_to_all.20.arrived_ref, bf16[3,20,40,128]{3,2,1,0:T(8,128)(2,1)} %bitcast.23, ...), custom_call_target="tpu_custom_call" | custom-call | tf_op jit(solution)/shard_map/back_modes/pallas_call | solution.py:448
  214.7 3.6 %all-to-all-start.3 = ((bf16[8,48,1280]{2,1,0:T(8,128)(2,1)}), bf16[8,48,1280]{2,1,0:T(8,128)(2,1)S(1)}, u32[]{:S(2)}, u32[]{:S(2)}) async-start(bf16[8,48,1280]{2,1,0:T(8,128)(2,1)} %get-tuple-element.54), calls=%async_computation.3 | async-start | bytes 1966080 | tf_op jit(solution)/shard_map/all_to_all | solution.py:521
  218.2 5.8 %collective-permute-start.17 = (bf16[120,128]{1,0:T(8,128)(2,1)}, bf16[120,128]{1,0:T(8,128)(2,1)S(1)}, u32[]{:S(2)}, u32[]{:S(2)}) collective-permute-start(bf16[120,128]{1,0:T(8,128)(2,1)} %get-tuple-element.55), channel_id=1, source_target_pairs={{0,0},{8,32},{16,64},{24,96},{32,8},{40,40},{48,72},{56,104},{64,1... | collective-permute-start | bytes 92168 | tf_op jit(solution)/shard_map/ppermute | solution.py:530
  224.5 3.2 %collective-permute-start.20 = (bf16[120,128]{1,0:T(8,128)(2,1)}, bf16[120,128]{1,0:T(8,128)(2,1)S(1)}, u32[]{:S(2)}, u32[]{:S(2)}) collective-permute-start(bf16[120,128]{1,0:T(8,128)(2,1)} %get-tuple-element.58), channel_id=1, source_target_pairs={{0,24},{8,56},{16,88},{24,120},{32,0},{40,32},{48,64},{56,96},{64,... | collective-permute-start | bytes 92168 | tf_op jit(solution)/shard_map/ppermute | solution.py:530
  227.7 1.5 collective-permute-done.19.g2
  229.2 3.6 %collective-permute-done.20.g3 = bf16[120,128]{1,0:T(8,128)(2,1)S(1)} collective-permute-done((bf16[120,128]{1,0:T(8,128)(2,1)}, bf16[120,128]{1,0:T(8,128)(2,1)S(1)}, u32[]{:S(2)}, u32[]{:S(2)}) %collective-permute-start.20) | collective-permute-done | bytes 30752 | tf_op jit(solution)/shard_map/ppermute | solution.py:530
  232.8 0.9 copy-done.1
  233.7 5.1 %from_lines.3.i0 = bf16[4,48,1280]{2,1,0:T(8,128)(2,1)} custom-call(s32[3]{0:T(128)} %pad_add_fusion.where_ref, bf16[8,48,1280]{2,1,0:T(8,128)(2,1)} %copy-done.1, bf16[8,384,192]{2,1,0:T(8,128)(2,1)} %constant.25.clone.table_ref), custom_call_target="tpu_custom_call" | custom-call | tf_op jit(solution)/shard_map/from_lines/pallas_call | solution.py:310
  238.8 1.2 collective-permute-start.21
  240.1 3.1 %collective-permute-start.22 = (bf16[4,48,1280]{2,1,0:T(8,128)(2,1)}, bf16[4,48,1280]{2,1,0:T(8,128)(2,1)S(1)}, u32[]{:S(2)}, u32[]{:S(2)}) collective-permute-start(bf16[4,48,1280]{2,1,0:T(8,128)(2,1)} %from_lines.3.i0), channel_id=1, source_target_pairs={{0,8},{8,0},{16,24},{24,16},{1,9},{9,1},{17,25},{25,17},{2,10},{10... | collective-permute-start | bytes 1474568 | tf_op jit(solution)/shard_map/ppermute | solution.py:499
  243.2 5.0 %collective-permute-done.21.i1 = bf16[4,48,1280]{2,1,0:T(8,128)(2,1)S(1)} collective-permute-done((bf16[4,48,1280]{2,1,0:T(8,128)(2,1)}, bf16[4,48,1280]{2,1,0:T(8,128)(2,1)S(1)}, u32[]{:S(2)}, u32[]{:S(2)}) %collective-permute-start.21) | collective-permute-done | bytes 491552 | tf_op jit(solution)/shard_map/ppermute | solution.py:499
  248.2 4.6 %collective-permute-start.23 = (bf16[4,48,1280]{2,1,0:T(8,128)(2,1)S(1)}, bf16[4,48,1280]{2,1,0:T(8,128)(2,1)S(1)}, u32[]{:S(2)}, u32[]{:S(2)}) collective-permute-start(bf16[4,48,1280]{2,1,0:T(8,128)(2,1)S(1)} %collective-permute-done.21.i1), channel_id=1, source_target_pairs={{0,8},{8,0},{16,24},{24,16},{1,9},{9,1},{17,25},{25,17},{2,10},{10... | collective-permute-start | bytes 1474568 | tf_op jit(solution)/shard_map/ppermute | solution.py:499
  252.8 1.1 fusion.1.mixer_ref
  253.9 3.1 %outer_sum.1 = f32[3,20,40,128]{3,2,1,0:T(8,128)} custom-call(bf16[120,128]{1,0:T(8,128)(2,1)} %copy-done.20, bf16[120,128]{1,0:T(8,128)(2,1)} %copy-done.21, bf16[120,128]{1,0:T(8,128)(2,1)} %copy-done.22, bf16[120,128]{1,0:T(8,128)(2,1)} %copy-done.23, bf16[120,128]{1,0:T(8,128)(2,1)} %copy-done.24, bf16[120,128]{1,0:T(8,128)(2,1)} %copy-done.25, ...), custom_call_target="tpu_custom_call" | custom-call | tf_op jit(solution)/shard_map/outer_sum/pallas_call | solution.py:490
  257.9 15.7 %end_columns.1 = bf16[20,64,2048]{2,1,0:T(8,128)(2,1)} custom-call(s32[3]{0:T(128)} %pad_add_fusion.where_ref, bf16[4,48,1280]{2,1,0:T(8,128)(2,1)} %from_lines.3.i0, bf16[4,48,1280]{2,1,0:T(8,128)(2,1)} %copy-done.17, bf16[4,48,1280]{2,1,0:T(8,128)(2,1)} %copy-done.18, bf16[4,48,1280]{2,1,0:T(8,128)(2,1)} %copy-done.19, ...), custom_call_target="tpu_custom_call" | custom-call | tf_op jit(solution)/shard_map/end_columns/pallas_call | solution.py:266
  (80 shorter events, 7.4 us)
Async XLA Ops:
  0.6 133.3 %copy-start = (bf16[20,20]{1,0:T(8,128)(2,1)S(1)}, bf16[20,20]{1,0:T(8,128)(2,1)}, u32[]{:S(2)}) copy-start(bf16[20,20]{1,0:T(8,128)(2,1)} %param.12) | copy-start | bytes 2404
  0.6 11.2 %copy-start.28 = (bf16[3,20,20,2,128]{4,3,2,1,0:T(2,128)(2,1)S(1)}, bf16[3,20,20,2,128]{4,3,2,1,0:T(2,128)(2,1)}, u32[]{:S(2)}) copy-start(bf16[3,20,20,2,128]{4,3,2,1,0:T(2,128)(2,1)} %param.11) | copy-start | bytes 1843204
  10.5 4.6 %collective-permute-start.2 = (bf16[4,48,1280]{2,1,0:T(8,128)(2,1)}, bf16[4,48,1280]{2,1,0:T(8,128)(2,1)S(1)}, u32[]{:S(2)}, u32[]{:S(2)}) collective-permute-start(bf16[4,48,1280]{2,1,0:T(8,128)(2,1)} %get-tuple-element.39), channel_id=1, source_target_pairs={{0,8},{8,0},{16,24},{24,16},{1,9},{9,1},{17,25},{25,17},{2,10},{10... | collective-permute-start | bytes 1474568 | tf_op jit(solution)/shard_map/ppermute | solution.py:499
  11.9 11.7 %collective-permute-start = (bf16[3,20,20,2,128]{4,3,2,1,0:T(2,128)(2,1)S(1)}, bf16[3,20,20,2,128]{4,3,2,1,0:T(2,128)(2,1)S(1)}, u32[]{:S(2)}, u32[]{:S(2)}) collective-permute-start(bf16[3,20,20,2,128]{4,3,2,1,0:T(2,128)(2,1)S(1)} %copy-done.28), channel_id=1, source_target_pairs={{0,0},{8,32},{16,64},{24,96},{32,8},{40,40},{48,72},{56,104},{64,1... | collective-permute-start | bytes 1843208 | tf_op jit(solution)/shard_map/ppermute | solution.py:539
  15.0 4.5 %collective-permute-start.1 = (bf16[4,48,1280]{2,1,0:T(8,128)(2,1)}, bf16[4,48,1280]{2,1,0:T(8,128)(2,1)S(1)}, u32[]{:S(2)}, u32[]{:S(2)}) collective-permute-start(bf16[4,48,1280]{2,1,0:T(8,128)(2,1)} %get-tuple-element.37), channel_id=1, source_target_pairs={{0,8},{8,0},{16,24},{24,16},{1,9},{9,1},{17,25},{25,17},{2,10},{10... | collective-permute-start | bytes 1474568 | tf_op jit(solution)/shard_map/ppermute | solution.py:499
  16.3 25.7 %collective-permute-start.3 = (bf16[4,48,1280]{2,1,0:T(8,128)(2,1)S(1)}, bf16[4,48,1280]{2,1,0:T(8,128)(2,1)S(1)}, u32[]{:S(2)}, u32[]{:S(2)}) collective-permute-start(bf16[4,48,1280]{2,1,0:T(8,128)(2,1)S(1)} %add_convert_fusion.1), channel_id=1, source_target_pairs={{0,16},{8,24},{16,0},{24,8},{1,17},{9,25},{17,1},{25,9},{2,18},{10... | collective-permute-start | bytes 1474568 | tf_op jit(solution)/shard_map/ppermute | solution.py:499
  19.4 22.6 %copy-start.11 = (bf16[4,48,1280]{2,1,0:T(8,128)(2,1)}, bf16[4,48,1280]{2,1,0:T(8,128)(2,1)S(1)}, u32[]{:S(2)}) copy-start(bf16[4,48,1280]{2,1,0:T(8,128)(2,1)S(1)} %collective-permute-done.1.b_ref) | copy-start | bytes 1474564
  23.6 62.4 %copy-start.4 = (bf16[3,20,20,2,128]{4,3,2,1,0:T(2,128)(2,1)}, bf16[3,20,20,2,128]{4,3,2,1,0:T(2,128)(2,1)S(1)}, u32[]{:S(2)}) copy-start(bf16[3,20,20,2,128]{4,3,2,1,0:T(2,128)(2,1)S(1)} %collective-permute-done) | copy-start | bytes 1843204
  48.1 85.8 %copy-start.8 = (bf16[320,20]{1,0:T(8,128)(2,1)S(1)}, bf16[320,20]{1,0:T(8,128)(2,1)}, u32[]{:S(2)}) copy-start(bf16[320,20]{1,0:T(8,128)(2,1)} %constant.22.clone) | copy-start | bytes 38404
  48.1 37.9 %all-to-all-start = ((bf16[8,48,1280]{2,1,0:T(8,128)(2,1)}), bf16[8,48,1280]{2,1,0:T(8,128)(2,1)S(1)}, u32[]{:S(2)}, u32[]{:S(2)}) async-start(bf16[8,48,1280]{2,1,0:T(8,128)(2,1)} %to_lines.2), calls=%async_computation | async-start | bytes 1966080 | tf_op jit(solution)/shard_map/all_to_all | solution.py:521
  55.6 16.4 %collective-permute-start.6 = (bf16[3,20,20,2,128]{4,3,2,1,0:T(2,128)(2,1)S(1)}, bf16[3,20,20,2,128]{4,3,2,1,0:T(2,128)(2,1)S(1)}, u32[]{:S(2)}, u32[]{:S(2)}) collective-permute-start(bf16[3,20,20,2,128]{4,3,2,1,0:T(2,128)(2,1)S(1)} %collective-permute-done), channel_id=1, source_target_pairs={{96,0},{0,32},{32,64},{64,96},{97,1},{1,33},{33,65},{65,97},{98,2}... | collective-permute-start | bytes 1843208 | tf_op jit(solution)/shard_map/ppermute | solution.py:511
  55.6 30.4 %collective-permute-start.5 = (bf16[3,20,20,2,128]{4,3,2,1,0:T(2,128)(2,1)S(1)}, bf16[3,20,20,2,128]{4,3,2,1,0:T(2,128)(2,1)S(1)}, u32[]{:S(2)}, u32[]{:S(2)}) collective-permute-start(bf16[3,20,20,2,128]{4,3,2,1,0:T(2,128)(2,1)S(1)} %collective-permute-done), channel_id=1, source_target_pairs={{64,0},{96,32},{0,64},{32,96},{65,1},{97,33},{1,65},{33,97},{66,2}... | collective-permute-start | bytes 1843208 | tf_op jit(solution)/shard_map/ppermute | solution.py:511
  59.7 26.3 %collective-permute-start.4 = (bf16[3,20,20,2,128]{4,3,2,1,0:T(2,128)(2,1)S(1)}, bf16[3,20,20,2,128]{4,3,2,1,0:T(2,128)(2,1)S(1)}, u32[]{:S(2)}, u32[]{:S(2)}) collective-permute-start(bf16[3,20,20,2,128]{4,3,2,1,0:T(2,128)(2,1)S(1)} %collective-permute-done), channel_id=1, source_target_pairs={{32,0},{64,32},{96,64},{0,96},{33,1},{65,33},{97,65},{1,97},{34,2}... | collective-permute-start | bytes 1843208 | tf_op jit(solution)/shard_map/ppermute | solution.py:511
  72.0 14.1 %copy-start.5 = (bf16[3,20,20,2,128]{4,3,2,1,0:T(2,128)(2,1)}, bf16[3,20,20,2,128]{4,3,2,1,0:T(2,128)(2,1)S(1)}, u32[]{:S(2)}) copy-start(bf16[3,20,20,2,128]{4,3,2,1,0:T(2,128)(2,1)S(1)} %collective-permute-done.6) | copy-start | bytes 1843204
  86.0 1.1 copy-start.7
  86.1 1.3 copy-start.3
  93.1 21.0 %all-to-all-start.1 = ((bf16[8,48,1280]{2,1,0:T(8,128)(2,1)}), bf16[8,48,1280]{2,1,0:T(8,128)(2,1)S(1)}, u32[]{:S(2)}, u32[]{:S(2)}) async-start(bf16[8,48,1280]{2,1,0:T(8,128)(2,1)} %get-tuple-element.43), calls=%async_computation.1 | async-start | bytes 1966080 | tf_op jit(solution)/shard_map/all_to_all | solution.py:521
  99.4 7.5 %collective-permute-start.7 = (bf16[120,128]{1,0:T(8,128)(2,1)}, bf16[120,128]{1,0:T(8,128)(2,1)S(1)}, u32[]{:S(2)}, u32[]{:S(2)}) collective-permute-start(bf16[120,128]{1,0:T(8,128)(2,1)} %get-tuple-element.44), channel_id=1, source_target_pairs={{0,0},{8,32},{16,64},{24,96},{32,8},{40,40},{48,72},{56,104},{64,1... | collective-permute-start | bytes 92168 | tf_op jit(solution)/shard_map/ppermute | solution.py:530
  104.1 2.8 %collective-permute-start.8 = (bf16[120,128]{1,0:T(8,128)(2,1)}, bf16[120,128]{1,0:T(8,128)(2,1)S(1)}, u32[]{:S(2)}, u32[]{:S(2)}) collective-permute-start(bf16[120,128]{1,0:T(8,128)(2,1)} %get-tuple-element.45), channel_id=1, source_target_pairs={{0,8},{8,40},{16,72},{24,104},{32,16},{40,48},{48,80},{56,112},{64... | collective-permute-start | bytes 92168 | tf_op jit(solution)/shard_map/ppermute | solution.py:530
  104.2 5.2 %collective-permute-start.9 = (bf16[120,128]{1,0:T(8,128)(2,1)}, bf16[120,128]{1,0:T(8,128)(2,1)S(1)}, u32[]{:S(2)}, u32[]{:S(2)}) collective-permute-start(bf16[120,128]{1,0:T(8,128)(2,1)} %get-tuple-element.46), channel_id=1, source_target_pairs={{0,16},{8,48},{16,80},{24,112},{32,24},{40,56},{48,88},{56,120},{6... | collective-permute-start | bytes 92168 | tf_op jit(solution)/shard_map/ppermute | solution.py:530
  104.3 7.7 %collective-permute-start.10 = (bf16[120,128]{1,0:T(8,128)(2,1)}, bf16[120,128]{1,0:T(8,128)(2,1)S(1)}, u32[]{:S(2)}, u32[]{:S(2)}) collective-permute-start(bf16[120,128]{1,0:T(8,128)(2,1)} %get-tuple-element.47), channel_id=1, source_target_pairs={{0,24},{8,56},{16,88},{24,120},{32,0},{40,32},{48,64},{56,96},{64,... | collective-permute-start | bytes 92168 | tf_op jit(solution)/shard_map/ppermute | solution.py:530
  106.9 131.9 %copy-start.20 = (bf16[120,128]{1,0:T(8,128)(2,1)}, bf16[120,128]{1,0:T(8,128)(2,1)S(1)}, u32[]{:S(2)}) copy-start(bf16[120,128]{1,0:T(8,128)(2,1)S(1)} %collective-permute-done.7.s0) | copy-start | bytes 92164
  106.9 131.9 %copy-start.21 = (bf16[120,128]{1,0:T(8,128)(2,1)}, bf16[120,128]{1,0:T(8,128)(2,1)S(1)}, u32[]{:S(2)}) copy-start(bf16[120,128]{1,0:T(8,128)(2,1)S(1)} %collective-permute-done.8.s1) | copy-start | bytes 92164
  109.4 129.4 %copy-start.22 = (bf16[120,128]{1,0:T(8,128)(2,1)}, bf16[120,128]{1,0:T(8,128)(2,1)S(1)}, u32[]{:S(2)}) copy-start(bf16[120,128]{1,0:T(8,128)(2,1)S(1)} %collective-permute-done.9.s2) | copy-start | bytes 92164
  112.0 126.8 %copy-start.23 = (bf16[120,128]{1,0:T(8,128)(2,1)}, bf16[120,128]{1,0:T(8,128)(2,1)S(1)}, u32[]{:S(2)}) copy-start(bf16[120,128]{1,0:T(8,128)(2,1)S(1)} %collective-permute-done.10.s3) | copy-start | bytes 92164
  120.0 9.6 %collective-permute-start.11 = (bf16[4,48,1280]{2,1,0:T(8,128)(2,1)}, bf16[4,48,1280]{2,1,0:T(8,128)(2,1)S(1)}, u32[]{:S(2)}, u32[]{:S(2)}) collective-permute-start(bf16[4,48,1280]{2,1,0:T(8,128)(2,1)} %from_lines.2.i0), channel_id=1, source_target_pairs={{0,16},{8,24},{16,0},{24,8},{1,17},{9,25},{17,1},{25,9},{2,18},{10... | collective-permute-start | bytes 1474568 | tf_op jit(solution)/shard_map/ppermute | solution.py:499
  121.5 14.4 %collective-permute-start.12 = (bf16[4,48,1280]{2,1,0:T(8,128)(2,1)}, bf16[4,48,1280]{2,1,0:T(8,128)(2,1)S(1)}, u32[]{:S(2)}, u32[]{:S(2)}) collective-permute-start(bf16[4,48,1280]{2,1,0:T(8,128)(2,1)} %from_lines.2.i0), channel_id=1, source_target_pairs={{0,8},{8,0},{16,24},{24,16},{1,9},{9,1},{17,25},{25,17},{2,10},{10... | collective-permute-start | bytes 1474568 | tf_op jit(solution)/shard_map/ppermute | solution.py:499
  129.6 6.3 %copy-start.10 = (bf16[4,48,1280]{2,1,0:T(8,128)(2,1)}, bf16[4,48,1280]{2,1,0:T(8,128)(2,1)S(1)}, u32[]{:S(2)}) copy-start(bf16[4,48,1280]{2,1,0:T(8,128)(2,1)S(1)} %collective-permute-done.11.i1) | copy-start | bytes 1474564
  129.6 6.3 %collective-permute-start.13 = (bf16[4,48,1280]{2,1,0:T(8,128)(2,1)S(1)}, bf16[4,48,1280]{2,1,0:T(8,128)(2,1)S(1)}, u32[]{:S(2)}, u32[]{:S(2)}) collective-permute-start(bf16[4,48,1280]{2,1,0:T(8,128)(2,1)S(1)} %collective-permute-done.11.i1), channel_id=1, source_target_pairs={{0,8},{8,0},{16,24},{24,16},{1,9},{9,1},{17,25},{25,17},{2,10},{10... | collective-permute-start | bytes 1474568 | tf_op jit(solution)/shard_map/ppermute | solution.py:499
  135.9 1.0 copy-start.14
  164.8 2.2 collective-permute-start.15
  165.1 4.6 %collective-permute-start.14 = (bf16[4,48,1280]{2,1,0:T(8,128)(2,1)}, bf16[4,48,1280]{2,1,0:T(8,128)(2,1)S(1)}, u32[]{:S(2)}, u32[]{:S(2)}) collective-permute-start(bf16[4,48,1280]{2,1,0:T(8,128)(2,1)} %get-tuple-element.51), channel_id=1, source_target_pairs={{0,8},{8,0},{16,24},{24,16},{1,9},{9,1},{17,25},{25,17},{2,10},{10... | collective-permute-start | bytes 1474568 | tf_op jit(solution)/shard_map/ppermute | solution.py:499
  168.1 12.7 %collective-permute-start.16 = (bf16[4,48,1280]{2,1,0:T(8,128)(2,1)S(1)}, bf16[4,48,1280]{2,1,0:T(8,128)(2,1)S(1)}, u32[]{:S(2)}, u32[]{:S(2)}) collective-permute-start(bf16[4,48,1280]{2,1,0:T(8,128)(2,1)S(1)} %add_convert_fusion), channel_id=1, source_target_pairs={{0,16},{8,24},{16,0},{24,8},{1,17},{9,25},{17,1},{25,9},{2,18},{10... | collective-permute-start | bytes 1474568 | tf_op jit(solution)/shard_map/ppermute | solution.py:499
  169.7 11.2 %copy-start.13 = (bf16[4,48,1280]{2,1,0:T(8,128)(2,1)}, bf16[4,48,1280]{2,1,0:T(8,128)(2,1)S(1)}, u32[]{:S(2)}) copy-start(bf16[4,48,1280]{2,1,0:T(8,128)(2,1)S(1)} %collective-permute-done.14.b_ref) | copy-start | bytes 1474564
  186.9 65.8 %copy-start.9 = (bf16[320,320]{1,0:T(8,128)(2,1)S(1)}, bf16[320,320]{1,0:T(8,128)(2,1)}, u32[]{:S(2)}) copy-start(bf16[320,320]{1,0:T(8,128)(2,1)} %constant.26.clone) | copy-start | bytes 614404
  214.7 18.1 %all-to-all-start.3 = ((bf16[8,48,1280]{2,1,0:T(8,128)(2,1)}), bf16[8,48,1280]{2,1,0:T(8,128)(2,1)S(1)}, u32[]{:S(2)}, u32[]{:S(2)}) async-start(bf16[8,48,1280]{2,1,0:T(8,128)(2,1)} %get-tuple-element.54), calls=%async_computation.3 | async-start | bytes 1966080 | tf_op jit(solution)/shard_map/all_to_all | solution.py:521
  218.2 9.4 %collective-permute-start.17 = (bf16[120,128]{1,0:T(8,128)(2,1)}, bf16[120,128]{1,0:T(8,128)(2,1)S(1)}, u32[]{:S(2)}, u32[]{:S(2)}) collective-permute-start(bf16[120,128]{1,0:T(8,128)(2,1)} %get-tuple-element.55), channel_id=1, source_target_pairs={{0,0},{8,32},{16,64},{24,96},{32,8},{40,40},{48,72},{56,104},{64,1... | collective-permute-start | bytes 92168 | tf_op jit(solution)/shard_map/ppermute | solution.py:530
  224.1 3.6 %collective-permute-start.18 = (bf16[120,128]{1,0:T(8,128)(2,1)}, bf16[120,128]{1,0:T(8,128)(2,1)S(1)}, u32[]{:S(2)}, u32[]{:S(2)}) collective-permute-start(bf16[120,128]{1,0:T(8,128)(2,1)} %get-tuple-element.56), channel_id=1, source_target_pairs={{0,8},{8,40},{16,72},{24,104},{32,16},{40,48},{48,80},{56,112},{64... | collective-permute-start | bytes 92168 | tf_op jit(solution)/shard_map/ppermute | solution.py:530
  224.4 4.9 %collective-permute-start.19 = (bf16[120,128]{1,0:T(8,128)(2,1)}, bf16[120,128]{1,0:T(8,128)(2,1)S(1)}, u32[]{:S(2)}, u32[]{:S(2)}) collective-permute-start(bf16[120,128]{1,0:T(8,128)(2,1)} %get-tuple-element.57), channel_id=1, source_target_pairs={{0,16},{8,48},{16,80},{24,112},{32,24},{40,56},{48,88},{56,120},{6... | collective-permute-start | bytes 92168 | tf_op jit(solution)/shard_map/ppermute | solution.py:530
  224.5 8.3 %collective-permute-start.20 = (bf16[120,128]{1,0:T(8,128)(2,1)}, bf16[120,128]{1,0:T(8,128)(2,1)S(1)}, u32[]{:S(2)}, u32[]{:S(2)}) collective-permute-start(bf16[120,128]{1,0:T(8,128)(2,1)} %get-tuple-element.58), channel_id=1, source_target_pairs={{0,24},{8,56},{16,88},{24,120},{32,0},{40,32},{48,64},{56,96},{64,... | collective-permute-start | bytes 92168 | tf_op jit(solution)/shard_map/ppermute | solution.py:530
  227.7 26.2 %copy-start.24 = (bf16[120,128]{1,0:T(8,128)(2,1)}, bf16[120,128]{1,0:T(8,128)(2,1)S(1)}, u32[]{:S(2)}) copy-start(bf16[120,128]{1,0:T(8,128)(2,1)S(1)} %collective-permute-done.17.g0) | copy-start | bytes 92164
  227.7 26.2 %copy-start.25 = (bf16[120,128]{1,0:T(8,128)(2,1)}, bf16[120,128]{1,0:T(8,128)(2,1)S(1)}, u32[]{:S(2)}) copy-start(bf16[120,128]{1,0:T(8,128)(2,1)S(1)} %collective-permute-done.18.g1) | copy-start | bytes 92164
  229.2 24.6 %copy-start.26 = (bf16[120,128]{1,0:T(8,128)(2,1)}, bf16[120,128]{1,0:T(8,128)(2,1)S(1)}, u32[]{:S(2)}) copy-start(bf16[120,128]{1,0:T(8,128)(2,1)S(1)} %collective-permute-done.19.g2) | copy-start | bytes 92164
  232.8 21.1 %copy-start.27 = (bf16[120,128]{1,0:T(8,128)(2,1)}, bf16[120,128]{1,0:T(8,128)(2,1)S(1)}, u32[]{:S(2)}) copy-start(bf16[120,128]{1,0:T(8,128)(2,1)S(1)} %collective-permute-done.20.g3) | copy-start | bytes 92164
  238.8 9.3 %collective-permute-start.21 = (bf16[4,48,1280]{2,1,0:T(8,128)(2,1)}, bf16[4,48,1280]{2,1,0:T(8,128)(2,1)S(1)}, u32[]{:S(2)}, u32[]{:S(2)}) collective-permute-start(bf16[4,48,1280]{2,1,0:T(8,128)(2,1)} %from_lines.3.i0), channel_id=1, source_target_pairs={{0,16},{8,24},{16,0},{24,8},{1,17},{9,25},{17,1},{25,9},{2,18},{10... | collective-permute-start | bytes 1474568 | tf_op jit(solution)/shard_map/ppermute | solution.py:499
  240.1 16.9 %collective-permute-start.22 = (bf16[4,48,1280]{2,1,0:T(8,128)(2,1)}, bf16[4,48,1280]{2,1,0:T(8,128)(2,1)S(1)}, u32[]{:S(2)}, u32[]{:S(2)}) collective-permute-start(bf16[4,48,1280]{2,1,0:T(8,128)(2,1)} %from_lines.3.i0), channel_id=1, source_target_pairs={{0,8},{8,0},{16,24},{24,16},{1,9},{9,1},{17,25},{25,17},{2,10},{10... | collective-permute-start | bytes 1474568 | tf_op jit(solution)/shard_map/ppermute | solution.py:499
  248.2 8.8 %copy-start.17 = (bf16[4,48,1280]{2,1,0:T(8,128)(2,1)}, bf16[4,48,1280]{2,1,0:T(8,128)(2,1)S(1)}, u32[]{:S(2)}) copy-start(bf16[4,48,1280]{2,1,0:T(8,128)(2,1)S(1)} %collective-permute-done.21.i1) | copy-start | bytes 1474564
  248.2 8.8 %collective-permute-start.23 = (bf16[4,48,1280]{2,1,0:T(8,128)(2,1)S(1)}, bf16[4,48,1280]{2,1,0:T(8,128)(2,1)S(1)}, u32[]{:S(2)}, u32[]{:S(2)}) collective-permute-start(bf16[4,48,1280]{2,1,0:T(8,128)(2,1)S(1)} %collective-permute-done.21.i1), channel_id=1, source_target_pairs={{0,8},{8,0},{16,24},{24,16},{1,9},{9,1},{17,25},{25,17},{2,10},{10... | collective-permute-start | bytes 1474568 | tf_op jit(solution)/shard_map/ppermute | solution.py:499
  (8 other events, 6.9 us)

commit v2 on v1

--- a/solution.py
+++ b/solution.py
@@ -31,7 +31,8 @@
 GROUPS = CH // GROUP
 GL = GROUP * KX
 WIDE = CH * KX
-XB = 16
+XB = 8
+EB = 16
 ORDER = (0, 2, 1, 3)
 
 BF = jnp.bfloat16
@@ -102,84 +103,75 @@
     )
 
 
-def fill_width(wide_ref, blocks_ref):
+def fill_width(wide_ref, tall_ref, long_ref):
     rows = lax.broadcasted_iota(jnp.int32, (GL, GL), 0) // XL
     columns = lax.broadcasted_iota(jnp.int32, (GL, GL), 1) // KX
     for part in range(2):
         strip = wide_ref[0, part].astype(F32)
         full = jnp.concatenate([strip] * GROUP, axis=0)
-        blocks_ref[part] = jnp.where(rows == columns, full, 0.0).astype(BF)
-
-
-def forward_columns(source_ref, depth_ref, blocks_ref, outs):
+        block = jnp.where(rows == columns, full, 0.0).astype(BF)
+        tall_ref[GL * part : GL * (part + 1), :] = block
+        long_ref[:, GL * part : GL * (part + 1)] = block
+
+
+def forward_group(rows, depth_ref, tall_ref, outs, j):
     half = KZ * YB
-    for j in range(GROUPS):
-        rows = source_ref[GROUP * j : GROUP * (j + 1)].reshape(GROUP * XL, LANES)
-        planes = dot(depth_ref[0], rows, 1, 1).astype(BF)
-        by_cos = dot(planes, blocks_ref[0])
-        by_sin = dot(planes, blocks_ref[1])
-        real = by_cos[:half] + by_sin[half:]
-        imag = by_cos[half:] - by_sin[:half]
-        for pos in range(GX):
-            lo = pos * KB * YB
-            piece = jnp.concatenate([real[lo : lo + KB * YB], imag[lo : lo + KB * YB]], axis=0)
-            outs[pos][0, :, GL * j : GL * (j + 1)] = piece.astype(BF)
-
-
-def inverse_columns(ins, depth_ref, blocks_ref, total_ref):
-    half = KZ * YB
+    planes = dot(depth_ref[0], rows, 1, 1)
+    real = planes[:half]
+    imag = planes[half:]
+    sides = jnp.concatenate(
+        [jnp.concatenate([real, imag], axis=1), jnp.concatenate([imag, -real], axis=1)], axis=0
+    ).astype(BF)
+    lines = dot(sides, tall_ref[...])
+    for pos in range(GX):
+        lo = pos * KB * YB
+        piece = jnp.concatenate(
+            [lines[lo : lo + KB * YB], lines[half + lo : half + lo + KB * YB]], axis=0
+        )
+        outs[pos][0, :, GL * j : GL * (j + 1)] = piece.astype(BF)
+
+
+def inverse_group(ins, depth_ref, long_ref, j):
     part = KB * YB
-    for j in range(GROUPS):
-        pieces = [ref[0, :, GL * j : GL * (j + 1)].astype(F32) for ref in ins]
-        stacked = jnp.concatenate(
-            [piece[:part] for piece in pieces] + [piece[part:] for piece in pieces], axis=0
-        ).astype(BF)
-        by_cos = dot(stacked, blocks_ref[0], 1, 1)
-        by_sin = dot(stacked, blocks_ref[1], 1, 1)
-        real = by_cos[:half] - by_sin[half:]
-        imag = by_sin[:half] + by_cos[half:]
-        planes = jnp.concatenate([real, imag], axis=0).astype(BF)
-        values = dot(planes, depth_ref[0], 0, 0)
-        total_ref[GROUP * j : GROUP * (j + 1)] = values.reshape(GROUP, XL, LANES)
-
-
-def add_bypass(source_ref, mixer_ref, total_ref):
-    @pl.loop(0, XL // XB)
-    def _(i):
-        span = pl.ds(pl.multiple_of(i * XB, XB), XB)
+    pieces = [ref[0, :, GL * j : GL * (j + 1)].astype(F32) for ref in ins]
+    real = jnp.concatenate([piece[:part] for piece in pieces], axis=0)
+    imag = jnp.concatenate([piece[part:] for piece in pieces], axis=0)
+    sides = jnp.concatenate(
+        [jnp.concatenate([real, -imag], axis=1), jnp.concatenate([imag, real], axis=1)], axis=0
+    ).astype(BF)
+    planes = dot(long_ref[...], sides, 1, 1).astype(BF)
+    return dot(planes, depth_ref[0])
+
+
+def set_bypass(source_ref, mixer_ref, total_ref):
+    for i in range(XL // XB):
+        span = slice(i * XB, (i + 1) * XB)
         rows = source_ref[:, span, :].reshape(CH * XB, LANES)
-        mixed = dot(mixer_ref[...], rows).reshape(CH, XB, LANES)
-        total_ref[:, span, :] = total_ref[:, span, :] + mixed
-
-
-def start_kernel(where_ref, field_ref, depth_ref, wide_ref, o0, o1, o2, o3, blocks_ref):
+        total_ref[:, span, :] = dot(mixer_ref[...], rows).reshape(CH, XB, LANES)
+
+
+def group_rows(ref, j):
+    return ref[GROUP * j : GROUP * (j + 1)].reshape(GROUP * XL, LANES)
+
+
+def start_kernel(where_ref, field_ref, depth_ref, wide_ref, o0, o1, o2, o3, tall_ref, long_ref):
     @pl.when(pl.program_id(0) == 0)
     def _():
-        fill_width(wide_ref, blocks_ref)
-
-    forward_columns(field_ref, depth_ref, blocks_ref, (o0, o1, o2, o3))
+        fill_width(wide_ref, tall_ref, long_ref)
+
+    for j in range(GROUPS):
+        forward_group(group_rows(field_ref, j), depth_ref, tall_ref, (o0, o1, o2, o3), j)
 
 
 ROOT = math.sqrt(2.0 / math.pi)
 CUBE = 0.044715
 
 
-def middle_kernel(
-    where_ref, bias_ref, i0, i1, i2, i3, field_ref, upstream_ref, mixer_ref, depth_ref, wide_ref,
-    act_ref, grad_ref, o0, o1, o2, o3, blocks_ref, total_ref,
-):
-    @pl.when(pl.program_id(0) == 0)
-    def _():
-        fill_width(wide_ref, blocks_ref)
-
-    inverse_columns((i0, i1, i2, i3), depth_ref, blocks_ref, total_ref)
-    add_bypass(field_ref, mixer_ref, total_ref)
-
-    @pl.loop(0, CH)
-    def _(channel):
+def activate(bias_ref, upstream_ref, total_ref, act_ref, grad_ref, j):
+    for channel in range(GROUP * j, GROUP * (j + 1)):
         shift = bias_ref[channel]
-        for i in range(XL // XB):
-            span = slice(i * XB, (i + 1) * XB)
+        for i in range(XL // EB):
+            span = slice(i * EB, (i + 1) * EB)
             x = total_ref[channel, span, :] + shift
             square = x * x
             t = jnp.tanh(x * (ROOT + (ROOT * CUBE) * square))
@@ -190,23 +182,48 @@
             up = upstream_ref[channel, span, :].astype(F32)
             grad_ref[channel, span, :] = (up * slope).astype(BF)
 
-    forward_columns(grad_ref, depth_ref, blocks_ref, (o0, o1, o2, o3))
-
-
-def end_kernel(
-    where_ref, i0, i1, i2, i3, grad_ref, mixer_ref, depth_ref, wide_ref, out_ref,
-    blocks_ref, total_ref,
+
+def middle_kernel(
+    where_ref, bias_ref, i0, i1, i2, i3, field_ref, upstream_ref, mixer_ref, depth_ref, wide_ref,
+    act_ref, grad_ref, o0, o1, o2, o3, tall_ref, long_ref, total_ref,
 ):
     @pl.when(pl.program_id(0) == 0)
     def _():
-        fill_width(wide_ref, blocks_ref)
-
-    inverse_columns((i0, i1, i2, i3), depth_ref, blocks_ref, total_ref)
-    add_bypass(grad_ref, mixer_ref, total_ref)
-
-    @pl.loop(0, CH)
-    def _(channel):
-        out_ref[channel] = total_ref[channel].astype(BF)
+        fill_width(wide_ref, tall_ref, long_ref)
+
+    set_bypass(field_ref, mixer_ref, total_ref)
+
+    def inverse(j):
+        group = slice(GROUP * j, GROUP * (j + 1))
+        values = inverse_group((i0, i1, i2, i3), depth_ref, long_ref, j)
+        total_ref[group] = total_ref[group] + values.reshape(GROUP, XL, LANES)
+
+    def forward(j):
+        forward_group(group_rows(grad_ref, j), depth_ref, tall_ref, (o0, o1, o2, o3), j)
+
+    inverse(0)
+    for j in range(GROUPS):
+        if j + 1 < GROUPS:
+            inverse(j + 1)
+        activate(bias_ref, upstream_ref, total_ref, act_ref, grad_ref, j)
+        if j > 0:
+            forward(j - 1)
+    forward(GROUPS - 1)
+
+
+def end_kernel(
+    where_ref, i0, i1, i2, i3, grad_ref, mixer_ref, depth_ref, wide_ref, out_ref,
+    tall_ref, long_ref, total_ref,
+):
+    @pl.when(pl.program_id(0) == 0)
+    def _():
+        fill_width(wide_ref, tall_ref, long_ref)
+
+    set_bypass(grad_ref, mixer_ref, total_ref)
+    for j in range(GROUPS):
+        group = slice(GROUP * j, GROUP * (j + 1))
+        values = inverse_group((i0, i1, i2, i3), depth_ref, long_ref, j)
+        out_ref[group] = (total_ref[group] + values.reshape(GROUP, XL, LANES)).astype(BF)
 
 
 def column_specs():
@@ -220,7 +237,7 @@
 
 COEFFS = jax.ShapeDtypeStruct((STEPS, ROWS, WIDE), BF)
 COLUMNS = jax.ShapeDtypeStruct((CH, XL, YL * NZ), BF)
-BLOCKS = pltpu.VMEM((2, GL, GL), BF)
+BLOCKS = [pltpu.VMEM((2 * GL, GL), BF), pltpu.VMEM((GL, 2 * GL), BF)]
 TOTAL = pltpu.VMEM((CH, XL, LANES), F32)
 PARAMS = pltpu.CompilerParams(vmem_limit_bytes=56 * 1024 * 1024)
 
@@ -234,7 +251,7 @@
             grid=(STEPS,),
             in_specs=[columns, depth, wide],
             out_specs=[coeffs] * 4,
-            scratch_shapes=[BLOCKS],
+            scratch_shapes=BLOCKS,
         ),
         out_shape=[COEFFS] * 4,
         compiler_params=PARAMS,
@@ -253,7 +270,7 @@
             + [coeffs] * 4
             + [columns, columns, mix, depth, wide],
             out_specs=[columns, columns] + [coeffs] * 4,
-            scratch_shapes=[BLOCKS, TOTAL],
+            scratch_shapes=BLOCKS + [TOTAL],
         ),
         out_shape=[COLUMNS, COLUMNS] + [COEFFS] * 4,
         compiler_params=PARAMS,
@@ -270,7 +287,7 @@
             grid=(STEPS,),
             in_specs=[coeffs] * 4 + [columns, mix, depth, wide],
             out_specs=columns,
-            scratch_shapes=[BLOCKS, TOTAL],
+            scratch_shapes=BLOCKS + [TOTAL],
         ),
         out_shape=COLUMNS,
         compiler_params=PARAMS,
@@ -279,45 +296,43 @@
 
 
 def line_kernel(where_ref, a_ref, b_ref, c_ref, table_ref, out_ref):
-    total = a_ref[...].astype(F32) + b_ref[...].astype(F32) + c_ref[...].astype(F32)
-    rows = total.astype(BF).reshape(STEPS * ROWS, GL)
-    out_ref[...] = dot(table_ref[0], rows).astype(BF).reshape(GY, 48, GL)
-
-
-def to_lines(where, own, from_core, from_chip):
-    piece = pl.BlockSpec((STEPS, ROWS, GL), lambda i, w: (0, 0, i))
+    for j in range(GROUPS):
+        lanes = slice(GL * j, GL * (j + 1))
+        parts = [ref[:, :, lanes].astype(F32) for ref in (a_ref, b_ref, c_ref)]
+        rows = (parts[0] + parts[1] + parts[2]).astype(BF).reshape(STEPS * ROWS, GL)
+        out_ref[:, :, lanes] = dot(table_ref[0], rows).astype(BF).reshape(GY, 48, GL)
+
+
+def unline_kernel(where_ref, modes_ref, table_ref, out_ref):
+    for j in range(GROUPS):
+        lanes = slice(GL * j, GL * (j + 1))
+        rows = modes_ref[:, :, lanes].reshape(GY * 48, GL)
+        out_ref[:, :, lanes] = dot(table_ref[0], rows, 0, 0).astype(BF).reshape(STEPS, ROWS, GL)
+
+
+def line_call(kernel, name, where, ins, out_shape):
+    whole = pl.BlockSpec(ins[0].shape, lambda i, w: (0, 0, 0))
     table = pl.BlockSpec((1, GY * 48, STEPS * ROWS), lambda i, w: (w[2], 0, 0))
     return pl.pallas_call(
-        line_kernel,
+        kernel,
         grid_spec=pltpu.PrefetchScalarGridSpec(
             num_scalar_prefetch=1,
-            grid=(GROUPS,),
-            in_specs=[piece] * 3 + [table],
-            out_specs=pl.BlockSpec((GY, 48, GL), lambda i, w: (0, 0, i)),
+            grid=(1,),
+            in_specs=[whole] * len(ins) + [table],
+            out_specs=pl.BlockSpec(out_shape.shape, lambda i, w: (0, 0, 0)),
         ),
-        out_shape=jax.ShapeDtypeStruct((GY, 48, WIDE), BF),
-        name="to_lines",
-    )(where, own, from_core, from_chip, jnp.asarray(LINE))
-
-
-def unline_kernel(where_ref, modes_ref, table_ref, out_ref):
-    rows = modes_ref[...].reshape(GY * 48, GL)
-    out_ref[...] = dot(table_ref[0], rows, 0, 0).astype(BF).reshape(STEPS, ROWS, GL)
+        out_shape=out_shape,
+        name=name,
+    )(where, *ins, jnp.asarray(LINE))
+
+
+def to_lines(where, *parts):
+    out = jax.ShapeDtypeStruct((GY, 48, WIDE), BF)
+    return line_call(line_kernel, "to_lines", where, parts, out)
 
 
 def from_lines(where, modes):
-    table = pl.BlockSpec((1, GY * 48, STEPS * ROWS), lambda i, w: (w[2], 0, 0))
-    return pl.pallas_call(
-        unline_kernel,
-        grid_spec=pltpu.PrefetchScalarGridSpec(
-            num_scalar_prefetch=1,
-            grid=(GROUPS,),
-            in_specs=[pl.BlockSpec((GY, 48, GL), lambda i, w: (0, 0, i)), table],
-            out_specs=pl.BlockSpec((STEPS, ROWS, GL), lambda i, w: (0, 0, i)),
-        ),
-        out_shape=COEFFS,
-        name="from_lines",
-    )(where, modes, jnp.asarray(LINE))
+    return line_call(unline_kernel, "from_lines", where, (modes,), COEFFS)
 
 
 SETS = GX * KB
@@ -499,10 +514,17 @@
     return lax.ppermute(values, "gx", [(i, i ^ bit) for i in range(GX)])
 
 
-def start_slabs(pieces):
+def start_slabs(pieces, *waiting):
     own, far, near, across = pieces
     far_sum = (far.astype(F32) + swap(across, 1).astype(F32)).astype(BF)
-    return own, swap(near, 1), swap(far_sum, 2)
+    far_sum, *waiting = lax.optimization_barrier((far_sum, *waiting))
+    return own, swap(near, 1), swap(far_sum, 2), *waiting
+
+
+def share_slabs(own, *waiting):
+    far = swap(own, 2)
+    far, *waiting = lax.optimization_barrier((far, *waiting))
+    return own, far, swap(own, 1), swap(far, 1), *waiting
 
 
 def gather_weights(weight):
@@ -510,11 +532,6 @@
     for k in range(1, DP):
         held.append(lax.ppermute(weight, "dp", [((a + k) % DP, a) for a in range(DP)]))
     return [part.reshape(KB, CH, PAIR, 2 * HALF) for part in held]
-
-
-def share_slabs(own):
-    far = swap(own, 2)
-    return own, far, swap(own, 1), swap(far, 1)
 
 
 def exchange_lines(parts):
@@ -544,10 +561,9 @@
         return wide.astype(BF) * jnp.asarray(SAME)
 
     values = field[0]
-    own, *others = start_slabs(start_columns(where, values))
-    weight, *others = lax.optimization_barrier((weight, *others))
+    *parts, weight = start_slabs(start_columns(where, values), weight)
     weights = gather_weights(weight)
-    arrived = exchange_lines(to_lines(where, own, *others))
+    arrived = exchange_lines(to_lines(where, *parts))
     modes, *spectra = mode_call(mix_kernel, "mix_modes", where, arrived, weights)
     modes, *spectra = lax.optimization_barrier((exchange_lines(modes), *to_owners(spectra)))
     coeffs = share_slabs(from_lines(where, modes))
@@ -557,8 +573,7 @@
     arrived = exchange_lines(to_lines(where, *start_slabs(pieces)))
     modes, *grads = mode_call(back_kernel, "back_modes", where, arrived, weights)
     modes, *grads = lax.optimization_barrier((exchange_lines(modes), *to_owners(grads)))
-    coeffs = share_slabs(from_lines(where, modes))
-    weight_grad = outer_sum(spectra, grads)
+    *coeffs, weight_grad = share_slabs(from_lines(where, modes), outer_sum(spectra, grads))
     field_grad = end_columns(where, coeffs, grad, mixer_of(bypass_weight.T))
     return (
         activation[None],

time: 276 us -> 252 us (0.913)
  Pallas kernels: 88.1 us -> 66.1 us
  waiting for transfers between devices: 83.3 us -> 77 us
  starting transfers between devices: 66.6 us -> 72.4 us
    pallas_call x1, Pallas kernels: 27.9 us -> 18.8 us  [middle_columns(): pl.pallas_call(middle_kernel, grid_spec=pltpu.PrefetchScalarGridSpec(num_...]
    ppermute x12, waiting for transfers between devices: 41.2 us -> 32.3 us  [swap(): return lax.ppermute(values, 'gx', [(i, i ^ bit) for i in range(GX)])]
    pallas_call x4, Pallas kernels: 20.7 us -> 13.2 us  [line_call(): pl.pallas_call(kernel, grid_spec=pltpu.PrefetchScalarGridSpec(num_scalar_...]
    pallas_call x1, Pallas kernels: 15.7 us -> 10.2 us  [end_columns(): pl.pallas_call(end_kernel, grid_spec=pltpu.PrefetchScalarGridSpec(num_sca...]
    ppermute x12, starting transfers between devices: 24.5 us -> 29.2 us  [swap(): return lax.ppermute(values, 'gx', [(i, i ^ bit) for i in range(GX)])]
    ppermute x1, waiting for transfers between devices: 4.19 us -> 7.07 us  [per_device(): weight = lax.ppermute(spectral_weight, ('dp', 'gx'), turn)]
  transfers between devices with their start and end apart: 27 -> 27, of which waited for: 13 -> 15; matrix products, arithmetic and copies ran while one was open for 2% -> 2% of each run, Pallas kernels for 1% -> 1%
where the time goes in v2:
time: 252 us; the launch traced here: 249 us
  waiting for transfers between devices  77 us (31%)
  starting transfers between devices  72.4 us (29%)
  Pallas kernels  66.1 us (26%)
  blocking collectives  20.1 us (8%)
  local copies, waits for them, and re-layouts  6.4 us (3%)
  other arithmetic  2.99 us (1%)
  matrix products  2.71 us (1%)
    ppermute x12, waiting for transfers between devices, swap(): return lax.ppermute(values, 'gx', [(i, i ^ bit) for i in range(GX)])  32.3 us
    ppermute x12, starting transfers between devices, swap(): return lax.ppermute(values, 'gx', [(i, i ^ bit) for i in range(GX)])  29.2 us
    ppermute x3, waiting for transfers between devices, gather_weights(): lax.ppermute(weight, 'dp', [((a + k) % DP, a) for a in range(DP)])  25.2 us
    all_to_all x1, blocking collectives, exchange_lines(): return lax.all_to_all(parts, 'gy', split_axis=0, concat_axis=0, tiled=True)  20.1 us
    pallas_call x1, Pallas kernels, middle_columns(): pl.pallas_call(middle_kernel, grid_spec=pltpu.PrefetchScalarGridSpec(num_...  18.8 us
    ppermute x8, starting transfers between devices, to_owners(): moved.append(lax.ppermute(chunk, ('dp', 'gx'), pairs))  17.9 us
    all_to_all x3, starting transfers between devices, exchange_lines(): return lax.all_to_all(parts, 'gy', split_axis=0, concat_axis=0, tiled=True)  17.7 us
    pallas_call x4, Pallas kernels, line_call(): pl.pallas_call(kernel, grid_spec=pltpu.PrefetchScalarGridSpec(num_scalar_...  13.2 us
  transfers between devices with their start and end apart: 27, of which 15 were waited for; matrix products, arithmetic and copies ran while one was open for 2% of the time, Pallas kernels for 1%

profile of v2, /device:TPU:1, one launch (start us, length us, event | category | flops | bytes accessed | tf_op | source)
XLA Modules:
  0.0 248.6 jit_solution(10095081117764098964)
XLA Ops:
  1.3 9.1 %start_columns.1 = (bf16[4,48,1280]{2,1,0:T(8,128)(2,1)}, bf16[4,48,1280]{2,1,0:T(8,128)(2,1)}, bf16[4,48,1280]{2,1,0:T(8,128)(2,1)}, bf16[4,48,1280]{2,1,0:T(8,128)(2,1)}) custom-call(s32[3]{0:T(128)} %pad_add_fusion.where_ref, bf16[20,64,2048]{2,1,0:T(8,128)(2,1)} %bitcast.18, bf16[4,192,512]{2,1,0:T(8,128)(2,1)} %constant.23.clone.depth_ref, ...), custom_call_target="tpu_custom_call" | custom-call | tf_op jit(solution)/shard_map/start_columns/pallas_call | solution.py:247
  10.4 1.4 collective-permute-start.1
  11.8 3.1 %collective-permute-start.2 = (bf16[3,20,20,2,128]{4,3,2,1,0:T(2,128)(2,1)S(1)}, bf16[3,20,20,2,128]{4,3,2,1,0:T(2,128)(2,1)S(1)}, u32[]{:S(2)}, u32[]{:S(2)}) collective-permute-start(bf16[3,20,20,2,128]{4,3,2,1,0:T(2,128)(2,1)S(1)} %copy-done.28), channel_id=1, source_target_pairs={{0,0},{8,32},{16,64},{24,96},{32,8},{40,40},{48,72},{56,104},{64,1... | collective-permute-start | bytes 1843208 | tf_op jit(solution)/shard_map/ppermute | solution.py:556
  15.0 1.2 add_convert_fusion.1
  16.2 7.1 %collective-permute-done.2 = bf16[3,20,20,2,128]{4,3,2,1,0:T(2,128)(2,1)S(1)} collective-permute-done((bf16[3,20,20,2,128]{4,3,2,1,0:T(2,128)(2,1)S(1)}, bf16[3,20,20,2,128]{4,3,2,1,0:T(2,128)(2,1)S(1)}, u32[]{:S(2)}, u32[]{:S(2)}) %collective-permute-start.2) | collective-permute-done | bytes 614432 | tf_op jit(solution)/shard_map/ppermute | solution.py:556
  23.3 10.2 %collective-permute-start.3 = (bf16[4,48,1280]{2,1,0:T(8,128)(2,1)S(1)}, bf16[4,48,1280]{2,1,0:T(8,128)(2,1)S(1)}, u32[]{:S(2)}, u32[]{:S(2)}) collective-permute-start(bf16[4,48,1280]{2,1,0:T(8,128)(2,1)S(1)} %add_convert_fusion.1), channel_id=1, source_target_pairs={{0,16},{8,24},{16,0},{24,8},{1,17},{9,25},{17,1},{25,9},{2,18},{10... | collective-permute-start | bytes 1474568 | tf_op jit(solution)/shard_map/ppermute | solution.py:514
  33.5 8.5 %collective-permute-done.3.c_ref = bf16[4,48,1280]{2,1,0:T(8,128)(2,1)S(1)} collective-permute-done((bf16[4,48,1280]{2,1,0:T(8,128)(2,1)S(1)}, bf16[4,48,1280]{2,1,0:T(8,128)(2,1)S(1)}, u32[]{:S(2)}, u32[]{:S(2)}) %collective-permute-start.3) | collective-permute-done | bytes 491552 | tf_op jit(solution)/shard_map/ppermute | solution.py:514
  42.8 3.5 %to_lines.2 = bf16[8,48,1280]{2,1,0:T(8,128)(2,1)} custom-call(s32[3]{0:T(128)} %pad_add_fusion.where_ref, bf16[4,48,1280]{2,1,0:T(8,128)(2,1)} %get-tuple-element.37.a_ref, bf16[4,48,1280]{2,1,0:T(8,128)(2,1)} %copy-done.10, bf16[4,48,1280]{2,1,0:T(8,128)(2,1)} %copy-done.14, bf16[8,384,192]{2,1,0:T(8,128)(2,1)} %constant.25.clone.table_ref), custom_call_target="tpu_custom_call" | custom-call | tf_op jit(solution)/shard_map/to_lines/pallas_call | solution.py:316
  46.3 7.5 %all-to-all-start = ((bf16[8,48,1280]{2,1,0:T(8,128)(2,1)}), bf16[8,48,1280]{2,1,0:T(8,128)(2,1)S(1)}, u32[]{:S(2)}, u32[]{:S(2)}) async-start(bf16[8,48,1280]{2,1,0:T(8,128)(2,1)} %to_lines.2), calls=%async_computation | async-start | bytes 1966080 | tf_op jit(solution)/shard_map/all_to_all | solution.py:538
  53.8 2.5 %collective-permute-start.5 = (bf16[3,20,20,2,128]{4,3,2,1,0:T(2,128)(2,1)S(1)}, bf16[3,20,20,2,128]{4,3,2,1,0:T(2,128)(2,1)S(1)}, u32[]{:S(2)}, u32[]{:S(2)}) collective-permute-start(bf16[3,20,20,2,128]{4,3,2,1,0:T(2,128)(2,1)S(1)} %collective-permute-done.2), channel_id=1, source_target_pairs={{64,0},{96,32},{0,64},{32,96},{65,1},{97,33},{1,65},{33,97},{66,2}... | collective-permute-start | bytes 1843208 | tf_op jit(solution)/shard_map/ppermute | solution.py:533
  56.3 2.0 collective-permute-start.4
  58.3 13.4 %collective-permute-done.6 = bf16[3,20,20,2,128]{4,3,2,1,0:T(2,128)(2,1)S(1)} collective-permute-done((bf16[3,20,20,2,128]{4,3,2,1,0:T(2,128)(2,1)S(1)}, bf16[3,20,20,2,128]{4,3,2,1,0:T(2,128)(2,1)S(1)}, u32[]{:S(2)}, u32[]{:S(2)}) %collective-permute-start.6) | collective-permute-done | bytes 614432 | tf_op jit(solution)/shard_map/ppermute | solution.py:533
  71.7 9.2 %collective-permute-done.5 = bf16[3,20,20,2,128]{4,3,2,1,0:T(2,128)(2,1)S(1)} collective-permute-done((bf16[3,20,20,2,128]{4,3,2,1,0:T(2,128)(2,1)S(1)}, bf16[3,20,20,2,128]{4,3,2,1,0:T(2,128)(2,1)S(1)}, u32[]{:S(2)}, u32[]{:S(2)}) %collective-permute-start.5) | collective-permute-done | bytes 614432 | tf_op jit(solution)/shard_map/ppermute | solution.py:533
  80.9 2.6 %collective-permute-done.4 = bf16[3,20,20,2,128]{4,3,2,1,0:T(2,128)(2,1)S(1)} collective-permute-done((bf16[3,20,20,2,128]{4,3,2,1,0:T(2,128)(2,1)S(1)}, bf16[3,20,20,2,128]{4,3,2,1,0:T(2,128)(2,1)S(1)}, u32[]{:S(2)}, u32[]{:S(2)}) %collective-permute-start.4) | collective-permute-done | bytes 614432 | tf_op jit(solution)/shard_map/ppermute | solution.py:533
  84.6 5.7 %mix_modes.1 = (bf16[8,48,1280]{2,1,0:T(8,128)(2,1)}, bf16[120,128]{1,0:T(8,128)(2,1)}, bf16[120,128]{1,0:T(8,128)(2,1)}, bf16[120,128]{1,0:T(8,128)(2,1)}, bf16[120,128]{1,0:T(8,128)(2,1)}) custom-call(s32[3]{0:T(128)} %pad_add_fusion.where_ref, bf16[8,48,1280]{2,1,0:T(8,128)(2,1)} %copy-done.3, bf16[3,20,40,128]{3,2,1,0:T(8,128)(2,1)} %bitcast.22, ...), custom_call_target="tpu_custom_call" | custom-call | tf_op jit(solution)/shard_map/mix_modes/pallas_call | solution.py:463
  90.3 6.7 %all-to-all-start.1 = ((bf16[8,48,1280]{2,1,0:T(8,128)(2,1)}), bf16[8,48,1280]{2,1,0:T(8,128)(2,1)S(1)}, u32[]{:S(2)}, u32[]{:S(2)}) async-start(bf16[8,48,1280]{2,1,0:T(8,128)(2,1)} %get-tuple-element.43), calls=%async_computation.1 | async-start | bytes 1966080 | tf_op jit(solution)/shard_map/all_to_all | solution.py:538
  97.0 5.0 %collective-permute-start.7 = (bf16[120,128]{1,0:T(8,128)(2,1)}, bf16[120,128]{1,0:T(8,128)(2,1)S(1)}, u32[]{:S(2)}, u32[]{:S(2)}) collective-permute-start(bf16[120,128]{1,0:T(8,128)(2,1)} %get-tuple-element.44), channel_id=1, source_target_pairs={{0,0},{8,32},{16,64},{24,96},{32,8},{40,40},{48,72},{56,104},{64,1... | collective-permute-start | bytes 92168 | tf_op jit(solution)/shard_map/ppermute | solution.py:547
  102.9 2.1 collective-permute-start.10
  105.0 2.2 collective-permute-done.9.s2
  107.2 2.7 %collective-permute-done.10.s3 = bf16[120,128]{1,0:T(8,128)(2,1)S(1)} collective-permute-done((bf16[120,128]{1,0:T(8,128)(2,1)}, bf16[120,128]{1,0:T(8,128)(2,1)S(1)}, u32[]{:S(2)}, u32[]{:S(2)}) %collective-permute-start.10) | collective-permute-done | bytes 30752 | tf_op jit(solution)/shard_map/ppermute | solution.py:547
  109.9 2.4 all-to-all-done.1.modes_ref
  112.4 0.9 copy-done.2
  113.3 3.1 %from_lines.2.i0 = bf16[4,48,1280]{2,1,0:T(8,128)(2,1)} custom-call(s32[3]{0:T(128)} %pad_add_fusion.where_ref, bf16[8,48,1280]{2,1,0:T(8,128)(2,1)} %copy-done.2, bf16[8,384,192]{2,1,0:T(8,128)(2,1)} %constant.25.clone.table_ref), custom_call_target="tpu_custom_call" | custom-call | tf_op jit(solution)/shard_map/from_lines/pallas_call | solution.py:316
  116.5 2.3 collective-permute-start.11
  118.8 1.6 collective-permute-start.12
  120.4 7.9 %collective-permute-done.11.i1 = bf16[4,48,1280]{2,1,0:T(8,128)(2,1)S(1)} collective-permute-done((bf16[4,48,1280]{2,1,0:T(8,128)(2,1)}, bf16[4,48,1280]{2,1,0:T(8,128)(2,1)S(1)}, u32[]{:S(2)}, u32[]{:S(2)}) %collective-permute-start.11) | collective-permute-done | bytes 491552 | tf_op jit(solution)/shard_map/ppermute | solution.py:514
  128.3 2.9 %collective-permute-start.13 = (bf16[4,48,1280]{2,1,0:T(8,128)(2,1)S(1)}, bf16[4,48,1280]{2,1,0:T(8,128)(2,1)S(1)}, u32[]{:S(2)}, u32[]{:S(2)}) collective-permute-start(bf16[4,48,1280]{2,1,0:T(8,128)(2,1)S(1)} %collective-permute-done.11.i1), channel_id=1, source_target_pairs={{0,8},{8,0},{16,24},{24,16},{1,9},{9,1},{17,25},{25,17},{2,10},{10... | collective-permute-start | bytes 1474568 | tf_op jit(solution)/shard_map/ppermute | solution.py:514
  131.2 1.8 fusion.mixer_ref
  134.0 18.8 %middle_columns.1 = (bf16[20,64,2048]{2,1,0:T(8,128)(2,1)}, bf16[20,64,2048]{2,1,0:T(8,128)(2,1)}, bf16[4,48,1280]{2,1,0:T(8,128)(2,1)}, bf16[4,48,1280]{2,1,0:T...) custom-call(s32[3]{0:T(128)} %pad_add_fusion.where_ref, f32[20]{0:T(128)} %bias_ref.1, ...), custom_call_target="tpu_custom_call" | custom-call | tf_op jit(solution)/shard_map/middle_columns/pallas_call | solution.py:264
  153.4 1.6 collective-permute-done.15
  154.9 1.2 add_convert_fusion
  156.1 1.7 collective-permute-start.16
  157.8 11.2 %collective-permute-done.16.c_ref = bf16[4,48,1280]{2,1,0:T(8,128)(2,1)S(1)} collective-permute-done((bf16[4,48,1280]{2,1,0:T(8,128)(2,1)S(1)}, bf16[4,48,1280]{2,1,0:T(8,128)(2,1)S(1)}, u32[]{:S(2)}, u32[]{:S(2)}) %collective-permute-start.16) | collective-permute-done | bytes 491552 | tf_op jit(solution)/shard_map/ppermute | solution.py:514
  169.9 3.5 %to_lines.3 = bf16[8,48,1280]{2,1,0:T(8,128)(2,1)} custom-call(s32[3]{0:T(128)} %pad_add_fusion.where_ref, bf16[4,48,1280]{2,1,0:T(8,128)(2,1)} %get-tuple-element.50.a_ref, bf16[4,48,1280]{2,1,0:T(8,128)(2,1)} %copy-done.12, bf16[4,48,1280]{2,1,0:T(8,128)(2,1)} %copy-done.15, bf16[8,384,192]{2,1,0:T(8,128)(2,1)} %constant.25.clone.table_ref), custom_call_target="tpu_custom_call" | custom-call | tf_op jit(solution)/shard_map/to_lines/pallas_call | solution.py:316
  173.3 20.1 %all_to_all.20.arrived_ref = bf16[8,48,1280]{2,1,0:T(8,128)(2,1)} all-to-all(bf16[8,48,1280]{2,1,0:T(8,128)(2,1)} %to_lines.3), channel_id=1, replica_groups=mesh['dp'=4,'gx'=4,'gy'=8] {'gy'}, dimensions={0} | all-to-all | bytes 1966080 | tf_op jit(solution)/shard_map/all_to_all | solution.py:538
  193.4 6.0 %back_modes.1 = (bf16[8,48,1280]{2,1,0:T(8,128)(2,1)}, bf16[120,128]{1,0:T(8,128)(2,1)}, bf16[120,128]{1,0:T(8,128)(2,1)}, bf16[120,128]{1,0:T(8,128)(2,1)}, bf16[120,128]{1,0:T(8,128)(2,1)}) custom-call(s32[3]{0:T(128)} %pad_add_fusion.where_ref, bf16[8,48,1280]{2,1,0:T(8,128)(2,1)} %all_to_all.20.arrived_ref, bf16[3,20,40,128]{3,2,1,0:T(8,128)(2,1)} %bitcast.23, ...), custom_call_target="tpu_custom_call" | custom-call | tf_op jit(solution)/shard_map/back_modes/pallas_call | solution.py:463
  199.4 3.6 %all-to-all-start.3 = ((bf16[8,48,1280]{2,1,0:T(8,128)(2,1)}), bf16[8,48,1280]{2,1,0:T(8,128)(2,1)S(1)}, u32[]{:S(2)}, u32[]{:S(2)}) async-start(bf16[8,48,1280]{2,1,0:T(8,128)(2,1)} %get-tuple-element.54), calls=%async_computation.3 | async-start | bytes 1966080 | tf_op jit(solution)/shard_map/all_to_all | solution.py:538
  203.0 7.4 %collective-permute-start.17 = (bf16[120,128]{1,0:T(8,128)(2,1)}, bf16[120,128]{1,0:T(8,128)(2,1)S(1)}, u32[]{:S(2)}, u32[]{:S(2)}) collective-permute-start(bf16[120,128]{1,0:T(8,128)(2,1)} %get-tuple-element.55), channel_id=1, source_target_pairs={{0,0},{8,32},{16,64},{24,96},{32,8},{40,40},{48,72},{56,104},{64,1... | collective-permute-start | bytes 92168 | tf_op jit(solution)/shard_map/ppermute | solution.py:547
  210.5 2.4 collective-permute-start.20
  213.0 2.6 %collective-permute-done.19.g2 = bf16[120,128]{1,0:T(8,128)(2,1)S(1)} collective-permute-done((bf16[120,128]{1,0:T(8,128)(2,1)}, bf16[120,128]{1,0:T(8,128)(2,1)S(1)}, u32[]{:S(2)}, u32[]{:S(2)}) %collective-permute-start.19) | collective-permute-done | bytes 30752 | tf_op jit(solution)/shard_map/ppermute | solution.py:547
  215.5 2.5 %collective-permute-done.20.g3 = bf16[120,128]{1,0:T(8,128)(2,1)S(1)} collective-permute-done((bf16[120,128]{1,0:T(8,128)(2,1)}, bf16[120,128]{1,0:T(8,128)(2,1)S(1)}, u32[]{:S(2)}, u32[]{:S(2)}) %collective-permute-start.20) | collective-permute-done | bytes 30752 | tf_op jit(solution)/shard_map/ppermute | solution.py:547
  218.1 0.9 copy-done.1
  219.0 3.1 %from_lines.3.i0 = bf16[4,48,1280]{2,1,0:T(8,128)(2,1)} custom-call(s32[3]{0:T(128)} %pad_add_fusion.where_ref, bf16[8,48,1280]{2,1,0:T(8,128)(2,1)} %copy-done.1, bf16[8,384,192]{2,1,0:T(8,128)(2,1)} %constant.25.clone.table_ref), custom_call_target="tpu_custom_call" | custom-call | tf_op jit(solution)/shard_map/from_lines/pallas_call | solution.py:316
  222.8 3.2 %collective-permute-start.22 = (bf16[4,48,1280]{2,1,0:T(8,128)(2,1)}, bf16[4,48,1280]{2,1,0:T(8,128)(2,1)S(1)}, u32[]{:S(2)}, u32[]{:S(2)}) collective-permute-start(bf16[4,48,1280]{2,1,0:T(8,128)(2,1)} %from_lines.3.i0), channel_id=1, source_target_pairs={{0,8},{8,0},{16,24},{24,16},{1,9},{9,1},{17,25},{25,17},{2,10},{10... | collective-permute-start | bytes 1474568 | tf_op jit(solution)/shard_map/ppermute | solution.py:514
  226.0 3.1 %outer_sum.1 = f32[3,20,40,128]{3,2,1,0:T(8,128)} custom-call(bf16[120,128]{1,0:T(8,128)(2,1)} %copy-done.20, bf16[120,128]{1,0:T(8,128)(2,1)} %copy-done.21, bf16[120,128]{1,0:T(8,128)(2,1)} %copy-done.22, bf16[120,128]{1,0:T(8,128)(2,1)} %copy-done.23, bf16[120,128]{1,0:T(8,128)(2,1)} %copy-done.24, bf16[120,128]{1,0:T(8,128)(2,1)} %copy-done.25, ...), custom_call_target="tpu_custom_call" | custom-call | tf_op jit(solution)/shard_map/outer_sum/pallas_call | solution.py:505
  229.1 2.5 collective-permute-done.21.i1
  231.5 4.6 %collective-permute-start.23 = (bf16[4,48,1280]{2,1,0:T(8,128)(2,1)S(1)}, bf16[4,48,1280]{2,1,0:T(8,128)(2,1)S(1)}, u32[]{:S(2)}, u32[]{:S(2)}) collective-permute-start(bf16[4,48,1280]{2,1,0:T(8,128)(2,1)S(1)} %collective-permute-done.21.i1), channel_id=1, source_target_pairs={{0,8},{8,0},{16,24},{24,16},{1,9},{9,1},{17,25},{25,17},{2,10},{10... | collective-permute-start | bytes 1474568 | tf_op jit(solution)/shard_map/ppermute | solution.py:514
  238.4 10.2 %end_columns.1 = bf16[20,64,2048]{2,1,0:T(8,128)(2,1)} custom-call(s32[3]{0:T(128)} %pad_add_fusion.where_ref, bf16[4,48,1280]{2,1,0:T(8,128)(2,1)} %from_lines.3.i0, bf16[4,48,1280]{2,1,0:T(8,128)(2,1)} %copy-done.16, bf16[4,48,1280]{2,1,0:T(8,128)(2,1)} %copy-done.17, bf16[4,48,1280]{2,1,0:T(8,128)(2,1)} %copy-done.18, ...), custom_call_target="tpu_custom_call" | custom-call | tf_op jit(solution)/shard_map/end_columns/pallas_call | solution.py:283
  (80 shorter events, 8.9 us)
Async XLA Ops:
  0.6 130.6 %copy-start = (bf16[20,20]{1,0:T(8,128)(2,1)S(1)}, bf16[20,20]{1,0:T(8,128)(2,1)}, u32[]{:S(2)}) copy-start(bf16[20,20]{1,0:T(8,128)(2,1)} %param.12) | copy-start | bytes 2404
  0.6 11.2 %copy-start.28 = (bf16[3,20,20,2,128]{4,3,2,1,0:T(2,128)(2,1)S(1)}, bf16[3,20,20,2,128]{4,3,2,1,0:T(2,128)(2,1)}, u32[]{:S(2)}) copy-start(bf16[3,20,20,2,128]{4,3,2,1,0:T(2,128)(2,1)} %param.11) | copy-start | bytes 1843204
  10.4 4.6 %collective-permute-start.1 = (bf16[4,48,1280]{2,1,0:T(8,128)(2,1)}, bf16[4,48,1280]{2,1,0:T(8,128)(2,1)S(1)}, u32[]{:S(2)}, u32[]{:S(2)}) collective-permute-start(bf16[4,48,1280]{2,1,0:T(8,128)(2,1)} %get-tuple-element.40), channel_id=1, source_target_pairs={{0,8},{8,0},{16,24},{24,16},{1,9},{9,1},{17,25},{25,17},{2,10},{10... | collective-permute-start | bytes 1474568 | tf_op jit(solution)/shard_map/ppermute | solution.py:514
  11.8 11.5 %collective-permute-start.2 = (bf16[3,20,20,2,128]{4,3,2,1,0:T(2,128)(2,1)S(1)}, bf16[3,20,20,2,128]{4,3,2,1,0:T(2,128)(2,1)S(1)}, u32[]{:S(2)}, u32[]{:S(2)}) collective-permute-start(bf16[3,20,20,2,128]{4,3,2,1,0:T(2,128)(2,1)S(1)} %copy-done.28), channel_id=1, source_target_pairs={{0,0},{8,32},{16,64},{24,96},{32,8},{40,40},{48,72},{56,104},{64,1... | collective-permute-start | bytes 1843208 | tf_op jit(solution)/shard_map/ppermute | solution.py:556
  14.9 18.6 %collective-permute-start = (bf16[4,48,1280]{2,1,0:T(8,128)(2,1)}, bf16[4,48,1280]{2,1,0:T(8,128)(2,1)S(1)}, u32[]{:S(2)}, u32[]{:S(2)}) collective-permute-start(bf16[4,48,1280]{2,1,0:T(8,128)(2,1)} %get-tuple-element.38), channel_id=1, source_target_pairs={{0,8},{8,0},{16,24},{24,16},{1,9},{9,1},{17,25},{25,17},{2,10},{10... | collective-permute-start | bytes 1474568 | tf_op jit(solution)/shard_map/ppermute | solution.py:514
  23.3 60.2 %copy-start.4 = (bf16[3,20,20,2,128]{4,3,2,1,0:T(2,128)(2,1)}, bf16[3,20,20,2,128]{4,3,2,1,0:T(2,128)(2,1)S(1)}, u32[]{:S(2)}) copy-start(bf16[3,20,20,2,128]{4,3,2,1,0:T(2,128)(2,1)S(1)} %collective-permute-done.2) | copy-start | bytes 1843204
  23.3 18.7 %collective-permute-start.3 = (bf16[4,48,1280]{2,1,0:T(8,128)(2,1)S(1)}, bf16[4,48,1280]{2,1,0:T(8,128)(2,1)S(1)}, u32[]{:S(2)}, u32[]{:S(2)}) collective-permute-start(bf16[4,48,1280]{2,1,0:T(8,128)(2,1)S(1)} %add_convert_fusion.1), channel_id=1, source_target_pairs={{0,16},{8,24},{16,0},{24,8},{1,17},{9,25},{17,1},{25,9},{2,18},{10... | collective-permute-start | bytes 1474568 | tf_op jit(solution)/shard_map/ppermute | solution.py:514
  33.5 8.5 %copy-start.10 = (bf16[4,48,1280]{2,1,0:T(8,128)(2,1)}, bf16[4,48,1280]{2,1,0:T(8,128)(2,1)S(1)}, u32[]{:S(2)}) copy-start(bf16[4,48,1280]{2,1,0:T(8,128)(2,1)S(1)} %collective-permute-done.b_ref) | copy-start | bytes 1474564
  46.3 84.9 %copy-start.8 = (bf16[160,20]{1,0:T(8,128)(2,1)S(1)}, bf16[160,20]{1,0:T(8,128)(2,1)}, u32[]{:S(2)}) copy-start(bf16[160,20]{1,0:T(8,128)(2,1)} %constant.22.clone) | copy-start | bytes 19204
  46.3 37.2 %all-to-all-start = ((bf16[8,48,1280]{2,1,0:T(8,128)(2,1)}), bf16[8,48,1280]{2,1,0:T(8,128)(2,1)S(1)}, u32[]{:S(2)}, u32[]{:S(2)}) async-start(bf16[8,48,1280]{2,1,0:T(8,128)(2,1)} %to_lines.2), calls=%async_computation | async-start | bytes 1966080 | tf_op jit(solution)/shard_map/all_to_all | solution.py:538
  53.8 17.9 %collective-permute-start.6 = (bf16[3,20,20,2,128]{4,3,2,1,0:T(2,128)(2,1)S(1)}, bf16[3,20,20,2,128]{4,3,2,1,0:T(2,128)(2,1)S(1)}, u32[]{:S(2)}, u32[]{:S(2)}) collective-permute-start(bf16[3,20,20,2,128]{4,3,2,1,0:T(2,128)(2,1)S(1)} %collective-permute-done.2), channel_id=1, source_target_pairs={{96,0},{0,32},{32,64},{64,96},{97,1},{1,33},{33,65},{65,97},{98,2}... | collective-permute-start | bytes 1843208 | tf_op jit(solution)/shard_map/ppermute | solution.py:533
  53.8 27.1 %collective-permute-start.5 = (bf16[3,20,20,2,128]{4,3,2,1,0:T(2,128)(2,1)S(1)}, bf16[3,20,20,2,128]{4,3,2,1,0:T(2,128)(2,1)S(1)}, u32[]{:S(2)}, u32[]{:S(2)}) collective-permute-start(bf16[3,20,20,2,128]{4,3,2,1,0:T(2,128)(2,1)S(1)} %collective-permute-done.2), channel_id=1, source_target_pairs={{64,0},{96,32},{0,64},{32,96},{65,1},{97,33},{1,65},{33,97},{66,2}... | collective-permute-start | bytes 1843208 | tf_op jit(solution)/shard_map/ppermute | solution.py:533
  56.3 27.2 %collective-permute-start.4 = (bf16[3,20,20,2,128]{4,3,2,1,0:T(2,128)(2,1)S(1)}, bf16[3,20,20,2,128]{4,3,2,1,0:T(2,128)(2,1)S(1)}, u32[]{:S(2)}, u32[]{:S(2)}) collective-permute-start(bf16[3,20,20,2,128]{4,3,2,1,0:T(2,128)(2,1)S(1)} %collective-permute-done.2), channel_id=1, source_target_pairs={{32,0},{64,32},{96,64},{0,96},{33,1},{65,33},{97,65},{1,97},{34,2}... | collective-permute-start | bytes 1843208 | tf_op jit(solution)/shard_map/ppermute | solution.py:533
  71.7 11.8 %copy-start.5 = (bf16[3,20,20,2,128]{4,3,2,1,0:T(2,128)(2,1)}, bf16[3,20,20,2,128]{4,3,2,1,0:T(2,128)(2,1)S(1)}, u32[]{:S(2)}) copy-start(bf16[3,20,20,2,128]{4,3,2,1,0:T(2,128)(2,1)S(1)} %collective-permute-done.6) | copy-start | bytes 1843204
  80.9 2.7 %copy-start.6 = (bf16[3,20,20,2,128]{4,3,2,1,0:T(2,128)(2,1)}, bf16[3,20,20,2,128]{4,3,2,1,0:T(2,128)(2,1)S(1)}, u32[]{:S(2)}) copy-start(bf16[3,20,20,2,128]{4,3,2,1,0:T(2,128)(2,1)S(1)} %collective-permute-done.5) | copy-start | bytes 1843204
  83.5 1.1 copy-start.3
  90.3 22.0 %all-to-all-start.1 = ((bf16[8,48,1280]{2,1,0:T(8,128)(2,1)}), bf16[8,48,1280]{2,1,0:T(8,128)(2,1)S(1)}, u32[]{:S(2)}, u32[]{:S(2)}) async-start(bf16[8,48,1280]{2,1,0:T(8,128)(2,1)} %get-tuple-element.43), calls=%async_computation.1 | async-start | bytes 1966080 | tf_op jit(solution)/shard_map/all_to_all | solution.py:538
  97.0 8.0 %collective-permute-start.7 = (bf16[120,128]{1,0:T(8,128)(2,1)}, bf16[120,128]{1,0:T(8,128)(2,1)S(1)}, u32[]{:S(2)}, u32[]{:S(2)}) collective-permute-start(bf16[120,128]{1,0:T(8,128)(2,1)} %get-tuple-element.44), channel_id=1, source_target_pairs={{0,0},{8,32},{16,64},{24,96},{32,8},{40,40},{48,72},{56,104},{64,1... | collective-permute-start | bytes 92168 | tf_op jit(solution)/shard_map/ppermute | solution.py:547
  102.0 3.0 %collective-permute-start.8 = (bf16[120,128]{1,0:T(8,128)(2,1)}, bf16[120,128]{1,0:T(8,128)(2,1)S(1)}, u32[]{:S(2)}, u32[]{:S(2)}) collective-permute-start(bf16[120,128]{1,0:T(8,128)(2,1)} %get-tuple-element.45), channel_id=1, source_target_pairs={{0,8},{8,40},{16,72},{24,104},{32,16},{40,48},{48,80},{56,112},{64... | collective-permute-start | bytes 92168 | tf_op jit(solution)/shard_map/ppermute | solution.py:547
  102.1 5.1 %collective-permute-start.9 = (bf16[120,128]{1,0:T(8,128)(2,1)}, bf16[120,128]{1,0:T(8,128)(2,1)S(1)}, u32[]{:S(2)}, u32[]{:S(2)}) collective-permute-start(bf16[120,128]{1,0:T(8,128)(2,1)} %get-tuple-element.46), channel_id=1, source_target_pairs={{0,16},{8,48},{16,80},{24,112},{32,24},{40,56},{48,88},{56,120},{6... | collective-permute-start | bytes 92168 | tf_op jit(solution)/shard_map/ppermute | solution.py:547
  102.9 7.1 %collective-permute-start.10 = (bf16[120,128]{1,0:T(8,128)(2,1)}, bf16[120,128]{1,0:T(8,128)(2,1)S(1)}, u32[]{:S(2)}, u32[]{:S(2)}) collective-permute-start(bf16[120,128]{1,0:T(8,128)(2,1)} %get-tuple-element.47), channel_id=1, source_target_pairs={{0,24},{8,56},{16,88},{24,120},{32,0},{40,32},{48,64},{56,96},{64,... | collective-permute-start | bytes 92168 | tf_op jit(solution)/shard_map/ppermute | solution.py:547
  105.0 117.2 %copy-start.20 = (bf16[120,128]{1,0:T(8,128)(2,1)}, bf16[120,128]{1,0:T(8,128)(2,1)S(1)}, u32[]{:S(2)}) copy-start(bf16[120,128]{1,0:T(8,128)(2,1)S(1)} %collective-permute-done.7.s0) | copy-start | bytes 92164
  105.0 117.1 %copy-start.21 = (bf16[120,128]{1,0:T(8,128)(2,1)}, bf16[120,128]{1,0:T(8,128)(2,1)S(1)}, u32[]{:S(2)}) copy-start(bf16[120,128]{1,0:T(8,128)(2,1)S(1)} %collective-permute-done.8.s1) | copy-start | bytes 92164
  107.2 114.9 %copy-start.22 = (bf16[120,128]{1,0:T(8,128)(2,1)}, bf16[120,128]{1,0:T(8,128)(2,1)S(1)}, u32[]{:S(2)}) copy-start(bf16[120,128]{1,0:T(8,128)(2,1)S(1)} %collective-permute-done.9.s2) | copy-start | bytes 92164
  109.9 112.2 %copy-start.23 = (bf16[120,128]{1,0:T(8,128)(2,1)}, bf16[120,128]{1,0:T(8,128)(2,1)S(1)}, u32[]{:S(2)}) copy-start(bf16[120,128]{1,0:T(8,128)(2,1)S(1)} %collective-permute-done.10.s3) | copy-start | bytes 92164
  116.5 11.8 %collective-permute-start.11 = (bf16[4,48,1280]{2,1,0:T(8,128)(2,1)}, bf16[4,48,1280]{2,1,0:T(8,128)(2,1)S(1)}, u32[]{:S(2)}, u32[]{:S(2)}) collective-permute-start(bf16[4,48,1280]{2,1,0:T(8,128)(2,1)} %from_lines.2.i0), channel_id=1, source_target_pairs={{0,16},{8,24},{16,0},{24,8},{1,17},{9,25},{17,1},{25,9},{2,18},{10... | collective-permute-start | bytes 1474568 | tf_op jit(solution)/shard_map/ppermute | solution.py:514
  118.8 14.2 %collective-permute-start.12 = (bf16[4,48,1280]{2,1,0:T(8,128)(2,1)}, bf16[4,48,1280]{2,1,0:T(8,128)(2,1)S(1)}, u32[]{:S(2)}, u32[]{:S(2)}) collective-permute-start(bf16[4,48,1280]{2,1,0:T(8,128)(2,1)} %from_lines.2.i0), channel_id=1, source_target_pairs={{0,8},{8,0},{16,24},{24,16},{1,9},{9,1},{17,25},{25,17},{2,10},{10... | collective-permute-start | bytes 1474568 | tf_op jit(solution)/shard_map/ppermute | solution.py:514
  128.3 4.7 %copy-start.9 = (bf16[4,48,1280]{2,1,0:T(8,128)(2,1)}, bf16[4,48,1280]{2,1,0:T(8,128)(2,1)S(1)}, u32[]{:S(2)}) copy-start(bf16[4,48,1280]{2,1,0:T(8,128)(2,1)S(1)} %collective-permute-done.11.i1) | copy-start | bytes 1474564
  128.3 4.7 %collective-permute-start.13 = (bf16[4,48,1280]{2,1,0:T(8,128)(2,1)S(1)}, bf16[4,48,1280]{2,1,0:T(8,128)(2,1)S(1)}, u32[]{:S(2)}, u32[]{:S(2)}) collective-permute-start(bf16[4,48,1280]{2,1,0:T(8,128)(2,1)S(1)} %collective-permute-done.11.i1), channel_id=1, source_target_pairs={{0,8},{8,0},{16,24},{24,16},{1,9},{9,1},{17,25},{25,17},{2,10},{10... | collective-permute-start | bytes 1474568 | tf_op jit(solution)/shard_map/ppermute | solution.py:514
  133.0 1.0 copy-start.13
  152.8 2.2 collective-permute-start.15
  153.0 4.9 %collective-permute-start.14 = (bf16[4,48,1280]{2,1,0:T(8,128)(2,1)}, bf16[4,48,1280]{2,1,0:T(8,128)(2,1)S(1)}, u32[]{:S(2)}, u32[]{:S(2)}) collective-permute-start(bf16[4,48,1280]{2,1,0:T(8,128)(2,1)} %get-tuple-element.51), channel_id=1, source_target_pairs={{0,8},{8,0},{16,24},{24,16},{1,9},{9,1},{17,25},{25,17},{2,10},{10... | collective-permute-start | bytes 1474568 | tf_op jit(solution)/shard_map/ppermute | solution.py:514
  156.1 13.0 %collective-permute-start.16 = (bf16[4,48,1280]{2,1,0:T(8,128)(2,1)S(1)}, bf16[4,48,1280]{2,1,0:T(8,128)(2,1)S(1)}, u32[]{:S(2)}, u32[]{:S(2)}) collective-permute-start(bf16[4,48,1280]{2,1,0:T(8,128)(2,1)S(1)} %add_convert_fusion), channel_id=1, source_target_pairs={{0,16},{8,24},{16,0},{24,8},{1,17},{9,25},{17,1},{25,9},{2,18},{10... | collective-permute-start | bytes 1474568 | tf_op jit(solution)/shard_map/ppermute | solution.py:514
  157.8 11.2 %copy-start.12 = (bf16[4,48,1280]{2,1,0:T(8,128)(2,1)}, bf16[4,48,1280]{2,1,0:T(8,128)(2,1)S(1)}, u32[]{:S(2)}) copy-start(bf16[4,48,1280]{2,1,0:T(8,128)(2,1)S(1)} %collective-permute-done.14.b_ref) | copy-start | bytes 1474564
  193.4 42.7 %copy-start.19 = (bf16[160,160]{1,0:T(8,128)(2,1)S(1)}, bf16[160,160]{1,0:T(8,128)(2,1)}, u32[]{:S(2)}) copy-start(bf16[160,160]{1,0:T(8,128)(2,1)} %constant.26.clone) | copy-start | bytes 153604
  199.4 18.6 %all-to-all-start.3 = ((bf16[8,48,1280]{2,1,0:T(8,128)(2,1)}), bf16[8,48,1280]{2,1,0:T(8,128)(2,1)S(1)}, u32[]{:S(2)}, u32[]{:S(2)}) async-start(bf16[8,48,1280]{2,1,0:T(8,128)(2,1)} %get-tuple-element.54), calls=%async_computation.3 | async-start | bytes 1966080 | tf_op jit(solution)/shard_map/all_to_all | solution.py:538
  203.0 10.0 %collective-permute-start.17 = (bf16[120,128]{1,0:T(8,128)(2,1)}, bf16[120,128]{1,0:T(8,128)(2,1)S(1)}, u32[]{:S(2)}, u32[]{:S(2)}) collective-permute-start(bf16[120,128]{1,0:T(8,128)(2,1)} %get-tuple-element.55), channel_id=1, source_target_pairs={{0,0},{8,32},{16,64},{24,96},{32,8},{40,40},{48,72},{56,104},{64,1... | collective-permute-start | bytes 92168 | tf_op jit(solution)/shard_map/ppermute | solution.py:547
  210.3 2.6 %collective-permute-start.18 = (bf16[120,128]{1,0:T(8,128)(2,1)}, bf16[120,128]{1,0:T(8,128)(2,1)S(1)}, u32[]{:S(2)}, u32[]{:S(2)}) collective-permute-start(bf16[120,128]{1,0:T(8,128)(2,1)} %get-tuple-element.56), channel_id=1, source_target_pairs={{0,8},{8,40},{16,72},{24,104},{32,16},{40,48},{48,80},{56,112},{64... | collective-permute-start | bytes 92168 | tf_op jit(solution)/shard_map/ppermute | solution.py:547
  210.4 5.1 %collective-permute-start.19 = (bf16[120,128]{1,0:T(8,128)(2,1)}, bf16[120,128]{1,0:T(8,128)(2,1)S(1)}, u32[]{:S(2)}, u32[]{:S(2)}) collective-permute-start(bf16[120,128]{1,0:T(8,128)(2,1)} %get-tuple-element.57), channel_id=1, source_target_pairs={{0,16},{8,48},{16,80},{24,112},{32,24},{40,56},{48,88},{56,120},{6... | collective-permute-start | bytes 92168 | tf_op jit(solution)/shard_map/ppermute | solution.py:547
  210.5 7.5 %collective-permute-start.20 = (bf16[120,128]{1,0:T(8,128)(2,1)}, bf16[120,128]{1,0:T(8,128)(2,1)S(1)}, u32[]{:S(2)}, u32[]{:S(2)}) collective-permute-start(bf16[120,128]{1,0:T(8,128)(2,1)} %get-tuple-element.58), channel_id=1, source_target_pairs={{0,24},{8,56},{16,88},{24,120},{32,0},{40,32},{48,64},{56,96},{64,... | collective-permute-start | bytes 92168 | tf_op jit(solution)/shard_map/ppermute | solution.py:547
  212.9 13.0 %copy-start.24 = (bf16[120,128]{1,0:T(8,128)(2,1)}, bf16[120,128]{1,0:T(8,128)(2,1)S(1)}, u32[]{:S(2)}) copy-start(bf16[120,128]{1,0:T(8,128)(2,1)S(1)} %collective-permute-done.17.g0) | copy-start | bytes 92164
  212.9 13.0 %copy-start.25 = (bf16[120,128]{1,0:T(8,128)(2,1)}, bf16[120,128]{1,0:T(8,128)(2,1)S(1)}, u32[]{:S(2)}) copy-start(bf16[120,128]{1,0:T(8,128)(2,1)S(1)} %collective-permute-done.18.g1) | copy-start | bytes 92164
  215.5 10.4 %copy-start.26 = (bf16[120,128]{1,0:T(8,128)(2,1)}, bf16[120,128]{1,0:T(8,128)(2,1)S(1)}, u32[]{:S(2)}) copy-start(bf16[120,128]{1,0:T(8,128)(2,1)S(1)} %collective-permute-done.19.g2) | copy-start | bytes 92164
  218.0 7.9 %copy-start.27 = (bf16[120,128]{1,0:T(8,128)(2,1)}, bf16[120,128]{1,0:T(8,128)(2,1)S(1)}, u32[]{:S(2)}) copy-start(bf16[120,128]{1,0:T(8,128)(2,1)S(1)} %collective-permute-done.20.g3) | copy-start | bytes 92164
  222.2 9.4 %collective-permute-start.21 = (bf16[4,48,1280]{2,1,0:T(8,128)(2,1)}, bf16[4,48,1280]{2,1,0:T(8,128)(2,1)S(1)}, u32[]{:S(2)}, u32[]{:S(2)}) collective-permute-start(bf16[4,48,1280]{2,1,0:T(8,128)(2,1)} %from_lines.3.i0), channel_id=1, source_target_pairs={{0,16},{8,24},{16,0},{24,8},{1,17},{9,25},{17,1},{25,9},{2,18},{10... | collective-permute-start | bytes 1474568 | tf_op jit(solution)/shard_map/ppermute | solution.py:514
  222.8 14.2 %collective-permute-start.22 = (bf16[4,48,1280]{2,1,0:T(8,128)(2,1)}, bf16[4,48,1280]{2,1,0:T(8,128)(2,1)S(1)}, u32[]{:S(2)}, u32[]{:S(2)}) collective-permute-start(bf16[4,48,1280]{2,1,0:T(8,128)(2,1)} %from_lines.3.i0), channel_id=1, source_target_pairs={{0,8},{8,0},{16,24},{24,16},{1,9},{9,1},{17,25},{25,17},{2,10},{10... | collective-permute-start | bytes 1474568 | tf_op jit(solution)/shard_map/ppermute | solution.py:514
  231.5 6.1 %copy-start.16 = (bf16[4,48,1280]{2,1,0:T(8,128)(2,1)}, bf16[4,48,1280]{2,1,0:T(8,128)(2,1)S(1)}, u32[]{:S(2)}) copy-start(bf16[4,48,1280]{2,1,0:T(8,128)(2,1)S(1)} %collective-permute-done.21.i1) | copy-start | bytes 1474564
  231.5 6.0 %collective-permute-start.23 = (bf16[4,48,1280]{2,1,0:T(8,128)(2,1)S(1)}, bf16[4,48,1280]{2,1,0:T(8,128)(2,1)S(1)}, u32[]{:S(2)}, u32[]{:S(2)}) collective-permute-start(bf16[4,48,1280]{2,1,0:T(8,128)(2,1)S(1)} %collective-permute-done.21.i1), channel_id=1, source_target_pairs={{0,8},{8,0},{16,24},{24,16},{1,9},{9,1},{17,25},{25,17},{2,10},{10... | collective-permute-start | bytes 1474568 | tf_op jit(solution)/shard_map/ppermute | solution.py:514
  (8 other events, 6.7 us)

commit v3 on v2

--- a/solution.py
+++ b/solution.py
@@ -51,23 +51,22 @@
 
 
 def depth_tables():
-    out = np.zeros((GX, 2, GX, KB, YB, YB, NZ), np.float32)
+    out = np.zeros((GX, 2, GX, KB, LANES), np.float32)
     for b in range(GX):
         for pos, delta in enumerate(ORDER):
             freqs = (b ^ delta) * KB + np.arange(KB)
             cosine, sine = wave(freqs, np.arange(NZ), NZ)
-            for y in range(YB):
-                out[b, 0, pos, :, y, y] = cosine
-                out[b, 1, pos, :, y, y] = -sine
-    return out.reshape(GX, 2 * KZ * YB, LANES).astype(ml_dtypes.bfloat16)
+            out[b, 0, pos] = np.tile(cosine, (1, YB))
+            out[b, 1, pos] = np.tile(-sine, (1, YB))
+    return out.reshape(GX, 2 * KZ, LANES).astype(ml_dtypes.bfloat16)
 
 
 def width_tables():
-    out = np.zeros((GX, 2, XL, GL), np.float32)
+    out = np.zeros((GX, 2, XL, KX), np.float32)
     for b in range(GX):
         cosine, sine = wave(kept(KX), b * XL + np.arange(XL), NX)
-        out[b, 0] = np.tile(cosine.T, (1, GROUP))
-        out[b, 1] = np.tile(sine.T, (1, GROUP))
+        out[b, 0] = cosine.T
+        out[b, 1] = sine.T
     return out.astype(ml_dtypes.bfloat16)
 
 
@@ -103,12 +102,17 @@
     )
 
 
-def fill_width(wide_ref, tall_ref, long_ref):
+def fill_tables(strip_ref, wide_ref, depth_ref, tall_ref, long_ref):
+    strips = jnp.broadcast_to(strip_ref[0].astype(F32)[:, None, :], (2 * KZ, YB, LANES))
+    row = lax.broadcasted_iota(jnp.int32, (2 * KZ, YB, LANES), 1)
+    column = lax.broadcasted_iota(jnp.int32, (2 * KZ, YB, LANES), 2) // NZ
+    blocks = jnp.where(row == column, strips, 0.0)
+    depth_ref[...] = blocks.reshape(2 * KZ * YB, LANES).astype(BF)
     rows = lax.broadcasted_iota(jnp.int32, (GL, GL), 0) // XL
     columns = lax.broadcasted_iota(jnp.int32, (GL, GL), 1) // KX
     for part in range(2):
         strip = wide_ref[0, part].astype(F32)
-        full = jnp.concatenate([strip] * GROUP, axis=0)
+        full = jnp.concatenate([jnp.concatenate([strip] * GROUP, axis=1)] * GROUP, axis=0)
         block = jnp.where(rows == columns, full, 0.0).astype(BF)
         tall_ref[GL * part : GL * (part + 1), :] = block
         long_ref[:, GL * part : GL * (part + 1)] = block
@@ -116,7 +120,7 @@
 
 def forward_group(rows, depth_ref, tall_ref, outs, j):
     half = KZ * YB
-    planes = dot(depth_ref[0], rows, 1, 1)
+    planes = dot(depth_ref[...], rows, 1, 1)
     real = planes[:half]
     imag = planes[half:]
     sides = jnp.concatenate(
@@ -140,7 +144,7 @@
         [jnp.concatenate([real, -imag], axis=1), jnp.concatenate([imag, real], axis=1)], axis=0
     ).astype(BF)
     planes = dot(long_ref[...], sides, 1, 1).astype(BF)
-    return dot(planes, depth_ref[0])
+    return dot(planes, depth_ref[...])
 
 
 def set_bypass(source_ref, mixer_ref, total_ref):
@@ -154,10 +158,12 @@
     return ref[GROUP * j : GROUP * (j + 1)].reshape(GROUP * XL, LANES)
 
 
-def start_kernel(where_ref, field_ref, depth_ref, wide_ref, o0, o1, o2, o3, tall_ref, long_ref):
+def start_kernel(
+    where_ref, field_ref, strip_ref, wide_ref, o0, o1, o2, o3, depth_ref, tall_ref, long_ref
+):
     @pl.when(pl.program_id(0) == 0)
     def _():
-        fill_width(wide_ref, tall_ref, long_ref)
+        fill_tables(strip_ref, wide_ref, depth_ref, tall_ref, long_ref)
 
     for j in range(GROUPS):
         forward_group(group_rows(field_ref, j), depth_ref, tall_ref, (o0, o1, o2, o3), j)
@@ -184,12 +190,12 @@
 
 
 def middle_kernel(
-    where_ref, bias_ref, i0, i1, i2, i3, field_ref, upstream_ref, mixer_ref, depth_ref, wide_ref,
-    act_ref, grad_ref, o0, o1, o2, o3, tall_ref, long_ref, total_ref,
+    where_ref, bias_ref, i0, i1, i2, i3, field_ref, upstream_ref, mixer_ref, strip_ref, wide_ref,
+    act_ref, grad_ref, o0, o1, o2, o3, depth_ref, tall_ref, long_ref, total_ref,
 ):
     @pl.when(pl.program_id(0) == 0)
     def _():
-        fill_width(wide_ref, tall_ref, long_ref)
+        fill_tables(strip_ref, wide_ref, depth_ref, tall_ref, long_ref)
 
     set_bypass(field_ref, mixer_ref, total_ref)
 
@@ -212,12 +218,12 @@
 
 
 def end_kernel(
-    where_ref, i0, i1, i2, i3, grad_ref, mixer_ref, depth_ref, wide_ref, out_ref,
-    tall_ref, long_ref, total_ref,
+    where_ref, i0, i1, i2, i3, grad_ref, mixer_ref, strip_ref, wide_ref, out_ref,
+    depth_ref, tall_ref, long_ref, total_ref,
 ):
     @pl.when(pl.program_id(0) == 0)
     def _():
-        fill_width(wide_ref, tall_ref, long_ref)
+        fill_tables(strip_ref, wide_ref, depth_ref, tall_ref, long_ref)
 
     set_bypass(grad_ref, mixer_ref, total_ref)
     for j in range(GROUPS):
@@ -226,18 +232,26 @@
         out_ref[group] = (total_ref[group] + values.reshape(GROUP, XL, LANES)).astype(BF)
 
 
+def cost(micros):
+    return pl.CostEstimate(flops=0, bytes_accessed=micros * 3_000_000, transcendentals=0)
+
+
 def column_specs():
     columns = pl.BlockSpec((CH, XL, LANES), lambda i, w: (0, 0, i))
     coeffs = pl.BlockSpec((1, ROWS, WIDE), lambda i, w: (i, 0, 0))
-    depth = pl.BlockSpec((1, 2 * KZ * YB, LANES), lambda i, w: (w[1], 0, 0))
-    wide = pl.BlockSpec((1, 2, XL, GL), lambda i, w: (w[1], 0, 0, 0))
+    depth = pl.BlockSpec((1, 2 * KZ, LANES), lambda i, w: (w[1], 0, 0))
+    wide = pl.BlockSpec((1, 2, XL, KX), lambda i, w: (w[1], 0, 0, 0))
     mixer = pl.BlockSpec((CH * XB, CH * XB), lambda i, w: (0, 0))
     return columns, coeffs, depth, wide, mixer
 
 
 COEFFS = jax.ShapeDtypeStruct((STEPS, ROWS, WIDE), BF)
 COLUMNS = jax.ShapeDtypeStruct((CH, XL, YL * NZ), BF)
-BLOCKS = [pltpu.VMEM((2 * GL, GL), BF), pltpu.VMEM((GL, 2 * GL), BF)]
+BLOCKS = [
+    pltpu.VMEM((2 * KZ * YB, LANES), BF),
+    pltpu.VMEM((2 * GL, GL), BF),
+    pltpu.VMEM((GL, 2 * GL), BF),
+]
 TOTAL = pltpu.VMEM((CH, XL, LANES), F32)
 PARAMS = pltpu.CompilerParams(vmem_limit_bytes=56 * 1024 * 1024)
 
@@ -255,6 +269,7 @@
         ),
         out_shape=[COEFFS] * 4,
         compiler_params=PARAMS,
+        cost_estimate=cost(8),
         name="start_columns",
     )(where, field, jnp.asarray(DEPTH), jnp.asarray(WIDTH))
 
@@ -274,6 +289,7 @@
         ),
         out_shape=[COLUMNS, COLUMNS] + [COEFFS] * 4,
         compiler_params=PARAMS,
+        cost_estimate=cost(19),
         name="middle_columns",
     )(where, bias, *coeffs_in, field, upstream, mixer, jnp.asarray(DEPTH), jnp.asarray(WIDTH))
 
@@ -291,6 +307,7 @@
         ),
         out_shape=COLUMNS,
         compiler_params=PARAMS,
+        cost_estimate=cost(10),
         name="end_columns",
     )(where, *coeffs_in, grad, mixer, jnp.asarray(DEPTH), jnp.asarray(WIDTH))
 
@@ -322,6 +339,7 @@
             out_specs=pl.BlockSpec(out_shape.shape, lambda i, w: (0, 0, 0)),
         ),
         out_shape=out_shape,
+        cost_estimate=cost(3),
         name=name,
     )(where, *ins, jnp.asarray(LINE))
 
@@ -335,6 +353,7 @@
     return line_call(unline_kernel, "from_lines", where, (modes,), COEFFS)
 
 
+UNROLL = 4
 SETS = GX * KB
 PAIR = 2 * CH
 HALF = KX
@@ -405,7 +424,7 @@
 
 
 def set_row(where_ref, k):
-    block = lax.rem(where_ref[0] + k, DP) * KB + pl.program_id(0)
+    block = (lax.rem(where_ref[0] + k, DP) ^ (2 * (where_ref[1] & 1))) * KB + pl.program_id(0)
     return pl.multiple_of(block * PAIR, 8)
 
 
@@ -421,12 +440,18 @@
 
     for k, weight_ref in enumerate((w0, w1, w2, w3)):
         base = set_row(where_ref, k)
-        by_real = jnp.zeros((PAIR, 2 * HALF), F32)
-        by_imag = jnp.zeros((PAIR, 2 * HALF), F32)
-        for c in range(CH):
-            weight = weight_ref[0, c].astype(F32)
-            by_real = by_real + weight * in_ref[pl.ds(base + 2 * c, 1), :]
-            by_imag = by_imag + weight * in_ref[pl.ds(base + 2 * c + 1, 1), :]
+
+        def add(i, totals, weight_ref=weight_ref, base=base):
+            by_real, by_imag = totals
+            for r in range(UNROLL):
+                c = i * UNROLL + r
+                weight = weight_ref[0, c].astype(F32)
+                by_real = by_real + weight * in_ref[pl.ds(base + 2 * c, 1), :]
+                by_imag = by_imag + weight * in_ref[pl.ds(base + 2 * c + 1, 1), :]
+            return by_real, by_imag
+
+        zero = jnp.zeros((PAIR, 2 * HALF), F32)
+        by_real, by_imag = lax.fori_loop(0, CH // UNROLL, add, (zero, zero))
         mix_ref[pl.ds(base, PAIR), :] = (by_real + turned(by_imag)).astype(BF).astype(F32)
 
     @pl.when(step == KB - 1)
@@ -448,10 +473,16 @@
         base = set_row(where_ref, k)
         grad = in_ref[pl.ds(base, PAIR), :]
         other = -turned(grad)
-        for c in range(CH):
-            weight = weight_ref[0, c].astype(F32)
-            mix_ref[pl.ds(base + 2 * c, 1), :] = jnp.sum(weight * grad, axis=0, keepdims=True)
-            mix_ref[pl.ds(base + 2 * c + 1, 1), :] = jnp.sum(weight * other, axis=0, keepdims=True)
+
+        @pl.loop(0, CH // UNROLL)
+        def _(i, weight_ref=weight_ref, base=base, grad=grad, other=other):
+            for r in range(UNROLL):
+                c = i * UNROLL + r
+                weight = weight_ref[0, c].astype(F32)
+                mix_ref[pl.ds(base + 2 * c, 1), :] = jnp.sum(weight * grad, axis=0, keepdims=True)
+                mix_ref[pl.ds(base + 2 * c + 1, 1), :] = jnp.sum(
+                    weight * other, axis=0, keepdims=True
+                )
 
     @pl.when(step == KB - 1)
     def _():
@@ -476,6 +507,7 @@
         ),
         out_shape=[jax.ShapeDtypeStruct((GY, 48, WIDE), BF)]
         + [jax.ShapeDtypeStruct((KB * PAIR, 2 * HALF), BF)] * 4,
+        cost_estimate=cost(5),
         name=name,
     )(where, arrived, *weights)
 
@@ -506,6 +538,7 @@
         outer_kernel,
         out_shape=jax.ShapeDtypeStruct((KB, CH, PAIR, 2 * HALF), F32),
         scratch_shapes=[pltpu.VMEM((DP, KB * PAIR, 2 * HALF), F32)],
+        cost_estimate=cost(3),
         name="outer_sum",
     )(*spectra, *grads)
 
@@ -514,11 +547,10 @@
     return lax.ppermute(values, "gx", [(i, i ^ bit) for i in range(GX)])
 
 
-def start_slabs(pieces, *waiting):
+def start_slabs(pieces):
     own, far, near, across = pieces
     far_sum = (far.astype(F32) + swap(across, 1).astype(F32)).astype(BF)
-    far_sum, *waiting = lax.optimization_barrier((far_sum, *waiting))
-    return own, swap(near, 1), swap(far_sum, 2), *waiting
+    return own, swap(near, 1), swap(far_sum, 2)
 
 
 def share_slabs(own, *waiting):
@@ -552,7 +584,7 @@
     where = jnp.stack(
         [lax.axis_index("dp"), lax.axis_index("gx"), lax.axis_index("gy")]
     ).astype(jnp.int32)
-    turn = [(a * GX + b, b * GX + a) for a in range(DP) for b in range(GX)]
+    turn = [(a * GX + b, (b ^ (2 * (a % 2))) * GX + a) for a in range(DP) for b in range(GX)]
     weight = lax.ppermute(spectral_weight, ("dp", "gx"), turn)
     spread = jnp.asarray(SPREAD)
 
@@ -561,9 +593,13 @@
         return wide.astype(BF) * jnp.asarray(SAME)
 
     values = field[0]
-    *parts, weight = start_slabs(start_columns(where, values), weight)
+    *pieces, weight = lax.optimization_barrier((*start_columns(where, values), weight))
+    parts = start_slabs(pieces)
     weights = gather_weights(weight)
-    arrived = exchange_lines(to_lines(where, *parts))
+    lines, weights[1], weights[3] = lax.optimization_barrier(
+        (to_lines(where, *parts), weights[1], weights[3])
+    )
+    arrived = exchange_lines(lines)
     modes, *spectra = mode_call(mix_kernel, "mix_modes", where, arrived, weights)
     modes, *spectra = lax.optimization_barrier((exchange_lines(modes), *to_owners(spectra)))
     coeffs = share_slabs(from_lines(where, modes))

time: 252 us -> 228 us (0.905)
  waiting for transfers between devices: 77 us -> 59.7 us
  starting transfers between devices: 72.4 us -> 66.2 us
    ppermute x3, waiting for transfers between devices: 25.2 us -> 14.6 us  [gather_weights(): lax.ppermute(weight, 'dp', [((a + k) % DP, a) for a in range(DP)])]
    ppermute x1, waiting for transfers between devices: 7.07 us -> 0.01 us  [per_device(): weight = lax.ppermute(spectral_weight, ('dp', 'gx'), turn)]
    all_to_all x3, waiting for transfers between devices: 2.45 us -> 7.13 us  [exchange_lines(): return lax.all_to_all(parts, 'gy', split_axis=0, concat_axis=0, tiled=True)]
    ppermute x12, starting transfers between devices: 29.2 us -> 25.2 us  [swap(): return lax.ppermute(values, 'gx', [(i, i ^ bit) for i in range(GX)])]
    ppermute x8, starting transfers between devices: 17.9 us -> 14.1 us  [to_owners(): moved.append(lax.ppermute(chunk, ('dp', 'gx'), pairs))]
    unnamed x58 -> x56, local copies, waits for them, and re-layouts: 6.4 us -> 6.38 us
  transfers between devices with their start and end apart: 27 -> 27, of which waited for: 15 -> 13; matrix products, arithmetic and copies ran while one was open for 2% -> 2% of each run, Pallas kernels for 1% -> 7%
where the time goes in v3:
time: 228 us; the launch traced here: 227 us
  Pallas kernels  66.6 us (29%)
  starting transfers between devices  66.2 us (29%)
  waiting for transfers between devices  59.7 us (26%)
  blocking collectives  21.8 us (10%)
  local copies, waits for them, and re-layouts  6.38 us (3%)
  other arithmetic  2.92 us (1%)
  matrix products  2.7 us (1%)
    ppermute x12, waiting for transfers between devices, swap(): return lax.ppermute(values, 'gx', [(i, i ^ bit) for i in range(GX)])  30.1 us
    ppermute x12, starting transfers between devices, swap(): return lax.ppermute(values, 'gx', [(i, i ^ bit) for i in range(GX)])  25.2 us
    all_to_all x1, blocking collectives, exchange_lines(): return lax.all_to_all(parts, 'gy', split_axis=0, concat_axis=0, tiled=True)  21.8 us
    pallas_call x1, Pallas kernels, middle_columns(): pl.pallas_call(middle_kernel, grid_spec=pltpu.PrefetchScalarGridSpec(num_...  18.8 us
    all_to_all x3, starting transfers between devices, exchange_lines(): return lax.all_to_all(parts, 'gy', split_axis=0, concat_axis=0, tiled=True)  17.6 us
    ppermute x3, waiting for transfers between devices, gather_weights(): lax.ppermute(weight, 'dp', [((a + k) % DP, a) for a in range(DP)])  14.6 us
    ppermute x8, starting transfers between devices, to_owners(): moved.append(lax.ppermute(chunk, ('dp', 'gx'), pairs))  14.1 us
    pallas_call x4, Pallas kernels, line_call(): pl.pallas_call(kernel, grid_spec=pltpu.PrefetchScalarGridSpec(num_scalar_...  13.1 us
  transfers between devices with their start and end apart: 27, of which 13 were waited for; matrix products, arithmetic and copies ran while one was open for 2% of the time, Pallas kernels for 7%

profile of v3, /device:TPU:1, one launch (start us, length us, event | category | flops | bytes accessed | tf_op | source)
XLA Modules:
  0.0 227.1 jit_solution(8984645544654735843)
XLA Ops:
  0.6 4.5 %collective-permute-start = (bf16[3,20,20,2,128]{4,3,2,1,0:T(2,128)(2,1)}, bf16[3,20,20,2,128]{4,3,2,1,0:T(2,128)(2,1)S(1)}, u32[]{:S(2)}, u32[]{:S(2)}) collective-permute-start(bf16[3,20,20,2,128]{4,3,2,1,0:T(2,128)(2,1)} %param.11), channel_id=1, source_target_pairs={{0,0},{8,32},{16,64},{24,96},{32,72},{40,104},{48,8},{56,40},{64,1... | collective-permute-start | bytes 1843208 | tf_op jit(solution)/shard_map/ppermute | solution.py:588
  5.7 9.1 %start_columns.1 = (bf16[4,48,1280]{2,1,0:T(8,128)(2,1)}, bf16[4,48,1280]{2,1,0:T(8,128)(2,1)}, bf16[4,48,1280]{2,1,0:T(8,128)(2,1)}, bf16[4,48,1280]{2,1,0:T(8,128)(2,1)}) custom-call(s32[3]{0:T(128)} %pad_add_fusion.where_ref, bf16[20,64,2048]{2,1,0:T(8,128)(2,1)} %bitcast.18, bf16[4,24,512]{2,1,0:T(8,128)(2,1)} %constant.23.clone.strip_ref, ...), custom_call_target="tpu_custom_call" | custom-call | bytes 24000000 | tf_op jit(solution)/shard_map/start_columns/pallas_call | solution.py:261
  15.0 1.4 collective-permute-start.5
  16.3 2.1 collective-permute-start.4
  18.8 1.2 add_convert_fusion.1
  20.0 2.7 %collective-permute-start.3 = (bf16[4,48,1280]{2,1,0:T(8,128)(2,1)S(1)}, bf16[4,48,1280]{2,1,0:T(8,128)(2,1)S(1)}, u32[]{:S(2)}, u32[]{:S(2)}) collective-permute-start(bf16[4,48,1280]{2,1,0:T(8,128)(2,1)S(1)} %add_convert_fusion.1), channel_id=1, source_target_pairs={{0,16},{8,24},{16,0},{24,8},{1,17},{9,25},{17,1},{25,9},{2,18},{10... | collective-permute-start | bytes 1474568 | tf_op jit(solution)/shard_map/ppermute | solution.py:547
  22.7 11.6 %collective-permute-done.3.c_ref = bf16[4,48,1280]{2,1,0:T(8,128)(2,1)S(1)} collective-permute-done((bf16[4,48,1280]{2,1,0:T(8,128)(2,1)S(1)}, bf16[4,48,1280]{2,1,0:T(8,128)(2,1)S(1)}, u32[]{:S(2)}, u32[]{:S(2)}) %collective-permute-start.3) | collective-permute-done | bytes 491552 | tf_op jit(solution)/shard_map/ppermute | solution.py:547
  35.1 3.5 %to_lines.2 = bf16[8,48,1280]{2,1,0:T(8,128)(2,1)} custom-call(s32[3]{0:T(128)} %pad_add_fusion.where_ref, bf16[4,48,1280]{2,1,0:T(8,128)(2,1)} %get-tuple-element.47.a_ref, bf16[4,48,1280]{2,1,0:T(8,128)(2,1)} %copy-done.13, bf16[4,48,1280]{2,1,0:T(8,128)(2,1)} %copy-done.17, bf16[8,384,192]{2,1,0:T(8,128)(2,1)} %constant.25.clone.table_ref), custom_call_target="tpu_custom_call" | custom-call | bytes 9000000 | tf_op jit(solution)/shard_map/to_lines/pallas_call | solution.py:333
  38.5 7.7 %all-to-all-start = ((bf16[8,48,1280]{2,1,0:T(8,128)(2,1)}), bf16[8,48,1280]{2,1,0:T(8,128)(2,1)S(1)}, u32[]{:S(2)}, u32[]{:S(2)}) async-start(bf16[8,48,1280]{2,1,0:T(8,128)(2,1)} %to_lines.2), calls=%async_computation | async-start | bytes 1966080 | tf_op jit(solution)/shard_map/all_to_all | solution.py:570
  46.2 1.4 collective-permute-start.6
  47.6 14.6 %collective-permute-done.6 = bf16[3,20,20,2,128]{4,3,2,1,0:T(2,128)(2,1)S(1)} collective-permute-done((bf16[3,20,20,2,128]{4,3,2,1,0:T(2,128)(2,1)S(1)}, bf16[3,20,20,2,128]{4,3,2,1,0:T(2,128)(2,1)S(1)}, u32[]{:S(2)}, u32[]{:S(2)}) %collective-permute-start.6) | collective-permute-done | bytes 614432 | tf_op jit(solution)/shard_map/ppermute | solution.py:565
  63.4 5.8 %mix_modes.1 = (bf16[8,48,1280]{2,1,0:T(8,128)(2,1)}, bf16[120,128]{1,0:T(8,128)(2,1)}, bf16[120,128]{1,0:T(8,128)(2,1)}, bf16[120,128]{1,0:T(8,128)(2,1)}, bf16[120,128]{1,0:T(8,128)(2,1)}) custom-call(s32[3]{0:T(128)} %pad_add_fusion.where_ref, bf16[8,48,1280]{2,1,0:T(8,128)(2,1)} %copy-done.3, bf16[3,20,40,128]{3,2,1,0:T(8,128)(2,1)} %bitcast.22, ...), custom_call_target="tpu_custom_call" | custom-call | bytes 15000000 | tf_op jit(solution)/shard_map/mix_modes/pallas_call | solution.py:494
  69.2 6.4 %all-to-all-start.1 = ((bf16[8,48,1280]{2,1,0:T(8,128)(2,1)}), bf16[8,48,1280]{2,1,0:T(8,128)(2,1)S(1)}, u32[]{:S(2)}, u32[]{:S(2)}) async-start(bf16[8,48,1280]{2,1,0:T(8,128)(2,1)} %get-tuple-element.55), calls=%async_computation.1 | async-start | bytes 1966080 | tf_op jit(solution)/shard_map/all_to_all | solution.py:570
  75.5 3.2 %collective-permute-start.7 = (bf16[120,128]{1,0:T(8,128)(2,1)}, bf16[120,128]{1,0:T(8,128)(2,1)S(1)}, u32[]{:S(2)}, u32[]{:S(2)}) collective-permute-start(bf16[120,128]{1,0:T(8,128)(2,1)} %get-tuple-element.56), channel_id=1, source_target_pairs={{0,0},{8,32},{16,64},{24,96},{32,8},{40,40},{48,72},{56,104},{64,1... | collective-permute-start | bytes 92168 | tf_op jit(solution)/shard_map/ppermute | solution.py:579
  78.9 1.0 collective-permute-start.9
  79.8 2.6 %collective-permute-start.10 = (bf16[120,128]{1,0:T(8,128)(2,1)}, bf16[120,128]{1,0:T(8,128)(2,1)S(1)}, u32[]{:S(2)}, u32[]{:S(2)}) collective-permute-start(bf16[120,128]{1,0:T(8,128)(2,1)} %get-tuple-element.59), channel_id=1, source_target_pairs={{0,24},{8,56},{16,88},{24,120},{32,0},{40,32},{48,64},{56,96},{64,... | collective-permute-start | bytes 92168 | tf_op jit(solution)/shard_map/ppermute | solution.py:579
  82.4 2.1 collective-permute-done.9.s2
  84.5 2.2 collective-permute-done.10.s3
  86.7 3.3 %all-to-all-done.1.modes_ref = bf16[8,48,1280]{2,1,0:T(8,128)(2,1)S(1)} async-done(((bf16[8,48,1280]{2,1,0:T(8,128)(2,1)}), bf16[8,48,1280]{2,1,0:T(8,128)(2,1)S(1)}, u32[]{:S(2)}, u32[]{:S(2)}) %all-to-all-start.1) | async-done | bytes 983072 | tf_op jit(solution)/shard_map/all_to_all | solution.py:570
  90.0 0.9 copy-done.2
  91.0 3.1 %from_lines.2.i0 = bf16[4,48,1280]{2,1,0:T(8,128)(2,1)} custom-call(s32[3]{0:T(128)} %pad_add_fusion.where_ref, bf16[8,48,1280]{2,1,0:T(8,128)(2,1)} %copy-done.2, bf16[8,384,192]{2,1,0:T(8,128)(2,1)} %constant.25.clone.table_ref), custom_call_target="tpu_custom_call" | custom-call | bytes 9000000 | tf_op jit(solution)/shard_map/from_lines/pallas_call | solution.py:333
  94.1 1.6 collective-permute-start.11
  95.7 3.3 %collective-permute-start.12 = (bf16[4,48,1280]{2,1,0:T(8,128)(2,1)}, bf16[4,48,1280]{2,1,0:T(8,128)(2,1)S(1)}, u32[]{:S(2)}, u32[]{:S(2)}) collective-permute-start(bf16[4,48,1280]{2,1,0:T(8,128)(2,1)} %from_lines.2.i0), channel_id=1, source_target_pairs={{0,8},{8,0},{16,24},{24,16},{1,9},{9,1},{17,25},{25,17},{2,10},{10... | collective-permute-start | bytes 1474568 | tf_op jit(solution)/shard_map/ppermute | solution.py:547
  99.0 4.4 %collective-permute-done.11.i1 = bf16[4,48,1280]{2,1,0:T(8,128)(2,1)S(1)} collective-permute-done((bf16[4,48,1280]{2,1,0:T(8,128)(2,1)}, bf16[4,48,1280]{2,1,0:T(8,128)(2,1)S(1)}, u32[]{:S(2)}, u32[]{:S(2)}) %collective-permute-start.11) | collective-permute-done | bytes 491552 | tf_op jit(solution)/shard_map/ppermute | solution.py:547
  103.5 4.6 %collective-permute-start.13 = (bf16[4,48,1280]{2,1,0:T(8,128)(2,1)S(1)}, bf16[4,48,1280]{2,1,0:T(8,128)(2,1)S(1)}, u32[]{:S(2)}, u32[]{:S(2)}) collective-permute-start(bf16[4,48,1280]{2,1,0:T(8,128)(2,1)S(1)} %collective-permute-done.11.i1), channel_id=1, source_target_pairs={{0,8},{8,0},{16,24},{24,16},{1,9},{9,1},{17,25},{25,17},{2,10},{10... | collective-permute-start | bytes 1474568 | tf_op jit(solution)/shard_map/ppermute | solution.py:547
  108.1 1.8 fusion.mixer_ref
  110.8 18.8 %middle_columns.1 = (bf16[20,64,2048]{2,1,0:T(8,128)(2,1)}, bf16[20,64,2048]{2,1,0:T(8,128)(2,1)}, bf16[4,48,1280]{2,1,0:T(8,128)(2,1)}, bf16[4,48,1280]{2,1,0:T...) custom-call(s32[3]{0:T(128)} %pad_add_fusion.where_ref, f32[20]{0:T(128)} %bias_ref.1, ...), custom_call_target="tpu_custom_call" | custom-call | bytes 57000000 | tf_op jit(solution)/shard_map/middle_columns/pallas_call | solution.py:279
  130.3 1.6 collective-permute-done.15
  131.8 1.2 add_convert_fusion
  133.0 1.7 collective-permute-start.16
  134.7 11.2 %collective-permute-done.16.c_ref = bf16[4,48,1280]{2,1,0:T(8,128)(2,1)S(1)} collective-permute-done((bf16[4,48,1280]{2,1,0:T(8,128)(2,1)S(1)}, bf16[4,48,1280]{2,1,0:T(8,128)(2,1)S(1)}, u32[]{:S(2)}, u32[]{:S(2)}) %collective-permute-start.16) | collective-permute-done | bytes 491552 | tf_op jit(solution)/shard_map/ppermute | solution.py:547
  146.7 3.5 %to_lines.3 = bf16[8,48,1280]{2,1,0:T(8,128)(2,1)} custom-call(s32[3]{0:T(128)} %pad_add_fusion.where_ref, bf16[4,48,1280]{2,1,0:T(8,128)(2,1)} %get-tuple-element.62.a_ref, bf16[4,48,1280]{2,1,0:T(8,128)(2,1)} %copy-done.14, bf16[4,48,1280]{2,1,0:T(8,128)(2,1)} %copy-done.18, bf16[8,384,192]{2,1,0:T(8,128)(2,1)} %constant.25.clone.table_ref), custom_call_target="tpu_custom_call" | custom-call | bytes 9000000 | tf_op jit(solution)/shard_map/to_lines/pallas_call | solution.py:333
  150.2 21.8 %all_to_all.20.arrived_ref = bf16[8,48,1280]{2,1,0:T(8,128)(2,1)} all-to-all(bf16[8,48,1280]{2,1,0:T(8,128)(2,1)} %to_lines.3), channel_id=1, replica_groups=mesh['dp'=4,'gx'=4,'gy'=8] {'gy'}, dimensions={0} | all-to-all | bytes 1966080 | tf_op jit(solution)/shard_map/all_to_all | solution.py:570
  172.0 6.4 %back_modes.1 = (bf16[8,48,1280]{2,1,0:T(8,128)(2,1)}, bf16[120,128]{1,0:T(8,128)(2,1)}, bf16[120,128]{1,0:T(8,128)(2,1)}, bf16[120,128]{1,0:T(8,128)(2,1)}, bf16[120,128]{1,0:T(8,128)(2,1)}) custom-call(s32[3]{0:T(128)} %pad_add_fusion.where_ref, bf16[8,48,1280]{2,1,0:T(8,128)(2,1)} %all_to_all.20.arrived_ref, bf16[3,20,40,128]{3,2,1,0:T(8,128)(2,1)} %bitcast.23, ...), custom_call_target="tpu_custom_call" | custom-call | bytes 15000000 | tf_op jit(solution)/shard_map/back_modes/pallas_call | solution.py:494
  178.4 3.6 %all-to-all-start.3 = ((bf16[8,48,1280]{2,1,0:T(8,128)(2,1)}), bf16[8,48,1280]{2,1,0:T(8,128)(2,1)S(1)}, u32[]{:S(2)}, u32[]{:S(2)}) async-start(bf16[8,48,1280]{2,1,0:T(8,128)(2,1)} %get-tuple-element.66), calls=%async_computation.3 | async-start | bytes 1966080 | tf_op jit(solution)/shard_map/all_to_all | solution.py:570
  181.9 2.0 collective-permute-start.17
  184.1 2.4 %collective-permute-start.19 = (bf16[120,128]{1,0:T(8,128)(2,1)}, bf16[120,128]{1,0:T(8,128)(2,1)S(1)}, u32[]{:S(2)}, u32[]{:S(2)}) collective-permute-start(bf16[120,128]{1,0:T(8,128)(2,1)} %get-tuple-element.69), channel_id=1, source_target_pairs={{0,16},{8,48},{16,80},{24,112},{32,24},{40,56},{48,88},{56,120},{6... | collective-permute-start | bytes 92168 | tf_op jit(solution)/shard_map/ppermute | solution.py:579
  186.4 2.8 %collective-permute-start.20 = (bf16[120,128]{1,0:T(8,128)(2,1)}, bf16[120,128]{1,0:T(8,128)(2,1)S(1)}, u32[]{:S(2)}, u32[]{:S(2)}) collective-permute-start(bf16[120,128]{1,0:T(8,128)(2,1)} %get-tuple-element.70), channel_id=1, source_target_pairs={{0,24},{8,56},{16,88},{24,120},{32,0},{40,32},{48,64},{56,96},{64,... | collective-permute-start | bytes 92168 | tf_op jit(solution)/shard_map/ppermute | solution.py:579
  189.2 1.6 collective-permute-done.19.g2
  190.8 2.0 collective-permute-done.20.g3
  192.8 3.8 %all-to-all-done.3.modes_ref = bf16[8,48,1280]{2,1,0:T(8,128)(2,1)S(1)} async-done(((bf16[8,48,1280]{2,1,0:T(8,128)(2,1)}), bf16[8,48,1280]{2,1,0:T(8,128)(2,1)S(1)}, u32[]{:S(2)}, u32[]{:S(2)}) %all-to-all-start.3) | async-done | bytes 983072 | tf_op jit(solution)/shard_map/all_to_all | solution.py:570
  196.6 0.9 copy-done.1
  197.5 3.1 %from_lines.3.i0 = bf16[4,48,1280]{2,1,0:T(8,128)(2,1)} custom-call(s32[3]{0:T(128)} %pad_add_fusion.where_ref, bf16[8,48,1280]{2,1,0:T(8,128)(2,1)} %copy-done.1, bf16[8,384,192]{2,1,0:T(8,128)(2,1)} %constant.25.clone.table_ref), custom_call_target="tpu_custom_call" | custom-call | bytes 9000000 | tf_op jit(solution)/shard_map/from_lines/pallas_call | solution.py:333
  200.6 1.2 collective-permute-start.21
  201.9 3.7 %collective-permute-start.22 = (bf16[4,48,1280]{2,1,0:T(8,128)(2,1)}, bf16[4,48,1280]{2,1,0:T(8,128)(2,1)S(1)}, u32[]{:S(2)}, u32[]{:S(2)}) collective-permute-start(bf16[4,48,1280]{2,1,0:T(8,128)(2,1)} %from_lines.3.i0), channel_id=1, source_target_pairs={{0,8},{8,0},{16,24},{24,16},{1,9},{9,1},{17,25},{25,17},{2,10},{10... | collective-permute-start | bytes 1474568 | tf_op jit(solution)/shard_map/ppermute | solution.py:547
  205.6 3.1 %outer_sum.1 = f32[3,20,40,128]{3,2,1,0:T(8,128)} custom-call(bf16[120,128]{1,0:T(8,128)(2,1)} %copy-done.20, bf16[120,128]{1,0:T(8,128)(2,1)} %copy-done.21, bf16[120,128]{1,0:T(8,128)(2,1)} %copy-done.22, bf16[120,128]{1,0:T(8,128)(2,1)} %copy-done.23, bf16[120,128]{1,0:T(8,128)(2,1)} %copy-done.24, bf16[120,128]{1,0:T(8,128)(2,1)} %copy-done.25, ...), custom_call_target="tpu_custom_call" | custom-call | bytes 9000000 | tf_op jit(solution)/shard_map/outer_sum/pallas_call | solution.py:537
  209.3 5.2 %collective-permute-start.23 = (bf16[4,48,1280]{2,1,0:T(8,128)(2,1)S(1)}, bf16[4,48,1280]{2,1,0:T(8,128)(2,1)S(1)}, u32[]{:S(2)}, u32[]{:S(2)}) collective-permute-start(bf16[4,48,1280]{2,1,0:T(8,128)(2,1)S(1)} %collective-permute-done.21.i1), channel_id=1, source_target_pairs={{0,8},{8,0},{16,24},{24,16},{1,9},{9,1},{17,25},{25,17},{2,10},{10... | collective-permute-start | bytes 1474568 | tf_op jit(solution)/shard_map/ppermute | solution.py:547
  216.9 10.2 %end_columns.1 = bf16[20,64,2048]{2,1,0:T(8,128)(2,1)} custom-call(s32[3]{0:T(128)} %pad_add_fusion.where_ref, bf16[4,48,1280]{2,1,0:T(8,128)(2,1)} %from_lines.3.i0, bf16[4,48,1280]{2,1,0:T(8,128)(2,1)} %copy-done.9, bf16[4,48,1280]{2,1,0:T(8,128)(2,1)} %copy-done.10, bf16[4,48,1280]{2,1,0:T(8,128)(2,1)} %copy-done.16, ...), custom_call_target="tpu_custom_call" | custom-call | bytes 30000000 | tf_op jit(solution)/shard_map/end_columns/pallas_call | solution.py:299
  (78 shorter events, 8.5 us)
Async XLA Ops:
  0.6 107.4 %copy-start = (bf16[20,20]{1,0:T(8,128)(2,1)S(1)}, bf16[20,20]{1,0:T(8,128)(2,1)}, u32[]{:S(2)}) copy-start(bf16[20,20]{1,0:T(8,128)(2,1)} %param.12) | copy-start | bytes 2404
  0.6 14.2 %collective-permute-start = (bf16[3,20,20,2,128]{4,3,2,1,0:T(2,128)(2,1)}, bf16[3,20,20,2,128]{4,3,2,1,0:T(2,128)(2,1)S(1)}, u32[]{:S(2)}, u32[]{:S(2)}) collective-permute-start(bf16[3,20,20,2,128]{4,3,2,1,0:T(2,128)(2,1)} %param.11), channel_id=1, source_target_pairs={{0,0},{8,32},{16,64},{24,96},{32,72},{40,104},{48,8},{56,40},{64,1... | collective-permute-start | bytes 1843208 | tf_op jit(solution)/shard_map/ppermute | solution.py:588
  14.9 47.4 %copy-start.4 = (bf16[3,20,20,2,128]{4,3,2,1,0:T(2,128)(2,1)}, bf16[3,20,20,2,128]{4,3,2,1,0:T(2,128)(2,1)S(1)}, u32[]{:S(2)}) copy-start(bf16[3,20,20,2,128]{4,3,2,1,0:T(2,128)(2,1)S(1)} %collective-permute-done) | copy-start | bytes 1843204
  14.9 3.9 %collective-permute-start.2 = (bf16[4,48,1280]{2,1,0:T(8,128)(2,1)}, bf16[4,48,1280]{2,1,0:T(8,128)(2,1)S(1)}, u32[]{:S(2)}, u32[]{:S(2)}) collective-permute-start(bf16[4,48,1280]{2,1,0:T(8,128)(2,1)} %get-tuple-element.50), channel_id=1, source_target_pairs={{0,8},{8,0},{16,24},{24,16},{1,9},{9,1},{17,25},{25,17},{2,10},{10... | collective-permute-start | bytes 1474568 | tf_op jit(solution)/shard_map/ppermute | solution.py:547
  15.0 23.5 %collective-permute-start.5 = (bf16[3,20,20,2,128]{4,3,2,1,0:T(2,128)(2,1)S(1)}, bf16[3,20,20,2,128]{4,3,2,1,0:T(2,128)(2,1)S(1)}, u32[]{:S(2)}, u32[]{:S(2)}) collective-permute-start(bf16[3,20,20,2,128]{4,3,2,1,0:T(2,128)(2,1)S(1)} %collective-permute-done), channel_id=1, source_target_pairs={{96,0},{0,32},{32,64},{64,96},{97,1},{1,33},{33,65},{65,97},{98,2}... | collective-permute-start | bytes 1843208 | tf_op jit(solution)/shard_map/ppermute | solution.py:565
  16.3 22.2 %collective-permute-start.4 = (bf16[3,20,20,2,128]{4,3,2,1,0:T(2,128)(2,1)S(1)}, bf16[3,20,20,2,128]{4,3,2,1,0:T(2,128)(2,1)S(1)}, u32[]{:S(2)}, u32[]{:S(2)}) collective-permute-start(bf16[3,20,20,2,128]{4,3,2,1,0:T(2,128)(2,1)S(1)} %collective-permute-done), channel_id=1, source_target_pairs={{32,0},{64,32},{96,64},{0,96},{33,1},{65,33},{97,65},{1,97},{34,2}... | collective-permute-start | bytes 1843208 | tf_op jit(solution)/shard_map/ppermute | solution.py:565
  18.4 4.2 %collective-permute-start.1 = (bf16[4,48,1280]{2,1,0:T(8,128)(2,1)}, bf16[4,48,1280]{2,1,0:T(8,128)(2,1)S(1)}, u32[]{:S(2)}, u32[]{:S(2)}) collective-permute-start(bf16[4,48,1280]{2,1,0:T(8,128)(2,1)} %get-tuple-element.48), channel_id=1, source_target_pairs={{0,8},{8,0},{16,24},{24,16},{1,9},{9,1},{17,25},{25,17},{2,10},{10... | collective-permute-start | bytes 1474568 | tf_op jit(solution)/shard_map/ppermute | solution.py:547
  20.0 14.3 %collective-permute-start.3 = (bf16[4,48,1280]{2,1,0:T(8,128)(2,1)S(1)}, bf16[4,48,1280]{2,1,0:T(8,128)(2,1)S(1)}, u32[]{:S(2)}, u32[]{:S(2)}) collective-permute-start(bf16[4,48,1280]{2,1,0:T(8,128)(2,1)S(1)} %add_convert_fusion.1), channel_id=1, source_target_pairs={{0,16},{8,24},{16,0},{24,8},{1,17},{9,25},{17,1},{25,9},{2,18},{10... | collective-permute-start | bytes 1474568 | tf_op jit(solution)/shard_map/ppermute | solution.py:547
  22.7 11.6 %copy-start.13 = (bf16[4,48,1280]{2,1,0:T(8,128)(2,1)}, bf16[4,48,1280]{2,1,0:T(8,128)(2,1)S(1)}, u32[]{:S(2)}) copy-start(bf16[4,48,1280]{2,1,0:T(8,128)(2,1)S(1)} %collective-permute-done.1.b_ref) | copy-start | bytes 1474564
  38.5 69.6 %copy-start.8 = (bf16[160,20]{1,0:T(8,128)(2,1)S(1)}, bf16[160,20]{1,0:T(8,128)(2,1)}, u32[]{:S(2)}) copy-start(bf16[160,20]{1,0:T(8,128)(2,1)} %constant.22.clone) | copy-start | bytes 19204
  38.5 23.7 %copy-start.5 = (bf16[3,20,20,2,128]{4,3,2,1,0:T(2,128)(2,1)}, bf16[3,20,20,2,128]{4,3,2,1,0:T(2,128)(2,1)S(1)}, u32[]{:S(2)}) copy-start(bf16[3,20,20,2,128]{4,3,2,1,0:T(2,128)(2,1)S(1)} %collective-permute-done.5) | copy-start | bytes 1843204
  38.5 23.7 %copy-start.6 = (bf16[3,20,20,2,128]{4,3,2,1,0:T(2,128)(2,1)}, bf16[3,20,20,2,128]{4,3,2,1,0:T(2,128)(2,1)S(1)}, u32[]{:S(2)}) copy-start(bf16[3,20,20,2,128]{4,3,2,1,0:T(2,128)(2,1)S(1)} %collective-permute-done.4) | copy-start | bytes 1843204
  38.5 23.7 %all-to-all-start = ((bf16[8,48,1280]{2,1,0:T(8,128)(2,1)}), bf16[8,48,1280]{2,1,0:T(8,128)(2,1)S(1)}, u32[]{:S(2)}, u32[]{:S(2)}) async-start(bf16[8,48,1280]{2,1,0:T(8,128)(2,1)} %to_lines.2), calls=%async_computation | async-start | bytes 1966080 | tf_op jit(solution)/shard_map/all_to_all | solution.py:570
  46.2 16.0 %collective-permute-start.6 = (bf16[3,20,20,2,128]{4,3,2,1,0:T(2,128)(2,1)S(1)}, bf16[3,20,20,2,128]{4,3,2,1,0:T(2,128)(2,1)S(1)}, u32[]{:S(2)}, u32[]{:S(2)}) collective-permute-start(bf16[3,20,20,2,128]{4,3,2,1,0:T(2,128)(2,1)S(1)} %collective-permute-done), channel_id=1, source_target_pairs={{64,0},{96,32},{0,64},{32,96},{65,1},{97,33},{1,65},{33,97},{66,2}... | collective-permute-start | bytes 1843208 | tf_op jit(solution)/shard_map/ppermute | solution.py:565
  62.2 1.1 copy-start.3
  69.2 20.9 %all-to-all-start.1 = ((bf16[8,48,1280]{2,1,0:T(8,128)(2,1)}), bf16[8,48,1280]{2,1,0:T(8,128)(2,1)S(1)}, u32[]{:S(2)}, u32[]{:S(2)}) async-start(bf16[8,48,1280]{2,1,0:T(8,128)(2,1)} %get-tuple-element.55), calls=%async_computation.1 | async-start | bytes 1966080 | tf_op jit(solution)/shard_map/all_to_all | solution.py:570
  75.5 6.9 %collective-permute-start.7 = (bf16[120,128]{1,0:T(8,128)(2,1)}, bf16[120,128]{1,0:T(8,128)(2,1)S(1)}, u32[]{:S(2)}, u32[]{:S(2)}) collective-permute-start(bf16[120,128]{1,0:T(8,128)(2,1)} %get-tuple-element.56), channel_id=1, source_target_pairs={{0,0},{8,32},{16,64},{24,96},{32,8},{40,40},{48,72},{56,104},{64,1... | collective-permute-start | bytes 92168 | tf_op jit(solution)/shard_map/ppermute | solution.py:579
  78.8 3.6 %collective-permute-start.8 = (bf16[120,128]{1,0:T(8,128)(2,1)}, bf16[120,128]{1,0:T(8,128)(2,1)S(1)}, u32[]{:S(2)}, u32[]{:S(2)}) collective-permute-start(bf16[120,128]{1,0:T(8,128)(2,1)} %get-tuple-element.57), channel_id=1, source_target_pairs={{0,8},{8,40},{16,72},{24,104},{32,16},{40,48},{48,80},{56,112},{64... | collective-permute-start | bytes 92168 | tf_op jit(solution)/shard_map/ppermute | solution.py:579
  78.9 5.7 %collective-permute-start.9 = (bf16[120,128]{1,0:T(8,128)(2,1)}, bf16[120,128]{1,0:T(8,128)(2,1)S(1)}, u32[]{:S(2)}, u32[]{:S(2)}) collective-permute-start(bf16[120,128]{1,0:T(8,128)(2,1)} %get-tuple-element.58), channel_id=1, source_target_pairs={{0,16},{8,48},{16,80},{24,112},{32,24},{40,56},{48,88},{56,120},{6... | collective-permute-start | bytes 92168 | tf_op jit(solution)/shard_map/ppermute | solution.py:579
  79.8 6.9 %collective-permute-start.10 = (bf16[120,128]{1,0:T(8,128)(2,1)}, bf16[120,128]{1,0:T(8,128)(2,1)S(1)}, u32[]{:S(2)}, u32[]{:S(2)}) collective-permute-start(bf16[120,128]{1,0:T(8,128)(2,1)} %get-tuple-element.59), channel_id=1, source_target_pairs={{0,24},{8,56},{16,88},{24,120},{32,0},{40,32},{48,64},{56,96},{64,... | collective-permute-start | bytes 92168 | tf_op jit(solution)/shard_map/ppermute | solution.py:579
  82.4 118.2 %copy-start.20 = (bf16[120,128]{1,0:T(8,128)(2,1)}, bf16[120,128]{1,0:T(8,128)(2,1)S(1)}, u32[]{:S(2)}) copy-start(bf16[120,128]{1,0:T(8,128)(2,1)S(1)} %collective-permute-done.7.s0) | copy-start | bytes 92164
  82.4 118.2 %copy-start.21 = (bf16[120,128]{1,0:T(8,128)(2,1)}, bf16[120,128]{1,0:T(8,128)(2,1)S(1)}, u32[]{:S(2)}) copy-start(bf16[120,128]{1,0:T(8,128)(2,1)S(1)} %collective-permute-done.8.s1) | copy-start | bytes 92164
  84.5 116.1 %copy-start.22 = (bf16[120,128]{1,0:T(8,128)(2,1)}, bf16[120,128]{1,0:T(8,128)(2,1)S(1)}, u32[]{:S(2)}) copy-start(bf16[120,128]{1,0:T(8,128)(2,1)S(1)} %collective-permute-done.9.s2) | copy-start | bytes 92164
  86.7 113.9 %copy-start.23 = (bf16[120,128]{1,0:T(8,128)(2,1)}, bf16[120,128]{1,0:T(8,128)(2,1)S(1)}, u32[]{:S(2)}) copy-start(bf16[120,128]{1,0:T(8,128)(2,1)S(1)} %collective-permute-done.10.s3) | copy-start | bytes 92164
  90.0 0.9 copy-start.2
  94.1 9.3 %collective-permute-start.11 = (bf16[4,48,1280]{2,1,0:T(8,128)(2,1)}, bf16[4,48,1280]{2,1,0:T(8,128)(2,1)S(1)}, u32[]{:S(2)}, u32[]{:S(2)}) collective-permute-start(bf16[4,48,1280]{2,1,0:T(8,128)(2,1)} %from_lines.2.i0), channel_id=1, source_target_pairs={{0,16},{8,24},{16,0},{24,8},{1,17},{9,25},{17,1},{25,9},{2,18},{10... | collective-permute-start | bytes 1474568 | tf_op jit(solution)/shard_map/ppermute | solution.py:547
  95.7 14.2 %collective-permute-start.12 = (bf16[4,48,1280]{2,1,0:T(8,128)(2,1)}, bf16[4,48,1280]{2,1,0:T(8,128)(2,1)S(1)}, u32[]{:S(2)}, u32[]{:S(2)}) collective-permute-start(bf16[4,48,1280]{2,1,0:T(8,128)(2,1)} %from_lines.2.i0), channel_id=1, source_target_pairs={{0,8},{8,0},{16,24},{24,16},{1,9},{9,1},{17,25},{25,17},{2,10},{10... | collective-permute-start | bytes 1474568 | tf_op jit(solution)/shard_map/ppermute | solution.py:547
  103.4 6.4 %copy-start.11 = (bf16[4,48,1280]{2,1,0:T(8,128)(2,1)}, bf16[4,48,1280]{2,1,0:T(8,128)(2,1)S(1)}, u32[]{:S(2)}) copy-start(bf16[4,48,1280]{2,1,0:T(8,128)(2,1)S(1)} %collective-permute-done.11.i1) | copy-start | bytes 1474564
  103.5 6.4 %collective-permute-start.13 = (bf16[4,48,1280]{2,1,0:T(8,128)(2,1)S(1)}, bf16[4,48,1280]{2,1,0:T(8,128)(2,1)S(1)}, u32[]{:S(2)}, u32[]{:S(2)}) collective-permute-start(bf16[4,48,1280]{2,1,0:T(8,128)(2,1)S(1)} %collective-permute-done.11.i1), channel_id=1, source_target_pairs={{0,8},{8,0},{16,24},{24,16},{1,9},{9,1},{17,25},{25,17},{2,10},{10... | collective-permute-start | bytes 1474568 | tf_op jit(solution)/shard_map/ppermute | solution.py:547
  109.9 1.0 copy-start.15
  129.7 2.2 collective-permute-start.15
  129.9 4.8 %collective-permute-start.14 = (bf16[4,48,1280]{2,1,0:T(8,128)(2,1)}, bf16[4,48,1280]{2,1,0:T(8,128)(2,1)S(1)}, u32[]{:S(2)}, u32[]{:S(2)}) collective-permute-start(bf16[4,48,1280]{2,1,0:T(8,128)(2,1)} %get-tuple-element.63), channel_id=1, source_target_pairs={{0,8},{8,0},{16,24},{24,16},{1,9},{9,1},{17,25},{25,17},{2,10},{10... | collective-permute-start | bytes 1474568 | tf_op jit(solution)/shard_map/ppermute | solution.py:547
  133.0 13.0 %collective-permute-start.16 = (bf16[4,48,1280]{2,1,0:T(8,128)(2,1)S(1)}, bf16[4,48,1280]{2,1,0:T(8,128)(2,1)S(1)}, u32[]{:S(2)}, u32[]{:S(2)}) collective-permute-start(bf16[4,48,1280]{2,1,0:T(8,128)(2,1)S(1)} %add_convert_fusion), channel_id=1, source_target_pairs={{0,16},{8,24},{16,0},{24,8},{1,17},{9,25},{17,1},{25,9},{2,18},{10... | collective-permute-start | bytes 1474568 | tf_op jit(solution)/shard_map/ppermute | solution.py:547
  134.7 11.2 %copy-start.14 = (bf16[4,48,1280]{2,1,0:T(8,128)(2,1)}, bf16[4,48,1280]{2,1,0:T(8,128)(2,1)S(1)}, u32[]{:S(2)}) copy-start(bf16[4,48,1280]{2,1,0:T(8,128)(2,1)S(1)} %collective-permute-done.14.b_ref) | copy-start | bytes 1474564
  172.0 42.6 %copy-start.19 = (bf16[160,160]{1,0:T(8,128)(2,1)S(1)}, bf16[160,160]{1,0:T(8,128)(2,1)}, u32[]{:S(2)}) copy-start(bf16[160,160]{1,0:T(8,128)(2,1)} %constant.26.clone) | copy-start | bytes 153604
  178.4 18.2 %all-to-all-start.3 = ((bf16[8,48,1280]{2,1,0:T(8,128)(2,1)}), bf16[8,48,1280]{2,1,0:T(8,128)(2,1)S(1)}, u32[]{:S(2)}, u32[]{:S(2)}) async-start(bf16[8,48,1280]{2,1,0:T(8,128)(2,1)} %get-tuple-element.66), calls=%async_computation.3 | async-start | bytes 1966080 | tf_op jit(solution)/shard_map/all_to_all | solution.py:570
  181.9 7.3 %collective-permute-start.17 = (bf16[120,128]{1,0:T(8,128)(2,1)}, bf16[120,128]{1,0:T(8,128)(2,1)S(1)}, u32[]{:S(2)}, u32[]{:S(2)}) collective-permute-start(bf16[120,128]{1,0:T(8,128)(2,1)} %get-tuple-element.67), channel_id=1, source_target_pairs={{0,0},{8,32},{16,64},{24,96},{32,8},{40,40},{48,72},{56,104},{64,1... | collective-permute-start | bytes 92168 | tf_op jit(solution)/shard_map/ppermute | solution.py:579
  184.0 5.2 %collective-permute-start.18 = (bf16[120,128]{1,0:T(8,128)(2,1)}, bf16[120,128]{1,0:T(8,128)(2,1)S(1)}, u32[]{:S(2)}, u32[]{:S(2)}) collective-permute-start(bf16[120,128]{1,0:T(8,128)(2,1)} %get-tuple-element.68), channel_id=1, source_target_pairs={{0,8},{8,40},{16,72},{24,104},{32,16},{40,48},{48,80},{56,112},{64... | collective-permute-start | bytes 92168 | tf_op jit(solution)/shard_map/ppermute | solution.py:579
  184.1 6.7 %collective-permute-start.19 = (bf16[120,128]{1,0:T(8,128)(2,1)}, bf16[120,128]{1,0:T(8,128)(2,1)S(1)}, u32[]{:S(2)}, u32[]{:S(2)}) collective-permute-start(bf16[120,128]{1,0:T(8,128)(2,1)} %get-tuple-element.69), channel_id=1, source_target_pairs={{0,16},{8,48},{16,80},{24,112},{32,24},{40,56},{48,88},{56,120},{6... | collective-permute-start | bytes 92168 | tf_op jit(solution)/shard_map/ppermute | solution.py:579
  186.4 6.4 %collective-permute-start.20 = (bf16[120,128]{1,0:T(8,128)(2,1)}, bf16[120,128]{1,0:T(8,128)(2,1)S(1)}, u32[]{:S(2)}, u32[]{:S(2)}) collective-permute-start(bf16[120,128]{1,0:T(8,128)(2,1)} %get-tuple-element.70), channel_id=1, source_target_pairs={{0,24},{8,56},{16,88},{24,120},{32,0},{40,32},{48,64},{56,96},{64,... | collective-permute-start | bytes 92168 | tf_op jit(solution)/shard_map/ppermute | solution.py:579
  189.2 16.4 %copy-start.24 = (bf16[120,128]{1,0:T(8,128)(2,1)}, bf16[120,128]{1,0:T(8,128)(2,1)S(1)}, u32[]{:S(2)}) copy-start(bf16[120,128]{1,0:T(8,128)(2,1)S(1)} %collective-permute-done.17.g0) | copy-start | bytes 92164
  189.2 16.4 %copy-start.25 = (bf16[120,128]{1,0:T(8,128)(2,1)}, bf16[120,128]{1,0:T(8,128)(2,1)S(1)}, u32[]{:S(2)}) copy-start(bf16[120,128]{1,0:T(8,128)(2,1)S(1)} %collective-permute-done.18.g1) | copy-start | bytes 92164
  190.8 14.8 %copy-start.26 = (bf16[120,128]{1,0:T(8,128)(2,1)}, bf16[120,128]{1,0:T(8,128)(2,1)S(1)}, u32[]{:S(2)}) copy-start(bf16[120,128]{1,0:T(8,128)(2,1)S(1)} %collective-permute-done.19.g2) | copy-start | bytes 92164
  192.8 12.8 %copy-start.27 = (bf16[120,128]{1,0:T(8,128)(2,1)}, bf16[120,128]{1,0:T(8,128)(2,1)S(1)}, u32[]{:S(2)}) copy-start(bf16[120,128]{1,0:T(8,128)(2,1)S(1)} %collective-permute-done.20.g3) | copy-start | bytes 92164
  200.6 8.7 %collective-permute-start.21 = (bf16[4,48,1280]{2,1,0:T(8,128)(2,1)}, bf16[4,48,1280]{2,1,0:T(8,128)(2,1)S(1)}, u32[]{:S(2)}, u32[]{:S(2)}) collective-permute-start(bf16[4,48,1280]{2,1,0:T(8,128)(2,1)} %from_lines.3.i0), channel_id=1, source_target_pairs={{0,16},{8,24},{16,0},{24,8},{1,17},{9,25},{17,1},{25,9},{2,18},{10... | collective-permute-start | bytes 1474568 | tf_op jit(solution)/shard_map/ppermute | solution.py:547
  201.9 13.6 %collective-permute-start.22 = (bf16[4,48,1280]{2,1,0:T(8,128)(2,1)}, bf16[4,48,1280]{2,1,0:T(8,128)(2,1)S(1)}, u32[]{:S(2)}, u32[]{:S(2)}) collective-permute-start(bf16[4,48,1280]{2,1,0:T(8,128)(2,1)} %from_lines.3.i0), channel_id=1, source_target_pairs={{0,8},{8,0},{16,24},{24,16},{1,9},{9,1},{17,25},{25,17},{2,10},{10... | collective-permute-start | bytes 1474568 | tf_op jit(solution)/shard_map/ppermute | solution.py:547
  209.3 6.7 %copy-start.9 = (bf16[4,48,1280]{2,1,0:T(8,128)(2,1)}, bf16[4,48,1280]{2,1,0:T(8,128)(2,1)S(1)}, u32[]{:S(2)}) copy-start(bf16[4,48,1280]{2,1,0:T(8,128)(2,1)S(1)} %collective-permute-done.21.i1) | copy-start | bytes 1474564
  209.3 6.7 %collective-permute-start.23 = (bf16[4,48,1280]{2,1,0:T(8,128)(2,1)S(1)}, bf16[4,48,1280]{2,1,0:T(8,128)(2,1)S(1)}, u32[]{:S(2)}, u32[]{:S(2)}) collective-permute-start(bf16[4,48,1280]{2,1,0:T(8,128)(2,1)S(1)} %collective-permute-done.21.i1), channel_id=1, source_target_pairs={{0,8},{8,0},{16,24},{24,16},{1,9},{9,1},{17,25},{25,17},{2,10},{10... | collective-permute-start | bytes 1474568 | tf_op jit(solution)/shard_map/ppermute | solution.py:547
  (7 other events, 5.8 us)

commit v4 on v3

--- a/solution.py
+++ b/solution.py
@@ -118,7 +118,7 @@
         long_ref[:, GL * part : GL * (part + 1)] = block
 
 
-def forward_group(rows, depth_ref, tall_ref, outs, j):
+def forward_group(rows, depth_ref, tall_ref, outs, y):
     half = KZ * YB
     planes = dot(depth_ref[...], rows, 1, 1)
     real = planes[:half]
@@ -132,12 +132,12 @@
         piece = jnp.concatenate(
             [lines[lo : lo + KB * YB], lines[half + lo : half + lo + KB * YB]], axis=0
         )
-        outs[pos][0, :, GL * j : GL * (j + 1)] = piece.astype(BF)
-
-
-def inverse_group(ins, depth_ref, long_ref, j):
+        outs[pos][y] = piece.astype(BF)
+
+
+def inverse_group(ins, depth_ref, long_ref, y):
     part = KB * YB
-    pieces = [ref[0, :, GL * j : GL * (j + 1)].astype(F32) for ref in ins]
+    pieces = [ref[y].astype(F32) for ref in ins]
     real = jnp.concatenate([piece[:part] for piece in pieces], axis=0)
     imag = jnp.concatenate([piece[part:] for piece in pieces], axis=0)
     sides = jnp.concatenate(
@@ -147,15 +147,15 @@
     return dot(planes, depth_ref[...])
 
 
-def set_bypass(source_ref, mixer_ref, total_ref):
+def run_rows(ref, y):
+    return ref[:, :, LANES * y : LANES * (y + 1)].reshape(GROUP * XL, LANES)
+
+
+def bypass_kernel(source_ref, mixer_ref, out_ref):
     for i in range(XL // XB):
         span = slice(i * XB, (i + 1) * XB)
         rows = source_ref[:, span, :].reshape(CH * XB, LANES)
-        total_ref[:, span, :] = dot(mixer_ref[...], rows).reshape(CH, XB, LANES)
-
-
-def group_rows(ref, j):
-    return ref[GROUP * j : GROUP * (j + 1)].reshape(GROUP * XL, LANES)
+        out_ref[:, span, :] = dot(mixer_ref[...], rows).reshape(CH, XB, LANES)
 
 
 def start_kernel(
@@ -165,71 +165,71 @@
     def _():
         fill_tables(strip_ref, wide_ref, depth_ref, tall_ref, long_ref)
 
-    for j in range(GROUPS):
-        forward_group(group_rows(field_ref, j), depth_ref, tall_ref, (o0, o1, o2, o3), j)
+    for y in range(STEPS):
+        forward_group(run_rows(field_ref, y), depth_ref, tall_ref, (o0, o1, o2, o3), y)
 
 
 ROOT = math.sqrt(2.0 / math.pi)
 CUBE = 0.044715
 
 
-def activate(bias_ref, upstream_ref, total_ref, act_ref, grad_ref, j):
-    for channel in range(GROUP * j, GROUP * (j + 1)):
-        shift = bias_ref[channel]
+def activate(bias_ref, upstream_ref, total_ref, act_ref, grad_ref, y):
+    lanes = slice(LANES * y, LANES * (y + 1))
+    for channel in range(GROUP):
+        shift = bias_ref[GROUP * pl.program_id(0) + channel]
         for i in range(XL // EB):
             span = slice(i * EB, (i + 1) * EB)
-            x = total_ref[channel, span, :] + shift
+            x = total_ref[y, channel, span, :] + shift
             square = x * x
             t = jnp.tanh(x * (ROOT + (ROOT * CUBE) * square))
             h = 0.5 * t + 0.5
             act = x * h
             slope = h + act * (1.0 - h) * (2.0 * ROOT + (6.0 * ROOT * CUBE) * square)
-            act_ref[channel, span, :] = act.astype(BF)
-            up = upstream_ref[channel, span, :].astype(F32)
-            grad_ref[channel, span, :] = (up * slope).astype(BF)
+            act_ref[channel, span, lanes] = act.astype(BF)
+            up = upstream_ref[channel, span, lanes].astype(F32)
+            grad_ref[channel, span, lanes] = (up * slope).astype(BF)
 
 
 def middle_kernel(
-    where_ref, bias_ref, i0, i1, i2, i3, field_ref, upstream_ref, mixer_ref, strip_ref, wide_ref,
+    where_ref, bias_ref, i0, i1, i2, i3, bypass_ref, upstream_ref, strip_ref, wide_ref,
     act_ref, grad_ref, o0, o1, o2, o3, depth_ref, tall_ref, long_ref, total_ref,
 ):
     @pl.when(pl.program_id(0) == 0)
     def _():
         fill_tables(strip_ref, wide_ref, depth_ref, tall_ref, long_ref)
 
-    set_bypass(field_ref, mixer_ref, total_ref)
-
-    def inverse(j):
-        group = slice(GROUP * j, GROUP * (j + 1))
-        values = inverse_group((i0, i1, i2, i3), depth_ref, long_ref, j)
-        total_ref[group] = total_ref[group] + values.reshape(GROUP, XL, LANES)
-
-    def forward(j):
-        forward_group(group_rows(grad_ref, j), depth_ref, tall_ref, (o0, o1, o2, o3), j)
+    def inverse(y):
+        values = inverse_group((i0, i1, i2, i3), depth_ref, long_ref, y)
+        lanes = slice(LANES * y, LANES * (y + 1))
+        total_ref[y] = bypass_ref[:, :, lanes] + values.reshape(GROUP, XL, LANES)
+
+    def forward(y):
+        forward_group(run_rows(grad_ref, y), depth_ref, tall_ref, (o0, o1, o2, o3), y)
 
     inverse(0)
-    for j in range(GROUPS):
-        if j + 1 < GROUPS:
-            inverse(j + 1)
-        activate(bias_ref, upstream_ref, total_ref, act_ref, grad_ref, j)
-        if j > 0:
-            forward(j - 1)
-    forward(GROUPS - 1)
+    for y in range(STEPS):
+        if y + 1 < STEPS:
+            inverse(y + 1)
+        activate(bias_ref, upstream_ref, total_ref, act_ref, grad_ref, y)
+        if y > 0:
+            forward(y - 1)
+    forward(STEPS - 1)
 
 
 def end_kernel(
-    where_ref, i0, i1, i2, i3, grad_ref, mixer_ref, strip_ref, wide_ref, out_ref,
-    depth_ref, tall_ref, long_ref, total_ref,
+    where_ref, i0, i1, i2, i3, bypass_ref, strip_ref, wide_ref, out_ref,
+    depth_ref, tall_ref, long_ref,
 ):
     @pl.when(pl.program_id(0) == 0)
     def _():
         fill_tables(strip_ref, wide_ref, depth_ref, tall_ref, long_ref)
 
-    set_bypass(grad_ref, mixer_ref, total_ref)
-    for j in range(GROUPS):
-        group = slice(GROUP * j, GROUP * (j + 1))
-        values = inverse_group((i0, i1, i2, i3), depth_ref, long_ref, j)
-        out_ref[group] = (total_ref[group] + values.reshape(GROUP, XL, LANES)).astype(BF)
+    for y in range(STEPS):
+        values = inverse_group((i0, i1, i2, i3), depth_ref, long_ref, y)
+        lanes = slice(LANES * y, LANES * (y + 1))
+        out_ref[:, :, lanes] = (
+            bypass_ref[:, :, lanes] + values.reshape(GROUP, XL, LANES)
+        ).astype(BF)
 
 
 def cost(micros):
@@ -237,12 +237,11 @@
 
 
 def column_specs():
-    columns = pl.BlockSpec((CH, XL, LANES), lambda i, w: (0, 0, i))
-    coeffs = pl.BlockSpec((1, ROWS, WIDE), lambda i, w: (i, 0, 0))
-    depth = pl.BlockSpec((1, 2 * KZ, LANES), lambda i, w: (w[1], 0, 0))
-    wide = pl.BlockSpec((1, 2, XL, KX), lambda i, w: (w[1], 0, 0, 0))
-    mixer = pl.BlockSpec((CH * XB, CH * XB), lambda i, w: (0, 0))
-    return columns, coeffs, depth, wide, mixer
+    columns = pl.BlockSpec((GROUP, XL, YL * NZ), lambda j, w: (j, 0, 0))
+    coeffs = pl.BlockSpec((STEPS, ROWS, GL), lambda j, w: (0, 0, j))
+    depth = pl.BlockSpec((1, 2 * KZ, LANES), lambda j, w: (w[1], 0, 0))
+    wide = pl.BlockSpec((1, 2, XL, KX), lambda j, w: (w[1], 0, 0, 0))
+    return columns, coeffs, depth, wide
 
 
 COEFFS = jax.ShapeDtypeStruct((STEPS, ROWS, WIDE), BF)
@@ -252,17 +251,31 @@
     pltpu.VMEM((2 * GL, GL), BF),
     pltpu.VMEM((GL, 2 * GL), BF),
 ]
-TOTAL = pltpu.VMEM((CH, XL, LANES), F32)
-PARAMS = pltpu.CompilerParams(vmem_limit_bytes=56 * 1024 * 1024)
+TOTAL = pltpu.VMEM((STEPS, GROUP, XL, LANES), F32)
+PARAMS = pltpu.CompilerParams(vmem_limit_bytes=63 * 1024 * 1024)
+
+
+def bypass_columns(source, mixer):
+    columns = pl.BlockSpec((CH, XL, LANES), lambda i: (0, 0, i))
+    return pl.pallas_call(
+        bypass_kernel,
+        grid=(STEPS,),
+        in_specs=[columns, pl.BlockSpec((CH * XB, CH * XB), lambda i: (0, 0))],
+        out_specs=columns,
+        out_shape=jax.ShapeDtypeStruct((CH, XL, YL * NZ), F32),
+        compiler_params=PARAMS,
+        cost_estimate=cost(6),
+        name="bypass_columns",
+    )(source, mixer)
 
 
 def start_columns(where, field):
-    columns, coeffs, depth, wide, _ = column_specs()
+    columns, coeffs, depth, wide = column_specs()
     return pl.pallas_call(
         start_kernel,
         grid_spec=pltpu.PrefetchScalarGridSpec(
             num_scalar_prefetch=1,
-            grid=(STEPS,),
+            grid=(GROUPS,),
             in_specs=[columns, depth, wide],
             out_specs=[coeffs] * 4,
             scratch_shapes=BLOCKS,
@@ -274,16 +287,16 @@
     )(where, field, jnp.asarray(DEPTH), jnp.asarray(WIDTH))
 
 
-def middle_columns(where, bias, coeffs_in, field, upstream, mixer):
-    columns, coeffs, depth, wide, mix = column_specs()
+def middle_columns(where, bias, coeffs_in, bypass, upstream):
+    columns, coeffs, depth, wide = column_specs()
     return pl.pallas_call(
         middle_kernel,
         grid_spec=pltpu.PrefetchScalarGridSpec(
             num_scalar_prefetch=1,
-            grid=(STEPS,),
+            grid=(GROUPS,),
             in_specs=[pl.BlockSpec(memory_space=pltpu.SMEM)]
             + [coeffs] * 4
-            + [columns, columns, mix, depth, wide],
+            + [columns, columns, depth, wide],
             out_specs=[columns, columns] + [coeffs] * 4,
             scratch_shapes=BLOCKS + [TOTAL],
         ),
@@ -291,25 +304,25 @@
         compiler_params=PARAMS,
         cost_estimate=cost(19),
         name="middle_columns",
-    )(where, bias, *coeffs_in, field, upstream, mixer, jnp.asarray(DEPTH), jnp.asarray(WIDTH))
-
-
-def end_columns(where, coeffs_in, grad, mixer):
-    columns, coeffs, depth, wide, mix = column_specs()
+    )(where, bias, *coeffs_in, bypass, upstream, jnp.asarray(DEPTH), jnp.asarray(WIDTH))
+
+
+def end_columns(where, coeffs_in, bypass):
+    columns, coeffs, depth, wide = column_specs()
     return pl.pallas_call(
         end_kernel,
         grid_spec=pltpu.PrefetchScalarGridSpec(
             num_scalar_prefetch=1,
-            grid=(STEPS,),
-            in_specs=[coeffs] * 4 + [columns, mix, depth, wide],
+            grid=(GROUPS,),
+            in_specs=[coeffs] * 4 + [columns, depth, wide],
             out_specs=columns,
-            scratch_shapes=BLOCKS + [TOTAL],
+            scratch_shapes=BLOCKS,
         ),
         out_shape=COLUMNS,
         compiler_params=PARAMS,
         cost_estimate=cost(10),
         name="end_columns",
-    )(where, *coeffs_in, grad, mixer, jnp.asarray(DEPTH), jnp.asarray(WIDTH))
+    )(where, *coeffs_in, bypass, jnp.asarray(DEPTH), jnp.asarray(WIDTH))
 
 
 def line_kernel(where_ref, a_ref, b_ref, c_ref, table_ref, out_ref):
@@ -339,6 +352,7 @@
             out_specs=pl.BlockSpec(out_shape.shape, lambda i, w: (0, 0, 0)),
         ),
         out_shape=out_shape,
+        compiler_params=PARAMS,
         cost_estimate=cost(3),
         name=name,
     )(where, *ins, jnp.asarray(LINE))
@@ -507,6 +521,7 @@
         ),
         out_shape=[jax.ShapeDtypeStruct((GY, 48, WIDE), BF)]
         + [jax.ShapeDtypeStruct((KB * PAIR, 2 * HALF), BF)] * 4,
+        compiler_params=PARAMS,
         cost_estimate=cost(5),
         name=name,
     )(where, arrived, *weights)
@@ -547,10 +562,11 @@
     return lax.ppermute(values, "gx", [(i, i ^ bit) for i in range(GX)])
 
 
-def start_slabs(pieces):
+def start_slabs(pieces, beside):
     own, far, near, across = pieces
     far_sum = (far.astype(F32) + swap(across, 1).astype(F32)).astype(BF)
-    return own, swap(near, 1), swap(far_sum, 2)
+    arrived, beside = lax.optimization_barrier((swap(far_sum, 2), beside))
+    return (own, swap(near, 1), arrived), beside
 
 
 def share_slabs(own, *waiting):
@@ -594,7 +610,7 @@
 
     values = field[0]
     *pieces, weight = lax.optimization_barrier((*start_columns(where, values), weight))
-    parts = start_slabs(pieces)
+    parts, bypass = start_slabs(pieces, bypass_columns(values, mixer_of(bypass_weight)))
     weights = gather_weights(weight)
     lines, weights[1], weights[3] = lax.optimization_barrier(
         (to_lines(where, *parts), weights[1], weights[3])
@@ -603,14 +619,13 @@
     modes, *spectra = mode_call(mix_kernel, "mix_modes", where, arrived, weights)
     modes, *spectra = lax.optimization_barrier((exchange_lines(modes), *to_owners(spectra)))
     coeffs = share_slabs(from_lines(where, modes))
-    activation, grad, *pieces = middle_columns(
-        where, bias, coeffs, values, cotangent[0], mixer_of(bypass_weight)
-    )
-    arrived = exchange_lines(to_lines(where, *start_slabs(pieces)))
+    activation, grad, *pieces = middle_columns(where, bias, coeffs, bypass, cotangent[0])
+    parts, bypass = start_slabs(pieces, bypass_columns(grad, mixer_of(bypass_weight.T)))
+    arrived = exchange_lines(to_lines(where, *parts))
     modes, *grads = mode_call(back_kernel, "back_modes", where, arrived, weights)
     modes, *grads = lax.optimization_barrier((exchange_lines(modes), *to_owners(grads)))
     *coeffs, weight_grad = share_slabs(from_lines(where, modes), outer_sum(spectra, grads))
-    field_grad = end_columns(where, coeffs, grad, mixer_of(bypass_weight.T))
+    field_grad = end_columns(where, coeffs, bypass)
     return (
         activation[None],
         field_grad[None],

time: 228 us -> 224 us (0.982)
  waiting for transfers between devices: 59.7 us -> 43.1 us
  Pallas kernels: 66.6 us -> 81.3 us
  local copies, waits for them, and re-layouts: 6.38 us -> 2.43 us
    pallas_call x0 -> x2, Pallas kernels: none -> 15.1 us  [bypass_columns(): pl.pallas_call(bypass_kernel, grid=(STEPS,), in_specs=[columns, pl.BlockS...]
    ppermute x12, waiting for transfers between devices: 30.1 us -> 17.8 us  [swap(): return lax.ppermute(values, 'gx', [(i, i ^ bit) for i in range(GX)])]
    unnamed x56 -> x36, local copies, waits for them, and re-layouts: 6.38 us -> 2.43 us
    all_to_all x3, waiting for transfers between devices: 7.13 us -> 4.55 us  [exchange_lines(): return lax.all_to_all(parts, 'gy', split_axis=0, concat_axis=0, tiled=True)]
    ppermute x12, starting transfers between devices: 25.2 us -> 22.6 us  [swap(): return lax.ppermute(values, 'gx', [(i, i ^ bit) for i in range(GX)])]
  transfers between devices with their start and end apart: 27 -> 27, of which waited for: 13 -> 14; matrix products, arithmetic and copies ran while one was open for 2% -> 2% of each run, Pallas kernels for 7% -> 14%
where the time goes in v4:
time: 224 us; the launch traced here: 223 us
  Pallas kernels  81.3 us (36%)
  starting transfers between devices  67.2 us (30%)
  waiting for transfers between devices  43.1 us (19%)
  blocking collectives  21.6 us (10%)
  other arithmetic  4.48 us (2%)
  local copies, waits for them, and re-layouts  2.43 us (1%)
    ppermute x12, starting transfers between devices, swap(): return lax.ppermute(values, 'gx', [(i, i ^ bit) for i in range(GX)])  22.6 us
    all_to_all x1, blocking collectives, exchange_lines(): return lax.all_to_all(parts, 'gy', split_axis=0, concat_axis=0, tiled=True)  21.6 us
    all_to_all x3, starting transfers between devices, exchange_lines(): return lax.all_to_all(parts, 'gy', split_axis=0, concat_axis=0, tiled=True)  18.2 us
    ppermute x12, waiting for transfers between devices, swap(): return lax.ppermute(values, 'gx', [(i, i ^ bit) for i in range(GX)])  17.8 us
    pallas_call x1, Pallas kernels, middle_columns(): pl.pallas_call(middle_kernel, grid_spec=pltpu.PrefetchScalarGridSpec(num_...  17.1 us
    ppermute x8, starting transfers between devices, to_owners(): moved.append(lax.ppermute(chunk, ('dp', 'gx'), pairs))  15.6 us
    pallas_call x2, Pallas kernels, bypass_columns(): pl.pallas_call(bypass_kernel, grid=(STEPS,), in_specs=[columns, pl.BlockS...  15.1 us
    pallas_call x4, Pallas kernels, line_call(): pl.pallas_call(kernel, grid_spec=pltpu.PrefetchScalarGridSpec(num_scalar_...  13.2 us
  transfers between devices with their start and end apart: 27, of which 14 were waited for; matrix products, arithmetic and copies ran while one was open for 2% of the time, Pallas kernels for 14%

profile of v4, /device:TPU:1, one launch (start us, length us, event | category | flops | bytes accessed | tf_op | source)
XLA Modules:
  0.0 222.8 jit_solution(14995448540505824919)
XLA Ops:
  0.7 4.6 %collective-permute-start = (bf16[3,20,20,2,128]{4,3,2,1,0:T(2,128)(2,1)}, bf16[3,20,20,2,128]{4,3,2,1,0:T(2,128)(2,1)S(1)}, u32[]{:S(2)}, u32[]{:S(2)}) collective-permute-start(bf16[3,20,20,2,128]{4,3,2,1,0:T(2,128)(2,1)} %param.11), channel_id=1, source_target_pairs={{0,0},{8,32},{16,64},{24,96},{32,72},{40,104},{48,8},{56,40},{64,1... | collective-permute-start | bytes 1843208 | tf_op jit(solution)/shard_map/ppermute | solution.py:604
  5.9 9.2 %start_columns.1 = (bf16[4,48,1280]{2,1,0:T(8,128)(2,1)}, bf16[4,48,1280]{2,1,0:T(8,128)(2,1)}, bf16[4,48,1280]{2,1,0:T(8,128)(2,1)}, bf16[4,48,1280]{2,1,0:T(8,128)(2,1)}) custom-call(s32[3]{0:T(128)} %pad_add_fusion.where_ref, bf16[20,64,2048]{2,1,0:T(8,128)(2,1)} %bitcast.18, bf16[4,24,512]{2,1,0:T(8,128)(2,1)} %constant.23.clone.strip_ref, ...), custom_call_target="tpu_custom_call" | custom-call | bytes 24000000 | tf_op jit(solution)/shard_map/start_columns/pallas_call | solution.py:274
  15.2 3.4 %collective-permute-start.4 = (bf16[3,20,20,2,128]{4,3,2,1,0:T(2,128)(2,1)S(1)}, bf16[3,20,20,2,128]{4,3,2,1,0:T(2,128)(2,1)}, u32[]{:S(2)}, u32[]{:S(2)}) collective-permute-start(bf16[3,20,20,2,128]{4,3,2,1,0:T(2,128)(2,1)S(1)} %collective-permute-done), channel_id=1, source_target_pairs={{32,0},{64,32},{96,64},{0,96},{33,1},{65,33},{97,65},{1,97},{34,2}... | collective-permute-start | bytes 1843208 | tf_op jit(solution)/shard_map/ppermute | solution.py:581
  18.6 1.9 add_convert_fusion.1
  20.5 1.4 collective-permute-start.3
  23.6 7.6 %bypass_columns.2.bypass_ref = f32[20,64,2048]{2,1,0:T(8,128)} custom-call(bf16[20,64,2048]{2,1,0:T(8,128)(2,1)} %bitcast.19, bf16[160,160]{1,0:T(8,128)(2,1)} %fusion.mixer_ref), custom_call_target="tpu_custom_call" | custom-call | bytes 18000000 | tf_op jit(solution)/shard_map/bypass_columns/pallas_call | solution.py:260
  31.1 2.3 %collective-permute-done.3.c_ref = bf16[4,48,1280]{2,1,0:T(8,128)(2,1)} collective-permute-done((bf16[4,48,1280]{2,1,0:T(8,128)(2,1)}, bf16[4,48,1280]{2,1,0:T(8,128)(2,1)}, u32[]{:S(2)}, u32[]{:S(2)}) %collective-permute-start.3) | collective-permute-done | bytes 491552 | tf_op jit(solution)/shard_map/ppermute | solution.py:562
  33.4 3.5 %to_lines.2 = bf16[8,48,1280]{2,1,0:T(8,128)(2,1)} custom-call(s32[3]{0:T(128)} %pad_add_fusion.where_ref, bf16[4,48,1280]{2,1,0:T(8,128)(2,1)} %get-tuple-element.51.a_ref, bf16[4,48,1280]{2,1,0:T(8,128)(2,1)} %collective-permute-done.1.b_ref, bf16[4,48,1280]{2,1,0:T(8,128)(2,1)} %collective-permute-done.3.c_ref, bf16[8,384,192]{2,1,0:T(8,128)(2,1)} %constant.26.clone.table_ref), custom_call_target="tpu_custom_call" | custom-call | bytes 9000000 | tf_op jit(solution)/shard_map/to_lines/pallas_call | solution.py:346
  36.8 7.7 %all-to-all-start = ((bf16[8,48,1280]{2,1,0:T(8,128)(2,1)}), bf16[8,48,1280]{2,1,0:T(8,128)(2,1)}, u32[]{:S(2)}, u32[]{:S(2)}) async-start(bf16[8,48,1280]{2,1,0:T(8,128)(2,1)} %to_lines.2), calls=%async_computation | async-start | bytes 1966080 | tf_op jit(solution)/shard_map/all_to_all | solution.py:586
  44.5 2.8 %collective-permute-start.6 = (bf16[3,20,20,2,128]{4,3,2,1,0:T(2,128)(2,1)S(1)}, bf16[3,20,20,2,128]{4,3,2,1,0:T(2,128)(2,1)S(1)}, u32[]{:S(2)}, u32[]{:S(2)}) collective-permute-start(bf16[3,20,20,2,128]{4,3,2,1,0:T(2,128)(2,1)S(1)} %collective-permute-done), channel_id=1, source_target_pairs={{64,0},{96,32},{0,64},{32,96},{65,1},{97,33},{1,65},{33,97},{66,2}... | collective-permute-start | bytes 1843208 | tf_op jit(solution)/shard_map/ppermute | solution.py:581
  47.3 12.7 %collective-permute-done.6 = bf16[3,20,20,2,128]{4,3,2,1,0:T(2,128)(2,1)S(1)} collective-permute-done((bf16[3,20,20,2,128]{4,3,2,1,0:T(2,128)(2,1)S(1)}, bf16[3,20,20,2,128]{4,3,2,1,0:T(2,128)(2,1)S(1)}, u32[]{:S(2)}, u32[]{:S(2)}) %collective-permute-start.6) | collective-permute-done | bytes 614432 | tf_op jit(solution)/shard_map/ppermute | solution.py:581
  60.9 5.8 %mix_modes.1 = (bf16[8,48,1280]{2,1,0:T(8,128)(2,1)}, bf16[120,128]{1,0:T(8,128)(2,1)}, bf16[120,128]{1,0:T(8,128)(2,1)}, bf16[120,128]{1,0:T(8,128)(2,1)}, bf16[120,128]{1,0:T(8,128)(2,1)}) custom-call(s32[3]{0:T(128)} %pad_add_fusion.where_ref, bf16[8,48,1280]{2,1,0:T(8,128)(2,1)} %all-to-all-done.arrived_ref, bf16[3,20,40,128]{3,2,1,0:T(8,128)(2,1)} %bitcast.22, ...), custom_call_target="tpu_custom_call" | custom-call | bytes 15000000 | tf_op jit(solution)/shard_map/mix_modes/pallas_call | solution.py:508
  66.7 6.3 %all-to-all-start.1 = ((bf16[8,48,1280]{2,1,0:T(8,128)(2,1)}), bf16[8,48,1280]{2,1,0:T(8,128)(2,1)}, u32[]{:S(2)}, u32[]{:S(2)}) async-start(bf16[8,48,1280]{2,1,0:T(8,128)(2,1)} %get-tuple-element.60), calls=%async_computation.1 | async-start | bytes 1966080 | tf_op jit(solution)/shard_map/all_to_all | solution.py:586
  73.1 6.2 %collective-permute-start.7 = (bf16[120,128]{1,0:T(8,128)(2,1)}, bf16[120,128]{1,0:T(8,128)(2,1)S(1)}, u32[]{:S(2)}, u32[]{:S(2)}) collective-permute-start(bf16[120,128]{1,0:T(8,128)(2,1)} %get-tuple-element.61), channel_id=1, source_target_pairs={{0,0},{8,32},{16,64},{24,96},{32,8},{40,40},{48,72},{56,104},{64,1... | collective-permute-start | bytes 92168 | tf_op jit(solution)/shard_map/ppermute | solution.py:595
  79.5 1.9 collective-permute-start.9
  81.5 3.1 %collective-permute-done.9.s2 = bf16[120,128]{1,0:T(8,128)(2,1)S(1)} collective-permute-done((bf16[120,128]{1,0:T(8,128)(2,1)}, bf16[120,128]{1,0:T(8,128)(2,1)S(1)}, u32[]{:S(2)}, u32[]{:S(2)}) %collective-permute-start.9) | collective-permute-done | bytes 30752 | tf_op jit(solution)/shard_map/ppermute | solution.py:595
  84.7 2.4 %all-to-all-done.1.modes_ref = bf16[8,48,1280]{2,1,0:T(8,128)(2,1)} async-done(((bf16[8,48,1280]{2,1,0:T(8,128)(2,1)}), bf16[8,48,1280]{2,1,0:T(8,128)(2,1)}, u32[]{:S(2)}, u32[]{:S(2)}) %all-to-all-start.1) | async-done | bytes 983072 | tf_op jit(solution)/shard_map/all_to_all | solution.py:586
  87.1 3.1 %from_lines.2.i0 = bf16[4,48,1280]{2,1,0:T(8,128)(2,1)} custom-call(s32[3]{0:T(128)} %pad_add_fusion.where_ref, bf16[8,48,1280]{2,1,0:T(8,128)(2,1)} %all-to-all-done.1.modes_ref, bf16[8,384,192]{2,1,0:T(8,128)(2,1)} %constant.26.clone.table_ref), custom_call_target="tpu_custom_call" | custom-call | bytes 9000000 | tf_op jit(solution)/shard_map/from_lines/pallas_call | solution.py:346
  90.2 2.9 %collective-permute-start.11 = (bf16[4,48,1280]{2,1,0:T(8,128)(2,1)}, bf16[4,48,1280]{2,1,0:T(8,128)(2,1)S(1)}, u32[]{:S(2)}, u32[]{:S(2)}) collective-permute-start(bf16[4,48,1280]{2,1,0:T(8,128)(2,1)} %from_lines.2.i0), channel_id=1, source_target_pairs={{0,16},{8,24},{16,0},{24,8},{1,17},{9,25},{17,1},{25,9},{2,18},{10... | collective-permute-start | bytes 1474568 | tf_op jit(solution)/shard_map/ppermute | solution.py:562
  93.1 1.9 collective-permute-start.12
  95.0 7.3 %collective-permute-done.11.i1 = bf16[4,48,1280]{2,1,0:T(8,128)(2,1)S(1)} collective-permute-done((bf16[4,48,1280]{2,1,0:T(8,128)(2,1)}, bf16[4,48,1280]{2,1,0:T(8,128)(2,1)S(1)}, u32[]{:S(2)}, u32[]{:S(2)}) %collective-permute-start.11) | collective-permute-done | bytes 491552 | tf_op jit(solution)/shard_map/ppermute | solution.py:562
  102.3 3.2 %collective-permute-start.13 = (bf16[4,48,1280]{2,1,0:T(8,128)(2,1)S(1)}, bf16[4,48,1280]{2,1,0:T(8,128)(2,1)S(1)}, u32[]{:S(2)}, u32[]{:S(2)}) collective-permute-start(bf16[4,48,1280]{2,1,0:T(8,128)(2,1)S(1)} %collective-permute-done.11.i1), channel_id=1, source_target_pairs={{0,8},{8,0},{16,24},{24,16},{1,9},{9,1},{17,25},{25,17},{2,10},{10... | collective-permute-start | bytes 1474568 | tf_op jit(solution)/shard_map/ppermute | solution.py:562
  105.5 1.5 collective-permute-done.13.i3
  107.7 17.1 %middle_columns.1 = (bf16[20,64,2048]{2,1,0:T(8,128)(2,1)}, bf16[20,64,2048]{2,1,0:T(8,128)(2,1)}, bf16[4,48,1280]{2,1,0:T(8,128)(2,1)}, bf16[4,48,1280]{2,1,0:T...) custom-call(s32[3]{0:T(128)} %pad_add_fusion.where_ref, f32[20]{0:T(128)} %bias_ref.1, ...), custom_call_target="tpu_custom_call" | custom-call | bytes 57000000 | tf_op jit(solution)/shard_map/middle_columns/pallas_call | solution.py:292
  125.4 1.7 collective-permute-done.15
  127.1 1.9 add_convert_fusion
  129.0 1.5 collective-permute-start.16
  131.1 0.9 fusion.1.mixer_ref
  132.0 7.6 %bypass_columns.3.bypass_ref = f32[20,64,2048]{2,1,0:T(8,128)} custom-call(bf16[20,64,2048]{2,1,0:T(8,128)(2,1)} %get-tuple-element.72.source_ref, bf16[160,160]{1,0:T(8,128)(2,1)} %fusion.1.mixer_ref), custom_call_target="tpu_custom_call" | custom-call | bytes 18000000 | tf_op jit(solution)/shard_map/bypass_columns/pallas_call | solution.py:260
  139.6 2.0 collective-permute-done.16.c_ref
  142.4 3.5 %to_lines.3 = bf16[8,48,1280]{2,1,0:T(8,128)(2,1)} custom-call(s32[3]{0:T(128)} %pad_add_fusion.where_ref, bf16[4,48,1280]{2,1,0:T(8,128)(2,1)} %get-tuple-element.68.a_ref, bf16[4,48,1280]{2,1,0:T(8,128)(2,1)} %collective-permute-done.14.b_ref, bf16[4,48,1280]{2,1,0:T(8,128)(2,1)} %copy-done.6, bf16[8,384,192]{2,1,0:T(8,128)(2,1)} %constant.26.clone.table_ref), custom_call_target="tpu_custom_call" | custom-call | bytes 9000000 | tf_op jit(solution)/shard_map/to_lines/pallas_call | solution.py:346
  145.9 21.6 %all_to_all.20.arrived_ref = bf16[8,48,1280]{2,1,0:T(8,128)(2,1)} all-to-all(bf16[8,48,1280]{2,1,0:T(8,128)(2,1)} %to_lines.3), channel_id=1, replica_groups=mesh['dp'=4,'gx'=4,'gy'=8] {'gy'}, dimensions={0} | all-to-all | bytes 1966080 | tf_op jit(solution)/shard_map/all_to_all | solution.py:586
  167.5 6.3 %back_modes.1 = (bf16[8,48,1280]{2,1,0:T(8,128)(2,1)}, bf16[120,128]{1,0:T(8,128)(2,1)}, bf16[120,128]{1,0:T(8,128)(2,1)}, bf16[120,128]{1,0:T(8,128)(2,1)}, bf16[120,128]{1,0:T(8,128)(2,1)}) custom-call(s32[3]{0:T(128)} %pad_add_fusion.where_ref, bf16[8,48,1280]{2,1,0:T(8,128)(2,1)} %all_to_all.20.arrived_ref, bf16[3,20,40,128]{3,2,1,0:T(8,128)(2,1)} %bitcast.23, ...), custom_call_target="tpu_custom_call" | custom-call | bytes 15000000 | tf_op jit(solution)/shard_map/back_modes/pallas_call | solution.py:508
  173.8 4.2 %all-to-all-start.3 = ((bf16[8,48,1280]{2,1,0:T(8,128)(2,1)}), bf16[8,48,1280]{2,1,0:T(8,128)(2,1)}, u32[]{:S(2)}, u32[]{:S(2)}) async-start(bf16[8,48,1280]{2,1,0:T(8,128)(2,1)} %get-tuple-element.74), calls=%async_computation.3 | async-start | bytes 1966080 | tf_op jit(solution)/shard_map/all_to_all | solution.py:586
  178.0 3.2 %collective-permute-start.17 = (bf16[120,128]{1,0:T(8,128)(2,1)}, bf16[120,128]{1,0:T(8,128)(2,1)S(1)}, u32[]{:S(2)}, u32[]{:S(2)}) collective-permute-start(bf16[120,128]{1,0:T(8,128)(2,1)} %get-tuple-element.75), channel_id=1, source_target_pairs={{0,0},{8,32},{16,64},{24,96},{32,8},{40,40},{48,72},{56,104},{64,1... | collective-permute-start | bytes 92168 | tf_op jit(solution)/shard_map/ppermute | solution.py:595
  181.3 1.7 collective-permute-start.19
  183.0 2.2 collective-permute-start.20
  185.2 2.3 %collective-permute-done.19.g2 = bf16[120,128]{1,0:T(8,128)(2,1)S(1)} collective-permute-done((bf16[120,128]{1,0:T(8,128)(2,1)}, bf16[120,128]{1,0:T(8,128)(2,1)S(1)}, u32[]{:S(2)}, u32[]{:S(2)}) %collective-permute-start.19) | collective-permute-done | bytes 30752 | tf_op jit(solution)/shard_map/ppermute | solution.py:595
  187.5 2.5 %collective-permute-done.20.g3 = bf16[120,128]{1,0:T(8,128)(2,1)S(1)} collective-permute-done((bf16[120,128]{1,0:T(8,128)(2,1)}, bf16[120,128]{1,0:T(8,128)(2,1)S(1)}, u32[]{:S(2)}, u32[]{:S(2)}) %collective-permute-start.20) | collective-permute-done | bytes 30752 | tf_op jit(solution)/shard_map/ppermute | solution.py:595
  190.0 2.2 all-to-all-done.3.modes_ref
  192.2 3.1 %from_lines.3.i0 = bf16[4,48,1280]{2,1,0:T(8,128)(2,1)} custom-call(s32[3]{0:T(128)} %pad_add_fusion.where_ref, bf16[8,48,1280]{2,1,0:T(8,128)(2,1)} %all-to-all-done.3.modes_ref, bf16[8,384,192]{2,1,0:T(8,128)(2,1)} %constant.26.clone.table_ref), custom_call_target="tpu_custom_call" | custom-call | bytes 9000000 | tf_op jit(solution)/shard_map/from_lines/pallas_call | solution.py:346
  195.3 2.0 collective-permute-start.21
  197.3 3.3 %collective-permute-start.22 = (bf16[4,48,1280]{2,1,0:T(8,128)(2,1)}, bf16[4,48,1280]{2,1,0:T(8,128)(2,1)}, u32[]{:S(2)}, u32[]{:S(2)}) collective-permute-start(bf16[4,48,1280]{2,1,0:T(8,128)(2,1)} %from_lines.3.i0), channel_id=1, source_target_pairs={{0,8},{8,0},{16,24},{24,16},{1,9},{9,1},{17,25},{25,17},{2,10},{10... | collective-permute-start | bytes 1474568 | tf_op jit(solution)/shard_map/ppermute | solution.py:562
  200.6 3.1 %outer_sum.1 = f32[3,20,40,128]{3,2,1,0:T(8,128)} custom-call(bf16[120,128]{1,0:T(8,128)(2,1)} %copy-done.11, bf16[120,128]{1,0:T(8,128)(2,1)} %copy-done.12, bf16[120,128]{1,0:T(8,128)(2,1)} %copy-done.13, bf16[120,128]{1,0:T(8,128)(2,1)} %copy-done.10, bf16[120,128]{1,0:T(8,128)(2,1)} %copy-done.14, bf16[120,128]{1,0:T(8,128)(2,1)} %copy-done.15, ...), custom_call_target="tpu_custom_call" | custom-call | bytes 9000000 | tf_op jit(solution)/shard_map/outer_sum/pallas_call | solution.py:552
  203.7 1.3 collective-permute-done.21.i1
  205.0 4.6 %collective-permute-start.23 = (bf16[4,48,1280]{2,1,0:T(8,128)(2,1)S(1)}, bf16[4,48,1280]{2,1,0:T(8,128)(2,1)}, u32[]{:S(2)}, u32[]{:S(2)}) collective-permute-start(bf16[4,48,1280]{2,1,0:T(8,128)(2,1)S(1)} %collective-permute-done.21.i1), channel_id=1, source_target_pairs={{0,8},{8,0},{16,24},{24,16},{1,9},{9,1},{17,25},{25,17},{2,10},{10... | collective-permute-start | bytes 1474568 | tf_op jit(solution)/shard_map/ppermute | solution.py:562
  209.6 1.6 collective-permute-done.23.i3
  211.3 11.5 %end_columns.1 = bf16[20,64,2048]{2,1,0:T(8,128)(2,1)} custom-call(s32[3]{0:T(128)} %pad_add_fusion.where_ref, bf16[4,48,1280]{2,1,0:T(8,128)(2,1)} %from_lines.3.i0, bf16[4,48,1280]{2,1,0:T(8,128)(2,1)} %copy-done.8, bf16[4,48,1280]{2,1,0:T(8,128)(2,1)} %collective-permute-done.22.i2, bf16[4,48,1280]{2,1,0:T(8,128)(2,1)} %collective-permute-done.23.i3, ...), custom_call_target="tpu_custom_call" | custom-call | bytes 30000000 | tf_op jit(solution)/shard_map/end_columns/pallas_call | solution.py:312
  (60 shorter events, 6.3 us)
Async XLA Ops:
  0.6 22.0 %copy-start = (bf16[20,20]{1,0:T(8,128)(2,1)S(1)}, bf16[20,20]{1,0:T(8,128)(2,1)}, u32[]{:S(2)}) copy-start(bf16[20,20]{1,0:T(8,128)(2,1)} %param.12) | copy-start | bytes 2404
  0.6 22.0 %copy-start.3 = (bf16[160,20]{1,0:T(8,128)(2,1)S(1)}, bf16[160,20]{1,0:T(8,128)(2,1)}, u32[]{:S(2)}) copy-start(bf16[160,20]{1,0:T(8,128)(2,1)} %constant.22.clone) | copy-start | bytes 19204
  0.7 22.0 %copy-start.9 = (bf16[160,160]{1,0:T(8,128)(2,1)S(1)}, bf16[160,160]{1,0:T(8,128)(2,1)}, u32[]{:S(2)}) copy-start(bf16[160,160]{1,0:T(8,128)(2,1)} %constant.25.clone) | copy-start | bytes 153604
  0.7 14.4 %collective-permute-start = (bf16[3,20,20,2,128]{4,3,2,1,0:T(2,128)(2,1)}, bf16[3,20,20,2,128]{4,3,2,1,0:T(2,128)(2,1)S(1)}, u32[]{:S(2)}, u32[]{:S(2)}) collective-permute-start(bf16[3,20,20,2,128]{4,3,2,1,0:T(2,128)(2,1)} %param.11), channel_id=1, source_target_pairs={{0,0},{8,32},{16,64},{24,96},{32,72},{40,104},{48,8},{56,40},{64,1... | collective-permute-start | bytes 1843208 | tf_op jit(solution)/shard_map/ppermute | solution.py:604
  15.1 29.4 %copy-start.1 = (bf16[3,20,20,2,128]{4,3,2,1,0:T(2,128)(2,1)}, bf16[3,20,20,2,128]{4,3,2,1,0:T(2,128)(2,1)S(1)}, u32[]{:S(2)}) copy-start(bf16[3,20,20,2,128]{4,3,2,1,0:T(2,128)(2,1)S(1)} %collective-permute-done) | copy-start | bytes 1843204
  15.1 3.5 %collective-permute-start.2 = (bf16[4,48,1280]{2,1,0:T(8,128)(2,1)}, bf16[4,48,1280]{2,1,0:T(8,128)(2,1)S(1)}, u32[]{:S(2)}, u32[]{:S(2)}) collective-permute-start(bf16[4,48,1280]{2,1,0:T(8,128)(2,1)} %get-tuple-element.54), channel_id=1, source_target_pairs={{0,8},{8,0},{16,24},{24,16},{1,9},{9,1},{17,25},{25,17},{2,10},{10... | collective-permute-start | bytes 1474568 | tf_op jit(solution)/shard_map/ppermute | solution.py:562
  15.2 21.6 %collective-permute-start.4 = (bf16[3,20,20,2,128]{4,3,2,1,0:T(2,128)(2,1)S(1)}, bf16[3,20,20,2,128]{4,3,2,1,0:T(2,128)(2,1)}, u32[]{:S(2)}, u32[]{:S(2)}) collective-permute-start(bf16[3,20,20,2,128]{4,3,2,1,0:T(2,128)(2,1)S(1)} %collective-permute-done), channel_id=1, source_target_pairs={{32,0},{64,32},{96,64},{0,96},{33,1},{65,33},{97,65},{1,97},{34,2}... | collective-permute-start | bytes 1843208 | tf_op jit(solution)/shard_map/ppermute | solution.py:581
  18.6 18.3 %collective-permute-start.5 = (bf16[3,20,20,2,128]{4,3,2,1,0:T(2,128)(2,1)S(1)}, bf16[3,20,20,2,128]{4,3,2,1,0:T(2,128)(2,1)}, u32[]{:S(2)}, u32[]{:S(2)}) collective-permute-start(bf16[3,20,20,2,128]{4,3,2,1,0:T(2,128)(2,1)S(1)} %collective-permute-done), channel_id=1, source_target_pairs={{96,0},{0,32},{32,64},{64,96},{97,1},{1,33},{33,65},{65,97},{98,2}... | collective-permute-start | bytes 1843208 | tf_op jit(solution)/shard_map/ppermute | solution.py:581
  20.5 12.8 %collective-permute-start.3 = (bf16[4,48,1280]{2,1,0:T(8,128)(2,1)}, bf16[4,48,1280]{2,1,0:T(8,128)(2,1)}, u32[]{:S(2)}, u32[]{:S(2)}) collective-permute-start(bf16[4,48,1280]{2,1,0:T(8,128)(2,1)} %add_convert_fusion.1), channel_id=1, source_target_pairs={{0,16},{8,24},{16,0},{24,8},{1,17},{9,25},{17,1},{25,9},{2,18},{10... | collective-permute-start | bytes 1474568 | tf_op jit(solution)/shard_map/ppermute | solution.py:562
  22.0 11.4 %collective-permute-start.1 = (bf16[4,48,1280]{2,1,0:T(8,128)(2,1)}, bf16[4,48,1280]{2,1,0:T(8,128)(2,1)}, u32[]{:S(2)}, u32[]{:S(2)}) collective-permute-start(bf16[4,48,1280]{2,1,0:T(8,128)(2,1)} %get-tuple-element.52), channel_id=1, source_target_pairs={{0,8},{8,0},{16,24},{24,16},{1,9},{9,1},{17,25},{25,17},{2,10},{10... | collective-permute-start | bytes 1474568 | tf_op jit(solution)/shard_map/ppermute | solution.py:562
  36.8 24.0 %all-to-all-start = ((bf16[8,48,1280]{2,1,0:T(8,128)(2,1)}), bf16[8,48,1280]{2,1,0:T(8,128)(2,1)}, u32[]{:S(2)}, u32[]{:S(2)}) async-start(bf16[8,48,1280]{2,1,0:T(8,128)(2,1)} %to_lines.2), calls=%async_computation | async-start | bytes 1966080 | tf_op jit(solution)/shard_map/all_to_all | solution.py:586
  44.5 15.5 %collective-permute-start.6 = (bf16[3,20,20,2,128]{4,3,2,1,0:T(2,128)(2,1)S(1)}, bf16[3,20,20,2,128]{4,3,2,1,0:T(2,128)(2,1)S(1)}, u32[]{:S(2)}, u32[]{:S(2)}) collective-permute-start(bf16[3,20,20,2,128]{4,3,2,1,0:T(2,128)(2,1)S(1)} %collective-permute-done), channel_id=1, source_target_pairs={{64,0},{96,32},{0,64},{32,96},{65,1},{97,33},{1,65},{33,97},{66,2}... | collective-permute-start | bytes 1843208 | tf_op jit(solution)/shard_map/ppermute | solution.py:581
  60.1 0.8 copy-start.2
  66.7 20.4 %all-to-all-start.1 = ((bf16[8,48,1280]{2,1,0:T(8,128)(2,1)}), bf16[8,48,1280]{2,1,0:T(8,128)(2,1)}, u32[]{:S(2)}, u32[]{:S(2)}) async-start(bf16[8,48,1280]{2,1,0:T(8,128)(2,1)} %get-tuple-element.60), calls=%async_computation.1 | async-start | bytes 1966080 | tf_op jit(solution)/shard_map/all_to_all | solution.py:586
  73.0 8.4 %collective-permute-start.10 = (bf16[120,128]{1,0:T(8,128)(2,1)}, bf16[120,128]{1,0:T(8,128)(2,1)S(1)}, u32[]{:S(2)}, u32[]{:S(2)}) collective-permute-start(bf16[120,128]{1,0:T(8,128)(2,1)} %get-tuple-element.64), channel_id=1, source_target_pairs={{0,24},{8,56},{16,88},{24,120},{32,0},{40,32},{48,64},{56,96},{64,... | collective-permute-start | bytes 92168 | tf_op jit(solution)/shard_map/ppermute | solution.py:595
  73.1 8.4 %collective-permute-start.7 = (bf16[120,128]{1,0:T(8,128)(2,1)}, bf16[120,128]{1,0:T(8,128)(2,1)S(1)}, u32[]{:S(2)}, u32[]{:S(2)}) collective-permute-start(bf16[120,128]{1,0:T(8,128)(2,1)} %get-tuple-element.61), channel_id=1, source_target_pairs={{0,0},{8,32},{16,64},{24,96},{32,8},{40,40},{48,72},{56,104},{64,1... | collective-permute-start | bytes 92168 | tf_op jit(solution)/shard_map/ppermute | solution.py:595
  79.4 2.2 collective-permute-start.8
  79.5 5.2 %collective-permute-start.9 = (bf16[120,128]{1,0:T(8,128)(2,1)}, bf16[120,128]{1,0:T(8,128)(2,1)S(1)}, u32[]{:S(2)}, u32[]{:S(2)}) collective-permute-start(bf16[120,128]{1,0:T(8,128)(2,1)} %get-tuple-element.63), channel_id=1, source_target_pairs={{0,16},{8,48},{16,80},{24,112},{32,24},{40,56},{48,88},{56,120},{6... | collective-permute-start | bytes 92168 | tf_op jit(solution)/shard_map/ppermute | solution.py:595
  81.4 43.5 %copy-start.10 = (bf16[120,128]{1,0:T(8,128)(2,1)}, bf16[120,128]{1,0:T(8,128)(2,1)S(1)}, u32[]{:S(2)}) copy-start(bf16[120,128]{1,0:T(8,128)(2,1)S(1)} %collective-permute-done.10.s3) | copy-start | bytes 92164
  81.5 43.3 %copy-start.11 = (bf16[120,128]{1,0:T(8,128)(2,1)}, bf16[120,128]{1,0:T(8,128)(2,1)S(1)}, u32[]{:S(2)}) copy-start(bf16[120,128]{1,0:T(8,128)(2,1)S(1)} %collective-permute-done.7.s0) | copy-start | bytes 92164
  81.5 43.3 %copy-start.12 = (bf16[120,128]{1,0:T(8,128)(2,1)}, bf16[120,128]{1,0:T(8,128)(2,1)S(1)}, u32[]{:S(2)}) copy-start(bf16[120,128]{1,0:T(8,128)(2,1)S(1)} %collective-permute-done.8.s1) | copy-start | bytes 92164
  84.7 40.2 %copy-start.13 = (bf16[120,128]{1,0:T(8,128)(2,1)}, bf16[120,128]{1,0:T(8,128)(2,1)S(1)}, u32[]{:S(2)}) copy-start(bf16[120,128]{1,0:T(8,128)(2,1)S(1)} %collective-permute-done.9.s2) | copy-start | bytes 92164
  90.2 12.1 %collective-permute-start.11 = (bf16[4,48,1280]{2,1,0:T(8,128)(2,1)}, bf16[4,48,1280]{2,1,0:T(8,128)(2,1)S(1)}, u32[]{:S(2)}, u32[]{:S(2)}) collective-permute-start(bf16[4,48,1280]{2,1,0:T(8,128)(2,1)} %from_lines.2.i0), channel_id=1, source_target_pairs={{0,16},{8,24},{16,0},{24,8},{1,17},{9,25},{17,1},{25,9},{2,18},{10... | collective-permute-start | bytes 1474568 | tf_op jit(solution)/shard_map/ppermute | solution.py:562
  93.1 12.4 %collective-permute-start.12 = (bf16[4,48,1280]{2,1,0:T(8,128)(2,1)}, bf16[4,48,1280]{2,1,0:T(8,128)(2,1)S(1)}, u32[]{:S(2)}, u32[]{:S(2)}) collective-permute-start(bf16[4,48,1280]{2,1,0:T(8,128)(2,1)} %from_lines.2.i0), channel_id=1, source_target_pairs={{0,8},{8,0},{16,24},{24,16},{1,9},{9,1},{17,25},{25,17},{2,10},{10... | collective-permute-start | bytes 1474568 | tf_op jit(solution)/shard_map/ppermute | solution.py:562
  102.3 5.4 %copy-start.4 = (bf16[4,48,1280]{2,1,0:T(8,128)(2,1)}, bf16[4,48,1280]{2,1,0:T(8,128)(2,1)S(1)}, u32[]{:S(2)}) copy-start(bf16[4,48,1280]{2,1,0:T(8,128)(2,1)S(1)} %collective-permute-done.11.i1) | copy-start | bytes 1474564
  102.3 4.7 %collective-permute-start.13 = (bf16[4,48,1280]{2,1,0:T(8,128)(2,1)S(1)}, bf16[4,48,1280]{2,1,0:T(8,128)(2,1)S(1)}, u32[]{:S(2)}, u32[]{:S(2)}) collective-permute-start(bf16[4,48,1280]{2,1,0:T(8,128)(2,1)S(1)} %collective-permute-done.11.i1), channel_id=1, source_target_pairs={{0,8},{8,0},{16,24},{24,16},{1,9},{9,1},{17,25},{25,17},{2,10},{10... | collective-permute-start | bytes 1474568 | tf_op jit(solution)/shard_map/ppermute | solution.py:562
  105.5 1.5 copy-start.5
  106.9 0.8 copy-start.7
  124.9 2.2 collective-permute-start.15
  129.0 12.6 %collective-permute-start.16 = (bf16[4,48,1280]{2,1,0:T(8,128)(2,1)}, bf16[4,48,1280]{2,1,0:T(8,128)(2,1)S(1)}, u32[]{:S(2)}, u32[]{:S(2)}) collective-permute-start(bf16[4,48,1280]{2,1,0:T(8,128)(2,1)} %add_convert_fusion), channel_id=1, source_target_pairs={{0,16},{8,24},{16,0},{24,8},{1,17},{9,25},{17,1},{25,9},{2,18},{10... | collective-permute-start | bytes 1474568 | tf_op jit(solution)/shard_map/ppermute | solution.py:562
  130.5 11.2 %collective-permute-start.14 = (bf16[4,48,1280]{2,1,0:T(8,128)(2,1)}, bf16[4,48,1280]{2,1,0:T(8,128)(2,1)}, u32[]{:S(2)}, u32[]{:S(2)}) collective-permute-start(bf16[4,48,1280]{2,1,0:T(8,128)(2,1)} %get-tuple-element.69), channel_id=1, source_target_pairs={{0,8},{8,0},{16,24},{24,16},{1,9},{9,1},{17,25},{25,17},{2,10},{10... | collective-permute-start | bytes 1474568 | tf_op jit(solution)/shard_map/ppermute | solution.py:562
  141.7 0.8 copy-start.6
  173.8 18.4 %all-to-all-start.3 = ((bf16[8,48,1280]{2,1,0:T(8,128)(2,1)}), bf16[8,48,1280]{2,1,0:T(8,128)(2,1)}, u32[]{:S(2)}, u32[]{:S(2)}) async-start(bf16[8,48,1280]{2,1,0:T(8,128)(2,1)} %get-tuple-element.74), calls=%async_computation.3 | async-start | bytes 1966080 | tf_op jit(solution)/shard_map/all_to_all | solution.py:586
  178.0 7.2 %collective-permute-start.17 = (bf16[120,128]{1,0:T(8,128)(2,1)}, bf16[120,128]{1,0:T(8,128)(2,1)S(1)}, u32[]{:S(2)}, u32[]{:S(2)}) collective-permute-start(bf16[120,128]{1,0:T(8,128)(2,1)} %get-tuple-element.75), channel_id=1, source_target_pairs={{0,0},{8,32},{16,64},{24,96},{32,8},{40,40},{48,72},{56,104},{64,1... | collective-permute-start | bytes 92168 | tf_op jit(solution)/shard_map/ppermute | solution.py:595
  181.2 4.0 %collective-permute-start.18 = (bf16[120,128]{1,0:T(8,128)(2,1)}, bf16[120,128]{1,0:T(8,128)(2,1)S(1)}, u32[]{:S(2)}, u32[]{:S(2)}) collective-permute-start(bf16[120,128]{1,0:T(8,128)(2,1)} %get-tuple-element.76), channel_id=1, source_target_pairs={{0,8},{8,40},{16,72},{24,104},{32,16},{40,48},{48,80},{56,112},{64... | collective-permute-start | bytes 92168 | tf_op jit(solution)/shard_map/ppermute | solution.py:595
  181.3 6.2 %collective-permute-start.19 = (bf16[120,128]{1,0:T(8,128)(2,1)}, bf16[120,128]{1,0:T(8,128)(2,1)S(1)}, u32[]{:S(2)}, u32[]{:S(2)}) collective-permute-start(bf16[120,128]{1,0:T(8,128)(2,1)} %get-tuple-element.77), channel_id=1, source_target_pairs={{0,16},{8,48},{16,80},{24,112},{32,24},{40,56},{48,88},{56,120},{6... | collective-permute-start | bytes 92168 | tf_op jit(solution)/shard_map/ppermute | solution.py:595
  183.0 7.0 %collective-permute-start.20 = (bf16[120,128]{1,0:T(8,128)(2,1)}, bf16[120,128]{1,0:T(8,128)(2,1)S(1)}, u32[]{:S(2)}, u32[]{:S(2)}) collective-permute-start(bf16[120,128]{1,0:T(8,128)(2,1)} %get-tuple-element.78), channel_id=1, source_target_pairs={{0,24},{8,56},{16,88},{24,120},{32,0},{40,32},{48,64},{56,96},{64,... | collective-permute-start | bytes 92168 | tf_op jit(solution)/shard_map/ppermute | solution.py:595
  185.2 15.4 %copy-start.14 = (bf16[120,128]{1,0:T(8,128)(2,1)}, bf16[120,128]{1,0:T(8,128)(2,1)S(1)}, u32[]{:S(2)}) copy-start(bf16[120,128]{1,0:T(8,128)(2,1)S(1)} %collective-permute-done.17.g0) | copy-start | bytes 92164
  185.2 15.4 %copy-start.15 = (bf16[120,128]{1,0:T(8,128)(2,1)}, bf16[120,128]{1,0:T(8,128)(2,1)S(1)}, u32[]{:S(2)}) copy-start(bf16[120,128]{1,0:T(8,128)(2,1)S(1)} %collective-permute-done.18.g1) | copy-start | bytes 92164
  187.5 13.1 %copy-start.16 = (bf16[120,128]{1,0:T(8,128)(2,1)}, bf16[120,128]{1,0:T(8,128)(2,1)S(1)}, u32[]{:S(2)}) copy-start(bf16[120,128]{1,0:T(8,128)(2,1)S(1)} %collective-permute-done.19.g2) | copy-start | bytes 92164
  190.0 10.6 %copy-start.17 = (bf16[120,128]{1,0:T(8,128)(2,1)}, bf16[120,128]{1,0:T(8,128)(2,1)S(1)}, u32[]{:S(2)}) copy-start(bf16[120,128]{1,0:T(8,128)(2,1)S(1)} %collective-permute-done.20.g3) | copy-start | bytes 92164
  195.3 9.7 %collective-permute-start.21 = (bf16[4,48,1280]{2,1,0:T(8,128)(2,1)}, bf16[4,48,1280]{2,1,0:T(8,128)(2,1)S(1)}, u32[]{:S(2)}, u32[]{:S(2)}) collective-permute-start(bf16[4,48,1280]{2,1,0:T(8,128)(2,1)} %from_lines.3.i0), channel_id=1, source_target_pairs={{0,16},{8,24},{16,0},{24,8},{1,17},{9,25},{17,1},{25,9},{2,18},{10... | collective-permute-start | bytes 1474568 | tf_op jit(solution)/shard_map/ppermute | solution.py:562
  197.3 12.4 %collective-permute-start.22 = (bf16[4,48,1280]{2,1,0:T(8,128)(2,1)}, bf16[4,48,1280]{2,1,0:T(8,128)(2,1)}, u32[]{:S(2)}, u32[]{:S(2)}) collective-permute-start(bf16[4,48,1280]{2,1,0:T(8,128)(2,1)} %from_lines.3.i0), channel_id=1, source_target_pairs={{0,8},{8,0},{16,24},{24,16},{1,9},{9,1},{17,25},{25,17},{2,10},{10... | collective-permute-start | bytes 1474568 | tf_op jit(solution)/shard_map/ppermute | solution.py:562
  205.0 6.2 %copy-start.8 = (bf16[4,48,1280]{2,1,0:T(8,128)(2,1)}, bf16[4,48,1280]{2,1,0:T(8,128)(2,1)S(1)}, u32[]{:S(2)}) copy-start(bf16[4,48,1280]{2,1,0:T(8,128)(2,1)S(1)} %collective-permute-done.21.i1) | copy-start | bytes 1474564
  205.0 6.2 %collective-permute-start.23 = (bf16[4,48,1280]{2,1,0:T(8,128)(2,1)S(1)}, bf16[4,48,1280]{2,1,0:T(8,128)(2,1)}, u32[]{:S(2)}, u32[]{:S(2)}) collective-permute-start(bf16[4,48,1280]{2,1,0:T(8,128)(2,1)S(1)} %collective-permute-done.21.i1), channel_id=1, source_target_pairs={{0,8},{8,0},{16,24},{24,16},{1,9},{9,1},{17,25},{25,17},{2,10},{10... | collective-permute-start | bytes 1474568 | tf_op jit(solution)/shard_map/ppermute | solution.py:562

commit v5 on v4

--- a/solution.py
+++ b/solution.py
@@ -155,7 +155,7 @@
     for i in range(XL // XB):
         span = slice(i * XB, (i + 1) * XB)
         rows = source_ref[:, span, :].reshape(CH * XB, LANES)
-        out_ref[:, span, :] = dot(mixer_ref[...], rows).reshape(CH, XB, LANES)
+        out_ref[:, span, :] = dot(mixer_ref[...], rows).reshape(CH, XB, LANES).astype(BF)
 
 
 def start_kernel(
@@ -201,7 +201,7 @@
     def inverse(y):
         values = inverse_group((i0, i1, i2, i3), depth_ref, long_ref, y)
         lanes = slice(LANES * y, LANES * (y + 1))
-        total_ref[y] = bypass_ref[:, :, lanes] + values.reshape(GROUP, XL, LANES)
+        total_ref[y] = bypass_ref[:, :, lanes].astype(F32) + values.reshape(GROUP, XL, LANES)
 
     def forward(y):
         forward_group(run_rows(grad_ref, y), depth_ref, tall_ref, (o0, o1, o2, o3), y)
@@ -228,7 +228,7 @@
         values = inverse_group((i0, i1, i2, i3), depth_ref, long_ref, y)
         lanes = slice(LANES * y, LANES * (y + 1))
         out_ref[:, :, lanes] = (
-            bypass_ref[:, :, lanes] + values.reshape(GROUP, XL, LANES)
+            bypass_ref[:, :, lanes].astype(F32) + values.reshape(GROUP, XL, LANES)
         ).astype(BF)
 
 
@@ -252,7 +252,8 @@
     pltpu.VMEM((GL, 2 * GL), BF),
 ]
 TOTAL = pltpu.VMEM((STEPS, GROUP, XL, LANES), F32)
-PARAMS = pltpu.CompilerParams(vmem_limit_bytes=63 * 1024 * 1024)
+PARAMS = pltpu.CompilerParams(vmem_limit_bytes=56 * 1024 * 1024)
+ALONE = pltpu.CompilerParams(vmem_limit_bytes=63 * 1024 * 1024)
 
 
 def bypass_columns(source, mixer):
@@ -262,7 +263,7 @@
         grid=(STEPS,),
         in_specs=[columns, pl.BlockSpec((CH * XB, CH * XB), lambda i: (0, 0))],
         out_specs=columns,
-        out_shape=jax.ShapeDtypeStruct((CH, XL, YL * NZ), F32),
+        out_shape=COLUMNS,
         compiler_params=PARAMS,
         cost_estimate=cost(6),
         name="bypass_columns",
@@ -333,15 +334,20 @@
         out_ref[:, :, lanes] = dot(table_ref[0], rows).astype(BF).reshape(GY, 48, GL)
 
 
-def unline_kernel(where_ref, modes_ref, table_ref, out_ref):
+def unline_kernel(where_ref, *refs):
+    *modes_refs, table_ref, out_ref, order_ref = refs
+    for k in range(GY):
+        owner = ((where_ref[2] + (k & 6)) & 7) ^ (k & 1)
+        start = pl.multiple_of(owner * 48, 16)
+        order_ref[48 * k : 48 * (k + 1)] = table_ref[0, pl.ds(start, 48), :]
     for j in range(GROUPS):
         lanes = slice(GL * j, GL * (j + 1))
-        rows = modes_ref[:, :, lanes].reshape(GY * 48, GL)
-        out_ref[:, :, lanes] = dot(table_ref[0], rows, 0, 0).astype(BF).reshape(STEPS, ROWS, GL)
-
-
-def line_call(kernel, name, where, ins, out_shape):
-    whole = pl.BlockSpec(ins[0].shape, lambda i, w: (0, 0, 0))
+        rows = jnp.concatenate([ref[:, lanes] for ref in modes_refs], axis=0)
+        out_ref[:, :, lanes] = dot(order_ref[...], rows, 0, 0).astype(BF).reshape(STEPS, ROWS, GL)
+
+
+def line_call(kernel, name, where, ins, out_shape, scratch=()):
+    whole = pl.BlockSpec(ins[0].shape, lambda i, w: (0,) * ins[0].ndim)
     table = pl.BlockSpec((1, GY * 48, STEPS * ROWS), lambda i, w: (w[2], 0, 0))
     return pl.pallas_call(
         kernel,
@@ -350,9 +356,10 @@
             grid=(1,),
             in_specs=[whole] * len(ins) + [table],
             out_specs=pl.BlockSpec(out_shape.shape, lambda i, w: (0, 0, 0)),
+            scratch_shapes=list(scratch),
         ),
         out_shape=out_shape,
-        compiler_params=PARAMS,
+        compiler_params=ALONE,
         cost_estimate=cost(3),
         name=name,
     )(where, *ins, jnp.asarray(LINE))
@@ -364,7 +371,8 @@
 
 
 def from_lines(where, modes):
-    return line_call(unline_kernel, "from_lines", where, (modes,), COEFFS)
+    order = pltpu.VMEM((GY * 48, STEPS * ROWS), BF)
+    return line_call(unline_kernel, "from_lines", where, modes, COEFFS, [order])
 
 
 UNROLL = 4
@@ -413,9 +421,7 @@
             sum_ref[(2 + part) * SETS : (3 + part) * SETS, lanes] = jnp.where(
                 low, pltpu.roll(even, HALF, 1), odd
             )
-    modes = sum_ref[...].astype(BF)
-    for owner in range(GY):
-        out_ref[owner] = modes
+    out_ref[...] = sum_ref[...].astype(BF)
 
 
 def fold_scale(where_ref):
@@ -512,16 +518,16 @@
             grid=(KB,),
             in_specs=[pl.BlockSpec((GY, 48, WIDE), lambda i, w: (0, 0, 0))]
             + [pl.BlockSpec((1, CH, PAIR, 2 * HALF), lambda i, w: (i, 0, 0, 0))] * 4,
-            out_specs=[pl.BlockSpec((GY, 48, WIDE), lambda i, w: (0, 0, 0))] + [chunk] * 4,
+            out_specs=[pl.BlockSpec((48, WIDE), lambda i, w: (0, 0))] + [chunk] * 4,
             scratch_shapes=[
                 pltpu.VMEM((48, WIDE), F32),
                 pltpu.VMEM((SETS * PAIR, 2 * HALF), F32),
                 pltpu.VMEM((SETS * PAIR, 2 * HALF), F32),
             ],
         ),
-        out_shape=[jax.ShapeDtypeStruct((GY, 48, WIDE), BF)]
+        out_shape=[jax.ShapeDtypeStruct((48, WIDE), BF)]
         + [jax.ShapeDtypeStruct((KB * PAIR, 2 * HALF), BF)] * 4,
-        compiler_params=PARAMS,
+        compiler_params=ALONE,
         cost_estimate=cost(5),
         name=name,
     )(where, arrived, *weights)
@@ -582,6 +588,14 @@
     return [part.reshape(KB, CH, PAIR, 2 * HALF) for part in held]
 
 
+def gather_lines(modes):
+    held = [modes, lax.ppermute(modes, "gy", [(g ^ 1, g) for g in range(GY)])]
+    for step in range(2, GY, 2):
+        pairs = [((g + step) % GY, g) for g in range(GY)]
+        held += [lax.ppermute(part, "gy", pairs) for part in held[:2]]
+    return held
+
+
 def exchange_lines(parts):
     return lax.all_to_all(parts, "gy", split_axis=0, concat_axis=0, tiled=True)
 
@@ -617,14 +631,14 @@
     )
     arrived = exchange_lines(lines)
     modes, *spectra = mode_call(mix_kernel, "mix_modes", where, arrived, weights)
-    modes, *spectra = lax.optimization_barrier((exchange_lines(modes), *to_owners(spectra)))
-    coeffs = share_slabs(from_lines(where, modes))
+    own = from_lines(where, gather_lines(modes))
+    *coeffs, s0, s1, s2, s3 = share_slabs(own, *to_owners(spectra))
     activation, grad, *pieces = middle_columns(where, bias, coeffs, bypass, cotangent[0])
     parts, bypass = start_slabs(pieces, bypass_columns(grad, mixer_of(bypass_weight.T)))
     arrived = exchange_lines(to_lines(where, *parts))
     modes, *grads = mode_call(back_kernel, "back_modes", where, arrived, weights)
-    modes, *grads = lax.optimization_barrier((exchange_lines(modes), *to_owners(grads)))
-    *coeffs, weight_grad = share_slabs(from_lines(where, modes), outer_sum(spectra, grads))
+    own = from_lines(where, gather_lines(modes))
+    *coeffs, weight_grad = share_slabs(own, outer_sum((s0, s1, s2, s3), to_owners(grads)))
     field_grad = end_columns(where, coeffs, bypass)
     return (
         activation[None],

time: 224 us -> 220 us (0.982)
  Pallas kernels: 81.3 us -> 76.7 us
  waiting for transfers between devices: 43.1 us -> 47 us
  starting transfers between devices: 67.2 us -> 63.5 us
  local copies, waits for them, and re-layouts: 2.43 us -> 4.83 us
    ppermute x0 -> x14, starting transfers between devices: none -> 15.4 us  [the longest x12 12.3 us: gather_lines(): held += [lax.ppermute(part, 'gy', pairs) for part in held[:2]]]
    ppermute x0 -> x14, waiting for transfers between devices: none -> 15.3 us  [the longest x12 12.9 us: gather_lines(): held += [lax.ppermute(part, 'gy', pairs) for part in held[:2]]]
    all_to_all x3 -> x1, starting transfers between devices: 18.2 us -> 7.67 us  [exchange_lines(): return lax.all_to_all(parts, 'gy', split_axis=0, concat_axis=0, tiled=True)]
    ppermute x12, starting transfers between devices: 22.6 us -> 12.1 us  [swap(): return lax.ppermute(values, 'gx', [(i, i ^ bit) for i in range(GX)])]
    ppermute x12, waiting for transfers between devices: 17.8 us -> 12.3 us  [swap(): return lax.ppermute(values, 'gx', [(i, i ^ bit) for i in range(GX)])]
    all_to_all x3 -> x1, waiting for transfers between devices: 4.55 us -> 0.01 us  [exchange_lines(): return lax.all_to_all(parts, 'gy', split_axis=0, concat_axis=0, tiled=True)]
    pallas_call x2, Pallas kernels: 15.1 us -> 12.4 us  [bypass_columns(): pl.pallas_call(bypass_kernel, grid=(STEPS,), in_specs=[columns, pl.BlockS...]
    unnamed x36 -> x66, local copies, waits for them, and re-layouts: 2.43 us -> 4.83 us
  transfers between devices with their start and end apart: 27 -> 39, of which waited for: 14 -> 21; matrix products, arithmetic and copies ran while one was open for 2% -> 2% of each run, Pallas kernels for 14% -> 13%
where the time goes in v5:
time: 220 us; the launch traced here: 218 us
  Pallas kernels  76.7 us (35%)
  starting transfers between devices  63.5 us (29%)
  waiting for transfers between devices  47 us (21%)
  blocking collectives  20.4 us (9%)
  local copies, waits for them, and re-layouts  4.83 us (2%)
  other arithmetic  3.01 us (1%)
    all_to_all x1, blocking collectives, exchange_lines(): return lax.all_to_all(parts, 'gy', split_axis=0, concat_axis=0, tiled=True)  20.4 us
    ppermute x8, starting transfers between devices, to_owners(): moved.append(lax.ppermute(chunk, ('dp', 'gx'), pairs))  17.7 us
    pallas_call x1, Pallas kernels, middle_columns(): pl.pallas_call(middle_kernel, grid_spec=pltpu.PrefetchScalarGridSpec(num_...  17.2 us
    pallas_call x4, Pallas kernels, line_call(): pl.pallas_call(kernel, grid_spec=pltpu.PrefetchScalarGridSpec(num_scalar_...  13.4 us
    ppermute x12, waiting for transfers between devices, gather_lines(): held += [lax.ppermute(part, 'gy', pairs) for part in held[:2]]  12.9 us
    ppermute x3, waiting for transfers between devices, gather_weights(): lax.ppermute(weight, 'dp', [((a + k) % DP, a) for a in range(DP)])  12.9 us
    pallas_call x2, Pallas kernels, bypass_columns(): pl.pallas_call(bypass_kernel, grid=(STEPS,), in_specs=[columns, pl.BlockS...  12.4 us
    ppermute x12, starting transfers between devices, gather_lines(): held += [lax.ppermute(part, 'gy', pairs) for part in held[:2]]  12.3 us
  transfers between devices with their start and end apart: 39, of which 21 were waited for; matrix products, arithmetic and copies ran while one was open for 2% of the time, Pallas kernels for 13%

profile of v5, /device:TPU:1, one launch (start us, length us, event | category | flops | bytes accessed | tf_op | source)
XLA Modules:
  0.0 218.2 jit_solution(7269462556747366468)
XLA Ops:
  0.7 4.6 %collective-permute-start = (bf16[3,20,20,2,128]{4,3,2,1,0:T(2,128)(2,1)}, bf16[3,20,20,2,128]{4,3,2,1,0:T(2,128)(2,1)S(1)}, u32[]{:S(2)}, u32[]{:S(2)}) collective-permute-start(bf16[3,20,20,2,128]{4,3,2,1,0:T(2,128)(2,1)} %param.11), channel_id=1, source_target_pairs={{0,0},{8,32},{16,64},{24,96},{32,72},{40,104},{48,8},{56,40},{64,1... | collective-permute-start | bytes 1843208 | tf_op jit(solution)/shard_map/ppermute | solution.py:618
  6.0 9.2 %start_columns.1 = (bf16[4,48,1280]{2,1,0:T(8,128)(2,1)}, bf16[4,48,1280]{2,1,0:T(8,128)(2,1)}, bf16[4,48,1280]{2,1,0:T(8,128)(2,1)}, bf16[4,48,1280]{2,1,0:T(8,128)(2,1)}) custom-call(s32[3]{0:T(128)} %pad_add_fusion.where_ref, bf16[20,64,2048]{2,1,0:T(8,128)(2,1)} %bitcast.18, bf16[4,24,512]{2,1,0:T(8,128)(2,1)} %constant.23.clone.strip_ref, ...), custom_call_target="tpu_custom_call" | custom-call | bytes 24000000 | tf_op jit(solution)/shard_map/start_columns/pallas_call | solution.py:275
  15.3 3.3 %collective-permute-start.4 = (bf16[3,20,20,2,128]{4,3,2,1,0:T(2,128)(2,1)S(1)}, bf16[3,20,20,2,128]{4,3,2,1,0:T(2,128)(2,1)}, u32[]{:S(2)}, u32[]{:S(2)}) collective-permute-start(bf16[3,20,20,2,128]{4,3,2,1,0:T(2,128)(2,1)S(1)} %collective-permute-done), channel_id=1, source_target_pairs={{32,0},{64,32},{96,64},{0,96},{33,1},{65,33},{97,65},{1,97},{34,2}... | collective-permute-start | bytes 1843208 | tf_op jit(solution)/shard_map/ppermute | solution.py:587
  18.6 1.2 add_convert_fusion.1
  19.8 1.6 collective-permute-start.3
  22.9 6.1 %bypass_columns.2.bypass_ref = bf16[20,64,2048]{2,1,0:T(8,128)(2,1)} custom-call(bf16[20,64,2048]{2,1,0:T(8,128)(2,1)} %bitcast.19, bf16[160,160]{1,0:T(8,128)(2,1)} %fusion.mixer_ref), custom_call_target="tpu_custom_call" | custom-call | bytes 18000000 | tf_op jit(solution)/shard_map/bypass_columns/pallas_call | solution.py:261
  29.1 3.5 %collective-permute-done.3.c_ref = bf16[4,48,1280]{2,1,0:T(8,128)(2,1)} collective-permute-done((bf16[4,48,1280]{2,1,0:T(8,128)(2,1)S(1)}, bf16[4,48,1280]{2,1,0:T(8,128)(2,1)}, u32[]{:S(2)}, u32[]{:S(2)}) %collective-permute-start.3) | collective-permute-done | bytes 491552 | tf_op jit(solution)/shard_map/ppermute | solution.py:568
  32.6 3.5 %to_lines.2 = bf16[8,48,1280]{2,1,0:T(8,128)(2,1)} custom-call(s32[3]{0:T(128)} %pad_add_fusion.where_ref, bf16[4,48,1280]{2,1,0:T(8,128)(2,1)} %get-tuple-element.46.a_ref, bf16[4,48,1280]{2,1,0:T(8,128)(2,1)} %collective-permute-done.1.b_ref, bf16[4,48,1280]{2,1,0:T(8,128)(2,1)} %collective-permute-done.3.c_ref, ...), custom_call_target="tpu_custom_call" | custom-call | bytes 9000000 | tf_op jit(solution)/shard_map/to_lines/pallas_call | solution.py:352
  36.0 7.7 %all-to-all-start = ((bf16[8,48,1280]{2,1,0:T(8,128)(2,1)}), bf16[8,48,1280]{2,1,0:T(8,128)(2,1)}, u32[]{:S(2)}, u32[]{:S(2)}) async-start(bf16[8,48,1280]{2,1,0:T(8,128)(2,1)} %to_lines.2), calls=%async_computation | async-start | bytes 1966080 | tf_op jit(solution)/shard_map/all_to_all | solution.py:600
  43.7 2.7 %collective-permute-start.6 = (bf16[3,20,20,2,128]{4,3,2,1,0:T(2,128)(2,1)S(1)}, bf16[3,20,20,2,128]{4,3,2,1,0:T(2,128)(2,1)S(1)}, u32[]{:S(2)}, u32[]{:S(2)}) collective-permute-start(bf16[3,20,20,2,128]{4,3,2,1,0:T(2,128)(2,1)S(1)} %collective-permute-done), channel_id=1, source_target_pairs={{64,0},{96,32},{0,64},{32,96},{65,1},{97,33},{1,65},{33,97},{66,2}... | collective-permute-start | bytes 1843208 | tf_op jit(solution)/shard_map/ppermute | solution.py:587
  46.4 12.9 %collective-permute-done.6 = bf16[3,20,20,2,128]{4,3,2,1,0:T(2,128)(2,1)S(1)} collective-permute-done((bf16[3,20,20,2,128]{4,3,2,1,0:T(2,128)(2,1)S(1)}, bf16[3,20,20,2,128]{4,3,2,1,0:T(2,128)(2,1)S(1)}, u32[]{:S(2)}, u32[]{:S(2)}) %collective-permute-start.6) | collective-permute-done | bytes 614432 | tf_op jit(solution)/shard_map/ppermute | solution.py:587
  60.1 5.5 %mix_modes.1 = (bf16[48,1280]{1,0:T(8,128)(2,1)}, bf16[120,128]{1,0:T(8,128)(2,1)}, bf16[120,128]{1,0:T(8,128)(2,1)}, bf16[120,128]{1,0:T(8,128)(2,1)}, bf16[120,128]{1,0:T(8,128)(2,1)}) custom-call(s32[3]{0:T(128)} %pad_add_fusion.where_ref, bf16[8,48,1280]{2,1,0:T(8,128)(2,1)} %all-to-all-done.arrived_ref, bf16[3,20,40,128]{3,2,1,0:T(8,128)(2,1)} %bitcast.22, ...), custom_call_target="tpu_custom_call" | custom-call | bytes 15000000 | tf_op jit(solution)/shard_map/mix_modes/pallas_call | solution.py:514
  65.6 2.7 %collective-permute-start.7 = (bf16[48,1280]{1,0:T(8,128)(2,1)}, bf16[48,1280]{1,0:T(8,128)(2,1)S(1)}, u32[]{:S(2)}, u32[]{:S(2)}) collective-permute-start(bf16[48,1280]{1,0:T(8,128)(2,1)} %get-tuple-element.55.refs_0_), channel_id=1, source_target_pairs={{1,0},{0,1},{3,2},{2,3},{5,4},{4,5},{7,6},{6,7},{9,8},{8,9},{11,10... | collective-permute-start | bytes 368648 | tf_op jit(solution)/shard_map/ppermute | solution.py:592
  68.3 2.7 %collective-permute-start.10 = (bf16[48,1280]{1,0:T(8,128)(2,1)}, bf16[48,1280]{1,0:T(8,128)(2,1)S(1)}, u32[]{:S(2)}, u32[]{:S(2)}) collective-permute-start(bf16[48,1280]{1,0:T(8,128)(2,1)} %get-tuple-element.55.refs_0_), channel_id=1, source_target_pairs={{4,0},{5,1},{6,2},{7,3},{0,4},{1,5},{2,6},{3,7},{12,8},{13,9},{14,... | collective-permute-start | bytes 368648 | tf_op jit(solution)/shard_map/ppermute | solution.py:595
  71.2 2.4 %collective-permute-start.8 = (bf16[48,1280]{1,0:T(8,128)(2,1)}, bf16[48,1280]{1,0:T(8,128)(2,1)S(1)}, u32[]{:S(2)}, u32[]{:S(2)}) collective-permute-start(bf16[48,1280]{1,0:T(8,128)(2,1)} %get-tuple-element.55.refs_0_), channel_id=1, source_target_pairs={{2,0},{3,1},{4,2},{5,3},{6,4},{7,5},{0,6},{1,7},{10,8},{11,9},{12,... | collective-permute-start | bytes 368648 | tf_op jit(solution)/shard_map/ppermute | solution.py:595
  74.3 2.1 collective-permute-start.9
  78.4 1.6 collective-permute-done.11.refs_5_
  82.2 3.3 %from_lines.2.i0 = bf16[4,48,1280]{2,1,0:T(8,128)(2,1)} custom-call(s32[3]{0:T(128)} %pad_add_fusion.where_ref, bf16[48,1280]{1,0:T(8,128)(2,1)} %get-tuple-element.55.refs_0_, bf16[48,1280]{1,0:T(8,128)(2,1)} %copy-done.13, bf16[48,1280]{1,0:T(8,128)(2,1)} %copy-done.19, bf16[48,1280]{1,0:T(8,128)(2,1)} %collective-permute-done.9.refs_3_, ...), custom_call_target="tpu_custom_call" | custom-call | bytes 9000000 | tf_op jit(solution)/shard_map/from_lines/pallas_call | solution.py:352
  85.7 5.8 %collective-permute-start.15 = (bf16[120,128]{1,0:T(8,128)(2,1)}, bf16[120,128]{1,0:T(8,128)(2,1)S(1)}, u32[]{:S(2)}, u32[]{:S(2)}) collective-permute-start(bf16[120,128]{1,0:T(8,128)(2,1)} %get-tuple-element.56), channel_id=1, source_target_pairs={{0,0},{8,32},{16,64},{24,96},{32,8},{40,40},{48,72},{56,104},{64,1... | collective-permute-start | bytes 92168 | tf_op jit(solution)/shard_map/ppermute | solution.py:609
  91.6 2.7 %collective-permute-start.17 = (bf16[120,128]{1,0:T(8,128)(2,1)}, bf16[120,128]{1,0:T(8,128)(2,1)S(1)}, u32[]{:S(2)}, u32[]{:S(2)}) collective-permute-start(bf16[120,128]{1,0:T(8,128)(2,1)} %get-tuple-element.58), channel_id=1, source_target_pairs={{0,16},{8,48},{16,80},{24,112},{32,24},{40,56},{48,88},{56,120},{6... | collective-permute-start | bytes 92168 | tf_op jit(solution)/shard_map/ppermute | solution.py:609
  95.1 2.5 %collective-permute-start.19 = (bf16[4,48,1280]{2,1,0:T(8,128)(2,1)}, bf16[4,48,1280]{2,1,0:T(8,128)(2,1)S(1)}, u32[]{:S(2)}, u32[]{:S(2)}) collective-permute-start(bf16[4,48,1280]{2,1,0:T(8,128)(2,1)} %from_lines.2.i0), channel_id=1, source_target_pairs={{0,8},{8,0},{16,24},{24,16},{1,9},{9,1},{17,25},{25,17},{2,10},{10... | collective-permute-start | bytes 1474568 | tf_op jit(solution)/shard_map/ppermute | solution.py:568
  97.7 2.0 collective-permute-done.18.s3
  99.7 1.2 collective-permute-start.20
  100.9 1.5 collective-permute-done.20.i3
  103.2 17.2 %middle_columns.1 = (bf16[20,64,2048]{2,1,0:T(8,128)(2,1)}, bf16[20,64,2048]{2,1,0:T(8,128)(2,1)}, bf16[4,48,1280]{2,1,0:T(8,128)(2,1)}, bf16[4,48,1280]{2,1,0:T...) custom-call(s32[3]{0:T(128)} %pad_add_fusion.where_ref, f32[20]{0:T(128)} %bias_ref.1, ...), custom_call_target="tpu_custom_call" | custom-call | bytes 57000000 | tf_op jit(solution)/shard_map/middle_columns/pallas_call | solution.py:293
  120.8 1.7 collective-permute-done.22
  122.5 1.2 add_convert_fusion
  123.7 2.4 %collective-permute-start.23 = (bf16[4,48,1280]{2,1,0:T(8,128)(2,1)S(1)}, bf16[4,48,1280]{2,1,0:T(8,128)(2,1)S(1)}, u32[]{:S(2)}, u32[]{:S(2)}) collective-permute-start(bf16[4,48,1280]{2,1,0:T(8,128)(2,1)S(1)} %add_convert_fusion), channel_id=1, source_target_pairs={{0,16},{8,24},{16,0},{24,8},{1,17},{9,25},{17,1},{25,9},{2,18},{10... | collective-permute-start | bytes 1474568 | tf_op jit(solution)/shard_map/ppermute | solution.py:568
  127.7 6.2 %bypass_columns.3.bypass_ref = bf16[20,64,2048]{2,1,0:T(8,128)(2,1)} custom-call(bf16[20,64,2048]{2,1,0:T(8,128)(2,1)} %get-tuple-element.67.source_ref, bf16[160,160]{1,0:T(8,128)(2,1)} %fusion.1.mixer_ref), custom_call_target="tpu_custom_call" | custom-call | bytes 18000000 | tf_op jit(solution)/shard_map/bypass_columns/pallas_call | solution.py:261
  133.9 3.5 %collective-permute-done.23.c_ref = bf16[4,48,1280]{2,1,0:T(8,128)(2,1)S(1)} collective-permute-done((bf16[4,48,1280]{2,1,0:T(8,128)(2,1)S(1)}, bf16[4,48,1280]{2,1,0:T(8,128)(2,1)S(1)}, u32[]{:S(2)}, u32[]{:S(2)}) %collective-permute-start.23) | collective-permute-done | bytes 491552 | tf_op jit(solution)/shard_map/ppermute | solution.py:568
  138.2 3.5 %to_lines.3 = bf16[8,48,1280]{2,1,0:T(8,128)(2,1)} custom-call(s32[3]{0:T(128)} %pad_add_fusion.where_ref, bf16[4,48,1280]{2,1,0:T(8,128)(2,1)} %get-tuple-element.63.a_ref, bf16[4,48,1280]{2,1,0:T(8,128)(2,1)} %collective-permute-done.21.b_ref, bf16[4,48,1280]{2,1,0:T(8,128)(2,1)} %copy-done.7, bf16[8,384,192]{2,1,0:T(8,128)(2,1)} %constant.26.clone.table_ref.refs_8_), custom_call_target="tpu_custom_call" | custom-call | bytes 9000000 | tf_op jit(solution)/shard_map/to_lines/pallas_call | solution.py:352
  141.7 20.4 %all_to_all.10.arrived_ref = bf16[8,48,1280]{2,1,0:T(8,128)(2,1)} all-to-all(bf16[8,48,1280]{2,1,0:T(8,128)(2,1)} %to_lines.3), channel_id=1, replica_groups=mesh['dp'=4,'gx'=4,'gy'=8] {'gy'}, dimensions={0} | all-to-all | bytes 1966080 | tf_op jit(solution)/shard_map/all_to_all | solution.py:600
  162.0 6.0 %back_modes.1 = (bf16[48,1280]{1,0:T(8,128)(2,1)}, bf16[120,128]{1,0:T(8,128)(2,1)}, bf16[120,128]{1,0:T(8,128)(2,1)}, bf16[120,128]{1,0:T(8,128)(2,1)}, bf16[120,128]{1,0:T(8,128)(2,1)}) custom-call(s32[3]{0:T(128)} %pad_add_fusion.where_ref, bf16[8,48,1280]{2,1,0:T(8,128)(2,1)} %all_to_all.10.arrived_ref, bf16[3,20,40,128]{3,2,1,0:T(8,128)(2,1)} %bitcast.23, ...), custom_call_target="tpu_custom_call" | custom-call | bytes 15000000 | tf_op jit(solution)/shard_map/back_modes/pallas_call | solution.py:514
  168.5 1.5 collective-permute-start.25
  169.9 1.2 collective-permute-start.27
  171.1 2.4 %collective-permute-done.24.refs_1_ = bf16[48,1280]{1,0:T(8,128)(2,1)S(1)} collective-permute-done((bf16[48,1280]{1,0:T(8,128)(2,1)}, bf16[48,1280]{1,0:T(8,128)(2,1)S(1)}, u32[]{:S(2)}, u32[]{:S(2)}) %collective-permute-start.24) | collective-permute-done | bytes 122912 | tf_op jit(solution)/shard_map/ppermute | solution.py:592
  176.7 1.7 collective-permute-done.26.refs_3_
  178.4 2.2 %collective-permute-done.28.refs_5_ = bf16[48,1280]{1,0:T(8,128)(2,1)S(1)} collective-permute-done((bf16[48,1280]{1,0:T(8,128)(2,1)S(1)}, bf16[48,1280]{1,0:T(8,128)(2,1)S(1)}, u32[]{:S(2)}, u32[]{:S(2)}) %collective-permute-start.28) | collective-permute-done | bytes 122912 | tf_op jit(solution)/shard_map/ppermute | solution.py:595
  180.6 1.7 collective-permute-done.30.refs_7_
  183.0 3.3 %from_lines.3.i0 = bf16[4,48,1280]{2,1,0:T(8,128)(2,1)} custom-call(s32[3]{0:T(128)} %pad_add_fusion.where_ref, bf16[48,1280]{1,0:T(8,128)(2,1)} %get-tuple-element.69.refs_0_, bf16[48,1280]{1,0:T(8,128)(2,1)} %copy-done.12, bf16[48,1280]{1,0:T(8,128)(2,1)} %copy-done.14, bf16[48,1280]{1,0:T(8,128)(2,1)} %copy-done.20, bf16[48,1280]{1,0:T(8,128)(2,1)} %copy-done.16, ...), custom_call_target="tpu_custom_call" | custom-call | bytes 9000000 | tf_op jit(solution)/shard_map/from_lines/pallas_call | solution.py:352
  186.9 4.8 %collective-permute-start.32 = (bf16[120,128]{1,0:T(8,128)(2,1)}, bf16[120,128]{1,0:T(8,128)(2,1)S(1)}, u32[]{:S(2)}, u32[]{:S(2)}) collective-permute-start(bf16[120,128]{1,0:T(8,128)(2,1)} %get-tuple-element.74), channel_id=1, source_target_pairs={{0,0},{8,32},{16,64},{24,96},{32,8},{40,40},{48,72},{56,104},{64,1... | collective-permute-start | bytes 92168 | tf_op jit(solution)/shard_map/ppermute | solution.py:609
  191.8 2.6 %collective-permute-start.34 = (bf16[120,128]{1,0:T(8,128)(2,1)}, bf16[120,128]{1,0:T(8,128)(2,1)S(1)}, u32[]{:S(2)}, u32[]{:S(2)}) collective-permute-start(bf16[120,128]{1,0:T(8,128)(2,1)} %get-tuple-element.76), channel_id=1, source_target_pairs={{0,16},{8,48},{16,80},{24,112},{32,24},{40,56},{48,88},{56,120},{6... | collective-permute-start | bytes 92168 | tf_op jit(solution)/shard_map/ppermute | solution.py:609
  195.2 1.4 collective-permute-done.34.g2
  196.6 3.2 %collective-permute-done.35.g3 = bf16[120,128]{1,0:T(8,128)(2,1)S(1)} collective-permute-done((bf16[120,128]{1,0:T(8,128)(2,1)}, bf16[120,128]{1,0:T(8,128)(2,1)S(1)}, u32[]{:S(2)}, u32[]{:S(2)}) %collective-permute-start.35) | collective-permute-done | bytes 30752 | tf_op jit(solution)/shard_map/ppermute | solution.py:609
  200.4 3.1 %outer_sum.1 = f32[3,20,40,128]{3,2,1,0:T(8,128)} custom-call(bf16[120,128]{1,0:T(8,128)(2,1)} %copy-done.25, bf16[120,128]{1,0:T(8,128)(2,1)} %copy-done.26, bf16[120,128]{1,0:T(8,128)(2,1)} %copy-done.27, bf16[120,128]{1,0:T(8,128)(2,1)} %copy-done.28, bf16[120,128]{1,0:T(8,128)(2,1)} %copy-done.29, bf16[120,128]{1,0:T(8,128)(2,1)} %copy-done.30, ...), custom_call_target="tpu_custom_call" | custom-call | bytes 9000000 | tf_op jit(solution)/shard_map/outer_sum/pallas_call | solution.py:558
  203.5 1.4 collective-permute-start.36
  205.0 1.6 collective-permute-done.36.i2
  208.2 10.0 %end_columns.1 = bf16[20,64,2048]{2,1,0:T(8,128)(2,1)} custom-call(s32[3]{0:T(128)} %pad_add_fusion.where_ref, bf16[4,48,1280]{2,1,0:T(8,128)(2,1)} %from_lines.3.i0, bf16[4,48,1280]{2,1,0:T(8,128)(2,1)} %copy-done.4, bf16[4,48,1280]{2,1,0:T(8,128)(2,1)} %copy-done.8, bf16[4,48,1280]{2,1,0:T(8,128)(2,1)} %copy-done.10, ...), custom_call_target="tpu_custom_call" | custom-call | bytes 30000000 | tf_op jit(solution)/shard_map/end_columns/pallas_call | solution.py:313
  (114 shorter events, 21.3 us)
Async XLA Ops:
  0.6 21.4 %copy-start = (bf16[20,20]{1,0:T(8,128)(2,1)S(1)}, bf16[20,20]{1,0:T(8,128)(2,1)}, u32[]{:S(2)}) copy-start(bf16[20,20]{1,0:T(8,128)(2,1)} %param.12) | copy-start | bytes 2404
  0.6 21.4 %copy-start.3 = (bf16[160,20]{1,0:T(8,128)(2,1)S(1)}, bf16[160,20]{1,0:T(8,128)(2,1)}, u32[]{:S(2)}) copy-start(bf16[160,20]{1,0:T(8,128)(2,1)} %constant.22.clone) | copy-start | bytes 19204
  0.7 21.4 %copy-start.11 = (bf16[160,160]{1,0:T(8,128)(2,1)S(1)}, bf16[160,160]{1,0:T(8,128)(2,1)}, u32[]{:S(2)}) copy-start(bf16[160,160]{1,0:T(8,128)(2,1)} %constant.25.clone) | copy-start | bytes 153604
  0.7 14.5 %collective-permute-start = (bf16[3,20,20,2,128]{4,3,2,1,0:T(2,128)(2,1)}, bf16[3,20,20,2,128]{4,3,2,1,0:T(2,128)(2,1)S(1)}, u32[]{:S(2)}, u32[]{:S(2)}) collective-permute-start(bf16[3,20,20,2,128]{4,3,2,1,0:T(2,128)(2,1)} %param.11), channel_id=1, source_target_pairs={{0,0},{8,32},{16,64},{24,96},{32,72},{40,104},{48,8},{56,40},{64,1... | collective-permute-start | bytes 1843208 | tf_op jit(solution)/shard_map/ppermute | solution.py:618
  15.2 28.5 %copy-start.1 = (bf16[3,20,20,2,128]{4,3,2,1,0:T(2,128)(2,1)}, bf16[3,20,20,2,128]{4,3,2,1,0:T(2,128)(2,1)S(1)}, u32[]{:S(2)}) copy-start(bf16[3,20,20,2,128]{4,3,2,1,0:T(2,128)(2,1)S(1)} %collective-permute-done) | copy-start | bytes 1843204
  15.2 3.4 %collective-permute-start.2 = (bf16[4,48,1280]{2,1,0:T(8,128)(2,1)}, bf16[4,48,1280]{2,1,0:T(8,128)(2,1)S(1)}, u32[]{:S(2)}, u32[]{:S(2)}) collective-permute-start(bf16[4,48,1280]{2,1,0:T(8,128)(2,1)} %get-tuple-element.49), channel_id=1, source_target_pairs={{0,8},{8,0},{16,24},{24,16},{1,9},{9,1},{17,25},{25,17},{2,10},{10... | collective-permute-start | bytes 1474568 | tf_op jit(solution)/shard_map/ppermute | solution.py:568
  15.3 20.7 %collective-permute-start.4 = (bf16[3,20,20,2,128]{4,3,2,1,0:T(2,128)(2,1)S(1)}, bf16[3,20,20,2,128]{4,3,2,1,0:T(2,128)(2,1)}, u32[]{:S(2)}, u32[]{:S(2)}) collective-permute-start(bf16[3,20,20,2,128]{4,3,2,1,0:T(2,128)(2,1)S(1)} %collective-permute-done), channel_id=1, source_target_pairs={{32,0},{64,32},{96,64},{0,96},{33,1},{65,33},{97,65},{1,97},{34,2}... | collective-permute-start | bytes 1843208 | tf_op jit(solution)/shard_map/ppermute | solution.py:587
  18.6 17.4 %collective-permute-start.5 = (bf16[3,20,20,2,128]{4,3,2,1,0:T(2,128)(2,1)S(1)}, bf16[3,20,20,2,128]{4,3,2,1,0:T(2,128)(2,1)}, u32[]{:S(2)}, u32[]{:S(2)}) collective-permute-start(bf16[3,20,20,2,128]{4,3,2,1,0:T(2,128)(2,1)S(1)} %collective-permute-done), channel_id=1, source_target_pairs={{96,0},{0,32},{32,64},{64,96},{97,1},{1,33},{33,65},{65,97},{98,2}... | collective-permute-start | bytes 1843208 | tf_op jit(solution)/shard_map/ppermute | solution.py:587
  19.8 12.8 %collective-permute-start.3 = (bf16[4,48,1280]{2,1,0:T(8,128)(2,1)S(1)}, bf16[4,48,1280]{2,1,0:T(8,128)(2,1)}, u32[]{:S(2)}, u32[]{:S(2)}) collective-permute-start(bf16[4,48,1280]{2,1,0:T(8,128)(2,1)S(1)} %add_convert_fusion.1), channel_id=1, source_target_pairs={{0,16},{8,24},{16,0},{24,8},{1,17},{9,25},{17,1},{25,9},{2,18},{10... | collective-permute-start | bytes 1474568 | tf_op jit(solution)/shard_map/ppermute | solution.py:568
  21.3 11.2 %collective-permute-start.1 = (bf16[4,48,1280]{2,1,0:T(8,128)(2,1)}, bf16[4,48,1280]{2,1,0:T(8,128)(2,1)}, u32[]{:S(2)}, u32[]{:S(2)}) collective-permute-start(bf16[4,48,1280]{2,1,0:T(8,128)(2,1)} %get-tuple-element.47), channel_id=1, source_target_pairs={{0,8},{8,0},{16,24},{24,16},{1,9},{9,1},{17,25},{25,17},{2,10},{10... | collective-permute-start | bytes 1474568 | tf_op jit(solution)/shard_map/ppermute | solution.py:568
  36.0 24.1 %all-to-all-start = ((bf16[8,48,1280]{2,1,0:T(8,128)(2,1)}), bf16[8,48,1280]{2,1,0:T(8,128)(2,1)}, u32[]{:S(2)}, u32[]{:S(2)}) async-start(bf16[8,48,1280]{2,1,0:T(8,128)(2,1)} %to_lines.2), calls=%async_computation | async-start | bytes 1966080 | tf_op jit(solution)/shard_map/all_to_all | solution.py:600
  43.7 15.6 %collective-permute-start.6 = (bf16[3,20,20,2,128]{4,3,2,1,0:T(2,128)(2,1)S(1)}, bf16[3,20,20,2,128]{4,3,2,1,0:T(2,128)(2,1)S(1)}, u32[]{:S(2)}, u32[]{:S(2)}) collective-permute-start(bf16[3,20,20,2,128]{4,3,2,1,0:T(2,128)(2,1)S(1)} %collective-permute-done), channel_id=1, source_target_pairs={{64,0},{96,32},{0,64},{32,96},{65,1},{97,33},{1,65},{33,97},{66,2}... | collective-permute-start | bytes 1843208 | tf_op jit(solution)/shard_map/ppermute | solution.py:587
  65.6 8.0 %collective-permute-start.7 = (bf16[48,1280]{1,0:T(8,128)(2,1)}, bf16[48,1280]{1,0:T(8,128)(2,1)S(1)}, u32[]{:S(2)}, u32[]{:S(2)}) collective-permute-start(bf16[48,1280]{1,0:T(8,128)(2,1)} %get-tuple-element.55.refs_0_), channel_id=1, source_target_pairs={{1,0},{0,1},{3,2},{2,3},{5,4},{4,5},{7,6},{6,7},{9,8},{8,9},{11,10... | collective-permute-start | bytes 368648 | tf_op jit(solution)/shard_map/ppermute | solution.py:592
  68.3 6.0 %collective-permute-start.10 = (bf16[48,1280]{1,0:T(8,128)(2,1)}, bf16[48,1280]{1,0:T(8,128)(2,1)S(1)}, u32[]{:S(2)}, u32[]{:S(2)}) collective-permute-start(bf16[48,1280]{1,0:T(8,128)(2,1)} %get-tuple-element.55.refs_0_), channel_id=1, source_target_pairs={{4,0},{5,1},{6,2},{7,3},{0,4},{1,5},{2,6},{3,7},{12,8},{13,9},{14,... | collective-permute-start | bytes 368648 | tf_op jit(solution)/shard_map/ppermute | solution.py:595
  71.0 6.5 %collective-permute-start.12 = (bf16[48,1280]{1,0:T(8,128)(2,1)}, bf16[48,1280]{1,0:T(8,128)(2,1)S(1)}, u32[]{:S(2)}, u32[]{:S(2)}) collective-permute-start(bf16[48,1280]{1,0:T(8,128)(2,1)} %get-tuple-element.55.refs_0_), channel_id=1, source_target_pairs={{6,0},{7,1},{0,2},{1,3},{2,4},{3,5},{4,6},{5,7},{14,8},{15,9},{8,1... | collective-permute-start | bytes 368648 | tf_op jit(solution)/shard_map/ppermute | solution.py:595
  71.2 7.2 %collective-permute-start.8 = (bf16[48,1280]{1,0:T(8,128)(2,1)}, bf16[48,1280]{1,0:T(8,128)(2,1)S(1)}, u32[]{:S(2)}, u32[]{:S(2)}) collective-permute-start(bf16[48,1280]{1,0:T(8,128)(2,1)} %get-tuple-element.55.refs_0_), channel_id=1, source_target_pairs={{2,0},{3,1},{4,2},{5,3},{6,4},{7,5},{0,6},{1,7},{10,8},{11,9},{12,... | collective-permute-start | bytes 368648 | tf_op jit(solution)/shard_map/ppermute | solution.py:595
  73.6 6.4 %collective-permute-start.11 = (bf16[48,1280]{1,0:T(8,128)(2,1)S(1)}, bf16[48,1280]{1,0:T(8,128)(2,1)S(1)}, u32[]{:S(2)}, u32[]{:S(2)}) collective-permute-start(bf16[48,1280]{1,0:T(8,128)(2,1)S(1)} %collective-permute-done.7.refs_1_), channel_id=1, source_target_pairs={{4,0},{5,1},{6,2},{7,3},{0,4},{1,5},{2,6},{3,7},{12,8},{13,9},{14,... | collective-permute-start | bytes 368648 | tf_op jit(solution)/shard_map/ppermute | solution.py:595
  73.7 7.4 %collective-permute-start.13 = (bf16[48,1280]{1,0:T(8,128)(2,1)S(1)}, bf16[48,1280]{1,0:T(8,128)(2,1)S(1)}, u32[]{:S(2)}, u32[]{:S(2)}) collective-permute-start(bf16[48,1280]{1,0:T(8,128)(2,1)S(1)} %collective-permute-done.7.refs_1_), channel_id=1, source_target_pairs={{6,0},{7,1},{0,2},{1,3},{2,4},{3,5},{4,6},{5,7},{14,8},{15,9},{8,1... | collective-permute-start | bytes 368648 | tf_op jit(solution)/shard_map/ppermute | solution.py:595
  74.3 7.8 %collective-permute-start.9 = (bf16[48,1280]{1,0:T(8,128)(2,1)S(1)}, bf16[48,1280]{1,0:T(8,128)(2,1)}, u32[]{:S(2)}, u32[]{:S(2)}) collective-permute-start(bf16[48,1280]{1,0:T(8,128)(2,1)S(1)} %collective-permute-done.7.refs_1_), channel_id=1, source_target_pairs={{2,0},{3,1},{4,2},{5,3},{6,4},{7,5},{0,6},{1,7},{10,8},{11,9},{12,... | collective-permute-start | bytes 368648 | tf_op jit(solution)/shard_map/ppermute | solution.py:595
  85.4 14.2 %collective-permute-start.14 = (bf16[4,48,1280]{2,1,0:T(8,128)(2,1)}, bf16[4,48,1280]{2,1,0:T(8,128)(2,1)S(1)}, u32[]{:S(2)}, u32[]{:S(2)}) collective-permute-start(bf16[4,48,1280]{2,1,0:T(8,128)(2,1)} %from_lines.2.i0), channel_id=1, source_target_pairs={{0,16},{8,24},{16,0},{24,8},{1,17},{9,25},{17,1},{25,9},{2,18},{10... | collective-permute-start | bytes 1474568 | tf_op jit(solution)/shard_map/ppermute | solution.py:568
  85.7 9.4 %collective-permute-start.15 = (bf16[120,128]{1,0:T(8,128)(2,1)}, bf16[120,128]{1,0:T(8,128)(2,1)S(1)}, u32[]{:S(2)}, u32[]{:S(2)}) collective-permute-start(bf16[120,128]{1,0:T(8,128)(2,1)} %get-tuple-element.56), channel_id=1, source_target_pairs={{0,0},{8,32},{16,64},{24,96},{32,8},{40,40},{48,72},{56,104},{64,1... | collective-permute-start | bytes 92168 | tf_op jit(solution)/shard_map/ppermute | solution.py:609
  91.5 6.1 %collective-permute-start.16 = (bf16[120,128]{1,0:T(8,128)(2,1)}, bf16[120,128]{1,0:T(8,128)(2,1)S(1)}, u32[]{:S(2)}, u32[]{:S(2)}) collective-permute-start(bf16[120,128]{1,0:T(8,128)(2,1)} %get-tuple-element.57), channel_id=1, source_target_pairs={{0,8},{8,40},{16,72},{24,104},{32,16},{40,48},{48,80},{56,112},{64... | collective-permute-start | bytes 92168 | tf_op jit(solution)/shard_map/ppermute | solution.py:609
  91.6 6.1 %collective-permute-start.17 = (bf16[120,128]{1,0:T(8,128)(2,1)}, bf16[120,128]{1,0:T(8,128)(2,1)S(1)}, u32[]{:S(2)}, u32[]{:S(2)}) collective-permute-start(bf16[120,128]{1,0:T(8,128)(2,1)} %get-tuple-element.58), channel_id=1, source_target_pairs={{0,16},{8,48},{16,80},{24,112},{32,24},{40,56},{48,88},{56,120},{6... | collective-permute-start | bytes 92168 | tf_op jit(solution)/shard_map/ppermute | solution.py:609
  94.3 5.4 %collective-permute-start.18 = (bf16[120,128]{1,0:T(8,128)(2,1)}, bf16[120,128]{1,0:T(8,128)(2,1)S(1)}, u32[]{:S(2)}, u32[]{:S(2)}) collective-permute-start(bf16[120,128]{1,0:T(8,128)(2,1)} %get-tuple-element.59), channel_id=1, source_target_pairs={{0,24},{8,56},{16,88},{24,120},{32,0},{40,32},{48,64},{56,96},{64,... | collective-permute-start | bytes 92168 | tf_op jit(solution)/shard_map/ppermute | solution.py:609
  95.1 72.9 %copy-start.25 = (bf16[120,128]{1,0:T(8,128)(2,1)}, bf16[120,128]{1,0:T(8,128)(2,1)S(1)}, u32[]{:S(2)}) copy-start(bf16[120,128]{1,0:T(8,128)(2,1)S(1)} %collective-permute-done.15.s0) | copy-start | bytes 92164
  95.1 5.8 %collective-permute-start.19 = (bf16[4,48,1280]{2,1,0:T(8,128)(2,1)}, bf16[4,48,1280]{2,1,0:T(8,128)(2,1)S(1)}, u32[]{:S(2)}, u32[]{:S(2)}) collective-permute-start(bf16[4,48,1280]{2,1,0:T(8,128)(2,1)} %from_lines.2.i0), channel_id=1, source_target_pairs={{0,8},{8,0},{16,24},{24,16},{1,9},{9,1},{17,25},{25,17},{2,10},{10... | collective-permute-start | bytes 1474568 | tf_op jit(solution)/shard_map/ppermute | solution.py:568
  97.7 70.4 %copy-start.26 = (bf16[120,128]{1,0:T(8,128)(2,1)}, bf16[120,128]{1,0:T(8,128)(2,1)S(1)}, u32[]{:S(2)}) copy-start(bf16[120,128]{1,0:T(8,128)(2,1)S(1)} %collective-permute-done.16.s1) | copy-start | bytes 92164
  97.7 70.4 %copy-start.27 = (bf16[120,128]{1,0:T(8,128)(2,1)}, bf16[120,128]{1,0:T(8,128)(2,1)S(1)}, u32[]{:S(2)}) copy-start(bf16[120,128]{1,0:T(8,128)(2,1)S(1)} %collective-permute-done.17.s2) | copy-start | bytes 92164
  99.7 68.4 %copy-start.28 = (bf16[120,128]{1,0:T(8,128)(2,1)}, bf16[120,128]{1,0:T(8,128)(2,1)S(1)}, u32[]{:S(2)}) copy-start(bf16[120,128]{1,0:T(8,128)(2,1)S(1)} %collective-permute-done.18.s3) | copy-start | bytes 92164
  99.7 2.7 %collective-permute-start.20 = (bf16[4,48,1280]{2,1,0:T(8,128)(2,1)S(1)}, bf16[4,48,1280]{2,1,0:T(8,128)(2,1)S(1)}, u32[]{:S(2)}, u32[]{:S(2)}) collective-permute-start(bf16[4,48,1280]{2,1,0:T(8,128)(2,1)S(1)} %collective-permute-done.14.i1), channel_id=1, source_target_pairs={{0,8},{8,0},{16,24},{24,16},{1,9},{9,1},{17,25},{25,17},{2,10},{10... | collective-permute-start | bytes 1474568 | tf_op jit(solution)/shard_map/ppermute | solution.py:568
  120.4 2.2 collective-permute-start.22
  123.7 13.7 %collective-permute-start.23 = (bf16[4,48,1280]{2,1,0:T(8,128)(2,1)S(1)}, bf16[4,48,1280]{2,1,0:T(8,128)(2,1)S(1)}, u32[]{:S(2)}, u32[]{:S(2)}) collective-permute-start(bf16[4,48,1280]{2,1,0:T(8,128)(2,1)S(1)} %add_convert_fusion), channel_id=1, source_target_pairs={{0,16},{8,24},{16,0},{24,8},{1,17},{9,25},{17,1},{25,9},{2,18},{10... | collective-permute-start | bytes 1474568 | tf_op jit(solution)/shard_map/ppermute | solution.py:568
  126.1 11.3 %collective-permute-start.21 = (bf16[4,48,1280]{2,1,0:T(8,128)(2,1)}, bf16[4,48,1280]{2,1,0:T(8,128)(2,1)}, u32[]{:S(2)}, u32[]{:S(2)}) collective-permute-start(bf16[4,48,1280]{2,1,0:T(8,128)(2,1)} %get-tuple-element.64), channel_id=1, source_target_pairs={{0,8},{8,0},{16,24},{24,16},{1,9},{9,1},{17,25},{25,17},{2,10},{10... | collective-permute-start | bytes 1474568 | tf_op jit(solution)/shard_map/ppermute | solution.py:568
  168.0 5.5 %collective-permute-start.24 = (bf16[48,1280]{1,0:T(8,128)(2,1)}, bf16[48,1280]{1,0:T(8,128)(2,1)S(1)}, u32[]{:S(2)}, u32[]{:S(2)}) collective-permute-start(bf16[48,1280]{1,0:T(8,128)(2,1)} %get-tuple-element.69.refs_0_), channel_id=1, source_target_pairs={{1,0},{0,1},{3,2},{2,3},{5,4},{4,5},{7,6},{6,7},{9,8},{8,9},{11,10... | collective-permute-start | bytes 368648 | tf_op jit(solution)/shard_map/ppermute | solution.py:592
  168.5 6.3 %collective-permute-start.25 = (bf16[48,1280]{1,0:T(8,128)(2,1)}, bf16[48,1280]{1,0:T(8,128)(2,1)S(1)}, u32[]{:S(2)}, u32[]{:S(2)}) collective-permute-start(bf16[48,1280]{1,0:T(8,128)(2,1)} %get-tuple-element.69.refs_0_), channel_id=1, source_target_pairs={{2,0},{3,1},{4,2},{5,3},{6,4},{7,5},{0,6},{1,7},{10,8},{11,9},{12,... | collective-permute-start | bytes 368648 | tf_op jit(solution)/shard_map/ppermute | solution.py:595
  169.9 5.7 %collective-permute-start.27 = (bf16[48,1280]{1,0:T(8,128)(2,1)}, bf16[48,1280]{1,0:T(8,128)(2,1)S(1)}, u32[]{:S(2)}, u32[]{:S(2)}) collective-permute-start(bf16[48,1280]{1,0:T(8,128)(2,1)} %get-tuple-element.69.refs_0_), channel_id=1, source_target_pairs={{4,0},{5,1},{6,2},{7,3},{0,4},{1,5},{2,6},{3,7},{12,8},{13,9},{14,... | collective-permute-start | bytes 368648 | tf_op jit(solution)/shard_map/ppermute | solution.py:595
  171.1 5.6 %collective-permute-start.29 = (bf16[48,1280]{1,0:T(8,128)(2,1)}, bf16[48,1280]{1,0:T(8,128)(2,1)S(1)}, u32[]{:S(2)}, u32[]{:S(2)}) collective-permute-start(bf16[48,1280]{1,0:T(8,128)(2,1)} %get-tuple-element.69.refs_0_), channel_id=1, source_target_pairs={{6,0},{7,1},{0,2},{1,3},{2,4},{3,5},{4,6},{5,7},{14,8},{15,9},{8,1... | collective-permute-start | bytes 368648 | tf_op jit(solution)/shard_map/ppermute | solution.py:595
  173.6 8.7 %copy-start.12 = (bf16[48,1280]{1,0:T(8,128)(2,1)}, bf16[48,1280]{1,0:T(8,128)(2,1)S(1)}, u32[]{:S(2)}) copy-start(bf16[48,1280]{1,0:T(8,128)(2,1)S(1)} %collective-permute-done.24.refs_1_) | copy-start | bytes 368644
  173.6 4.8 %collective-permute-start.26 = (bf16[48,1280]{1,0:T(8,128)(2,1)S(1)}, bf16[48,1280]{1,0:T(8,128)(2,1)S(1)}, u32[]{:S(2)}, u32[]{:S(2)}) collective-permute-start(bf16[48,1280]{1,0:T(8,128)(2,1)S(1)} %collective-permute-done.24.refs_1_), channel_id=1, source_target_pairs={{2,0},{3,1},{4,2},{5,3},{6,4},{7,5},{0,6},{1,7},{10,8},{11,9},{12,... | collective-permute-start | bytes 368648 | tf_op jit(solution)/shard_map/ppermute | solution.py:595
  174.1 6.5 %collective-permute-start.28 = (bf16[48,1280]{1,0:T(8,128)(2,1)S(1)}, bf16[48,1280]{1,0:T(8,128)(2,1)S(1)}, u32[]{:S(2)}, u32[]{:S(2)}) collective-permute-start(bf16[48,1280]{1,0:T(8,128)(2,1)S(1)} %collective-permute-done.24.refs_1_), channel_id=1, source_target_pairs={{4,0},{5,1},{6,2},{7,3},{0,4},{1,5},{2,6},{3,7},{12,8},{13,9},{14,... | collective-permute-start | bytes 368648 | tf_op jit(solution)/shard_map/ppermute | solution.py:595
  174.8 7.5 %collective-permute-start.30 = (bf16[48,1280]{1,0:T(8,128)(2,1)S(1)}, bf16[48,1280]{1,0:T(8,128)(2,1)S(1)}, u32[]{:S(2)}, u32[]{:S(2)}) collective-permute-start(bf16[48,1280]{1,0:T(8,128)(2,1)S(1)} %collective-permute-done.24.refs_1_), channel_id=1, source_target_pairs={{6,0},{7,1},{0,2},{1,3},{2,4},{3,5},{4,6},{5,7},{14,8},{15,9},{8,1... | collective-permute-start | bytes 368648 | tf_op jit(solution)/shard_map/ppermute | solution.py:595
  186.3 18.6 %collective-permute-start.31 = (bf16[4,48,1280]{2,1,0:T(8,128)(2,1)}, bf16[4,48,1280]{2,1,0:T(8,128)(2,1)S(1)}, u32[]{:S(2)}, u32[]{:S(2)}) collective-permute-start(bf16[4,48,1280]{2,1,0:T(8,128)(2,1)} %from_lines.3.i0), channel_id=1, source_target_pairs={{0,16},{8,24},{16,0},{24,8},{1,17},{9,25},{17,1},{25,9},{2,18},{10... | collective-permute-start | bytes 1474568 | tf_op jit(solution)/shard_map/ppermute | solution.py:568
  186.9 8.3 %collective-permute-start.32 = (bf16[120,128]{1,0:T(8,128)(2,1)}, bf16[120,128]{1,0:T(8,128)(2,1)S(1)}, u32[]{:S(2)}, u32[]{:S(2)}) collective-permute-start(bf16[120,128]{1,0:T(8,128)(2,1)} %get-tuple-element.74), channel_id=1, source_target_pairs={{0,0},{8,32},{16,64},{24,96},{32,8},{40,40},{48,72},{56,104},{64,1... | collective-permute-start | bytes 92168 | tf_op jit(solution)/shard_map/ppermute | solution.py:609
  191.7 3.5 %collective-permute-start.33 = (bf16[120,128]{1,0:T(8,128)(2,1)}, bf16[120,128]{1,0:T(8,128)(2,1)S(1)}, u32[]{:S(2)}, u32[]{:S(2)}) collective-permute-start(bf16[120,128]{1,0:T(8,128)(2,1)} %get-tuple-element.75), channel_id=1, source_target_pairs={{0,8},{8,40},{16,72},{24,104},{32,16},{40,48},{48,80},{56,112},{64... | collective-permute-start | bytes 92168 | tf_op jit(solution)/shard_map/ppermute | solution.py:609
  191.8 4.8 %collective-permute-start.34 = (bf16[120,128]{1,0:T(8,128)(2,1)}, bf16[120,128]{1,0:T(8,128)(2,1)S(1)}, u32[]{:S(2)}, u32[]{:S(2)}) collective-permute-start(bf16[120,128]{1,0:T(8,128)(2,1)} %get-tuple-element.76), channel_id=1, source_target_pairs={{0,16},{8,48},{16,80},{24,112},{32,24},{40,56},{48,88},{56,120},{6... | collective-permute-start | bytes 92168 | tf_op jit(solution)/shard_map/ppermute | solution.py:609
  194.4 5.4 %collective-permute-start.35 = (bf16[120,128]{1,0:T(8,128)(2,1)}, bf16[120,128]{1,0:T(8,128)(2,1)S(1)}, u32[]{:S(2)}, u32[]{:S(2)}) collective-permute-start(bf16[120,128]{1,0:T(8,128)(2,1)} %get-tuple-element.77), channel_id=1, source_target_pairs={{0,24},{8,56},{16,88},{24,120},{32,0},{40,32},{48,64},{56,96},{64,... | collective-permute-start | bytes 92168 | tf_op jit(solution)/shard_map/ppermute | solution.py:609
  203.5 3.1 %collective-permute-start.36 = (bf16[4,48,1280]{2,1,0:T(8,128)(2,1)}, bf16[4,48,1280]{2,1,0:T(8,128)(2,1)S(1)}, u32[]{:S(2)}, u32[]{:S(2)}) collective-permute-start(bf16[4,48,1280]{2,1,0:T(8,128)(2,1)} %from_lines.3.i0), channel_id=1, source_target_pairs={{0,8},{8,0},{16,24},{24,16},{1,9},{9,1},{17,25},{25,17},{2,10},{10... | collective-permute-start | bytes 1474568 | tf_op jit(solution)/shard_map/ppermute | solution.py:568
  204.9 2.2 %collective-permute-start.37 = (bf16[4,48,1280]{2,1,0:T(8,128)(2,1)S(1)}, bf16[4,48,1280]{2,1,0:T(8,128)(2,1)S(1)}, u32[]{:S(2)}, u32[]{:S(2)}) collective-permute-start(bf16[4,48,1280]{2,1,0:T(8,128)(2,1)S(1)} %collective-permute-done.31.i1), channel_id=1, source_target_pairs={{0,8},{8,0},{16,24},{24,16},{1,9},{9,1},{17,25},{25,17},{2,10},{10... | collective-permute-start | bytes 1474568 | tf_op jit(solution)/shard_map/ppermute | solution.py:568
  (24 other events, 77.3 us)

commit v6 on v5

--- a/solution.py
+++ b/solution.py
@@ -326,27 +326,34 @@
     )(where, *coeffs_in, bypass, jnp.asarray(DEPTH), jnp.asarray(WIDTH))
 
 
-def line_kernel(where_ref, a_ref, b_ref, c_ref, table_ref, out_ref):
+def order_table(where_ref, table_ref, order_ref):
+    for k in range(GY):
+        owner = ((where_ref[2] + (k & 6)) & 7) ^ (k & 1)
+        start = pl.multiple_of(owner * 48, 16)
+        order_ref[48 * k : 48 * (k + 1)] = table_ref[0, pl.ds(start, 48), :]
+
+
+def line_kernel(where_ref, a_ref, b_ref, c_ref, table_ref, o0, o1, o2, o3, order_ref):
+    order_table(where_ref, table_ref, order_ref)
     for j in range(GROUPS):
         lanes = slice(GL * j, GL * (j + 1))
         parts = [ref[:, :, lanes].astype(F32) for ref in (a_ref, b_ref, c_ref)]
         rows = (parts[0] + parts[1] + parts[2]).astype(BF).reshape(STEPS * ROWS, GL)
-        out_ref[:, :, lanes] = dot(table_ref[0], rows).astype(BF).reshape(GY, 48, GL)
+        lines = dot(order_ref[...], rows).astype(BF)
+        for k, out_ref in enumerate((o0, o1, o2, o3)):
+            out_ref[:, :, lanes] = lines[96 * k : 96 * (k + 1)].reshape(2, 48, GL)
 
 
 def unline_kernel(where_ref, *refs):
     *modes_refs, table_ref, out_ref, order_ref = refs
-    for k in range(GY):
-        owner = ((where_ref[2] + (k & 6)) & 7) ^ (k & 1)
-        start = pl.multiple_of(owner * 48, 16)
-        order_ref[48 * k : 48 * (k + 1)] = table_ref[0, pl.ds(start, 48), :]
+    order_table(where_ref, table_ref, order_ref)
     for j in range(GROUPS):
         lanes = slice(GL * j, GL * (j + 1))
         rows = jnp.concatenate([ref[:, lanes] for ref in modes_refs], axis=0)
         out_ref[:, :, lanes] = dot(order_ref[...], rows, 0, 0).astype(BF).reshape(STEPS, ROWS, GL)
 
 
-def line_call(kernel, name, where, ins, out_shape, scratch=()):
+def line_call(kernel, name, where, ins, out_shapes):
     whole = pl.BlockSpec(ins[0].shape, lambda i, w: (0,) * ins[0].ndim)
     table = pl.BlockSpec((1, GY * 48, STEPS * ROWS), lambda i, w: (w[2], 0, 0))
     return pl.pallas_call(
@@ -355,10 +362,10 @@
             num_scalar_prefetch=1,
             grid=(1,),
             in_specs=[whole] * len(ins) + [table],
-            out_specs=pl.BlockSpec(out_shape.shape, lambda i, w: (0, 0, 0)),
-            scratch_shapes=list(scratch),
+            out_specs=[pl.BlockSpec(out.shape, lambda i, w: (0, 0, 0)) for out in out_shapes],
+            scratch_shapes=[pltpu.VMEM((GY * 48, STEPS * ROWS), BF)],
         ),
-        out_shape=out_shape,
+        out_shape=out_shapes,
         compiler_params=ALONE,
         cost_estimate=cost(3),
         name=name,
@@ -366,13 +373,12 @@
 
 
 def to_lines(where, *parts):
-    out = jax.ShapeDtypeStruct((GY, 48, WIDE), BF)
-    return line_call(line_kernel, "to_lines", where, parts, out)
+    out = jax.ShapeDtypeStruct((2, 48, WIDE), BF)
+    return line_call(line_kernel, "to_lines", where, parts, [out] * 4)
 
 
 def from_lines(where, modes):
-    order = pltpu.VMEM((GY * 48, STEPS * ROWS), BF)
-    return line_call(unline_kernel, "from_lines", where, modes, COEFFS, [order])
+    return line_call(unline_kernel, "from_lines", where, modes, [COEFFS])[0]
 
 
 UNROLL = 4
@@ -385,10 +391,11 @@
     return lax.broadcasted_iota(jnp.int32, (SETS, 2 * HALF), 1) < HALF
 
 
-def gather_modes(arrived_ref, sum_ref, modes_ref, scale=None):
-    total = arrived_ref[0].astype(F32)
-    for i in range(1, GY):
-        total = total + arrived_ref[i].astype(F32)
+def gather_modes(arrived, sum_ref, modes_ref, scale=None):
+    *sets, last_ref = arrived
+    total = last_ref[...].astype(F32)
+    for ref in sets:
+        total = total + ref[0].astype(F32)
     sum_ref[...] = total.astype(BF).astype(F32)
     low = low_lanes()
     for j in range(CH // 2):
@@ -449,14 +456,15 @@
 
 
 def mix_kernel(
-    where_ref, arrived_ref, w0, w1, w2, w3, out_ref, u0, u1, u2, u3, sum_ref, in_ref, mix_ref
+    where_ref, a0, a1, a2, a3, a4, w0, w1, w2, w3, out_ref, u0, u1, u2, u3,
+    sum_ref, in_ref, mix_ref,
 ):
     step = pl.program_id(0)
 
     @pl.when(step == 0)
     def _():
-        gather_modes(arrived_ref, sum_ref, in_ref)
-        hand_out(where_ref, in_ref, (u0, u1, u2, u3))
+        gather_modes((a0, a1, a2, a3, a4), sum_ref, in_ref)
+        hand_out(where_ref, in_ref, [ref.at[0] for ref in (u0, u1, u2, u3)])
 
     for k, weight_ref in enumerate((w0, w1, w2, w3)):
         base = set_row(where_ref, k)
@@ -480,14 +488,17 @@
 
 
 def back_kernel(
-    where_ref, arrived_ref, w0, w1, w2, w3, out_ref, u0, u1, u2, u3, sum_ref, in_ref, mix_ref
+    where_ref, a0, a1, a2, a3, a4, w0, w1, w2, w3, s0, s1, s2, s3, out_ref, u0, u1, u2, u3,
+    sum_ref, in_ref, mix_ref,
 ):
     step = pl.program_id(0)
 
     @pl.when(step == 0)
     def _():
-        gather_modes(arrived_ref, sum_ref, in_ref, fold_scale(where_ref))
-        hand_out(where_ref, in_ref, (u0, u1, u2, u3))
+        gather_modes((a0, a1, a2, a3, a4), sum_ref, in_ref, fold_scale(where_ref))
+        hand_out(where_ref, in_ref, [ref.at[1] for ref in (u0, u1, u2, u3)])
+        for spec_ref, ref in zip((s0, s1, s2, s3), (u0, u1, u2, u3)):
+            ref[0] = spec_ref[0]
 
     for k, weight_ref in enumerate((w0, w1, w2, w3)):
         base = set_row(where_ref, k)
@@ -509,16 +520,22 @@
         spread_modes(mix_ref, sum_ref, out_ref)
 
 
-def mode_call(kernel, name, where, arrived, weights):
-    chunk = pl.BlockSpec((KB * PAIR, 2 * HALF), lambda i, w: (0, 0))
+def mode_call(kernel, name, where, arrived, weights, spectra=()):
+    sets = 2 if spectra else 1
+
+    def chunk(n):
+        return pl.BlockSpec((n, KB * PAIR, 2 * HALF), lambda i, w: (0, 0, 0))
+
     return pl.pallas_call(
         kernel,
         grid_spec=pltpu.PrefetchScalarGridSpec(
             num_scalar_prefetch=1,
             grid=(KB,),
-            in_specs=[pl.BlockSpec((GY, 48, WIDE), lambda i, w: (0, 0, 0))]
-            + [pl.BlockSpec((1, CH, PAIR, 2 * HALF), lambda i, w: (i, 0, 0, 0))] * 4,
-            out_specs=[pl.BlockSpec((48, WIDE), lambda i, w: (0, 0))] + [chunk] * 4,
+            in_specs=[pl.BlockSpec((1, 48, WIDE), lambda i, w: (0, 0, 0))] * 4
+            + [pl.BlockSpec((48, WIDE), lambda i, w: (0, 0))]
+            + [pl.BlockSpec((1, CH, PAIR, 2 * HALF), lambda i, w: (i, 0, 0, 0))] * 4
+            + [chunk(1)] * len(spectra),
+            out_specs=[pl.BlockSpec((48, WIDE), lambda i, w: (0, 0))] + [chunk(sets)] * 4,
             scratch_shapes=[
                 pltpu.VMEM((48, WIDE), F32),
                 pltpu.VMEM((SETS * PAIR, 2 * HALF), F32),
@@ -526,21 +543,22 @@
             ],
         ),
         out_shape=[jax.ShapeDtypeStruct((48, WIDE), BF)]
-        + [jax.ShapeDtypeStruct((KB * PAIR, 2 * HALF), BF)] * 4,
+        + [jax.ShapeDtypeStruct((sets, KB * PAIR, 2 * HALF), BF)] * 4,
         compiler_params=ALONE,
         cost_estimate=cost(5),
         name=name,
-    )(where, arrived, *weights)
-
-
-def outer_kernel(s0, s1, s2, s3, g0, g1, g2, g3, out_ref, spec_ref):
-    for k, ref in enumerate((s0, s1, s2, s3)):
-        spec_ref[k] = ref[...].astype(F32)
+    )(where, *arrived, *weights, *spectra)
+
+
+def outer_kernel(p0, p1, p2, p3, out_ref, spec_ref):
+    pairs = (p0, p1, p2, p3)
+    for k, ref in enumerate(pairs):
+        spec_ref[k] = ref[0].astype(F32)
     for i in range(KB):
         grads = []
         others = []
-        for ref in (g0, g1, g2, g3):
-            grad = ref[...].astype(F32)[i * PAIR : (i + 1) * PAIR]
+        for ref in pairs:
+            grad = ref[1].astype(F32)[i * PAIR : (i + 1) * PAIR]
             grads.append(grad)
             others.append(-turned(grad))
 
@@ -554,14 +572,14 @@
             out_ref[i, c] = total
 
 
-def outer_sum(spectra, grads):
+def outer_sum(pairs):
     return pl.pallas_call(
         outer_kernel,
         out_shape=jax.ShapeDtypeStruct((KB, CH, PAIR, 2 * HALF), F32),
         scratch_shapes=[pltpu.VMEM((DP, KB * PAIR, 2 * HALF), F32)],
         cost_estimate=cost(3),
         name="outer_sum",
-    )(*spectra, *grads)
+    )(*pairs)
 
 
 def swap(values, bit):
@@ -575,10 +593,9 @@
     return (own, swap(near, 1), arrived), beside
 
 
-def share_slabs(own, *waiting):
-    far = swap(own, 2)
-    far, *waiting = lax.optimization_barrier((far, *waiting))
-    return own, far, swap(own, 1), swap(far, 1), *waiting
+def share_slabs(own, *beside):
+    far, *beside = lax.optimization_barrier((swap(own, 2), *beside))
+    return own, far, swap(own, 1), swap(far, 1), *beside
 
 
 def gather_weights(weight):
@@ -596,8 +613,15 @@
     return held
 
 
-def exchange_lines(parts):
-    return lax.all_to_all(parts, "gy", split_axis=0, concat_axis=0, tiled=True)
+def sum_lines(sets, *waiting):
+    moved = [sets[0]]
+    for k in range(1, 4):
+        pairs = [(g, (g + 2 * k) % GY) for g in range(GY)]
+        moved.append(lax.ppermute(sets[k], "gy", pairs))
+    other = sum(part[1].astype(F32) for part in moved).astype(BF)
+    other, *waiting = lax.optimization_barrier((other, *waiting))
+    other = lax.ppermute(other, "gy", [(g ^ 1, g) for g in range(GY)])
+    return (*moved, other), waiting
 
 
 def to_owners(chunks):
@@ -626,20 +650,20 @@
     *pieces, weight = lax.optimization_barrier((*start_columns(where, values), weight))
     parts, bypass = start_slabs(pieces, bypass_columns(values, mixer_of(bypass_weight)))
     weights = gather_weights(weight)
-    lines, weights[1], weights[3] = lax.optimization_barrier(
-        (to_lines(where, *parts), weights[1], weights[3])
+    *sets, weights[1], weights[3] = lax.optimization_barrier(
+        (*to_lines(where, *parts), weights[1], weights[3])
     )
-    arrived = exchange_lines(lines)
+    arrived, (weights[2],) = sum_lines(sets, weights[2])
     modes, *spectra = mode_call(mix_kernel, "mix_modes", where, arrived, weights)
-    own = from_lines(where, gather_lines(modes))
-    *coeffs, s0, s1, s2, s3 = share_slabs(own, *to_owners(spectra))
+    coeffs = share_slabs(from_lines(where, gather_lines(modes)))
     activation, grad, *pieces = middle_columns(where, bias, coeffs, bypass, cotangent[0])
     parts, bypass = start_slabs(pieces, bypass_columns(grad, mixer_of(bypass_weight.T)))
-    arrived = exchange_lines(to_lines(where, *parts))
-    modes, *grads = mode_call(back_kernel, "back_modes", where, arrived, weights)
+    arrived, _ = sum_lines(to_lines(where, *parts))
+    modes, *pairs = mode_call(back_kernel, "back_modes", where, arrived, weights, spectra)
     own = from_lines(where, gather_lines(modes))
-    *coeffs, weight_grad = share_slabs(own, outer_sum((s0, s1, s2, s3), to_owners(grads)))
-    field_grad = end_columns(where, coeffs, bypass)
+    own, far, near, across, *pairs = share_slabs(own, *to_owners(pairs))
+    across, weight_grad = lax.optimization_barrier((across, outer_sum(pairs)))
+    field_grad = end_columns(where, (own, far, near, across), bypass)
     return (
         activation[None],
         field_grad[None],

time: 220 us -> 226 us (1.027)
  blocking collectives: 20.4 us -> 0 us
  waiting for transfers between devices: 47 us -> 64.2 us
  starting transfers between devices: 63.5 us -> 68.8 us
    ppermute x0 -> x8, waiting for transfers between devices: none -> 24.1 us  [the longest x6 18 us: sum_lines(): moved.append(lax.ppermute(sets[k], 'gy', pairs))]
    all_to_all x1 -> x0, blocking collectives: 20.4 us -> none  [exchange_lines(): return lax.all_to_all(parts, 'gy', split_axis=0, concat_axis=0, tiled=True)]
    ppermute x0 -> x8, starting transfers between devices: none -> 12.8 us  [the longest x6 8.41 us: sum_lines(): moved.append(lax.ppermute(sets[k], 'gy', pairs))]
    ppermute x8 -> x4, starting transfers between devices: 17.7 us -> 8.56 us  [to_owners(): moved.append(lax.ppermute(chunk, ('dp', 'gx'), pairs))]
    ppermute x3, waiting for transfers between devices: 12.9 us -> 4.1 us  [gather_weights(): lax.ppermute(weight, 'dp', [((a + k) % DP, a) for a in range(DP)])]
    all_to_all x1 -> x0, starting transfers between devices: 7.67 us -> none  [exchange_lines(): return lax.all_to_all(parts, 'gy', split_axis=0, concat_axis=0, tiled=True)]
    ppermute x12, starting transfers between devices: 12.1 us -> 18.1 us  [swap(): return lax.ppermute(values, 'gx', [(i, i ^ bit) for i in range(GX)])]
    ppermute x12, waiting for transfers between devices: 12.9 us -> 16.1 us  [gather_lines(): held += [lax.ppermute(part, 'gy', pairs) for part in held[:2]]]
  transfers between devices with their start and end apart: 39 -> 42, of which waited for: 21 -> 25; matrix products, arithmetic and copies ran while one was open for 2% -> 2% of each run, Pallas kernels for 13% -> 13%
where the time goes in v6:
time: 226 us; the launch traced here: 224 us
  Pallas kernels  76.5 us (34%)
  starting transfers between devices  68.8 us (30%)
  waiting for transfers between devices  64.2 us (28%)
  local copies, waits for them, and re-layouts  6.72 us (3%)
  other arithmetic  5.12 us (2%)
    ppermute x12, starting transfers between devices, swap(): return lax.ppermute(values, 'gx', [(i, i ^ bit) for i in range(GX)])  18.1 us
    ppermute x6, waiting for transfers between devices, sum_lines(): moved.append(lax.ppermute(sets[k], 'gy', pairs))  18 us
    pallas_call x1, Pallas kernels, middle_columns(): pl.pallas_call(middle_kernel, grid_spec=pltpu.PrefetchScalarGridSpec(num_...  17.3 us
    ppermute x12, waiting for transfers between devices, gather_lines(): held += [lax.ppermute(part, 'gy', pairs) for part in held[:2]]  16.1 us
    ppermute x12, waiting for transfers between devices, swap(): return lax.ppermute(values, 'gx', [(i, i ^ bit) for i in range(GX)])  14.3 us
    ppermute x12, starting transfers between devices, gather_lines(): held += [lax.ppermute(part, 'gy', pairs) for part in held[:2]]  14.3 us
    pallas_call x4, Pallas kernels, line_call(): pl.pallas_call(kernel, grid_spec=pltpu.PrefetchScalarGridSpec(num_scalar_...  13.3 us
    pallas_call x2, Pallas kernels, bypass_columns(): pl.pallas_call(bypass_kernel, grid=(STEPS,), in_specs=[columns, pl.BlockS...  12.4 us
  transfers between devices with their start and end apart: 42, of which 25 were waited for; matrix products, arithmetic and copies ran while one was open for 2% of the time, Pallas kernels for 13%

profile of v6, /device:TPU:1, one launch (start us, length us, event | category | flops | bytes accessed | tf_op | source)
XLA Modules:
  0.0 224.0 jit_solution(2015742908860947917)
XLA Ops:
  0.7 4.6 %collective-permute-start = (bf16[3,20,20,2,128]{4,3,2,1,0:T(2,128)(2,1)}, bf16[3,20,20,2,128]{4,3,2,1,0:T(2,128)(2,1)S(1)}, u32[]{:S(2)}, u32[]{:S(2)}) collective-permute-start(bf16[3,20,20,2,128]{4,3,2,1,0:T(2,128)(2,1)} %param.11), channel_id=1, source_target_pairs={{0,0},{8,32},{16,64},{24,96},{32,72},{40,104},{48,8},{56,40},{64,1... | collective-permute-start | bytes 1843208 | tf_op jit(solution)/shard_map/ppermute | solution.py:642
  6.0 9.2 %start_columns.1 = (bf16[4,48,1280]{2,1,0:T(8,128)(2,1)}, bf16[4,48,1280]{2,1,0:T(8,128)(2,1)}, bf16[4,48,1280]{2,1,0:T(8,128)(2,1)}, bf16[4,48,1280]{2,1,0:T(8,128)(2,1)}) custom-call(s32[3]{0:T(128)} %pad_add_fusion.where_ref, bf16[20,64,2048]{2,1,0:T(8,128)(2,1)} %bitcast.22, bf16[4,24,512]{2,1,0:T(8,128)(2,1)} %constant.23.clone.strip_ref, ...), custom_call_target="tpu_custom_call" | custom-call | bytes 24000000 | tf_op jit(solution)/shard_map/start_columns/pallas_call | solution.py:275
  15.3 3.3 %collective-permute-start.4 = (bf16[3,20,20,2,128]{4,3,2,1,0:T(2,128)(2,1)S(1)}, bf16[3,20,20,2,128]{4,3,2,1,0:T(2,128)(2,1)}, u32[]{:S(2)}, u32[]{:S(2)}) collective-permute-start(bf16[3,20,20,2,128]{4,3,2,1,0:T(2,128)(2,1)S(1)} %collective-permute-done), channel_id=1, source_target_pairs={{32,0},{64,32},{96,64},{0,96},{33,1},{65,33},{97,65},{1,97},{34,2}... | collective-permute-start | bytes 1843208 | tf_op jit(solution)/shard_map/ppermute | solution.py:604
  19.7 1.6 collective-permute-start.3
  22.9 6.1 %bypass_columns.2.bypass_ref = bf16[20,64,2048]{2,1,0:T(8,128)(2,1)} custom-call(bf16[20,64,2048]{2,1,0:T(8,128)(2,1)} %bitcast.23, bf16[160,160]{1,0:T(8,128)(2,1)} %fusion.mixer_ref), custom_call_target="tpu_custom_call" | custom-call | bytes 18000000 | tf_op jit(solution)/shard_map/bypass_columns/pallas_call | solution.py:261
  29.1 3.5 %collective-permute-done.3.c_ref = bf16[4,48,1280]{2,1,0:T(8,128)(2,1)} collective-permute-done((bf16[4,48,1280]{2,1,0:T(8,128)(2,1)S(1)}, bf16[4,48,1280]{2,1,0:T(8,128)(2,1)}, u32[]{:S(2)}, u32[]{:S(2)}) %collective-permute-start.3) | collective-permute-done | bytes 491552 | tf_op jit(solution)/shard_map/ppermute | solution.py:586
  32.6 3.4 %to_lines.2 = (bf16[2,48,1280]{2,1,0:T(8,128)(2,1)}, bf16[2,48,1280]{2,1,0:T(8,128)(2,1)}, bf16[2,48,1280]{2,1,0:T(8,128)(2,1)}, bf16[2,48,1280]{2,1,0:T(8,128)(2,1)}) custom-call(s32[3]{0:T(128)} %pad_add_fusion.where_ref, bf16[4,48,1280]{2,1,0:T(8,128)(2,1)} %get-tuple-element.59.a_ref, bf16[4,48,1280]{2,1,0:T(8,128)(2,1)} %collective-permute-done.1.b_ref, ...), custom_call_target="tpu_custom_call" | custom-call | bytes 9000000 | tf_op jit(solution)/shard_map/to_lines/pallas_call | solution.py:359
  35.9 1.7 collective-permute-start.6
  37.7 3.3 %collective-permute-start.7 = (bf16[2,48,1280]{2,1,0:T(8,128)(2,1)}, bf16[2,48,1280]{2,1,0:T(8,128)(2,1)S(1)}, u32[]{:S(2)}, u32[]{:S(2)}) collective-permute-start(bf16[2,48,1280]{2,1,0:T(8,128)(2,1)} %get-tuple-element.71), channel_id=1, source_target_pairs={{0,4},{1,5},{2,6},{3,7},{4,0},{5,1},{6,2},{7,3},{8,12},{9,13},{10,... | collective-permute-start | bytes 737288 | tf_op jit(solution)/shard_map/ppermute | solution.py:620
  41.7 2.6 %collective-permute-start.9 = (bf16[3,20,20,2,128]{4,3,2,1,0:T(2,128)(2,1)S(1)}, bf16[3,20,20,2,128]{4,3,2,1,0:T(2,128)(2,1)S(1)}, u32[]{:S(2)}, u32[]{:S(2)}) collective-permute-start(bf16[3,20,20,2,128]{4,3,2,1,0:T(2,128)(2,1)S(1)} %collective-permute-done), channel_id=1, source_target_pairs={{64,0},{96,32},{0,64},{32,96},{65,1},{97,33},{1,65},{33,97},{66,2}... | collective-permute-start | bytes 1843208 | tf_op jit(solution)/shard_map/ppermute | solution.py:604
  45.3 6.1 %collective-permute-done.7.a2 = bf16[2,48,1280]{2,1,0:T(8,128)(2,1)S(1)} collective-permute-done((bf16[2,48,1280]{2,1,0:T(8,128)(2,1)}, bf16[2,48,1280]{2,1,0:T(8,128)(2,1)S(1)}, u32[]{:S(2)}, u32[]{:S(2)}) %collective-permute-start.7) | collective-permute-done | bytes 245792 | tf_op jit(solution)/shard_map/ppermute | solution.py:620
  52.5 4.1 %collective-permute-done.9 = bf16[3,20,20,2,128]{4,3,2,1,0:T(2,128)(2,1)S(1)} collective-permute-done((bf16[3,20,20,2,128]{4,3,2,1,0:T(2,128)(2,1)S(1)}, bf16[3,20,20,2,128]{4,3,2,1,0:T(2,128)(2,1)S(1)}, u32[]{:S(2)}, u32[]{:S(2)}) %collective-permute-start.9) | collective-permute-done | bytes 614432 | tf_op jit(solution)/shard_map/ppermute | solution.py:604
  57.5 2.9 %collective-permute-start.10 = (bf16[48,1280]{1,0:T(8,128)(2,1)S(1)}, bf16[48,1280]{1,0:T(8,128)(2,1)S(1)}, u32[]{:S(2)}, u32[]{:S(2)}) collective-permute-start(bf16[48,1280]{1,0:T(8,128)(2,1)S(1)} %fusion.2), channel_id=1, source_target_pairs={{1,0},{0,1},{3,2},{2,3},{5,4},{4,5},{7,6},{6,7},{9,8},{8,9},{11,10... | collective-permute-start | bytes 368648 | tf_op jit(solution)/shard_map/ppermute | solution.py:623
  60.4 2.3 %collective-permute-done.10.a4 = bf16[48,1280]{1,0:T(8,128)(2,1)S(1)} collective-permute-done((bf16[48,1280]{1,0:T(8,128)(2,1)S(1)}, bf16[48,1280]{1,0:T(8,128)(2,1)S(1)}, u32[]{:S(2)}, u32[]{:S(2)}) %collective-permute-start.10) | collective-permute-done | bytes 122912 | tf_op jit(solution)/shard_map/ppermute | solution.py:623
  63.4 5.3 %mix_modes.1 = (bf16[48,1280]{1,0:T(8,128)(2,1)}, bf16[1,120,128]{2,1,0:T(8,128)(2,1)}, bf16[1,120,128]{2,1,0:T(8,128)(2,1)}, bf16[1,120,128]{2,1,0:T(8,128)(2,1)}, bf16[1,120,128]{2,1,0:T(8,128)(2,1)}) custom-call(s32[3]{0:T(128)} %pad_add_fusion.where_ref, bf16[2,48,1280]{2,1,0:T(8,128)(2,1)} %get-tuple-element.69.a0, bf16[2,48,1280]{2,1,0:T(8,128)(2,1)} %copy-done.7, ...), custom_call_target="tpu_custom_call" | custom-call | bytes 15000000 | tf_op jit(solution)/shard_map/mix_modes/pallas_call | solution.py:529
  68.7 3.0 %collective-permute-start.11 = (bf16[48,1280]{1,0:T(8,128)(2,1)}, bf16[48,1280]{1,0:T(8,128)(2,1)S(1)}, u32[]{:S(2)}, u32[]{:S(2)}) collective-permute-start(bf16[48,1280]{1,0:T(8,128)(2,1)} %get-tuple-element.77.refs_0_), channel_id=1, source_target_pairs={{1,0},{0,1},{3,2},{2,3},{5,4},{4,5},{7,6},{6,7},{9,8},{8,9},{11,10... | collective-permute-start | bytes 368648 | tf_op jit(solution)/shard_map/ppermute | solution.py:609
  72.0 2.2 collective-permute-start.14
  74.3 2.7 %collective-permute-start.13 = (bf16[48,1280]{1,0:T(8,128)(2,1)S(1)}, bf16[48,1280]{1,0:T(8,128)(2,1)S(1)}, u32[]{:S(2)}, u32[]{:S(2)}) collective-permute-start(bf16[48,1280]{1,0:T(8,128)(2,1)S(1)} %collective-permute-done.11.refs_1_), channel_id=1, source_target_pairs={{2,0},{3,1},{4,2},{5,3},{6,4},{7,5},{0,6},{1,7},{10,8},{11,9},{12,... | collective-permute-start | bytes 368648 | tf_op jit(solution)/shard_map/ppermute | solution.py:612
  77.8 1.6 collective-permute-done.16.refs_6_
  79.4 3.0 %collective-permute-done.13.refs_3_ = bf16[48,1280]{1,0:T(8,128)(2,1)S(1)} collective-permute-done((bf16[48,1280]{1,0:T(8,128)(2,1)S(1)}, bf16[48,1280]{1,0:T(8,128)(2,1)S(1)}, u32[]{:S(2)}, u32[]{:S(2)}) %collective-permute-start.13) | collective-permute-done | bytes 122912 | tf_op jit(solution)/shard_map/ppermute | solution.py:612
  83.8 2.1 collective-permute-done.17.refs_7_
  86.6 3.3 %from_lines.2.i0 = bf16[4,48,1280]{2,1,0:T(8,128)(2,1)} custom-call(s32[3]{0:T(128)} %pad_add_fusion.where_ref, bf16[48,1280]{1,0:T(8,128)(2,1)} %get-tuple-element.77.refs_0_, bf16[48,1280]{1,0:T(8,128)(2,1)} %copy-done.20, bf16[48,1280]{1,0:T(8,128)(2,1)} %copy-done.22, bf16[48,1280]{1,0:T(8,128)(2,1)} %copy-done.28, bf16[48,1280]{1,0:T(8,128)(2,1)} %copy-done.24, ...), custom_call_target="tpu_custom_call" | custom-call | bytes 9000000 | tf_op jit(solution)/shard_map/from_lines/pallas_call | solution.py:359
  90.7 4.2 %collective-permute-start.19 = (bf16[4,48,1280]{2,1,0:T(8,128)(2,1)}, bf16[4,48,1280]{2,1,0:T(8,128)(2,1)S(1)}, u32[]{:S(2)}, u32[]{:S(2)}) collective-permute-start(bf16[4,48,1280]{2,1,0:T(8,128)(2,1)} %from_lines.2.i0), channel_id=1, source_target_pairs={{0,8},{8,0},{16,24},{24,16},{1,9},{9,1},{17,25},{25,17},{2,10},{10... | collective-permute-start | bytes 1474568 | tf_op jit(solution)/shard_map/ppermute | solution.py:586
  94.9 3.8 %collective-permute-done.18.i1 = bf16[4,48,1280]{2,1,0:T(8,128)(2,1)S(1)} collective-permute-done((bf16[4,48,1280]{2,1,0:T(8,128)(2,1)}, bf16[4,48,1280]{2,1,0:T(8,128)(2,1)S(1)}, u32[]{:S(2)}, u32[]{:S(2)}) %collective-permute-start.18) | collective-permute-done | bytes 491552 | tf_op jit(solution)/shard_map/ppermute | solution.py:586
  98.7 5.0 %collective-permute-start.20 = (bf16[4,48,1280]{2,1,0:T(8,128)(2,1)S(1)}, bf16[4,48,1280]{2,1,0:T(8,128)(2,1)S(1)}, u32[]{:S(2)}, u32[]{:S(2)}) collective-permute-start(bf16[4,48,1280]{2,1,0:T(8,128)(2,1)S(1)} %collective-permute-done.18.i1), channel_id=1, source_target_pairs={{0,8},{8,0},{16,24},{24,16},{1,9},{9,1},{17,25},{25,17},{2,10},{10... | collective-permute-start | bytes 1474568 | tf_op jit(solution)/shard_map/ppermute | solution.py:586
  106.0 17.3 %middle_columns.1 = (bf16[20,64,2048]{2,1,0:T(8,128)(2,1)}, bf16[20,64,2048]{2,1,0:T(8,128)(2,1)}, bf16[4,48,1280]{2,1,0:T(8,128)(2,1)}, bf16[4,48,1280]{2,1,0:T...) custom-call(s32[3]{0:T(128)} %pad_add_fusion.where_ref, f32[20]{0:T(128)} %bias_ref.1, ...), custom_call_target="tpu_custom_call" | custom-call | bytes 57000000 | tf_op jit(solution)/shard_map/middle_columns/pallas_call | solution.py:293
  123.7 1.7 collective-permute-done.22
  129.1 6.2 %bypass_columns.3.bypass_ref = bf16[20,64,2048]{2,1,0:T(8,128)(2,1)} custom-call(bf16[20,64,2048]{2,1,0:T(8,128)(2,1)} %get-tuple-element.84.source_ref, bf16[160,160]{1,0:T(8,128)(2,1)} %fusion.1.mixer_ref), custom_call_target="tpu_custom_call" | custom-call | bytes 18000000 | tf_op jit(solution)/shard_map/bypass_columns/pallas_call | solution.py:261
  135.3 3.8 %collective-permute-done.23.c_ref = bf16[4,48,1280]{2,1,0:T(8,128)(2,1)S(1)} collective-permute-done((bf16[4,48,1280]{2,1,0:T(8,128)(2,1)S(1)}, bf16[4,48,1280]{2,1,0:T(8,128)(2,1)S(1)}, u32[]{:S(2)}, u32[]{:S(2)}) %collective-permute-start.23) | collective-permute-done | bytes 491552 | tf_op jit(solution)/shard_map/ppermute | solution.py:586
  139.9 3.4 %to_lines.3 = (bf16[2,48,1280]{2,1,0:T(8,128)(2,1)}, bf16[2,48,1280]{2,1,0:T(8,128)(2,1)}, bf16[2,48,1280]{2,1,0:T(8,128)(2,1)}, bf16[2,48,1280]{2,1,0:T(8,128)(2,1)}) custom-call(s32[3]{0:T(128)} %pad_add_fusion.where_ref, bf16[4,48,1280]{2,1,0:T(8,128)(2,1)} %get-tuple-element.80.a_ref, bf16[4,48,1280]{2,1,0:T(8,128)(2,1)} %collective-permute-done.21.b_ref, ...), custom_call_target="tpu_custom_call" | custom-call | bytes 9000000 | tf_op jit(solution)/shard_map/to_lines/pallas_call | solution.py:359
  143.3 2.0 collective-permute-start.25
  145.9 5.7 %collective-permute-done.24.a1 = bf16[2,48,1280]{2,1,0:T(8,128)(2,1)S(1)} collective-permute-done((bf16[2,48,1280]{2,1,0:T(8,128)(2,1)}, bf16[2,48,1280]{2,1,0:T(8,128)(2,1)S(1)}, u32[]{:S(2)}, u32[]{:S(2)}) %collective-permute-start.24) | collective-permute-done | bytes 245792 | tf_op jit(solution)/shard_map/ppermute | solution.py:620
  151.6 3.9 %collective-permute-done.25.a2 = bf16[2,48,1280]{2,1,0:T(8,128)(2,1)S(1)} collective-permute-done((bf16[2,48,1280]{2,1,0:T(8,128)(2,1)}, bf16[2,48,1280]{2,1,0:T(8,128)(2,1)S(1)}, u32[]{:S(2)}, u32[]{:S(2)}) %collective-permute-start.25) | collective-permute-done | bytes 245792 | tf_op jit(solution)/shard_map/ppermute | solution.py:620
  157.9 1.5 collective-permute-start.27
  159.4 3.8 %collective-permute-done.27.a4 = bf16[48,1280]{1,0:T(8,128)(2,1)S(1)} collective-permute-done((bf16[48,1280]{1,0:T(8,128)(2,1)S(1)}, bf16[48,1280]{1,0:T(8,128)(2,1)S(1)}, u32[]{:S(2)}, u32[]{:S(2)}) %collective-permute-start.27) | collective-permute-done | bytes 122912 | tf_op jit(solution)/shard_map/ppermute | solution.py:623
  163.9 5.9 %back_modes.1 = (bf16[48,1280]{1,0:T(8,128)(2,1)}, bf16[2,120,128]{2,1,0:T(8,128)(2,1)}, bf16[2,120,128]{2,1,0:T(8,128)(2,1)}, bf16[2,120,128]{2,1,0:T(8,128)(2,1)}, bf16[2,120,128]{2,1,0:T(8,128)(2,1)}) custom-call(s32[3]{0:T(128)} %pad_add_fusion.where_ref, bf16[2,48,1280]{2,1,0:T(8,128)(2,1)} %get-tuple-element.86.a0, bf16[2,48,1280]{2,1,0:T(8,128)(2,1)} %copy-done.4, ...), custom_call_target="tpu_custom_call" | custom-call | bytes 15000000 | tf_op jit(solution)/shard_map/back_modes/pallas_call | solution.py:529
  171.2 4.0 %collective-permute-start.29 = (bf16[48,1280]{1,0:T(8,128)(2,1)}, bf16[48,1280]{1,0:T(8,128)(2,1)S(1)}, u32[]{:S(2)}, u32[]{:S(2)}) collective-permute-start(bf16[48,1280]{1,0:T(8,128)(2,1)} %get-tuple-element.94.refs_0_), channel_id=1, source_target_pairs={{2,0},{3,1},{4,2},{5,3},{6,4},{7,5},{0,6},{1,7},{10,8},{11,9},{12,... | collective-permute-start | bytes 368648 | tf_op jit(solution)/shard_map/ppermute | solution.py:612
  175.8 2.8 %collective-permute-start.30 = (bf16[48,1280]{1,0:T(8,128)(2,1)S(1)}, bf16[48,1280]{1,0:T(8,128)(2,1)S(1)}, u32[]{:S(2)}, u32[]{:S(2)}) collective-permute-start(bf16[48,1280]{1,0:T(8,128)(2,1)S(1)} %collective-permute-done.28.refs_1_), channel_id=1, source_target_pairs={{2,0},{3,1},{4,2},{5,3},{6,4},{7,5},{0,6},{1,7},{10,8},{11,9},{12,... | collective-permute-start | bytes 368648 | tf_op jit(solution)/shard_map/ppermute | solution.py:612
  182.1 2.1 collective-permute-done.30.refs_3_
  185.1 2.5 %collective-permute-done.34.refs_7_ = bf16[48,1280]{1,0:T(8,128)(2,1)S(1)} collective-permute-done((bf16[48,1280]{1,0:T(8,128)(2,1)S(1)}, bf16[48,1280]{1,0:T(8,128)(2,1)S(1)}, u32[]{:S(2)}, u32[]{:S(2)}) %collective-permute-start.34) | collective-permute-done | bytes 122912 | tf_op jit(solution)/shard_map/ppermute | solution.py:612
  188.2 3.3 %from_lines.3.i0 = bf16[4,48,1280]{2,1,0:T(8,128)(2,1)} custom-call(s32[3]{0:T(128)} %pad_add_fusion.where_ref, bf16[48,1280]{1,0:T(8,128)(2,1)} %get-tuple-element.94.refs_0_, bf16[48,1280]{1,0:T(8,128)(2,1)} %copy-done.19, bf16[48,1280]{1,0:T(8,128)(2,1)} %copy-done.21, bf16[48,1280]{1,0:T(8,128)(2,1)} %copy-done.27, bf16[48,1280]{1,0:T(8,128)(2,1)} %copy-done.23, ...), custom_call_target="tpu_custom_call" | custom-call | bytes 9000000 | tf_op jit(solution)/shard_map/from_lines/pallas_call | solution.py:359
  192.2 5.2 %collective-permute-start.36 = (bf16[2,120,128]{2,1,0:T(8,128)(2,1)}, bf16[2,120,128]{2,1,0:T(8,128)(2,1)S(1)}, u32[]{:S(2)}, u32[]{:S(2)}) collective-permute-start(bf16[2,120,128]{2,1,0:T(8,128)(2,1)} %get-tuple-element.95), channel_id=1, source_target_pairs={{0,0},{8,32},{16,64},{24,96},{32,8},{40,40},{48,72},{56,104},{64,1... | collective-permute-start | bytes 184328 | tf_op jit(solution)/shard_map/ppermute | solution.py:633
  197.4 2.5 %collective-permute-start.38 = (bf16[2,120,128]{2,1,0:T(8,128)(2,1)}, bf16[2,120,128]{2,1,0:T(8,128)(2,1)S(1)}, u32[]{:S(2)}, u32[]{:S(2)}) collective-permute-start(bf16[2,120,128]{2,1,0:T(8,128)(2,1)} %get-tuple-element.97), channel_id=1, source_target_pairs={{0,16},{8,48},{16,80},{24,112},{32,24},{40,56},{48,88},{56,120},{6... | collective-permute-start | bytes 184328 | tf_op jit(solution)/shard_map/ppermute | solution.py:633
  200.8 2.5 %collective-permute-done.38.p2 = bf16[2,120,128]{2,1,0:T(8,128)(2,1)S(1)} collective-permute-done((bf16[2,120,128]{2,1,0:T(8,128)(2,1)}, bf16[2,120,128]{2,1,0:T(8,128)(2,1)S(1)}, u32[]{:S(2)}, u32[]{:S(2)}) %collective-permute-start.38) | collective-permute-done | bytes 61472 | tf_op jit(solution)/shard_map/ppermute | solution.py:633
  203.3 3.0 %collective-permute-done.39.p3 = bf16[2,120,128]{2,1,0:T(8,128)(2,1)S(1)} collective-permute-done((bf16[2,120,128]{2,1,0:T(8,128)(2,1)}, bf16[2,120,128]{2,1,0:T(8,128)(2,1)S(1)}, u32[]{:S(2)}, u32[]{:S(2)}) %collective-permute-start.39) | collective-permute-done | bytes 61472 | tf_op jit(solution)/shard_map/ppermute | solution.py:633
  206.3 2.9 %collective-permute-start.41 = (bf16[4,48,1280]{2,1,0:T(8,128)(2,1)S(1)}, bf16[4,48,1280]{2,1,0:T(8,128)(2,1)S(1)}, u32[]{:S(2)}, u32[]{:S(2)}) collective-permute-start(bf16[4,48,1280]{2,1,0:T(8,128)(2,1)S(1)} %collective-permute-done.35.i1), channel_id=1, source_target_pairs={{0,8},{8,0},{16,24},{24,16},{1,9},{9,1},{17,25},{25,17},{2,10},{10... | collective-permute-start | bytes 1474568 | tf_op jit(solution)/shard_map/ppermute | solution.py:586
  209.3 3.1 %outer_sum.1 = f32[3,20,40,128]{3,2,1,0:T(8,128)} custom-call(bf16[2,120,128]{2,1,0:T(8,128)(2,1)} %copy-done.35, bf16[2,120,128]{2,1,0:T(8,128)(2,1)} %copy-done.36, bf16[2,120,128]{2,1,0:T(8,128)(2,1)} %copy-done.37, bf16[2,120,128]{2,1,0:T(8,128)(2,1)} %copy-done.38), custom_call_target="tpu_custom_call" | custom-call | bytes 9000000 | tf_op jit(solution)/shard_map/outer_sum/pallas_call | solution.py:576
  214.0 10.0 %end_columns.1 = bf16[20,64,2048]{2,1,0:T(8,128)(2,1)} custom-call(s32[3]{0:T(128)} %pad_add_fusion.where_ref, bf16[4,48,1280]{2,1,0:T(8,128)(2,1)} %from_lines.3.i0, bf16[4,48,1280]{2,1,0:T(8,128)(2,1)} %copy-done.11, bf16[4,48,1280]{2,1,0:T(8,128)(2,1)} %copy-done.15, bf16[4,48,1280]{2,1,0:T(8,128)(2,1)} %copy-done.14, ...), custom_call_target="tpu_custom_call" | custom-call | bytes 30000000 | tf_op jit(solution)/shard_map/end_columns/pallas_call | solution.py:313
  (133 shorter events, 33.0 us)
Async XLA Ops:
  0.6 21.4 %copy-start = (bf16[20,20]{1,0:T(8,128)(2,1)S(1)}, bf16[20,20]{1,0:T(8,128)(2,1)}, u32[]{:S(2)}) copy-start(bf16[20,20]{1,0:T(8,128)(2,1)} %param.12) | copy-start | bytes 2404
  0.6 21.4 %copy-start.3 = (bf16[160,20]{1,0:T(8,128)(2,1)S(1)}, bf16[160,20]{1,0:T(8,128)(2,1)}, u32[]{:S(2)}) copy-start(bf16[160,20]{1,0:T(8,128)(2,1)} %constant.22.clone) | copy-start | bytes 19204
  0.7 21.4 %copy-start.17 = (bf16[160,160]{1,0:T(8,128)(2,1)S(1)}, bf16[160,160]{1,0:T(8,128)(2,1)}, u32[]{:S(2)}) copy-start(bf16[160,160]{1,0:T(8,128)(2,1)} %constant.25.clone) | copy-start | bytes 153604
  0.7 14.5 %collective-permute-start = (bf16[3,20,20,2,128]{4,3,2,1,0:T(2,128)(2,1)}, bf16[3,20,20,2,128]{4,3,2,1,0:T(2,128)(2,1)S(1)}, u32[]{:S(2)}, u32[]{:S(2)}) collective-permute-start(bf16[3,20,20,2,128]{4,3,2,1,0:T(2,128)(2,1)} %param.11), channel_id=1, source_target_pairs={{0,0},{8,32},{16,64},{24,96},{32,72},{40,104},{48,8},{56,40},{64,1... | collective-permute-start | bytes 1843208 | tf_op jit(solution)/shard_map/ppermute | solution.py:642
  15.2 26.5 %copy-start.1 = (bf16[3,20,20,2,128]{4,3,2,1,0:T(2,128)(2,1)}, bf16[3,20,20,2,128]{4,3,2,1,0:T(2,128)(2,1)S(1)}, u32[]{:S(2)}) copy-start(bf16[3,20,20,2,128]{4,3,2,1,0:T(2,128)(2,1)S(1)} %collective-permute-done) | copy-start | bytes 1843204
  15.2 3.4 %collective-permute-start.2 = (bf16[4,48,1280]{2,1,0:T(8,128)(2,1)}, bf16[4,48,1280]{2,1,0:T(8,128)(2,1)S(1)}, u32[]{:S(2)}, u32[]{:S(2)}) collective-permute-start(bf16[4,48,1280]{2,1,0:T(8,128)(2,1)} %get-tuple-element.62), channel_id=1, source_target_pairs={{0,8},{8,0},{16,24},{24,16},{1,9},{9,1},{17,25},{25,17},{2,10},{10... | collective-permute-start | bytes 1474568 | tf_op jit(solution)/shard_map/ppermute | solution.py:586
  15.3 20.6 %collective-permute-start.4 = (bf16[3,20,20,2,128]{4,3,2,1,0:T(2,128)(2,1)S(1)}, bf16[3,20,20,2,128]{4,3,2,1,0:T(2,128)(2,1)}, u32[]{:S(2)}, u32[]{:S(2)}) collective-permute-start(bf16[3,20,20,2,128]{4,3,2,1,0:T(2,128)(2,1)S(1)} %collective-permute-done), channel_id=1, source_target_pairs={{32,0},{64,32},{96,64},{0,96},{33,1},{65,33},{97,65},{1,97},{34,2}... | collective-permute-start | bytes 1843208 | tf_op jit(solution)/shard_map/ppermute | solution.py:604
  18.6 17.4 %collective-permute-start.5 = (bf16[3,20,20,2,128]{4,3,2,1,0:T(2,128)(2,1)S(1)}, bf16[3,20,20,2,128]{4,3,2,1,0:T(2,128)(2,1)}, u32[]{:S(2)}, u32[]{:S(2)}) collective-permute-start(bf16[3,20,20,2,128]{4,3,2,1,0:T(2,128)(2,1)S(1)} %collective-permute-done), channel_id=1, source_target_pairs={{96,0},{0,32},{32,64},{64,96},{97,1},{1,33},{33,65},{65,97},{98,2}... | collective-permute-start | bytes 1843208 | tf_op jit(solution)/shard_map/ppermute | solution.py:604
  19.7 12.8 %collective-permute-start.3 = (bf16[4,48,1280]{2,1,0:T(8,128)(2,1)S(1)}, bf16[4,48,1280]{2,1,0:T(8,128)(2,1)}, u32[]{:S(2)}, u32[]{:S(2)}) collective-permute-start(bf16[4,48,1280]{2,1,0:T(8,128)(2,1)S(1)} %add_convert_fusion.1), channel_id=1, source_target_pairs={{0,16},{8,24},{16,0},{24,8},{1,17},{9,25},{17,1},{25,9},{2,18},{10... | collective-permute-start | bytes 1474568 | tf_op jit(solution)/shard_map/ppermute | solution.py:586
  21.3 11.2 %collective-permute-start.1 = (bf16[4,48,1280]{2,1,0:T(8,128)(2,1)}, bf16[4,48,1280]{2,1,0:T(8,128)(2,1)}, u32[]{:S(2)}, u32[]{:S(2)}) collective-permute-start(bf16[4,48,1280]{2,1,0:T(8,128)(2,1)} %get-tuple-element.60), channel_id=1, source_target_pairs={{0,8},{8,0},{16,24},{24,16},{1,9},{9,1},{17,25},{25,17},{2,10},{10... | collective-permute-start | bytes 1474568 | tf_op jit(solution)/shard_map/ppermute | solution.py:586
  35.9 9.3 %collective-permute-start.6 = (bf16[2,48,1280]{2,1,0:T(8,128)(2,1)}, bf16[2,48,1280]{2,1,0:T(8,128)(2,1)S(1)}, u32[]{:S(2)}, u32[]{:S(2)}) collective-permute-start(bf16[2,48,1280]{2,1,0:T(8,128)(2,1)} %get-tuple-element.70), channel_id=1, source_target_pairs={{0,2},{1,3},{2,4},{3,5},{4,6},{5,7},{6,0},{7,1},{8,10},{9,11},{10,... | collective-permute-start | bytes 737288 | tf_op jit(solution)/shard_map/ppermute | solution.py:620
  37.7 13.7 %collective-permute-start.7 = (bf16[2,48,1280]{2,1,0:T(8,128)(2,1)}, bf16[2,48,1280]{2,1,0:T(8,128)(2,1)S(1)}, u32[]{:S(2)}, u32[]{:S(2)}) collective-permute-start(bf16[2,48,1280]{2,1,0:T(8,128)(2,1)} %get-tuple-element.71), channel_id=1, source_target_pairs={{0,4},{1,5},{2,6},{3,7},{4,0},{5,1},{6,2},{7,3},{8,12},{9,13},{10,... | collective-permute-start | bytes 737288 | tf_op jit(solution)/shard_map/ppermute | solution.py:620
  41.0 10.5 %collective-permute-start.8 = (bf16[2,48,1280]{2,1,0:T(8,128)(2,1)}, bf16[2,48,1280]{2,1,0:T(8,128)(2,1)S(1)}, u32[]{:S(2)}, u32[]{:S(2)}) collective-permute-start(bf16[2,48,1280]{2,1,0:T(8,128)(2,1)} %get-tuple-element.72), channel_id=1, source_target_pairs={{0,6},{1,7},{2,0},{3,1},{4,2},{5,3},{6,4},{7,5},{8,14},{9,15},{10,... | collective-permute-start | bytes 737288 | tf_op jit(solution)/shard_map/ppermute | solution.py:620
  41.7 15.0 %collective-permute-start.9 = (bf16[3,20,20,2,128]{4,3,2,1,0:T(2,128)(2,1)S(1)}, bf16[3,20,20,2,128]{4,3,2,1,0:T(2,128)(2,1)S(1)}, u32[]{:S(2)}, u32[]{:S(2)}) collective-permute-start(bf16[3,20,20,2,128]{4,3,2,1,0:T(2,128)(2,1)S(1)} %collective-permute-done), channel_id=1, source_target_pairs={{64,0},{96,32},{0,64},{32,96},{65,1},{97,33},{1,65},{33,97},{66,2}... | collective-permute-start | bytes 1843208 | tf_op jit(solution)/shard_map/ppermute | solution.py:604
  45.3 17.5 %copy-start.7 = (bf16[2,48,1280]{2,1,0:T(8,128)(2,1)}, bf16[2,48,1280]{2,1,0:T(8,128)(2,1)S(1)}, u32[]{:S(2)}) copy-start(bf16[2,48,1280]{2,1,0:T(8,128)(2,1)S(1)} %collective-permute-done.6.a1) | copy-start | bytes 737284
  57.5 5.2 %collective-permute-start.10 = (bf16[48,1280]{1,0:T(8,128)(2,1)S(1)}, bf16[48,1280]{1,0:T(8,128)(2,1)S(1)}, u32[]{:S(2)}, u32[]{:S(2)}) collective-permute-start(bf16[48,1280]{1,0:T(8,128)(2,1)S(1)} %fusion.2), channel_id=1, source_target_pairs={{1,0},{0,1},{3,2},{2,3},{5,4},{4,5},{7,6},{6,7},{9,8},{8,9},{11,10... | collective-permute-start | bytes 368648 | tf_op jit(solution)/shard_map/ppermute | solution.py:623
  68.7 5.5 %collective-permute-start.11 = (bf16[48,1280]{1,0:T(8,128)(2,1)}, bf16[48,1280]{1,0:T(8,128)(2,1)S(1)}, u32[]{:S(2)}, u32[]{:S(2)}) collective-permute-start(bf16[48,1280]{1,0:T(8,128)(2,1)} %get-tuple-element.77.refs_0_), channel_id=1, source_target_pairs={{1,0},{0,1},{3,2},{2,3},{5,4},{4,5},{7,6},{6,7},{9,8},{8,9},{11,10... | collective-permute-start | bytes 368648 | tf_op jit(solution)/shard_map/ppermute | solution.py:609
  71.7 5.2 %collective-permute-start.12 = (bf16[48,1280]{1,0:T(8,128)(2,1)}, bf16[48,1280]{1,0:T(8,128)(2,1)S(1)}, u32[]{:S(2)}, u32[]{:S(2)}) collective-permute-start(bf16[48,1280]{1,0:T(8,128)(2,1)} %get-tuple-element.77.refs_0_), channel_id=1, source_target_pairs={{2,0},{3,1},{4,2},{5,3},{6,4},{7,5},{0,6},{1,7},{10,8},{11,9},{12,... | collective-permute-start | bytes 368648 | tf_op jit(solution)/shard_map/ppermute | solution.py:612
  72.0 5.7 %collective-permute-start.14 = (bf16[48,1280]{1,0:T(8,128)(2,1)}, bf16[48,1280]{1,0:T(8,128)(2,1)S(1)}, u32[]{:S(2)}, u32[]{:S(2)}) collective-permute-start(bf16[48,1280]{1,0:T(8,128)(2,1)} %get-tuple-element.77.refs_0_), channel_id=1, source_target_pairs={{4,0},{5,1},{6,2},{7,3},{0,4},{1,5},{2,6},{3,7},{12,8},{13,9},{14,... | collective-permute-start | bytes 368648 | tf_op jit(solution)/shard_map/ppermute | solution.py:612
  74.2 5.2 %collective-permute-start.16 = (bf16[48,1280]{1,0:T(8,128)(2,1)}, bf16[48,1280]{1,0:T(8,128)(2,1)S(1)}, u32[]{:S(2)}, u32[]{:S(2)}) collective-permute-start(bf16[48,1280]{1,0:T(8,128)(2,1)} %get-tuple-element.77.refs_0_), channel_id=1, source_target_pairs={{6,0},{7,1},{0,2},{1,3},{2,4},{3,5},{4,6},{5,7},{14,8},{15,9},{8,1... | collective-permute-start | bytes 368648 | tf_op jit(solution)/shard_map/ppermute | solution.py:612
  74.3 8.2 %collective-permute-start.13 = (bf16[48,1280]{1,0:T(8,128)(2,1)S(1)}, bf16[48,1280]{1,0:T(8,128)(2,1)S(1)}, u32[]{:S(2)}, u32[]{:S(2)}) collective-permute-start(bf16[48,1280]{1,0:T(8,128)(2,1)S(1)} %collective-permute-done.11.refs_1_), channel_id=1, source_target_pairs={{2,0},{3,1},{4,2},{5,3},{6,4},{7,5},{0,6},{1,7},{10,8},{11,9},{12,... | collective-permute-start | bytes 368648 | tf_op jit(solution)/shard_map/ppermute | solution.py:612
  76.9 6.9 %collective-permute-start.15 = (bf16[48,1280]{1,0:T(8,128)(2,1)S(1)}, bf16[48,1280]{1,0:T(8,128)(2,1)S(1)}, u32[]{:S(2)}, u32[]{:S(2)}) collective-permute-start(bf16[48,1280]{1,0:T(8,128)(2,1)S(1)} %collective-permute-done.11.refs_1_), channel_id=1, source_target_pairs={{4,0},{5,1},{6,2},{7,3},{0,4},{1,5},{2,6},{3,7},{12,8},{13,9},{14,... | collective-permute-start | bytes 368648 | tf_op jit(solution)/shard_map/ppermute | solution.py:612
  76.9 9.0 %collective-permute-start.17 = (bf16[48,1280]{1,0:T(8,128)(2,1)S(1)}, bf16[48,1280]{1,0:T(8,128)(2,1)S(1)}, u32[]{:S(2)}, u32[]{:S(2)}) collective-permute-start(bf16[48,1280]{1,0:T(8,128)(2,1)S(1)} %collective-permute-done.11.refs_1_), channel_id=1, source_target_pairs={{6,0},{7,1},{0,2},{1,3},{2,4},{3,5},{4,6},{5,7},{14,8},{15,9},{8,1... | collective-permute-start | bytes 368648 | tf_op jit(solution)/shard_map/ppermute | solution.py:612
  89.9 8.8 %collective-permute-start.18 = (bf16[4,48,1280]{2,1,0:T(8,128)(2,1)}, bf16[4,48,1280]{2,1,0:T(8,128)(2,1)S(1)}, u32[]{:S(2)}, u32[]{:S(2)}) collective-permute-start(bf16[4,48,1280]{2,1,0:T(8,128)(2,1)} %from_lines.2.i0), channel_id=1, source_target_pairs={{0,16},{8,24},{16,0},{24,8},{1,17},{9,25},{17,1},{25,9},{2,18},{10... | collective-permute-start | bytes 1474568 | tf_op jit(solution)/shard_map/ppermute | solution.py:586
  90.7 13.0 %collective-permute-start.19 = (bf16[4,48,1280]{2,1,0:T(8,128)(2,1)}, bf16[4,48,1280]{2,1,0:T(8,128)(2,1)S(1)}, u32[]{:S(2)}, u32[]{:S(2)}) collective-permute-start(bf16[4,48,1280]{2,1,0:T(8,128)(2,1)} %from_lines.2.i0), channel_id=1, source_target_pairs={{0,8},{8,0},{16,24},{24,16},{1,9},{9,1},{17,25},{25,17},{2,10},{10... | collective-permute-start | bytes 1474568 | tf_op jit(solution)/shard_map/ppermute | solution.py:586
  98.7 6.5 %collective-permute-start.20 = (bf16[4,48,1280]{2,1,0:T(8,128)(2,1)S(1)}, bf16[4,48,1280]{2,1,0:T(8,128)(2,1)S(1)}, u32[]{:S(2)}, u32[]{:S(2)}) collective-permute-start(bf16[4,48,1280]{2,1,0:T(8,128)(2,1)S(1)} %collective-permute-done.18.i1), channel_id=1, source_target_pairs={{0,8},{8,0},{16,24},{24,16},{1,9},{9,1},{17,25},{25,17},{2,10},{10... | collective-permute-start | bytes 1474568 | tf_op jit(solution)/shard_map/ppermute | solution.py:586
  106.0 22.2 %copy-start.18 = (bf16[160,160]{1,0:T(8,128)(2,1)S(1)}, bf16[160,160]{1,0:T(8,128)(2,1)}, u32[]{:S(2)}) copy-start(bf16[160,160]{1,0:T(8,128)(2,1)} %constant.25.clone) | copy-start | bytes 153604
  123.3 2.2 collective-permute-start.22
  126.6 12.5 %collective-permute-start.23 = (bf16[4,48,1280]{2,1,0:T(8,128)(2,1)S(1)}, bf16[4,48,1280]{2,1,0:T(8,128)(2,1)S(1)}, u32[]{:S(2)}, u32[]{:S(2)}) collective-permute-start(bf16[4,48,1280]{2,1,0:T(8,128)(2,1)S(1)} %add_convert_fusion), channel_id=1, source_target_pairs={{0,16},{8,24},{16,0},{24,8},{1,17},{9,25},{17,1},{25,9},{2,18},{10... | collective-permute-start | bytes 1474568 | tf_op jit(solution)/shard_map/ppermute | solution.py:586
  127.5 11.6 %collective-permute-start.21 = (bf16[4,48,1280]{2,1,0:T(8,128)(2,1)}, bf16[4,48,1280]{2,1,0:T(8,128)(2,1)}, u32[]{:S(2)}, u32[]{:S(2)}) collective-permute-start(bf16[4,48,1280]{2,1,0:T(8,128)(2,1)} %get-tuple-element.81), channel_id=1, source_target_pairs={{0,8},{8,0},{16,24},{24,16},{1,9},{9,1},{17,25},{25,17},{2,10},{10... | collective-permute-start | bytes 1474568 | tf_op jit(solution)/shard_map/ppermute | solution.py:586
  143.3 8.4 %collective-permute-start.24 = (bf16[2,48,1280]{2,1,0:T(8,128)(2,1)}, bf16[2,48,1280]{2,1,0:T(8,128)(2,1)S(1)}, u32[]{:S(2)}, u32[]{:S(2)}) collective-permute-start(bf16[2,48,1280]{2,1,0:T(8,128)(2,1)} %get-tuple-element.87), channel_id=1, source_target_pairs={{0,2},{1,3},{2,4},{3,5},{4,6},{5,7},{6,0},{7,1},{8,10},{9,11},{10,... | collective-permute-start | bytes 737288 | tf_op jit(solution)/shard_map/ppermute | solution.py:620
  143.3 12.3 %collective-permute-start.25 = (bf16[2,48,1280]{2,1,0:T(8,128)(2,1)}, bf16[2,48,1280]{2,1,0:T(8,128)(2,1)S(1)}, u32[]{:S(2)}, u32[]{:S(2)}) collective-permute-start(bf16[2,48,1280]{2,1,0:T(8,128)(2,1)} %get-tuple-element.88), channel_id=1, source_target_pairs={{0,4},{1,5},{2,6},{3,7},{4,0},{5,1},{6,2},{7,3},{8,12},{9,13},{10,... | collective-permute-start | bytes 737288 | tf_op jit(solution)/shard_map/ppermute | solution.py:620
  145.3 11.6 %collective-permute-start.26 = (bf16[2,48,1280]{2,1,0:T(8,128)(2,1)}, bf16[2,48,1280]{2,1,0:T(8,128)(2,1)S(1)}, u32[]{:S(2)}, u32[]{:S(2)}) collective-permute-start(bf16[2,48,1280]{2,1,0:T(8,128)(2,1)} %get-tuple-element.89), channel_id=1, source_target_pairs={{0,6},{1,7},{2,0},{3,1},{4,2},{5,3},{6,4},{7,5},{8,14},{9,15},{10,... | collective-permute-start | bytes 737288 | tf_op jit(solution)/shard_map/ppermute | solution.py:620
  157.9 5.3 %collective-permute-start.27 = (bf16[48,1280]{1,0:T(8,128)(2,1)S(1)}, bf16[48,1280]{1,0:T(8,128)(2,1)S(1)}, u32[]{:S(2)}, u32[]{:S(2)}) collective-permute-start(bf16[48,1280]{1,0:T(8,128)(2,1)S(1)} %fusion.3), channel_id=1, source_target_pairs={{1,0},{0,1},{3,2},{2,3},{5,4},{4,5},{7,6},{6,7},{9,8},{8,9},{11,10... | collective-permute-start | bytes 368648 | tf_op jit(solution)/shard_map/ppermute | solution.py:623
  169.8 6.0 %collective-permute-start.28 = (bf16[48,1280]{1,0:T(8,128)(2,1)}, bf16[48,1280]{1,0:T(8,128)(2,1)S(1)}, u32[]{:S(2)}, u32[]{:S(2)}) collective-permute-start(bf16[48,1280]{1,0:T(8,128)(2,1)} %get-tuple-element.94.refs_0_), channel_id=1, source_target_pairs={{1,0},{0,1},{3,2},{2,3},{5,4},{4,5},{7,6},{6,7},{9,8},{8,9},{11,10... | collective-permute-start | bytes 368648 | tf_op jit(solution)/shard_map/ppermute | solution.py:609
  171.2 8.4 %collective-permute-start.29 = (bf16[48,1280]{1,0:T(8,128)(2,1)}, bf16[48,1280]{1,0:T(8,128)(2,1)S(1)}, u32[]{:S(2)}, u32[]{:S(2)}) collective-permute-start(bf16[48,1280]{1,0:T(8,128)(2,1)} %get-tuple-element.94.refs_0_), channel_id=1, source_target_pairs={{2,0},{3,1},{4,2},{5,3},{6,4},{7,5},{0,6},{1,7},{10,8},{11,9},{12,... | collective-permute-start | bytes 368648 | tf_op jit(solution)/shard_map/ppermute | solution.py:612
  175.2 5.6 %collective-permute-start.31 = (bf16[48,1280]{1,0:T(8,128)(2,1)}, bf16[48,1280]{1,0:T(8,128)(2,1)S(1)}, u32[]{:S(2)}, u32[]{:S(2)}) collective-permute-start(bf16[48,1280]{1,0:T(8,128)(2,1)} %get-tuple-element.94.refs_0_), channel_id=1, source_target_pairs={{4,0},{5,1},{6,2},{7,3},{0,4},{1,5},{2,6},{3,7},{12,8},{13,9},{14,... | collective-permute-start | bytes 368648 | tf_op jit(solution)/shard_map/ppermute | solution.py:612
  175.3 6.8 %collective-permute-start.33 = (bf16[48,1280]{1,0:T(8,128)(2,1)}, bf16[48,1280]{1,0:T(8,128)(2,1)S(1)}, u32[]{:S(2)}, u32[]{:S(2)}) collective-permute-start(bf16[48,1280]{1,0:T(8,128)(2,1)} %get-tuple-element.94.refs_0_), channel_id=1, source_target_pairs={{6,0},{7,1},{0,2},{1,3},{2,4},{3,5},{4,6},{5,7},{14,8},{15,9},{8,1... | collective-permute-start | bytes 368648 | tf_op jit(solution)/shard_map/ppermute | solution.py:612
  175.8 8.4 %collective-permute-start.30 = (bf16[48,1280]{1,0:T(8,128)(2,1)S(1)}, bf16[48,1280]{1,0:T(8,128)(2,1)S(1)}, u32[]{:S(2)}, u32[]{:S(2)}) collective-permute-start(bf16[48,1280]{1,0:T(8,128)(2,1)S(1)} %collective-permute-done.28.refs_1_), channel_id=1, source_target_pairs={{2,0},{3,1},{4,2},{5,3},{6,4},{7,5},{0,6},{1,7},{10,8},{11,9},{12,... | collective-permute-start | bytes 368648 | tf_op jit(solution)/shard_map/ppermute | solution.py:612
  178.6 6.5 %collective-permute-start.32 = (bf16[48,1280]{1,0:T(8,128)(2,1)S(1)}, bf16[48,1280]{1,0:T(8,128)(2,1)S(1)}, u32[]{:S(2)}, u32[]{:S(2)}) collective-permute-start(bf16[48,1280]{1,0:T(8,128)(2,1)S(1)} %collective-permute-done.28.refs_1_), channel_id=1, source_target_pairs={{4,0},{5,1},{6,2},{7,3},{0,4},{1,5},{2,6},{3,7},{12,8},{13,9},{14,... | collective-permute-start | bytes 368648 | tf_op jit(solution)/shard_map/ppermute | solution.py:612
  179.7 7.9 %collective-permute-start.34 = (bf16[48,1280]{1,0:T(8,128)(2,1)S(1)}, bf16[48,1280]{1,0:T(8,128)(2,1)S(1)}, u32[]{:S(2)}, u32[]{:S(2)}) collective-permute-start(bf16[48,1280]{1,0:T(8,128)(2,1)S(1)} %collective-permute-done.28.refs_1_), channel_id=1, source_target_pairs={{6,0},{7,1},{0,2},{1,3},{2,4},{3,5},{4,6},{5,7},{14,8},{15,9},{8,1... | collective-permute-start | bytes 368648 | tf_op jit(solution)/shard_map/ppermute | solution.py:612
  191.5 14.8 %collective-permute-start.35 = (bf16[4,48,1280]{2,1,0:T(8,128)(2,1)}, bf16[4,48,1280]{2,1,0:T(8,128)(2,1)S(1)}, u32[]{:S(2)}, u32[]{:S(2)}) collective-permute-start(bf16[4,48,1280]{2,1,0:T(8,128)(2,1)} %from_lines.3.i0), channel_id=1, source_target_pairs={{0,16},{8,24},{16,0},{24,8},{1,17},{9,25},{17,1},{25,9},{2,18},{10... | collective-permute-start | bytes 1474568 | tf_op jit(solution)/shard_map/ppermute | solution.py:586
  192.2 8.6 %collective-permute-start.36 = (bf16[2,120,128]{2,1,0:T(8,128)(2,1)}, bf16[2,120,128]{2,1,0:T(8,128)(2,1)S(1)}, u32[]{:S(2)}, u32[]{:S(2)}) collective-permute-start(bf16[2,120,128]{2,1,0:T(8,128)(2,1)} %get-tuple-element.95), channel_id=1, source_target_pairs={{0,0},{8,32},{16,64},{24,96},{32,8},{40,40},{48,72},{56,104},{64,1... | collective-permute-start | bytes 184328 | tf_op jit(solution)/shard_map/ppermute | solution.py:633
  197.3 3.4 %collective-permute-start.37 = (bf16[2,120,128]{2,1,0:T(8,128)(2,1)}, bf16[2,120,128]{2,1,0:T(8,128)(2,1)S(1)}, u32[]{:S(2)}, u32[]{:S(2)}) collective-permute-start(bf16[2,120,128]{2,1,0:T(8,128)(2,1)} %get-tuple-element.96), channel_id=1, source_target_pairs={{0,8},{8,40},{16,72},{24,104},{32,16},{40,48},{48,80},{56,112},{64... | collective-permute-start | bytes 184328 | tf_op jit(solution)/shard_map/ppermute | solution.py:633
  197.4 5.9 %collective-permute-start.38 = (bf16[2,120,128]{2,1,0:T(8,128)(2,1)}, bf16[2,120,128]{2,1,0:T(8,128)(2,1)S(1)}, u32[]{:S(2)}, u32[]{:S(2)}) collective-permute-start(bf16[2,120,128]{2,1,0:T(8,128)(2,1)} %get-tuple-element.97), channel_id=1, source_target_pairs={{0,16},{8,48},{16,80},{24,112},{32,24},{40,56},{48,88},{56,120},{6... | collective-permute-start | bytes 184328 | tf_op jit(solution)/shard_map/ppermute | solution.py:633
  199.9 6.3 %collective-permute-start.39 = (bf16[2,120,128]{2,1,0:T(8,128)(2,1)}, bf16[2,120,128]{2,1,0:T(8,128)(2,1)S(1)}, u32[]{:S(2)}, u32[]{:S(2)}) collective-permute-start(bf16[2,120,128]{2,1,0:T(8,128)(2,1)} %get-tuple-element.98), channel_id=1, source_target_pairs={{0,24},{8,56},{16,88},{24,120},{32,0},{40,32},{48,64},{56,96},{64,... | collective-permute-start | bytes 184328 | tf_op jit(solution)/shard_map/ppermute | solution.py:633
  206.3 6.2 %collective-permute-start.41 = (bf16[4,48,1280]{2,1,0:T(8,128)(2,1)S(1)}, bf16[4,48,1280]{2,1,0:T(8,128)(2,1)S(1)}, u32[]{:S(2)}, u32[]{:S(2)}) collective-permute-start(bf16[4,48,1280]{2,1,0:T(8,128)(2,1)S(1)} %collective-permute-done.35.i1), channel_id=1, source_target_pairs={{0,8},{8,0},{16,24},{24,16},{1,9},{9,1},{17,25},{25,17},{2,10},{10... | collective-permute-start | bytes 1474568 | tf_op jit(solution)/shard_map/ppermute | solution.py:586
  209.2 3.3 %collective-permute-start.40 = (bf16[4,48,1280]{2,1,0:T(8,128)(2,1)}, bf16[4,48,1280]{2,1,0:T(8,128)(2,1)S(1)}, u32[]{:S(2)}, u32[]{:S(2)}) collective-permute-start(bf16[4,48,1280]{2,1,0:T(8,128)(2,1)} %from_lines.3.i0), channel_id=1, source_target_pairs={{0,8},{8,0},{16,24},{24,16},{1,9},{9,1},{17,25},{25,17},{2,10},{10... | collective-permute-start | bytes 1474568 | tf_op jit(solution)/shard_map/ppermute | solution.py:586
  (33 other events, 166.4 us)

commit v7 on v5

--- a/solution.py
+++ b/solution.py
@@ -118,21 +118,24 @@
         long_ref[:, GL * part : GL * (part + 1)] = block
 
 
-def forward_group(rows, depth_ref, tall_ref, outs, y):
+def forward_runs(source_ref, depth_ref, tall_ref, outs, runs):
     half = KZ * YB
-    planes = dot(depth_ref[...], rows, 1, 1)
-    real = planes[:half]
-    imag = planes[half:]
-    sides = jnp.concatenate(
-        [jnp.concatenate([real, imag], axis=1), jnp.concatenate([imag, -real], axis=1)], axis=0
-    ).astype(BF)
-    lines = dot(sides, tall_ref[...])
-    for pos in range(GX):
-        lo = pos * KB * YB
-        piece = jnp.concatenate(
-            [lines[lo : lo + KB * YB], lines[half + lo : half + lo + KB * YB]], axis=0
-        )
-        outs[pos][y] = piece.astype(BF)
+    part = KB * YB
+    sides = []
+    for y in runs:
+        planes = dot(depth_ref[...], run_rows(source_ref, y), 1, 1)
+        real = planes[:half]
+        imag = planes[half:]
+        sides.append(jnp.concatenate([real, imag], axis=1).astype(BF))
+        sides.append(jnp.concatenate([imag, -real], axis=1).astype(BF))
+    lines = dot(jnp.concatenate(sides, axis=0), tall_ref[...])
+    for n, y in enumerate(runs):
+        for pos in range(GX):
+            lo = 2 * half * n + pos * part
+            piece = jnp.concatenate(
+                [lines[lo : lo + part], lines[half + lo : half + lo + part]], axis=0
+            )
+            outs[pos][y] = piece.astype(BF)
 
 
 def inverse_group(ins, depth_ref, long_ref, y):
@@ -151,11 +154,13 @@
     return ref[:, :, LANES * y : LANES * (y + 1)].reshape(GROUP * XL, LANES)
 
 
-def bypass_kernel(source_ref, mixer_ref, out_ref):
+def bypass_kernel(shift_ref, source_ref, mixer_ref, out_ref):
     for i in range(XL // XB):
         span = slice(i * XB, (i + 1) * XB)
         rows = source_ref[:, span, :].reshape(CH * XB, LANES)
-        out_ref[:, span, :] = dot(mixer_ref[...], rows).reshape(CH, XB, LANES).astype(BF)
+        mixed = dot(mixer_ref[...], rows).reshape(CH, XB, LANES)
+        for channel in range(CH):
+            out_ref[channel, span, :] = (mixed[channel] + shift_ref[channel]).astype(BF)
 
 
 def start_kernel(
@@ -165,33 +170,30 @@
     def _():
         fill_tables(strip_ref, wide_ref, depth_ref, tall_ref, long_ref)
 
-    for y in range(STEPS):
-        forward_group(run_rows(field_ref, y), depth_ref, tall_ref, (o0, o1, o2, o3), y)
+    forward_runs(field_ref, depth_ref, tall_ref, (o0, o1, o2, o3), range(STEPS))
 
 
 ROOT = math.sqrt(2.0 / math.pi)
 CUBE = 0.044715
 
 
-def activate(bias_ref, upstream_ref, total_ref, act_ref, grad_ref, y):
+def activate(upstream_ref, total_ref, act_ref, grad_ref, y):
     lanes = slice(LANES * y, LANES * (y + 1))
     for channel in range(GROUP):
-        shift = bias_ref[GROUP * pl.program_id(0) + channel]
         for i in range(XL // EB):
             span = slice(i * EB, (i + 1) * EB)
-            x = total_ref[y, channel, span, :] + shift
+            x = total_ref[y, channel, span, :]
             square = x * x
             t = jnp.tanh(x * (ROOT + (ROOT * CUBE) * square))
             h = 0.5 * t + 0.5
             act = x * h
             slope = h + act * (1.0 - h) * (2.0 * ROOT + (6.0 * ROOT * CUBE) * square)
             act_ref[channel, span, lanes] = act.astype(BF)
-            up = upstream_ref[channel, span, lanes].astype(F32)
-            grad_ref[channel, span, lanes] = (up * slope).astype(BF)
+            grad_ref[channel, span, lanes] = upstream_ref[channel, span, lanes] * slope.astype(BF)
 
 
 def middle_kernel(
-    where_ref, bias_ref, i0, i1, i2, i3, bypass_ref, upstream_ref, strip_ref, wide_ref,
+    where_ref, i0, i1, i2, i3, bypass_ref, upstream_ref, strip_ref, wide_ref,
     act_ref, grad_ref, o0, o1, o2, o3, depth_ref, tall_ref, long_ref, total_ref,
 ):
     @pl.when(pl.program_id(0) == 0)
@@ -203,17 +205,17 @@
         lanes = slice(LANES * y, LANES * (y + 1))
         total_ref[y] = bypass_ref[:, :, lanes].astype(F32) + values.reshape(GROUP, XL, LANES)
 
-    def forward(y):
-        forward_group(run_rows(grad_ref, y), depth_ref, tall_ref, (o0, o1, o2, o3), y)
+    def forward(*runs):
+        forward_runs(grad_ref, depth_ref, tall_ref, (o0, o1, o2, o3), runs)
 
     inverse(0)
     for y in range(STEPS):
         if y + 1 < STEPS:
             inverse(y + 1)
-        activate(bias_ref, upstream_ref, total_ref, act_ref, grad_ref, y)
-        if y > 0:
-            forward(y - 1)
-    forward(STEPS - 1)
+        activate(upstream_ref, total_ref, act_ref, grad_ref, y)
+        if y == 2:
+            forward(0, 1)
+    forward(2, 3)
 
 
 def end_kernel(
@@ -256,18 +258,22 @@
 ALONE = pltpu.CompilerParams(vmem_limit_bytes=63 * 1024 * 1024)
 
 
-def bypass_columns(source, mixer):
+def bypass_columns(source, mixer, shift):
     columns = pl.BlockSpec((CH, XL, LANES), lambda i: (0, 0, i))
     return pl.pallas_call(
         bypass_kernel,
         grid=(STEPS,),
-        in_specs=[columns, pl.BlockSpec((CH * XB, CH * XB), lambda i: (0, 0))],
+        in_specs=[
+            pl.BlockSpec(memory_space=pltpu.SMEM),
+            columns,
+            pl.BlockSpec((CH * XB, CH * XB), lambda i: (0, 0)),
+        ],
         out_specs=columns,
         out_shape=COLUMNS,
         compiler_params=PARAMS,
         cost_estimate=cost(6),
         name="bypass_columns",
-    )(source, mixer)
+    )(shift, source, mixer)
 
 
 def start_columns(where, field):
@@ -288,16 +294,14 @@
     )(where, field, jnp.asarray(DEPTH), jnp.asarray(WIDTH))
 
 
-def middle_columns(where, bias, coeffs_in, bypass, upstream):
+def middle_columns(where, coeffs_in, bypass, upstream):
     columns, coeffs, depth, wide = column_specs()
     return pl.pallas_call(
         middle_kernel,
         grid_spec=pltpu.PrefetchScalarGridSpec(
             num_scalar_prefetch=1,
             grid=(GROUPS,),
-            in_specs=[pl.BlockSpec(memory_space=pltpu.SMEM)]
-            + [coeffs] * 4
-            + [columns, columns, depth, wide],
+            in_specs=[coeffs] * 4 + [columns, columns, depth, wide],
             out_specs=[columns, columns] + [coeffs] * 4,
             scratch_shapes=BLOCKS + [TOTAL],
         ),
@@ -305,7 +309,7 @@
         compiler_params=PARAMS,
         cost_estimate=cost(19),
         name="middle_columns",
-    )(where, bias, *coeffs_in, bypass, upstream, jnp.asarray(DEPTH), jnp.asarray(WIDTH))
+    )(where, *coeffs_in, bypass, upstream, jnp.asarray(DEPTH), jnp.asarray(WIDTH))
 
 
 def end_columns(where, coeffs_in, bypass):
@@ -326,6 +330,13 @@
     )(where, *coeffs_in, bypass, jnp.asarray(DEPTH), jnp.asarray(WIDTH))
 
 
+def order_table(where_ref, table_ref, order_ref):
+    for k in range(GY):
+        owner = ((where_ref[2] + (k & 6)) & 7) ^ (k & 1)
+        start = pl.multiple_of(owner * 48, 16)
+        order_ref[48 * k : 48 * (k + 1)] = table_ref[0, pl.ds(start, 48), :]
+
+
 def line_kernel(where_ref, a_ref, b_ref, c_ref, table_ref, out_ref):
     for j in range(GROUPS):
         lanes = slice(GL * j, GL * (j + 1))
@@ -334,7 +345,14 @@
         out_ref[:, :, lanes] = dot(table_ref[0], rows).astype(BF).reshape(GY, 48, GL)
 
 
-def unline_kernel(where_ref, *refs):
+def unline_kernel(where_ref, modes_ref, table_ref, out_ref):
+    for j in range(GROUPS):
+        lanes = slice(GL * j, GL * (j + 1))
+        rows = modes_ref[:, :, lanes].reshape(GY * 48, GL)
+        out_ref[:, :, lanes] = dot(table_ref[0], rows, 0, 0).astype(BF).reshape(STEPS, ROWS, GL)
+
+
+def unline_set_kernel(where_ref, *refs):
     *modes_refs, table_ref, out_ref, order_ref = refs
     for k in range(GY):
         owner = ((where_ref[2] + (k & 6)) & 7) ^ (k & 1)
@@ -346,7 +364,7 @@
         out_ref[:, :, lanes] = dot(order_ref[...], rows, 0, 0).astype(BF).reshape(STEPS, ROWS, GL)
 
 
-def line_call(kernel, name, where, ins, out_shape, scratch=()):
+def line_call(kernel, name, where, ins, out, scratch=()):
     whole = pl.BlockSpec(ins[0].shape, lambda i, w: (0,) * ins[0].ndim)
     table = pl.BlockSpec((1, GY * 48, STEPS * ROWS), lambda i, w: (w[2], 0, 0))
     return pl.pallas_call(
@@ -355,10 +373,10 @@
             num_scalar_prefetch=1,
             grid=(1,),
             in_specs=[whole] * len(ins) + [table],
-            out_specs=pl.BlockSpec(out_shape.shape, lambda i, w: (0, 0, 0)),
+            out_specs=pl.BlockSpec(out.shape, lambda i, w: (0, 0, 0)),
             scratch_shapes=list(scratch),
         ),
-        out_shape=out_shape,
+        out_shape=out,
         compiler_params=ALONE,
         cost_estimate=cost(3),
         name=name,
@@ -371,8 +389,12 @@
 
 
 def from_lines(where, modes):
+    return line_call(unline_kernel, "from_lines", where, (modes,), COEFFS)
+
+
+def from_line_set(where, modes):
     order = pltpu.VMEM((GY * 48, STEPS * ROWS), BF)
-    return line_call(unline_kernel, "from_lines", where, modes, COEFFS, [order])
+    return line_call(unline_set_kernel, "from_line_set", where, modes, COEFFS, [order])
 
 
 UNROLL = 4
@@ -385,10 +407,10 @@
     return lax.broadcasted_iota(jnp.int32, (SETS, 2 * HALF), 1) < HALF
 
 
-def gather_modes(arrived_ref, sum_ref, modes_ref, scale=None):
-    total = arrived_ref[0].astype(F32)
+def gather_modes(arrived, sum_ref, modes_ref, scale=None):
+    total = arrived[0].astype(F32)
     for i in range(1, GY):
-        total = total + arrived_ref[i].astype(F32)
+        total = total + arrived[i].astype(F32)
     sum_ref[...] = total.astype(BF).astype(F32)
     low = low_lanes()
     for j in range(CH // 2):
@@ -421,7 +443,9 @@
             sum_ref[(2 + part) * SETS : (3 + part) * SETS, lanes] = jnp.where(
                 low, pltpu.roll(even, HALF, 1), odd
             )
-    out_ref[...] = sum_ref[...].astype(BF)
+    modes = sum_ref[...].astype(BF)
+    for copy in range(out_ref.shape[0]):
+        out_ref[copy] = modes
 
 
 def fold_scale(where_ref):
@@ -449,14 +473,15 @@
 
 
 def mix_kernel(
-    where_ref, arrived_ref, w0, w1, w2, w3, out_ref, u0, u1, u2, u3, sum_ref, in_ref, mix_ref
+    where_ref, arrived_ref, w0, w1, w2, w3, out_ref, u0, u1, u2, u3,
+    sum_ref, in_ref, mix_ref,
 ):
     step = pl.program_id(0)
 
     @pl.when(step == 0)
     def _():
         gather_modes(arrived_ref, sum_ref, in_ref)
-        hand_out(where_ref, in_ref, (u0, u1, u2, u3))
+        hand_out(where_ref, in_ref, [ref.at[0] for ref in (u0, u1, u2, u3)])
 
     for k, weight_ref in enumerate((w0, w1, w2, w3)):
         base = set_row(where_ref, k)
@@ -480,14 +505,17 @@
 
 
 def back_kernel(
-    where_ref, arrived_ref, w0, w1, w2, w3, out_ref, u0, u1, u2, u3, sum_ref, in_ref, mix_ref
+    where_ref, arrived_ref, w0, w1, w2, w3, s0, s1, s2, s3, out_ref, u0, u1, u2, u3,
+    sum_ref, in_ref, mix_ref,
 ):
     step = pl.program_id(0)
 
     @pl.when(step == 0)
     def _():
         gather_modes(arrived_ref, sum_ref, in_ref, fold_scale(where_ref))
-        hand_out(where_ref, in_ref, (u0, u1, u2, u3))
+        hand_out(where_ref, in_ref, [ref.at[1] for ref in (u0, u1, u2, u3)])
+        for spec_ref, ref in zip((s0, s1, s2, s3), (u0, u1, u2, u3)):
+            ref[0] = spec_ref[0]
 
     for k, weight_ref in enumerate((w0, w1, w2, w3)):
         base = set_row(where_ref, k)
@@ -509,38 +537,45 @@
         spread_modes(mix_ref, sum_ref, out_ref)
 
 
-def mode_call(kernel, name, where, arrived, weights):
-    chunk = pl.BlockSpec((KB * PAIR, 2 * HALF), lambda i, w: (0, 0))
+def mode_call(kernel, name, where, arrived, weights, spectra=()):
+    sets, copies = (2, GY) if spectra else (1, 1)
+
+    def chunk(n):
+        return pl.BlockSpec((n, KB * PAIR, 2 * HALF), lambda i, w: (0, 0, 0))
+
     return pl.pallas_call(
         kernel,
         grid_spec=pltpu.PrefetchScalarGridSpec(
             num_scalar_prefetch=1,
             grid=(KB,),
             in_specs=[pl.BlockSpec((GY, 48, WIDE), lambda i, w: (0, 0, 0))]
-            + [pl.BlockSpec((1, CH, PAIR, 2 * HALF), lambda i, w: (i, 0, 0, 0))] * 4,
-            out_specs=[pl.BlockSpec((48, WIDE), lambda i, w: (0, 0))] + [chunk] * 4,
+            + [pl.BlockSpec((1, CH, PAIR, 2 * HALF), lambda i, w: (i, 0, 0, 0))] * 4
+            + [chunk(1)] * len(spectra),
+            out_specs=[pl.BlockSpec((copies, 48, WIDE), lambda i, w: (0, 0, 0))]
+            + [chunk(sets)] * 4,
             scratch_shapes=[
                 pltpu.VMEM((48, WIDE), F32),
                 pltpu.VMEM((SETS * PAIR, 2 * HALF), F32),
                 pltpu.VMEM((SETS * PAIR, 2 * HALF), F32),
             ],
         ),
-        out_shape=[jax.ShapeDtypeStruct((48, WIDE), BF)]
-        + [jax.ShapeDtypeStruct((KB * PAIR, 2 * HALF), BF)] * 4,
+        out_shape=[jax.ShapeDtypeStruct((copies, 48, WIDE), BF)]
+        + [jax.ShapeDtypeStruct((sets, KB * PAIR, 2 * HALF), BF)] * 4,
         compiler_params=ALONE,
         cost_estimate=cost(5),
         name=name,
-    )(where, arrived, *weights)
-
-
-def outer_kernel(s0, s1, s2, s3, g0, g1, g2, g3, out_ref, spec_ref):
-    for k, ref in enumerate((s0, s1, s2, s3)):
-        spec_ref[k] = ref[...].astype(F32)
+    )(where, arrived, *weights, *spectra)
+
+
+def outer_kernel(p0, p1, p2, p3, out_ref, spec_ref):
+    pairs = (p0, p1, p2, p3)
+    for k, ref in enumerate(pairs):
+        spec_ref[k] = ref[0].astype(F32)
     for i in range(KB):
         grads = []
         others = []
-        for ref in (g0, g1, g2, g3):
-            grad = ref[...].astype(F32)[i * PAIR : (i + 1) * PAIR]
+        for ref in pairs:
+            grad = ref[1].astype(F32)[i * PAIR : (i + 1) * PAIR]
             grads.append(grad)
             others.append(-turned(grad))
 
@@ -554,14 +589,14 @@
             out_ref[i, c] = total
 
 
-def outer_sum(spectra, grads):
+def outer_sum(pairs):
     return pl.pallas_call(
         outer_kernel,
         out_shape=jax.ShapeDtypeStruct((KB, CH, PAIR, 2 * HALF), F32),
         scratch_shapes=[pltpu.VMEM((DP, KB * PAIR, 2 * HALF), F32)],
         cost_estimate=cost(3),
         name="outer_sum",
-    )(*spectra, *grads)
+    )(*pairs)
 
 
 def swap(values, bit):
@@ -575,10 +610,9 @@
     return (own, swap(near, 1), arrived), beside
 
 
-def share_slabs(own, *waiting):
-    far = swap(own, 2)
-    far, *waiting = lax.optimization_barrier((far, *waiting))
-    return own, far, swap(own, 1), swap(far, 1), *waiting
+def share_slabs(own, *beside):
+    far, *beside = lax.optimization_barrier((swap(own, 2), *beside))
+    return own, far, swap(own, 1), swap(far, 1), *beside
 
 
 def gather_weights(weight):
@@ -624,21 +658,21 @@
 
     values = field[0]
     *pieces, weight = lax.optimization_barrier((*start_columns(where, values), weight))
-    parts, bypass = start_slabs(pieces, bypass_columns(values, mixer_of(bypass_weight)))
+    parts, bypass = start_slabs(pieces, bypass_columns(values, mixer_of(bypass_weight), bias))
     weights = gather_weights(weight)
     lines, weights[1], weights[3] = lax.optimization_barrier(
         (to_lines(where, *parts), weights[1], weights[3])
     )
     arrived = exchange_lines(lines)
     modes, *spectra = mode_call(mix_kernel, "mix_modes", where, arrived, weights)
-    own = from_lines(where, gather_lines(modes))
-    *coeffs, s0, s1, s2, s3 = share_slabs(own, *to_owners(spectra))
-    activation, grad, *pieces = middle_columns(where, bias, coeffs, bypass, cotangent[0])
-    parts, bypass = start_slabs(pieces, bypass_columns(grad, mixer_of(bypass_weight.T)))
+    coeffs = share_slabs(from_line_set(where, gather_lines(modes[0])))
+    activation, grad, *pieces = middle_columns(where, coeffs, bypass, cotangent[0])
+    mixer = mixer_of(bypass_weight.T)
+    parts, bypass = start_slabs(pieces, bypass_columns(grad, mixer, jnp.zeros_like(bias)))
     arrived = exchange_lines(to_lines(where, *parts))
-    modes, *grads = mode_call(back_kernel, "back_modes", where, arrived, weights)
-    own = from_lines(where, gather_lines(modes))
-    *coeffs, weight_grad = share_slabs(own, outer_sum((s0, s1, s2, s3), to_owners(grads)))
+    modes, *pairs = mode_call(back_kernel, "back_modes", where, arrived, weights, spectra)
+    modes, *pairs = lax.optimization_barrier((exchange_lines(modes), *to_owners(pairs)))
+    *coeffs, weight_grad = share_slabs(from_lines(where, modes), outer_sum(pairs))
     field_grad = end_columns(where, coeffs, bypass)
     return (
         activation[None],

time: 220 us -> 215 us (0.977)
  Pallas kernels: 76.7 us -> 73.9 us
  waiting for transfers between devices: 47 us -> 44.4 us
  starting transfers between devices: 63.5 us -> 66.1 us
    ppermute x12, starting transfers between devices: 12.1 us -> 23.2 us  [swap(): return lax.ppermute(values, 'gx', [(i, i ^ bit) for i in range(GX)])]
    ppermute x8 -> x4, starting transfers between devices: 17.7 us -> 8.56 us  [to_owners(): moved.append(lax.ppermute(chunk, ('dp', 'gx'), pairs))]
    ppermute x12 -> x6, waiting for transfers between devices: 12.9 us -> 5.66 us  [gather_lines(): held += [lax.ppermute(part, 'gy', pairs) for part in held[:2]]]
    ppermute x12, waiting for transfers between devices: 12.3 us -> 19 us  [swap(): return lax.ppermute(values, 'gx', [(i, i ^ bit) for i in range(GX)])]
    all_to_all x1 -> x2, starting transfers between devices: 7.67 us -> 11.9 us  [exchange_lines(): return lax.all_to_all(parts, 'gy', split_axis=0, concat_axis=0, tiled=True)]
    ppermute x12 -> x6, starting transfers between devices: 12.3 us -> 8.15 us  [gather_lines(): held += [lax.ppermute(part, 'gy', pairs) for part in held[:2]]]
    ppermute x2 -> x1, waiting for transfers between devices: 2.42 us -> 0.01 us  [gather_lines(): held = [modes, lax.ppermute(modes, 'gy', [(g ^ 1, g) for g in range(GY)])]]
    unnamed x66 -> x44, local copies, waits for them, and re-layouts: 4.83 us -> 3.29 us
  transfers between devices with their start and end apart: 39 -> 29, of which waited for: 21 -> 16; matrix products, arithmetic and copies ran while one was open for 2% -> 2% of each run, Pallas kernels for 13% -> 12%
where the time goes in v7:
time: 215 us; the launch traced here: 214 us
  Pallas kernels  73.9 us (34%)
  starting transfers between devices  66.1 us (31%)
  waiting for transfers between devices  44.4 us (21%)
  blocking collectives  19.8 us (9%)
  local copies, waits for them, and re-layouts  3.8 us (2%)
  other arithmetic  3 us (1%)
    ppermute x12, starting transfers between devices, swap(): return lax.ppermute(values, 'gx', [(i, i ^ bit) for i in range(GX)])  23.2 us
    all_to_all x1, blocking collectives, exchange_lines(): return lax.all_to_all(parts, 'gy', split_axis=0, concat_axis=0, tiled=True)  19.8 us
    ppermute x12, waiting for transfers between devices, swap(): return lax.ppermute(values, 'gx', [(i, i ^ bit) for i in range(GX)])  19 us
    pallas_call x1, Pallas kernels, middle_columns(): pl.pallas_call(middle_kernel, grid_spec=pltpu.PrefetchScalarGridSpec(num_...  15.6 us
    pallas_call x4, Pallas kernels, line_call(): pl.pallas_call(kernel, grid_spec=pltpu.PrefetchScalarGridSpec(num_scalar_...  13.3 us
    ppermute x3, waiting for transfers between devices, gather_weights(): lax.ppermute(weight, 'dp', [((a + k) % DP, a) for a in range(DP)])  12.7 us
    pallas_call x2, Pallas kernels, bypass_columns(): pl.pallas_call(bypass_kernel, grid=(STEPS,), in_specs=[pl.BlockSpec(memor...  12.4 us
    all_to_all x2, starting transfers between devices, exchange_lines(): return lax.all_to_all(parts, 'gy', split_axis=0, concat_axis=0, tiled=True)  11.9 us
  transfers between devices with their start and end apart: 29, of which 16 were waited for; matrix products, arithmetic and copies ran while one was open for 2% of the time, Pallas kernels for 12%

profile of v7, /device:TPU:1, one launch (start us, length us, event | category | flops | bytes accessed | tf_op | source)
XLA Modules:
  0.0 213.6 jit_solution(6583424091469523497)
XLA Ops:
  0.7 4.6 %collective-permute-start = (bf16[3,20,20,2,128]{4,3,2,1,0:T(2,128)(2,1)}, bf16[3,20,20,2,128]{4,3,2,1,0:T(2,128)(2,1)S(1)}, u32[]{:S(2)}, u32[]{:S(2)}) collective-permute-start(bf16[3,20,20,2,128]{4,3,2,1,0:T(2,128)(2,1)} %param.11), channel_id=1, source_target_pairs={{0,0},{8,32},{16,64},{24,96},{32,72},{40,104},{48,8},{56,40},{64,1... | collective-permute-start | bytes 1843208 | tf_op jit(solution)/shard_map/ppermute | solution.py:652
  6.0 7.6 %start_columns.1 = (bf16[4,48,1280]{2,1,0:T(8,128)(2,1)}, bf16[4,48,1280]{2,1,0:T(8,128)(2,1)}, bf16[4,48,1280]{2,1,0:T(8,128)(2,1)}, bf16[4,48,1280]{2,1,0:T(8,128)(2,1)}) custom-call(s32[3]{0:T(128)} %pad_add_fusion.where_ref, bf16[20,64,2048]{2,1,0:T(8,128)(2,1)} %bitcast.19, bf16[4,24,512]{2,1,0:T(8,128)(2,1)} %constant.25.clone.strip_ref, ...), custom_call_target="tpu_custom_call" | custom-call | bytes 24000000 | tf_op jit(solution)/shard_map/start_columns/pallas_call | solution.py:281
  14.4 4.2 %collective-permute-start.4 = (bf16[3,20,20,2,128]{4,3,2,1,0:T(2,128)(2,1)S(1)}, bf16[3,20,20,2,128]{4,3,2,1,0:T(2,128)(2,1)}, u32[]{:S(2)}, u32[]{:S(2)}) collective-permute-start(bf16[3,20,20,2,128]{4,3,2,1,0:T(2,128)(2,1)S(1)} %collective-permute-done), channel_id=1, source_target_pairs={{32,0},{64,32},{96,64},{0,96},{33,1},{65,33},{97,65},{1,97},{34,2}... | collective-permute-start | bytes 1843208 | tf_op jit(solution)/shard_map/ppermute | solution.py:621
  18.6 1.2 add_convert_fusion.1
  19.8 1.5 collective-permute-start.3
  22.8 6.2 %bypass_columns.2.bypass_ref = bf16[20,64,2048]{2,1,0:T(8,128)(2,1)} custom-call(f32[20]{0:T(128)} %shift_ref.1, bf16[20,64,2048]{2,1,0:T(8,128)(2,1)} %bitcast.20, bf16[160,160]{1,0:T(8,128)(2,1)} %fusion.mixer_ref), custom_call_target="tpu_custom_call" | custom-call | bytes 18000000 | tf_op jit(solution)/shard_map/bypass_columns/pallas_call | solution.py:263
  29.0 3.5 %collective-permute-done.3.c_ref = bf16[4,48,1280]{2,1,0:T(8,128)(2,1)} collective-permute-done((bf16[4,48,1280]{2,1,0:T(8,128)(2,1)S(1)}, bf16[4,48,1280]{2,1,0:T(8,128)(2,1)}, u32[]{:S(2)}, u32[]{:S(2)}) %collective-permute-start.3) | collective-permute-done | bytes 491552 | tf_op jit(solution)/shard_map/ppermute | solution.py:603
  32.5 3.5 %to_lines.2 = bf16[8,48,1280]{2,1,0:T(8,128)(2,1)} custom-call(s32[3]{0:T(128)} %pad_add_fusion.where_ref, bf16[4,48,1280]{2,1,0:T(8,128)(2,1)} %get-tuple-element.46.a_ref, bf16[4,48,1280]{2,1,0:T(8,128)(2,1)} %collective-permute-done.1.b_ref, bf16[4,48,1280]{2,1,0:T(8,128)(2,1)} %collective-permute-done.3.c_ref, ...), custom_call_target="tpu_custom_call" | custom-call | bytes 9000000 | tf_op jit(solution)/shard_map/to_lines/pallas_call | solution.py:370
  35.9 7.7 %all-to-all-start = ((bf16[8,48,1280]{2,1,0:T(8,128)(2,1)}), bf16[8,48,1280]{2,1,0:T(8,128)(2,1)}, u32[]{:S(2)}, u32[]{:S(2)}) async-start(bf16[8,48,1280]{2,1,0:T(8,128)(2,1)} %to_lines.2), calls=%async_computation | async-start | bytes 1966080 | tf_op jit(solution)/shard_map/all_to_all | solution.py:634
  43.6 2.8 %collective-permute-start.6 = (bf16[3,20,20,2,128]{4,3,2,1,0:T(2,128)(2,1)S(1)}, bf16[3,20,20,2,128]{4,3,2,1,0:T(2,128)(2,1)S(1)}, u32[]{:S(2)}, u32[]{:S(2)}) collective-permute-start(bf16[3,20,20,2,128]{4,3,2,1,0:T(2,128)(2,1)S(1)} %collective-permute-done), channel_id=1, source_target_pairs={{64,0},{96,32},{0,64},{32,96},{65,1},{97,33},{1,65},{33,97},{66,2}... | collective-permute-start | bytes 1843208 | tf_op jit(solution)/shard_map/ppermute | solution.py:621
  46.4 12.7 %collective-permute-done.6 = bf16[3,20,20,2,128]{4,3,2,1,0:T(2,128)(2,1)S(1)} collective-permute-done((bf16[3,20,20,2,128]{4,3,2,1,0:T(2,128)(2,1)S(1)}, bf16[3,20,20,2,128]{4,3,2,1,0:T(2,128)(2,1)S(1)}, u32[]{:S(2)}, u32[]{:S(2)}) %collective-permute-start.6) | collective-permute-done | bytes 614432 | tf_op jit(solution)/shard_map/ppermute | solution.py:621
  60.0 5.5 %mix_modes.1 = (bf16[1,48,1280]{2,1,0:T(8,128)(2,1)}, bf16[1,120,128]{2,1,0:T(8,128)(2,1)}, bf16[1,120,128]{2,1,0:T(8,128)(2,1)}, bf16[1,120,128]{2,1,0:T(8,128)(2,1)}, bf16[1,120,128]{2,1,0:T(8,128)(2,1)}) custom-call(s32[3]{0:T(128)} %pad_add_fusion.where_ref, bf16[8,48,1280]{2,1,0:T(8,128)(2,1)} %all-to-all-done.arrived_ref, ...), custom_call_target="tpu_custom_call" | custom-call | bytes 15000000 | tf_op jit(solution)/shard_map/mix_modes/pallas_call | solution.py:546
  65.5 2.7 %collective-permute-start.7 = (bf16[48,1280]{1,0:T(8,128)(2,1)}, bf16[48,1280]{1,0:T(8,128)(2,1)S(1)}, u32[]{:S(2)}, u32[]{:S(2)}) collective-permute-start(bf16[48,1280]{1,0:T(8,128)(2,1)} %bitcast.28), channel_id=1, source_target_pairs={{1,0},{0,1},{3,2},{2,3},{5,4},{4,5},{7,6},{6,7},{9,8},{8,9},{11,10... | collective-permute-start | bytes 368648 | tf_op jit(solution)/shard_map/ppermute | solution.py:626
  68.2 2.7 %collective-permute-start.10 = (bf16[48,1280]{1,0:T(8,128)(2,1)}, bf16[48,1280]{1,0:T(8,128)(2,1)S(1)}, u32[]{:S(2)}, u32[]{:S(2)}) collective-permute-start(bf16[48,1280]{1,0:T(8,128)(2,1)} %bitcast.29), channel_id=1, source_target_pairs={{4,0},{5,1},{6,2},{7,3},{0,4},{1,5},{2,6},{3,7},{12,8},{13,9},{14,... | collective-permute-start | bytes 368648 | tf_op jit(solution)/shard_map/ppermute | solution.py:629
  71.2 2.4 %collective-permute-start.8 = (bf16[48,1280]{1,0:T(8,128)(2,1)}, bf16[48,1280]{1,0:T(8,128)(2,1)S(1)}, u32[]{:S(2)}, u32[]{:S(2)}) collective-permute-start(bf16[48,1280]{1,0:T(8,128)(2,1)} %bitcast.31), channel_id=1, source_target_pairs={{2,0},{3,1},{4,2},{5,3},{6,4},{7,5},{0,6},{1,7},{10,8},{11,9},{12,... | collective-permute-start | bytes 368648 | tf_op jit(solution)/shard_map/ppermute | solution.py:629
  74.2 2.1 collective-permute-start.9
  76.3 1.0 collective-permute-done.12.refs_6_
  77.3 1.0 collective-permute-done.8.refs_2_
  78.4 1.5 collective-permute-done.11.refs_5_
  79.9 1.2 collective-permute-done.13.refs_7_
  81.1 0.9 collective-permute-done.9.refs_3_
  82.0 3.3 %from_line_set.1.i0 = bf16[4,48,1280]{2,1,0:T(8,128)(2,1)} custom-call(s32[3]{0:T(128)} %pad_add_fusion.where_ref, bf16[48,1280]{1,0:T(8,128)(2,1)} %bitcast.32, bf16[48,1280]{1,0:T(8,128)(2,1)} %copy-done.12, bf16[48,1280]{1,0:T(8,128)(2,1)} %copy-done.15, bf16[48,1280]{1,0:T(8,128)(2,1)} %collective-permute-done.9.refs_3_, bf16[48,1280]{1,0:T(8,128)(2,1)} %copy-done.13, ...), custom_call_target="tpu_custom_call" | custom-call | bytes 9000000 | tf_op jit(solution)/shard_map/from_line_set/pallas_call | solution.py:370
  85.5 4.0 %collective-permute-start.15 = (bf16[4,48,1280]{2,1,0:T(8,128)(2,1)}, bf16[4,48,1280]{2,1,0:T(8,128)(2,1)S(1)}, u32[]{:S(2)}, u32[]{:S(2)}) collective-permute-start(bf16[4,48,1280]{2,1,0:T(8,128)(2,1)} %from_line_set.1.i0), channel_id=1, source_target_pairs={{0,8},{8,0},{16,24},{24,16},{1,9},{9,1},{17,25},{25,17},{2,10},{10... | collective-permute-start | bytes 1474568 | tf_op jit(solution)/shard_map/ppermute | solution.py:603
  89.5 5.1 %collective-permute-done.14.i1 = bf16[4,48,1280]{2,1,0:T(8,128)(2,1)S(1)} collective-permute-done((bf16[4,48,1280]{2,1,0:T(8,128)(2,1)}, bf16[4,48,1280]{2,1,0:T(8,128)(2,1)S(1)}, u32[]{:S(2)}, u32[]{:S(2)}) %collective-permute-start.14) | collective-permute-done | bytes 491552 | tf_op jit(solution)/shard_map/ppermute | solution.py:603
  94.7 4.5 %collective-permute-start.16 = (bf16[4,48,1280]{2,1,0:T(8,128)(2,1)S(1)}, bf16[4,48,1280]{2,1,0:T(8,128)(2,1)S(1)}, u32[]{:S(2)}, u32[]{:S(2)}) collective-permute-start(bf16[4,48,1280]{2,1,0:T(8,128)(2,1)S(1)} %collective-permute-done.14.i1), channel_id=1, source_target_pairs={{0,8},{8,0},{16,24},{24,16},{1,9},{9,1},{17,25},{25,17},{2,10},{10... | collective-permute-start | bytes 1474568 | tf_op jit(solution)/shard_map/ppermute | solution.py:603
  99.2 1.5 collective-permute-done.16.i3
  101.5 15.6 %middle_columns.1 = (bf16[20,64,2048]{2,1,0:T(8,128)(2,1)}, bf16[20,64,2048]{2,1,0:T(8,128)(2,1)}, bf16[4,48,1280]{2,1,0:T(8,128)(2,1)}, bf16[4,48,1280]{2,1,0:T...) custom-call(s32[3]{0:T(128)} %pad_add_fusion.where_ref, bf16[4,48,1280]{2,1,0:T(8,128)(2,1)} %from_line_set.1.i0, ...), custom_call_target="tpu_custom_call" | custom-call | bytes 57000000 | tf_op jit(solution)/shard_map/middle_columns/pallas_call | solution.py:299
  117.5 1.7 collective-permute-done.18
  119.2 1.2 add_convert_fusion
  122.7 6.2 %bypass_columns.3.bypass_ref = bf16[20,64,2048]{2,1,0:T(8,128)(2,1)} custom-call(f32[20]{0:T(128)} %broadcast_1_shift_ref.2.shift_ref, bf16[20,64,2048]{2,1,0:T(8,128)(2,1)} %get-tuple-element.62.source_ref, bf16[160,160]{1,0:T(8,128)(2,1)} %fusion.1.mixer_ref), custom_call_target="tpu_custom_call" | custom-call | bytes 18000000 | tf_op jit(solution)/shard_map/bypass_columns/pallas_call | solution.py:263
  128.9 3.9 %collective-permute-done.19.c_ref = bf16[4,48,1280]{2,1,0:T(8,128)(2,1)S(1)} collective-permute-done((bf16[4,48,1280]{2,1,0:T(8,128)(2,1)S(1)}, bf16[4,48,1280]{2,1,0:T(8,128)(2,1)S(1)}, u32[]{:S(2)}, u32[]{:S(2)}) %collective-permute-start.19) | collective-permute-done | bytes 491552 | tf_op jit(solution)/shard_map/ppermute | solution.py:603
  133.6 3.5 %to_lines.3 = bf16[8,48,1280]{2,1,0:T(8,128)(2,1)} custom-call(s32[3]{0:T(128)} %pad_add_fusion.where_ref, bf16[4,48,1280]{2,1,0:T(8,128)(2,1)} %get-tuple-element.58.a_ref, bf16[4,48,1280]{2,1,0:T(8,128)(2,1)} %collective-permute-done.17.b_ref, bf16[4,48,1280]{2,1,0:T(8,128)(2,1)} %copy-done.8, bf16[8,384,192]{2,1,0:T(8,128)(2,1)} %constant.28.clone.table_ref.refs_8_), custom_call_target="tpu_custom_call" | custom-call | bytes 9000000 | tf_op jit(solution)/shard_map/to_lines/pallas_call | solution.py:370
  137.1 19.8 %all_to_all.15.arrived_ref = bf16[8,48,1280]{2,1,0:T(8,128)(2,1)} all-to-all(bf16[8,48,1280]{2,1,0:T(8,128)(2,1)} %to_lines.3), channel_id=1, replica_groups=mesh['dp'=4,'gx'=4,'gy'=8] {'gy'}, dimensions={0} | all-to-all | bytes 1966080 | tf_op jit(solution)/shard_map/all_to_all | solution.py:634
  156.9 6.4 %back_modes.1 = (bf16[8,48,1280]{2,1,0:T(8,128)(2,1)}, bf16[2,120,128]{2,1,0:T(8,128)(2,1)}, bf16[2,120,128]{2,1,0:T(8,128)(2,1)}, bf16[2,120,128]{2,1,0:T(8,128)(2,1)}, bf16[2,120,128]{2,1,0:T(8,128)(2,1)}) custom-call(s32[3]{0:T(128)} %pad_add_fusion.where_ref, bf16[8,48,1280]{2,1,0:T(8,128)(2,1)} %all_to_all.15.arrived_ref, ...), custom_call_target="tpu_custom_call" | custom-call | bytes 15000000 | tf_op jit(solution)/shard_map/back_modes/pallas_call | solution.py:546
  163.3 4.2 %all-to-all-start.2 = ((bf16[8,48,1280]{2,1,0:T(8,128)(2,1)}), bf16[8,48,1280]{2,1,0:T(8,128)(2,1)}, u32[]{:S(2)}, u32[]{:S(2)}) async-start(bf16[8,48,1280]{2,1,0:T(8,128)(2,1)} %get-tuple-element.68), calls=%async_computation.2 | async-start | bytes 1966080 | tf_op jit(solution)/shard_map/all_to_all | solution.py:634
  167.5 5.2 %collective-permute-start.20 = (bf16[2,120,128]{2,1,0:T(8,128)(2,1)}, bf16[2,120,128]{2,1,0:T(8,128)(2,1)S(1)}, u32[]{:S(2)}, u32[]{:S(2)}) collective-permute-start(bf16[2,120,128]{2,1,0:T(8,128)(2,1)} %get-tuple-element.69), channel_id=1, source_target_pairs={{0,0},{8,32},{16,64},{24,96},{32,8},{40,40},{48,72},{56,104},{64,1... | collective-permute-start | bytes 184328 | tf_op jit(solution)/shard_map/ppermute | solution.py:643
  172.8 1.1 collective-permute-start.22
  173.9 2.2 %collective-permute-start.23 = (bf16[2,120,128]{2,1,0:T(8,128)(2,1)}, bf16[2,120,128]{2,1,0:T(8,128)(2,1)S(1)}, u32[]{:S(2)}, u32[]{:S(2)}) collective-permute-start(bf16[2,120,128]{2,1,0:T(8,128)(2,1)} %get-tuple-element.72), channel_id=1, source_target_pairs={{0,24},{8,56},{16,88},{24,120},{32,0},{40,32},{48,64},{56,96},{64,... | collective-permute-start | bytes 184328 | tf_op jit(solution)/shard_map/ppermute | solution.py:643
  176.1 2.6 %collective-permute-done.22.p2 = bf16[2,120,128]{2,1,0:T(8,128)(2,1)S(1)} collective-permute-done((bf16[2,120,128]{2,1,0:T(8,128)(2,1)}, bf16[2,120,128]{2,1,0:T(8,128)(2,1)S(1)}, u32[]{:S(2)}, u32[]{:S(2)}) %collective-permute-start.22) | collective-permute-done | bytes 61472 | tf_op jit(solution)/shard_map/ppermute | solution.py:643
  178.7 3.6 %collective-permute-done.23.p3 = bf16[2,120,128]{2,1,0:T(8,128)(2,1)S(1)} collective-permute-done((bf16[2,120,128]{2,1,0:T(8,128)(2,1)}, bf16[2,120,128]{2,1,0:T(8,128)(2,1)S(1)}, u32[]{:S(2)}, u32[]{:S(2)}) %collective-permute-start.23) | collective-permute-done | bytes 61472 | tf_op jit(solution)/shard_map/ppermute | solution.py:643
  182.3 3.1 %from_lines.1.i0 = bf16[4,48,1280]{2,1,0:T(8,128)(2,1)} custom-call(s32[3]{0:T(128)} %pad_add_fusion.where_ref, bf16[8,48,1280]{2,1,0:T(8,128)(2,1)} %all-to-all-done.2.modes_ref, bf16[8,384,192]{2,1,0:T(8,128)(2,1)} %constant.28.clone.table_ref.refs_8_), custom_call_target="tpu_custom_call" | custom-call | bytes 9000000 | tf_op jit(solution)/shard_map/from_lines/pallas_call | solution.py:370
  185.4 3.6 %collective-permute-start.24 = (bf16[4,48,1280]{2,1,0:T(8,128)(2,1)}, bf16[4,48,1280]{2,1,0:T(8,128)(2,1)S(1)}, u32[]{:S(2)}, u32[]{:S(2)}) collective-permute-start(bf16[4,48,1280]{2,1,0:T(8,128)(2,1)} %from_lines.1.i0), channel_id=1, source_target_pairs={{0,16},{8,24},{16,0},{24,8},{1,17},{9,25},{17,1},{25,9},{2,18},{10... | collective-permute-start | bytes 1474568 | tf_op jit(solution)/shard_map/ppermute | solution.py:603
  189.0 3.1 %collective-permute-start.25 = (bf16[4,48,1280]{2,1,0:T(8,128)(2,1)}, bf16[4,48,1280]{2,1,0:T(8,128)(2,1)S(1)}, u32[]{:S(2)}, u32[]{:S(2)}) collective-permute-start(bf16[4,48,1280]{2,1,0:T(8,128)(2,1)} %from_lines.1.i0), channel_id=1, source_target_pairs={{0,8},{8,0},{16,24},{24,16},{1,9},{9,1},{17,25},{25,17},{2,10},{10... | collective-permute-start | bytes 1474568 | tf_op jit(solution)/shard_map/ppermute | solution.py:603
  192.1 3.1 %outer_sum.1 = f32[3,20,40,128]{3,2,1,0:T(8,128)} custom-call(bf16[2,120,128]{2,1,0:T(8,128)(2,1)} %copy-done.18, bf16[2,120,128]{2,1,0:T(8,128)(2,1)} %copy-done.19, bf16[2,120,128]{2,1,0:T(8,128)(2,1)} %copy-done.20, bf16[2,120,128]{2,1,0:T(8,128)(2,1)} %copy-done.21), custom_call_target="tpu_custom_call" | custom-call | bytes 9000000 | tf_op jit(solution)/shard_map/outer_sum/pallas_call | solution.py:593
  195.2 1.8 collective-permute-done.24.i1
  197.0 4.3 %collective-permute-start.26 = (bf16[4,48,1280]{2,1,0:T(8,128)(2,1)S(1)}, bf16[4,48,1280]{2,1,0:T(8,128)(2,1)S(1)}, u32[]{:S(2)}, u32[]{:S(2)}) collective-permute-start(bf16[4,48,1280]{2,1,0:T(8,128)(2,1)S(1)} %collective-permute-done.24.i1), channel_id=1, source_target_pairs={{0,8},{8,0},{16,24},{24,16},{1,9},{9,1},{17,25},{25,17},{2,10},{10... | collective-permute-start | bytes 1474568 | tf_op jit(solution)/shard_map/ppermute | solution.py:603
  201.4 1.5 collective-permute-done.26.i3
  203.7 10.0 %end_columns.1 = bf16[20,64,2048]{2,1,0:T(8,128)(2,1)} custom-call(s32[3]{0:T(128)} %pad_add_fusion.where_ref, bf16[4,48,1280]{2,1,0:T(8,128)(2,1)} %from_lines.1.i0, bf16[4,48,1280]{2,1,0:T(8,128)(2,1)} %copy-done.4, bf16[4,48,1280]{2,1,0:T(8,128)(2,1)} %copy-done.6, bf16[4,48,1280]{2,1,0:T(8,128)(2,1)} %copy-done.10, ...), custom_call_target="tpu_custom_call" | custom-call | bytes 30000000 | tf_op jit(solution)/shard_map/end_columns/pallas_call | solution.py:317
  (73 shorter events, 10.3 us)
Async XLA Ops:
  0.6 21.2 %copy-start = (bf16[20,20]{1,0:T(8,128)(2,1)S(1)}, bf16[20,20]{1,0:T(8,128)(2,1)}, u32[]{:S(2)}) copy-start(bf16[20,20]{1,0:T(8,128)(2,1)} %param.12) | copy-start | bytes 2404
  0.6 21.2 %copy-start.3 = (bf16[160,20]{1,0:T(8,128)(2,1)S(1)}, bf16[160,20]{1,0:T(8,128)(2,1)}, u32[]{:S(2)}) copy-start(bf16[160,20]{1,0:T(8,128)(2,1)} %constant.24.clone) | copy-start | bytes 19204
  0.7 21.2 %copy-start.11 = (bf16[160,160]{1,0:T(8,128)(2,1)S(1)}, bf16[160,160]{1,0:T(8,128)(2,1)}, u32[]{:S(2)}) copy-start(bf16[160,160]{1,0:T(8,128)(2,1)} %constant.27.clone) | copy-start | bytes 153604
  0.7 13.7 %collective-permute-start = (bf16[3,20,20,2,128]{4,3,2,1,0:T(2,128)(2,1)}, bf16[3,20,20,2,128]{4,3,2,1,0:T(2,128)(2,1)S(1)}, u32[]{:S(2)}, u32[]{:S(2)}) collective-permute-start(bf16[3,20,20,2,128]{4,3,2,1,0:T(2,128)(2,1)} %param.11), channel_id=1, source_target_pairs={{0,0},{8,32},{16,64},{24,96},{32,72},{40,104},{48,8},{56,40},{64,1... | collective-permute-start | bytes 1843208 | tf_op jit(solution)/shard_map/ppermute | solution.py:652
  14.4 29.3 %copy-start.1 = (bf16[3,20,20,2,128]{4,3,2,1,0:T(2,128)(2,1)}, bf16[3,20,20,2,128]{4,3,2,1,0:T(2,128)(2,1)S(1)}, u32[]{:S(2)}) copy-start(bf16[3,20,20,2,128]{4,3,2,1,0:T(2,128)(2,1)S(1)} %collective-permute-done) | copy-start | bytes 1843204
  14.4 4.2 %collective-permute-start.2 = (bf16[4,48,1280]{2,1,0:T(8,128)(2,1)}, bf16[4,48,1280]{2,1,0:T(8,128)(2,1)S(1)}, u32[]{:S(2)}, u32[]{:S(2)}) collective-permute-start(bf16[4,48,1280]{2,1,0:T(8,128)(2,1)} %get-tuple-element.49), channel_id=1, source_target_pairs={{0,8},{8,0},{16,24},{24,16},{1,9},{9,1},{17,25},{25,17},{2,10},{10... | collective-permute-start | bytes 1474568 | tf_op jit(solution)/shard_map/ppermute | solution.py:603
  14.4 21.6 %collective-permute-start.4 = (bf16[3,20,20,2,128]{4,3,2,1,0:T(2,128)(2,1)S(1)}, bf16[3,20,20,2,128]{4,3,2,1,0:T(2,128)(2,1)}, u32[]{:S(2)}, u32[]{:S(2)}) collective-permute-start(bf16[3,20,20,2,128]{4,3,2,1,0:T(2,128)(2,1)S(1)} %collective-permute-done), channel_id=1, source_target_pairs={{32,0},{64,32},{96,64},{0,96},{33,1},{65,33},{97,65},{1,97},{34,2}... | collective-permute-start | bytes 1843208 | tf_op jit(solution)/shard_map/ppermute | solution.py:621
  18.6 17.4 %collective-permute-start.5 = (bf16[3,20,20,2,128]{4,3,2,1,0:T(2,128)(2,1)S(1)}, bf16[3,20,20,2,128]{4,3,2,1,0:T(2,128)(2,1)}, u32[]{:S(2)}, u32[]{:S(2)}) collective-permute-start(bf16[3,20,20,2,128]{4,3,2,1,0:T(2,128)(2,1)S(1)} %collective-permute-done), channel_id=1, source_target_pairs={{96,0},{0,32},{32,64},{64,96},{97,1},{1,33},{33,65},{65,97},{98,2}... | collective-permute-start | bytes 1843208 | tf_op jit(solution)/shard_map/ppermute | solution.py:621
  19.8 12.7 %collective-permute-start.3 = (bf16[4,48,1280]{2,1,0:T(8,128)(2,1)S(1)}, bf16[4,48,1280]{2,1,0:T(8,128)(2,1)}, u32[]{:S(2)}, u32[]{:S(2)}) collective-permute-start(bf16[4,48,1280]{2,1,0:T(8,128)(2,1)S(1)} %add_convert_fusion.1), channel_id=1, source_target_pairs={{0,16},{8,24},{16,0},{24,8},{1,17},{9,25},{17,1},{25,9},{2,18},{10... | collective-permute-start | bytes 1474568 | tf_op jit(solution)/shard_map/ppermute | solution.py:603
  21.2 11.3 %collective-permute-start.1 = (bf16[4,48,1280]{2,1,0:T(8,128)(2,1)}, bf16[4,48,1280]{2,1,0:T(8,128)(2,1)}, u32[]{:S(2)}, u32[]{:S(2)}) collective-permute-start(bf16[4,48,1280]{2,1,0:T(8,128)(2,1)} %get-tuple-element.47), channel_id=1, source_target_pairs={{0,8},{8,0},{16,24},{24,16},{1,9},{9,1},{17,25},{25,17},{2,10},{10... | collective-permute-start | bytes 1474568 | tf_op jit(solution)/shard_map/ppermute | solution.py:603
  35.9 24.1 %all-to-all-start = ((bf16[8,48,1280]{2,1,0:T(8,128)(2,1)}), bf16[8,48,1280]{2,1,0:T(8,128)(2,1)}, u32[]{:S(2)}, u32[]{:S(2)}) async-start(bf16[8,48,1280]{2,1,0:T(8,128)(2,1)} %to_lines.2), calls=%async_computation | async-start | bytes 1966080 | tf_op jit(solution)/shard_map/all_to_all | solution.py:634
  43.6 15.5 %collective-permute-start.6 = (bf16[3,20,20,2,128]{4,3,2,1,0:T(2,128)(2,1)S(1)}, bf16[3,20,20,2,128]{4,3,2,1,0:T(2,128)(2,1)S(1)}, u32[]{:S(2)}, u32[]{:S(2)}) collective-permute-start(bf16[3,20,20,2,128]{4,3,2,1,0:T(2,128)(2,1)S(1)} %collective-permute-done), channel_id=1, source_target_pairs={{64,0},{96,32},{0,64},{32,96},{65,1},{97,33},{1,65},{33,97},{66,2}... | collective-permute-start | bytes 1843208 | tf_op jit(solution)/shard_map/ppermute | solution.py:621
  59.2 0.9 copy-start.2
  65.5 8.0 %collective-permute-start.7 = (bf16[48,1280]{1,0:T(8,128)(2,1)}, bf16[48,1280]{1,0:T(8,128)(2,1)S(1)}, u32[]{:S(2)}, u32[]{:S(2)}) collective-permute-start(bf16[48,1280]{1,0:T(8,128)(2,1)} %bitcast.28), channel_id=1, source_target_pairs={{1,0},{0,1},{3,2},{2,3},{5,4},{4,5},{7,6},{6,7},{9,8},{8,9},{11,10... | collective-permute-start | bytes 368648 | tf_op jit(solution)/shard_map/ppermute | solution.py:626
  68.2 6.1 %collective-permute-start.10 = (bf16[48,1280]{1,0:T(8,128)(2,1)}, bf16[48,1280]{1,0:T(8,128)(2,1)S(1)}, u32[]{:S(2)}, u32[]{:S(2)}) collective-permute-start(bf16[48,1280]{1,0:T(8,128)(2,1)} %bitcast.29), channel_id=1, source_target_pairs={{4,0},{5,1},{6,2},{7,3},{0,4},{1,5},{2,6},{3,7},{12,8},{13,9},{14,... | collective-permute-start | bytes 368648 | tf_op jit(solution)/shard_map/ppermute | solution.py:629
  70.9 6.5 %collective-permute-start.12 = (bf16[48,1280]{1,0:T(8,128)(2,1)}, bf16[48,1280]{1,0:T(8,128)(2,1)S(1)}, u32[]{:S(2)}, u32[]{:S(2)}) collective-permute-start(bf16[48,1280]{1,0:T(8,128)(2,1)} %bitcast.30), channel_id=1, source_target_pairs={{6,0},{7,1},{0,2},{1,3},{2,4},{3,5},{4,6},{5,7},{14,8},{15,9},{8,1... | collective-permute-start | bytes 368648 | tf_op jit(solution)/shard_map/ppermute | solution.py:629
  71.2 7.2 %collective-permute-start.8 = (bf16[48,1280]{1,0:T(8,128)(2,1)}, bf16[48,1280]{1,0:T(8,128)(2,1)S(1)}, u32[]{:S(2)}, u32[]{:S(2)}) collective-permute-start(bf16[48,1280]{1,0:T(8,128)(2,1)} %bitcast.31), channel_id=1, source_target_pairs={{2,0},{3,1},{4,2},{5,3},{6,4},{7,5},{0,6},{1,7},{10,8},{11,9},{12,... | collective-permute-start | bytes 368648 | tf_op jit(solution)/shard_map/ppermute | solution.py:629
  73.5 8.5 %copy-start.12 = (bf16[48,1280]{1,0:T(8,128)(2,1)}, bf16[48,1280]{1,0:T(8,128)(2,1)S(1)}, u32[]{:S(2)}) copy-start(bf16[48,1280]{1,0:T(8,128)(2,1)S(1)} %collective-permute-done.7.refs_1_) | copy-start | bytes 368644
  73.5 6.3 %collective-permute-start.11 = (bf16[48,1280]{1,0:T(8,128)(2,1)S(1)}, bf16[48,1280]{1,0:T(8,128)(2,1)S(1)}, u32[]{:S(2)}, u32[]{:S(2)}) collective-permute-start(bf16[48,1280]{1,0:T(8,128)(2,1)S(1)} %collective-permute-done.7.refs_1_), channel_id=1, source_target_pairs={{4,0},{5,1},{6,2},{7,3},{0,4},{1,5},{2,6},{3,7},{12,8},{13,9},{14,... | collective-permute-start | bytes 368648 | tf_op jit(solution)/shard_map/ppermute | solution.py:629
  73.7 7.4 %collective-permute-start.13 = (bf16[48,1280]{1,0:T(8,128)(2,1)S(1)}, bf16[48,1280]{1,0:T(8,128)(2,1)S(1)}, u32[]{:S(2)}, u32[]{:S(2)}) collective-permute-start(bf16[48,1280]{1,0:T(8,128)(2,1)S(1)} %collective-permute-done.7.refs_1_), channel_id=1, source_target_pairs={{6,0},{7,1},{0,2},{1,3},{2,4},{3,5},{4,6},{5,7},{14,8},{15,9},{8,1... | collective-permute-start | bytes 368648 | tf_op jit(solution)/shard_map/ppermute | solution.py:629
  74.2 7.8 %copy-start.13 = (bf16[48,1280]{1,0:T(8,128)(2,1)}, bf16[48,1280]{1,0:T(8,128)(2,1)S(1)}, u32[]{:S(2)}) copy-start(bf16[48,1280]{1,0:T(8,128)(2,1)S(1)} %collective-permute-done.10.refs_4_) | copy-start | bytes 368644
  74.2 7.8 %collective-permute-start.9 = (bf16[48,1280]{1,0:T(8,128)(2,1)S(1)}, bf16[48,1280]{1,0:T(8,128)(2,1)}, u32[]{:S(2)}, u32[]{:S(2)}) collective-permute-start(bf16[48,1280]{1,0:T(8,128)(2,1)S(1)} %collective-permute-done.7.refs_1_), channel_id=1, source_target_pairs={{2,0},{3,1},{4,2},{5,3},{6,4},{7,5},{0,6},{1,7},{10,8},{11,9},{12,... | collective-permute-start | bytes 368648 | tf_op jit(solution)/shard_map/ppermute | solution.py:629
  77.3 4.7 %copy-start.14 = (bf16[48,1280]{1,0:T(8,128)(2,1)}, bf16[48,1280]{1,0:T(8,128)(2,1)S(1)}, u32[]{:S(2)}) copy-start(bf16[48,1280]{1,0:T(8,128)(2,1)S(1)} %collective-permute-done.12.refs_6_) | copy-start | bytes 368644
  78.4 3.7 %copy-start.15 = (bf16[48,1280]{1,0:T(8,128)(2,1)}, bf16[48,1280]{1,0:T(8,128)(2,1)S(1)}, u32[]{:S(2)}) copy-start(bf16[48,1280]{1,0:T(8,128)(2,1)S(1)} %collective-permute-done.8.refs_2_) | copy-start | bytes 368644
  79.9 2.2 %copy-start.16 = (bf16[48,1280]{1,0:T(8,128)(2,1)}, bf16[48,1280]{1,0:T(8,128)(2,1)S(1)}, u32[]{:S(2)}) copy-start(bf16[48,1280]{1,0:T(8,128)(2,1)S(1)} %collective-permute-done.11.refs_5_) | copy-start | bytes 368644
  81.1 1.0 copy-start.17
  85.3 9.3 %collective-permute-start.14 = (bf16[4,48,1280]{2,1,0:T(8,128)(2,1)}, bf16[4,48,1280]{2,1,0:T(8,128)(2,1)S(1)}, u32[]{:S(2)}, u32[]{:S(2)}) collective-permute-start(bf16[4,48,1280]{2,1,0:T(8,128)(2,1)} %from_line_set.1.i0), channel_id=1, source_target_pairs={{0,16},{8,24},{16,0},{24,8},{1,17},{9,25},{17,1},{25,9},{2,18},{10... | collective-permute-start | bytes 1474568 | tf_op jit(solution)/shard_map/ppermute | solution.py:603
  85.5 13.7 %collective-permute-start.15 = (bf16[4,48,1280]{2,1,0:T(8,128)(2,1)}, bf16[4,48,1280]{2,1,0:T(8,128)(2,1)S(1)}, u32[]{:S(2)}, u32[]{:S(2)}) collective-permute-start(bf16[4,48,1280]{2,1,0:T(8,128)(2,1)} %from_line_set.1.i0), channel_id=1, source_target_pairs={{0,8},{8,0},{16,24},{24,16},{1,9},{9,1},{17,25},{25,17},{2,10},{10... | collective-permute-start | bytes 1474568 | tf_op jit(solution)/shard_map/ppermute | solution.py:603
  94.7 6.0 %copy-start.5 = (bf16[4,48,1280]{2,1,0:T(8,128)(2,1)}, bf16[4,48,1280]{2,1,0:T(8,128)(2,1)S(1)}, u32[]{:S(2)}) copy-start(bf16[4,48,1280]{2,1,0:T(8,128)(2,1)S(1)} %collective-permute-done.14.i1) | copy-start | bytes 1474564
  94.7 6.0 %collective-permute-start.16 = (bf16[4,48,1280]{2,1,0:T(8,128)(2,1)S(1)}, bf16[4,48,1280]{2,1,0:T(8,128)(2,1)S(1)}, u32[]{:S(2)}, u32[]{:S(2)}) collective-permute-start(bf16[4,48,1280]{2,1,0:T(8,128)(2,1)S(1)} %collective-permute-done.14.i1), channel_id=1, source_target_pairs={{0,8},{8,0},{16,24},{24,16},{1,9},{9,1},{17,25},{25,17},{2,10},{10... | collective-permute-start | bytes 1474568 | tf_op jit(solution)/shard_map/ppermute | solution.py:603
  99.2 1.5 copy-start.7
  117.0 2.2 %collective-permute-start.18 = (bf16[4,48,1280]{2,1,0:T(8,128)(2,1)}, bf16[4,48,1280]{2,1,0:T(8,128)(2,1)S(1)}, u32[]{:S(2)}, u32[]{:S(2)}) collective-permute-start(bf16[4,48,1280]{2,1,0:T(8,128)(2,1)} %get-tuple-element.61), channel_id=1, source_target_pairs={{0,8},{8,0},{16,24},{24,16},{1,9},{9,1},{17,25},{25,17},{2,10},{10... | collective-permute-start | bytes 1474568 | tf_op jit(solution)/shard_map/ppermute | solution.py:603
  120.4 12.5 %collective-permute-start.19 = (bf16[4,48,1280]{2,1,0:T(8,128)(2,1)S(1)}, bf16[4,48,1280]{2,1,0:T(8,128)(2,1)S(1)}, u32[]{:S(2)}, u32[]{:S(2)}) collective-permute-start(bf16[4,48,1280]{2,1,0:T(8,128)(2,1)S(1)} %add_convert_fusion), channel_id=1, source_target_pairs={{0,16},{8,24},{16,0},{24,8},{1,17},{9,25},{17,1},{25,9},{2,18},{10... | collective-permute-start | bytes 1474568 | tf_op jit(solution)/shard_map/ppermute | solution.py:603
  120.6 12.3 %collective-permute-start.17 = (bf16[4,48,1280]{2,1,0:T(8,128)(2,1)}, bf16[4,48,1280]{2,1,0:T(8,128)(2,1)}, u32[]{:S(2)}, u32[]{:S(2)}) collective-permute-start(bf16[4,48,1280]{2,1,0:T(8,128)(2,1)} %get-tuple-element.59), channel_id=1, source_target_pairs={{0,8},{8,0},{16,24},{24,16},{1,9},{9,1},{17,25},{25,17},{2,10},{10... | collective-permute-start | bytes 1474568 | tf_op jit(solution)/shard_map/ppermute | solution.py:603
  163.3 19.0 %all-to-all-start.2 = ((bf16[8,48,1280]{2,1,0:T(8,128)(2,1)}), bf16[8,48,1280]{2,1,0:T(8,128)(2,1)}, u32[]{:S(2)}, u32[]{:S(2)}) async-start(bf16[8,48,1280]{2,1,0:T(8,128)(2,1)} %get-tuple-element.68), calls=%async_computation.2 | async-start | bytes 1966080 | tf_op jit(solution)/shard_map/all_to_all | solution.py:634
  167.5 8.6 %collective-permute-start.20 = (bf16[2,120,128]{2,1,0:T(8,128)(2,1)}, bf16[2,120,128]{2,1,0:T(8,128)(2,1)S(1)}, u32[]{:S(2)}, u32[]{:S(2)}) collective-permute-start(bf16[2,120,128]{2,1,0:T(8,128)(2,1)} %get-tuple-element.69), channel_id=1, source_target_pairs={{0,0},{8,32},{16,64},{24,96},{32,8},{40,40},{48,72},{56,104},{64,1... | collective-permute-start | bytes 184328 | tf_op jit(solution)/shard_map/ppermute | solution.py:643
  172.7 3.4 %collective-permute-start.21 = (bf16[2,120,128]{2,1,0:T(8,128)(2,1)}, bf16[2,120,128]{2,1,0:T(8,128)(2,1)S(1)}, u32[]{:S(2)}, u32[]{:S(2)}) collective-permute-start(bf16[2,120,128]{2,1,0:T(8,128)(2,1)} %get-tuple-element.70), channel_id=1, source_target_pairs={{0,8},{8,40},{16,72},{24,104},{32,16},{40,48},{48,80},{56,112},{64... | collective-permute-start | bytes 184328 | tf_op jit(solution)/shard_map/ppermute | solution.py:643
  172.8 5.9 %collective-permute-start.22 = (bf16[2,120,128]{2,1,0:T(8,128)(2,1)}, bf16[2,120,128]{2,1,0:T(8,128)(2,1)S(1)}, u32[]{:S(2)}, u32[]{:S(2)}) collective-permute-start(bf16[2,120,128]{2,1,0:T(8,128)(2,1)} %get-tuple-element.71), channel_id=1, source_target_pairs={{0,16},{8,48},{16,80},{24,112},{32,24},{40,56},{48,88},{56,120},{6... | collective-permute-start | bytes 184328 | tf_op jit(solution)/shard_map/ppermute | solution.py:643
  173.9 8.4 %collective-permute-start.23 = (bf16[2,120,128]{2,1,0:T(8,128)(2,1)}, bf16[2,120,128]{2,1,0:T(8,128)(2,1)S(1)}, u32[]{:S(2)}, u32[]{:S(2)}) collective-permute-start(bf16[2,120,128]{2,1,0:T(8,128)(2,1)} %get-tuple-element.72), channel_id=1, source_target_pairs={{0,24},{8,56},{16,88},{24,120},{32,0},{40,32},{48,64},{56,96},{64,... | collective-permute-start | bytes 184328 | tf_op jit(solution)/shard_map/ppermute | solution.py:643
  176.1 16.0 %copy-start.18 = (bf16[2,120,128]{2,1,0:T(8,128)(2,1)}, bf16[2,120,128]{2,1,0:T(8,128)(2,1)S(1)}, u32[]{:S(2)}) copy-start(bf16[2,120,128]{2,1,0:T(8,128)(2,1)S(1)} %collective-permute-done.20.p0) | copy-start | bytes 184324
  176.1 16.0 %copy-start.19 = (bf16[2,120,128]{2,1,0:T(8,128)(2,1)}, bf16[2,120,128]{2,1,0:T(8,128)(2,1)S(1)}, u32[]{:S(2)}) copy-start(bf16[2,120,128]{2,1,0:T(8,128)(2,1)S(1)} %collective-permute-done.21.p1) | copy-start | bytes 184324
  178.7 13.3 %copy-start.20 = (bf16[2,120,128]{2,1,0:T(8,128)(2,1)}, bf16[2,120,128]{2,1,0:T(8,128)(2,1)S(1)}, u32[]{:S(2)}) copy-start(bf16[2,120,128]{2,1,0:T(8,128)(2,1)S(1)} %collective-permute-done.22.p2) | copy-start | bytes 184324
  182.3 9.8 %copy-start.21 = (bf16[2,120,128]{2,1,0:T(8,128)(2,1)}, bf16[2,120,128]{2,1,0:T(8,128)(2,1)S(1)}, u32[]{:S(2)}) copy-start(bf16[2,120,128]{2,1,0:T(8,128)(2,1)S(1)} %collective-permute-done.23.p3) | copy-start | bytes 184324
  185.4 11.6 %collective-permute-start.24 = (bf16[4,48,1280]{2,1,0:T(8,128)(2,1)}, bf16[4,48,1280]{2,1,0:T(8,128)(2,1)S(1)}, u32[]{:S(2)}, u32[]{:S(2)}) collective-permute-start(bf16[4,48,1280]{2,1,0:T(8,128)(2,1)} %from_lines.1.i0), channel_id=1, source_target_pairs={{0,16},{8,24},{16,0},{24,8},{1,17},{9,25},{17,1},{25,9},{2,18},{10... | collective-permute-start | bytes 1474568 | tf_op jit(solution)/shard_map/ppermute | solution.py:603
  189.0 12.4 %collective-permute-start.25 = (bf16[4,48,1280]{2,1,0:T(8,128)(2,1)}, bf16[4,48,1280]{2,1,0:T(8,128)(2,1)S(1)}, u32[]{:S(2)}, u32[]{:S(2)}) collective-permute-start(bf16[4,48,1280]{2,1,0:T(8,128)(2,1)} %from_lines.1.i0), channel_id=1, source_target_pairs={{0,8},{8,0},{16,24},{24,16},{1,9},{9,1},{17,25},{25,17},{2,10},{10... | collective-permute-start | bytes 1474568 | tf_op jit(solution)/shard_map/ppermute | solution.py:603
  197.0 5.8 %copy-start.4 = (bf16[4,48,1280]{2,1,0:T(8,128)(2,1)}, bf16[4,48,1280]{2,1,0:T(8,128)(2,1)S(1)}, u32[]{:S(2)}) copy-start(bf16[4,48,1280]{2,1,0:T(8,128)(2,1)S(1)} %collective-permute-done.24.i1) | copy-start | bytes 1474564
  197.0 5.8 %collective-permute-start.26 = (bf16[4,48,1280]{2,1,0:T(8,128)(2,1)S(1)}, bf16[4,48,1280]{2,1,0:T(8,128)(2,1)S(1)}, u32[]{:S(2)}, u32[]{:S(2)}) collective-permute-start(bf16[4,48,1280]{2,1,0:T(8,128)(2,1)S(1)} %collective-permute-done.24.i1), channel_id=1, source_target_pairs={{0,8},{8,0},{16,24},{24,16},{1,9},{9,1},{17,25},{25,17},{2,10},{10... | collective-permute-start | bytes 1474568 | tf_op jit(solution)/shard_map/ppermute | solution.py:603
  201.4 1.5 copy-start.6
  (3 other events, 2.4 us)

commit v8 on v7

--- a/solution.py
+++ b/solution.py
@@ -138,16 +138,19 @@
             outs[pos][y] = piece.astype(BF)
 
 
-def inverse_group(ins, depth_ref, long_ref, y):
+def inverse_runs(ins, depth_ref, long_ref, runs):
     part = KB * YB
-    pieces = [ref[y].astype(F32) for ref in ins]
-    real = jnp.concatenate([piece[:part] for piece in pieces], axis=0)
-    imag = jnp.concatenate([piece[part:] for piece in pieces], axis=0)
-    sides = jnp.concatenate(
-        [jnp.concatenate([real, -imag], axis=1), jnp.concatenate([imag, real], axis=1)], axis=0
-    ).astype(BF)
-    planes = dot(long_ref[...], sides, 1, 1).astype(BF)
-    return dot(planes, depth_ref[...])
+    planes = []
+    for y in runs:
+        pieces = [ref[y].astype(F32) for ref in ins]
+        real = jnp.concatenate([piece[:part] for piece in pieces], axis=0)
+        imag = jnp.concatenate([piece[part:] for piece in pieces], axis=0)
+        sides = jnp.concatenate(
+            [jnp.concatenate([real, -imag], axis=1), jnp.concatenate([imag, real], axis=1)],
+            axis=0,
+        ).astype(BF)
+        planes.append(dot(long_ref[...], sides, 1, 1).astype(BF))
+    return dot(jnp.concatenate(planes, axis=0), depth_ref[...])
 
 
 def run_rows(ref, y):
@@ -200,21 +203,26 @@
     def _():
         fill_tables(strip_ref, wide_ref, depth_ref, tall_ref, long_ref)
 
-    def inverse(y):
-        values = inverse_group((i0, i1, i2, i3), depth_ref, long_ref, y)
-        lanes = slice(LANES * y, LANES * (y + 1))
-        total_ref[y] = bypass_ref[:, :, lanes].astype(F32) + values.reshape(GROUP, XL, LANES)
+    def inverse(*runs):
+        values = inverse_runs((i0, i1, i2, i3), depth_ref, long_ref, runs)
+        for n, y in enumerate(runs):
+            lanes = slice(LANES * y, LANES * (y + 1))
+            own = values[GL * n : GL * (n + 1)].reshape(GROUP, XL, LANES)
+            total_ref[y] = bypass_ref[:, :, lanes].astype(F32) + own
 
     def forward(*runs):
         forward_runs(grad_ref, depth_ref, tall_ref, (o0, o1, o2, o3), runs)
 
-    inverse(0)
-    for y in range(STEPS):
-        if y + 1 < STEPS:
-            inverse(y + 1)
+    def activation(y):
         activate(upstream_ref, total_ref, act_ref, grad_ref, y)
-        if y == 2:
-            forward(0, 1)
+
+    inverse(0, 1)
+    activation(0)
+    inverse(2, 3)
+    activation(1)
+    activation(2)
+    forward(0, 1)
+    activation(3)
     forward(2, 3)
 
 
@@ -226,12 +234,13 @@
     def _():
         fill_tables(strip_ref, wide_ref, depth_ref, tall_ref, long_ref)
 
-    for y in range(STEPS):
-        values = inverse_group((i0, i1, i2, i3), depth_ref, long_ref, y)
-        lanes = slice(LANES * y, LANES * (y + 1))
-        out_ref[:, :, lanes] = (
-            bypass_ref[:, :, lanes].astype(F32) + values.reshape(GROUP, XL, LANES)
-        ).astype(BF)
+    for first in range(0, STEPS, 2):
+        runs = (first, first + 1)
+        values = inverse_runs((i0, i1, i2, i3), depth_ref, long_ref, runs)
+        for n, y in enumerate(runs):
+            lanes = slice(LANES * y, LANES * (y + 1))
+            own = values[GL * n : GL * (n + 1)].reshape(GROUP, XL, LANES)
+            out_ref[:, :, lanes] = (bypass_ref[:, :, lanes].astype(F32) + own).astype(BF)
 
 
 def cost(micros):
@@ -255,7 +264,7 @@
 ]
 TOTAL = pltpu.VMEM((STEPS, GROUP, XL, LANES), F32)
 PARAMS = pltpu.CompilerParams(vmem_limit_bytes=56 * 1024 * 1024)
-ALONE = pltpu.CompilerParams(vmem_limit_bytes=63 * 1024 * 1024)
+ALONE = pltpu.CompilerParams(vmem_limit_bytes=67_043_328)
 
 
 def bypass_columns(source, mixer, shift):
@@ -324,7 +333,7 @@
             scratch_shapes=BLOCKS,
         ),
         out_shape=COLUMNS,
-        compiler_params=PARAMS,
+        compiler_params=ALONE,
         cost_estimate=cost(10),
         name="end_columns",
     )(where, *coeffs_in, bypass, jnp.asarray(DEPTH), jnp.asarray(WIDTH))

time: 215 us -> 213 us (level)
    ppermute x12, starting transfers between devices: 23.2 us -> 26.3 us  [swap(): return lax.ppermute(values, 'gx', [(i, i ^ bit) for i in range(GX)])]
    ppermute x3, starting transfers between devices: 7.02 us -> 4.65 us  [gather_weights(): lax.ppermute(weight, 'dp', [((a + k) % DP, a) for a in range(DP)])]
  transfers between devices with their start and end apart: 29 -> 29, of which waited for: 16 -> 16; matrix products, arithmetic and copies ran while one was open for 2% -> 2% of each run, Pallas kernels for 12% -> 13%
where the time goes in v8:
time: 213 us; the launch traced here: 212 us
  Pallas kernels  73.1 us (34%)
  starting transfers between devices  67.3 us (32%)
  waiting for transfers between devices  43.1 us (20%)
  blocking collectives  19.9 us (9%)
  other arithmetic  2.85 us (1%)
  local copies, waits for them, and re-layouts  2.77 us (1%)
    ppermute x12, starting transfers between devices, swap(): return lax.ppermute(values, 'gx', [(i, i ^ bit) for i in range(GX)])  26.3 us
    all_to_all x1, blocking collectives, exchange_lines(): return lax.all_to_all(parts, 'gy', split_axis=0, concat_axis=0, tiled=True)  19.9 us
    ppermute x12, waiting for transfers between devices, swap(): return lax.ppermute(values, 'gx', [(i, i ^ bit) for i in range(GX)])  18.3 us
    pallas_call x1, Pallas kernels, middle_columns(): pl.pallas_call(middle_kernel, grid_spec=pltpu.PrefetchScalarGridSpec(num_...  15.4 us
    pallas_call x4, Pallas kernels, line_call(): pl.pallas_call(kernel, grid_spec=pltpu.PrefetchScalarGridSpec(num_scalar_...  13.3 us
    ppermute x3, waiting for transfers between devices, gather_weights(): lax.ppermute(weight, 'dp', [((a + k) % DP, a) for a in range(DP)])  12.8 us
    pallas_call x2, Pallas kernels, bypass_columns(): pl.pallas_call(bypass_kernel, grid=(STEPS,), in_specs=[pl.BlockSpec(memor...  12.5 us
    all_to_all x2, starting transfers between devices, exchange_lines(): return lax.all_to_all(parts, 'gy', split_axis=0, concat_axis=0, tiled=True)  11.8 us
  transfers between devices with their start and end apart: 29, of which 16 were waited for; matrix products, arithmetic and copies ran while one was open for 2% of the time, Pallas kernels for 13%

profile of v8, /device:TPU:1, one launch (start us, length us, event | category | flops | bytes accessed | tf_op | source)
XLA Modules:
  0.0 211.6 jit_solution(12838084857033472797)
XLA Ops:
  0.7 4.6 %collective-permute-start = (bf16[3,20,20,2,128]{4,3,2,1,0:T(2,128)(2,1)}, bf16[3,20,20,2,128]{4,3,2,1,0:T(2,128)(2,1)}, u32[]{:S(2)}, u32[]{:S(2)}) collective-permute-start(bf16[3,20,20,2,128]{4,3,2,1,0:T(2,128)(2,1)} %param.11), channel_id=1, source_target_pairs={{0,0},{8,32},{16,64},{24,96},{32,72},{40,104},{48,8},{56,40},{64,1... | collective-permute-start | bytes 1843208 | tf_op jit(solution)/shard_map/ppermute | solution.py:661
  5.9 7.6 %start_columns.1 = (bf16[4,48,1280]{2,1,0:T(8,128)(2,1)}, bf16[4,48,1280]{2,1,0:T(8,128)(2,1)}, bf16[4,48,1280]{2,1,0:T(8,128)(2,1)}, bf16[4,48,1280]{2,1,0:T(8,128)(2,1)}) custom-call(s32[3]{0:T(128)} %pad_add_fusion.where_ref, bf16[20,64,2048]{2,1,0:T(8,128)(2,1)} %bitcast.19, bf16[4,24,512]{2,1,0:T(8,128)(2,1)} %constant.25.clone.strip_ref, ...), custom_call_target="tpu_custom_call" | custom-call | bytes 24000000 | tf_op jit(solution)/shard_map/start_columns/pallas_call | solution.py:290
  13.5 1.0 collective-permute-done
  14.5 2.4 %collective-permute-start.2 = (bf16[4,48,1280]{2,1,0:T(8,128)(2,1)}, bf16[4,48,1280]{2,1,0:T(8,128)(2,1)S(1)}, u32[]{:S(2)}, u32[]{:S(2)}) collective-permute-start(bf16[4,48,1280]{2,1,0:T(8,128)(2,1)} %get-tuple-element.49), channel_id=1, source_target_pairs={{0,8},{8,0},{16,24},{24,16},{1,9},{9,1},{17,25},{25,17},{2,10},{10... | collective-permute-start | bytes 1474568 | tf_op jit(solution)/shard_map/ppermute | solution.py:612
  16.9 1.8 collective-permute-start.4
  18.7 1.1 add_convert_fusion.1
  19.8 1.5 collective-permute-start.3
  22.9 6.2 %bypass_columns.2.bypass_ref = bf16[20,64,2048]{2,1,0:T(8,128)(2,1)} custom-call(f32[20]{0:T(128)} %shift_ref.1, bf16[20,64,2048]{2,1,0:T(8,128)(2,1)} %bitcast.20, bf16[160,160]{1,0:T(8,128)(2,1)} %fusion.mixer_ref), custom_call_target="tpu_custom_call" | custom-call | bytes 18000000 | tf_op jit(solution)/shard_map/bypass_columns/pallas_call | solution.py:272
  29.1 3.5 %collective-permute-done.3.c_ref = bf16[4,48,1280]{2,1,0:T(8,128)(2,1)} collective-permute-done((bf16[4,48,1280]{2,1,0:T(8,128)(2,1)S(1)}, bf16[4,48,1280]{2,1,0:T(8,128)(2,1)}, u32[]{:S(2)}, u32[]{:S(2)}) %collective-permute-start.3) | collective-permute-done | bytes 491552 | tf_op jit(solution)/shard_map/ppermute | solution.py:612
  32.5 3.5 %to_lines.2 = bf16[8,48,1280]{2,1,0:T(8,128)(2,1)} custom-call(s32[3]{0:T(128)} %pad_add_fusion.where_ref, bf16[4,48,1280]{2,1,0:T(8,128)(2,1)} %get-tuple-element.46.a_ref, bf16[4,48,1280]{2,1,0:T(8,128)(2,1)} %collective-permute-done.1.b_ref, bf16[4,48,1280]{2,1,0:T(8,128)(2,1)} %collective-permute-done.3.c_ref, ...), custom_call_target="tpu_custom_call" | custom-call | bytes 9000000 | tf_op jit(solution)/shard_map/to_lines/pallas_call | solution.py:379
  36.0 7.6 %all-to-all-start = ((bf16[8,48,1280]{2,1,0:T(8,128)(2,1)}), bf16[8,48,1280]{2,1,0:T(8,128)(2,1)}, u32[]{:S(2)}, u32[]{:S(2)}) async-start(bf16[8,48,1280]{2,1,0:T(8,128)(2,1)} %to_lines.2), calls=%async_computation | async-start | bytes 1966080 | tf_op jit(solution)/shard_map/all_to_all | solution.py:643
  43.6 2.9 %collective-permute-start.6 = (bf16[3,20,20,2,128]{4,3,2,1,0:T(2,128)(2,1)}, bf16[3,20,20,2,128]{4,3,2,1,0:T(2,128)(2,1)}, u32[]{:S(2)}, u32[]{:S(2)}) collective-permute-start(bf16[3,20,20,2,128]{4,3,2,1,0:T(2,128)(2,1)} %collective-permute-done), channel_id=1, source_target_pairs={{64,0},{96,32},{0,64},{32,96},{65,1},{97,33},{1,65},{33,97},{66,2}... | collective-permute-start | bytes 1843208 | tf_op jit(solution)/shard_map/ppermute | solution.py:630
  46.4 12.8 %collective-permute-done.6 = bf16[3,20,20,2,128]{4,3,2,1,0:T(2,128)(2,1)} collective-permute-done((bf16[3,20,20,2,128]{4,3,2,1,0:T(2,128)(2,1)}, bf16[3,20,20,2,128]{4,3,2,1,0:T(2,128)(2,1)}, u32[]{:S(2)}, u32[]{:S(2)}) %collective-permute-start.6) | collective-permute-done | bytes 614432 | tf_op jit(solution)/shard_map/ppermute | solution.py:630
  59.2 5.5 %mix_modes.1 = (bf16[1,48,1280]{2,1,0:T(8,128)(2,1)}, bf16[1,120,128]{2,1,0:T(8,128)(2,1)}, bf16[1,120,128]{2,1,0:T(8,128)(2,1)}, bf16[1,120,128]{2,1,0:T(8,128)(2,1)}, bf16[1,120,128]{2,1,0:T(8,128)(2,1)}) custom-call(s32[3]{0:T(128)} %pad_add_fusion.where_ref, bf16[8,48,1280]{2,1,0:T(8,128)(2,1)} %all-to-all-done.arrived_ref, ...), custom_call_target="tpu_custom_call" | custom-call | bytes 15000000 | tf_op jit(solution)/shard_map/mix_modes/pallas_call | solution.py:555
  64.7 2.8 %collective-permute-start.7 = (bf16[48,1280]{1,0:T(8,128)(2,1)}, bf16[48,1280]{1,0:T(8,128)(2,1)S(1)}, u32[]{:S(2)}, u32[]{:S(2)}) collective-permute-start(bf16[48,1280]{1,0:T(8,128)(2,1)} %bitcast.24), channel_id=1, source_target_pairs={{1,0},{0,1},{3,2},{2,3},{5,4},{4,5},{7,6},{6,7},{9,8},{8,9},{11,10... | collective-permute-start | bytes 368648 | tf_op jit(solution)/shard_map/ppermute | solution.py:635
  67.5 2.7 %collective-permute-start.10 = (bf16[48,1280]{1,0:T(8,128)(2,1)}, bf16[48,1280]{1,0:T(8,128)(2,1)S(1)}, u32[]{:S(2)}, u32[]{:S(2)}) collective-permute-start(bf16[48,1280]{1,0:T(8,128)(2,1)} %bitcast.25), channel_id=1, source_target_pairs={{4,0},{5,1},{6,2},{7,3},{0,4},{1,5},{2,6},{3,7},{12,8},{13,9},{14,... | collective-permute-start | bytes 368648 | tf_op jit(solution)/shard_map/ppermute | solution.py:638
  70.4 2.4 %collective-permute-start.8 = (bf16[48,1280]{1,0:T(8,128)(2,1)}, bf16[48,1280]{1,0:T(8,128)(2,1)S(1)}, u32[]{:S(2)}, u32[]{:S(2)}) collective-permute-start(bf16[48,1280]{1,0:T(8,128)(2,1)} %bitcast.27), channel_id=1, source_target_pairs={{2,0},{3,1},{4,2},{5,3},{6,4},{7,5},{0,6},{1,7},{10,8},{11,9},{12,... | collective-permute-start | bytes 368648 | tf_op jit(solution)/shard_map/ppermute | solution.py:638
  73.5 2.2 %collective-permute-start.9 = (bf16[48,1280]{1,0:T(8,128)(2,1)S(1)}, bf16[48,1280]{1,0:T(8,128)(2,1)}, u32[]{:S(2)}, u32[]{:S(2)}) collective-permute-start(bf16[48,1280]{1,0:T(8,128)(2,1)S(1)} %collective-permute-done.7.refs_1_), channel_id=1, source_target_pairs={{2,0},{3,1},{4,2},{5,3},{6,4},{7,5},{0,6},{1,7},{10,8},{11,9},{12,... | collective-permute-start | bytes 368648 | tf_op jit(solution)/shard_map/ppermute | solution.py:638
  75.6 1.1 collective-permute-done.12.refs_6_
  77.6 1.5 collective-permute-done.11.refs_5_
  79.1 1.2 collective-permute-done.13.refs_7_
  81.2 3.3 %from_line_set.1.i0 = bf16[4,48,1280]{2,1,0:T(8,128)(2,1)} custom-call(s32[3]{0:T(128)} %pad_add_fusion.where_ref, bf16[48,1280]{1,0:T(8,128)(2,1)} %bitcast.28, bf16[48,1280]{1,0:T(8,128)(2,1)} %copy-done.8, bf16[48,1280]{1,0:T(8,128)(2,1)} %copy-done.11, bf16[48,1280]{1,0:T(8,128)(2,1)} %collective-permute-done.9.refs_3_, bf16[48,1280]{1,0:T(8,128)(2,1)} %copy-done.9, ...), custom_call_target="tpu_custom_call" | custom-call | bytes 9000000 | tf_op jit(solution)/shard_map/from_line_set/pallas_call | solution.py:379
  85.0 4.1 %collective-permute-start.15 = (bf16[4,48,1280]{2,1,0:T(8,128)(2,1)}, bf16[4,48,1280]{2,1,0:T(8,128)(2,1)S(1)}, u32[]{:S(2)}, u32[]{:S(2)}) collective-permute-start(bf16[4,48,1280]{2,1,0:T(8,128)(2,1)} %from_line_set.1.i0), channel_id=1, source_target_pairs={{0,8},{8,0},{16,24},{24,16},{1,9},{9,1},{17,25},{25,17},{2,10},{10... | collective-permute-start | bytes 1474568 | tf_op jit(solution)/shard_map/ppermute | solution.py:612
  89.1 4.4 %collective-permute-done.14.i1 = bf16[4,48,1280]{2,1,0:T(8,128)(2,1)S(1)} collective-permute-done((bf16[4,48,1280]{2,1,0:T(8,128)(2,1)}, bf16[4,48,1280]{2,1,0:T(8,128)(2,1)S(1)}, u32[]{:S(2)}, u32[]{:S(2)}) %collective-permute-start.14) | collective-permute-done | bytes 491552 | tf_op jit(solution)/shard_map/ppermute | solution.py:612
  93.5 4.8 %collective-permute-start.16 = (bf16[4,48,1280]{2,1,0:T(8,128)(2,1)S(1)}, bf16[4,48,1280]{2,1,0:T(8,128)(2,1)S(1)}, u32[]{:S(2)}, u32[]{:S(2)}) collective-permute-start(bf16[4,48,1280]{2,1,0:T(8,128)(2,1)S(1)} %collective-permute-done.14.i1), channel_id=1, source_target_pairs={{0,8},{8,0},{16,24},{24,16},{1,9},{9,1},{17,25},{25,17},{2,10},{10... | collective-permute-start | bytes 1474568 | tf_op jit(solution)/shard_map/ppermute | solution.py:612
  98.3 1.5 collective-permute-done.16.i3
  100.6 15.4 %middle_columns.1 = (bf16[20,64,2048]{2,1,0:T(8,128)(2,1)}, bf16[20,64,2048]{2,1,0:T(8,128)(2,1)}, bf16[4,48,1280]{2,1,0:T(8,128)(2,1)}, bf16[4,48,1280]{2,1,0:T...) custom-call(s32[3]{0:T(128)} %pad_add_fusion.where_ref, bf16[4,48,1280]{2,1,0:T(8,128)(2,1)} %from_line_set.1.i0, ...), custom_call_target="tpu_custom_call" | custom-call | bytes 57000000 | tf_op jit(solution)/shard_map/middle_columns/pallas_call | solution.py:308
  116.4 1.7 collective-permute-done.18
  118.1 1.1 add_convert_fusion
  122.0 6.3 %bypass_columns.3.bypass_ref = bf16[20,64,2048]{2,1,0:T(8,128)(2,1)} custom-call(f32[20]{0:T(128)} %broadcast_1_shift_ref.2.shift_ref, bf16[20,64,2048]{2,1,0:T(8,128)(2,1)} %get-tuple-element.62.source_ref, bf16[160,160]{1,0:T(8,128)(2,1)} %fusion.1.mixer_ref), custom_call_target="tpu_custom_call" | custom-call | bytes 18000000 | tf_op jit(solution)/shard_map/bypass_columns/pallas_call | solution.py:272
  128.3 3.6 %collective-permute-done.19.c_ref = bf16[4,48,1280]{2,1,0:T(8,128)(2,1)} collective-permute-done((bf16[4,48,1280]{2,1,0:T(8,128)(2,1)S(1)}, bf16[4,48,1280]{2,1,0:T(8,128)(2,1)}, u32[]{:S(2)}, u32[]{:S(2)}) %collective-permute-start.19) | collective-permute-done | bytes 491552 | tf_op jit(solution)/shard_map/ppermute | solution.py:612
  131.9 3.5 %to_lines.3 = bf16[8,48,1280]{2,1,0:T(8,128)(2,1)} custom-call(s32[3]{0:T(128)} %pad_add_fusion.where_ref, bf16[4,48,1280]{2,1,0:T(8,128)(2,1)} %get-tuple-element.58.a_ref, bf16[4,48,1280]{2,1,0:T(8,128)(2,1)} %collective-permute-done.17.b_ref, bf16[4,48,1280]{2,1,0:T(8,128)(2,1)} %collective-permute-done.19.c_ref, ...), custom_call_target="tpu_custom_call" | custom-call | bytes 9000000 | tf_op jit(solution)/shard_map/to_lines/pallas_call | solution.py:379
  135.3 19.9 %all_to_all.15.arrived_ref = bf16[8,48,1280]{2,1,0:T(8,128)(2,1)} all-to-all(bf16[8,48,1280]{2,1,0:T(8,128)(2,1)} %to_lines.3), channel_id=1, replica_groups=mesh['dp'=4,'gx'=4,'gy'=8] {'gy'}, dimensions={0} | all-to-all | bytes 1966080 | tf_op jit(solution)/shard_map/all_to_all | solution.py:643
  155.2 6.3 %back_modes.1 = (bf16[8,48,1280]{2,1,0:T(8,128)(2,1)}, bf16[2,120,128]{2,1,0:T(8,128)(2,1)}, bf16[2,120,128]{2,1,0:T(8,128)(2,1)}, bf16[2,120,128]{2,1,0:T(8,128)(2,1)}, bf16[2,120,128]{2,1,0:T(8,128)(2,1)}) custom-call(s32[3]{0:T(128)} %pad_add_fusion.where_ref, bf16[8,48,1280]{2,1,0:T(8,128)(2,1)} %all_to_all.15.arrived_ref, ...), custom_call_target="tpu_custom_call" | custom-call | bytes 15000000 | tf_op jit(solution)/shard_map/back_modes/pallas_call | solution.py:555
  161.6 4.3 %all-to-all-start.2 = ((bf16[8,48,1280]{2,1,0:T(8,128)(2,1)}), bf16[8,48,1280]{2,1,0:T(8,128)(2,1)}, u32[]{:S(2)}, u32[]{:S(2)}) async-start(bf16[8,48,1280]{2,1,0:T(8,128)(2,1)} %get-tuple-element.68), calls=%async_computation.2 | async-start | bytes 1966080 | tf_op jit(solution)/shard_map/all_to_all | solution.py:643
  165.8 5.6 %collective-permute-start.20 = (bf16[2,120,128]{2,1,0:T(8,128)(2,1)}, bf16[2,120,128]{2,1,0:T(8,128)(2,1)}, u32[]{:S(2)}, u32[]{:S(2)}) collective-permute-start(bf16[2,120,128]{2,1,0:T(8,128)(2,1)} %get-tuple-element.69), channel_id=1, source_target_pairs={{0,0},{8,32},{16,64},{24,96},{32,8},{40,40},{48,72},{56,104},{64,1... | collective-permute-start | bytes 184328 | tf_op jit(solution)/shard_map/ppermute | solution.py:652
  171.6 1.8 collective-permute-start.22
  173.4 1.4 collective-permute-start.23
  174.7 2.6 %collective-permute-done.22.p2 = bf16[2,120,128]{2,1,0:T(8,128)(2,1)} collective-permute-done((bf16[2,120,128]{2,1,0:T(8,128)(2,1)}, bf16[2,120,128]{2,1,0:T(8,128)(2,1)}, u32[]{:S(2)}, u32[]{:S(2)}) %collective-permute-start.22) | collective-permute-done | bytes 61472 | tf_op jit(solution)/shard_map/ppermute | solution.py:652
  177.4 3.6 %collective-permute-done.23.p3 = bf16[2,120,128]{2,1,0:T(8,128)(2,1)} collective-permute-done((bf16[2,120,128]{2,1,0:T(8,128)(2,1)}, bf16[2,120,128]{2,1,0:T(8,128)(2,1)}, u32[]{:S(2)}, u32[]{:S(2)}) %collective-permute-start.23) | collective-permute-done | bytes 61472 | tf_op jit(solution)/shard_map/ppermute | solution.py:652
  181.0 3.1 %from_lines.1.i0 = bf16[4,48,1280]{2,1,0:T(8,128)(2,1)} custom-call(s32[3]{0:T(128)} %pad_add_fusion.where_ref, bf16[8,48,1280]{2,1,0:T(8,128)(2,1)} %all-to-all-done.2.modes_ref, bf16[8,384,192]{2,1,0:T(8,128)(2,1)} %constant.28.clone.table_ref.refs_8_), custom_call_target="tpu_custom_call" | custom-call | bytes 9000000 | tf_op jit(solution)/shard_map/from_lines/pallas_call | solution.py:379
  184.1 3.3 %collective-permute-start.24 = (bf16[4,48,1280]{2,1,0:T(8,128)(2,1)}, bf16[4,48,1280]{2,1,0:T(8,128)(2,1)S(1)}, u32[]{:S(2)}, u32[]{:S(2)}) collective-permute-start(bf16[4,48,1280]{2,1,0:T(8,128)(2,1)} %from_lines.1.i0), channel_id=1, source_target_pairs={{0,16},{8,24},{16,0},{24,8},{1,17},{9,25},{17,1},{25,9},{2,18},{10... | collective-permute-start | bytes 1474568 | tf_op jit(solution)/shard_map/ppermute | solution.py:612
  187.4 3.0 %collective-permute-start.25 = (bf16[4,48,1280]{2,1,0:T(8,128)(2,1)}, bf16[4,48,1280]{2,1,0:T(8,128)(2,1)}, u32[]{:S(2)}, u32[]{:S(2)}) collective-permute-start(bf16[4,48,1280]{2,1,0:T(8,128)(2,1)} %from_lines.1.i0), channel_id=1, source_target_pairs={{0,8},{8,0},{16,24},{24,16},{1,9},{9,1},{17,25},{25,17},{2,10},{10... | collective-permute-start | bytes 1474568 | tf_op jit(solution)/shard_map/ppermute | solution.py:612
  190.4 3.1 %outer_sum.1 = f32[3,20,40,128]{3,2,1,0:T(8,128)} custom-call(bf16[2,120,128]{2,1,0:T(8,128)(2,1)} %collective-permute-done.20.p0, bf16[2,120,128]{2,1,0:T(8,128)(2,1)} %collective-permute-done.21.p1, bf16[2,120,128]{2,1,0:T(8,128)(2,1)} %collective-permute-done.22.p2, bf16[2,120,128]{2,1,0:T(8,128)(2,1)} %collective-permute-done.23.p3), custom_call_target="tpu_custom_call" | custom-call | bytes 9000000 | tf_op jit(solution)/shard_map/outer_sum/pallas_call | solution.py:602
  193.5 2.0 collective-permute-done.24.i1
  196.3 4.2 %collective-permute-start.26 = (bf16[4,48,1280]{2,1,0:T(8,128)(2,1)S(1)}, bf16[4,48,1280]{2,1,0:T(8,128)(2,1)}, u32[]{:S(2)}, u32[]{:S(2)}) collective-permute-start(bf16[4,48,1280]{2,1,0:T(8,128)(2,1)S(1)} %collective-permute-done.24.i1), channel_id=1, source_target_pairs={{0,8},{8,0},{16,24},{24,16},{1,9},{9,1},{17,25},{25,17},{2,10},{10... | collective-permute-start | bytes 1474568 | tf_op jit(solution)/shard_map/ppermute | solution.py:612
  200.6 1.6 collective-permute-done.26.i3
  202.2 9.4 %end_columns.1 = bf16[20,64,2048]{2,1,0:T(8,128)(2,1)} custom-call(s32[3]{0:T(128)} %pad_add_fusion.where_ref, bf16[4,48,1280]{2,1,0:T(8,128)(2,1)} %from_lines.1.i0, bf16[4,48,1280]{2,1,0:T(8,128)(2,1)} %copy-done.2, bf16[4,48,1280]{2,1,0:T(8,128)(2,1)} %collective-permute-done.25.i2, bf16[4,48,1280]{2,1,0:T(8,128)(2,1)} %collective-permute-done.26.i3, ...), custom_call_target="tpu_custom_call" | custom-call | bytes 30000000 | tf_op jit(solution)/shard_map/end_columns/pallas_call | solution.py:326
  (61 shorter events, 10.4 us)
Async XLA Ops:
  0.6 21.3 %copy-start = (bf16[160,20]{1,0:T(8,128)(2,1)S(1)}, bf16[160,20]{1,0:T(8,128)(2,1)}, u32[]{:S(2)}) copy-start(bf16[160,20]{1,0:T(8,128)(2,1)} %constant.24.clone) | copy-start | bytes 19204
  0.6 21.3 %copy-start.6 = (bf16[160,160]{1,0:T(8,128)(2,1)S(1)}, bf16[160,160]{1,0:T(8,128)(2,1)}, u32[]{:S(2)}) copy-start(bf16[160,160]{1,0:T(8,128)(2,1)} %constant.27.clone) | copy-start | bytes 153604
  0.7 21.3 %copy-start.14 = (bf16[20,20]{1,0:T(8,128)(2,1)S(1)}, bf16[20,20]{1,0:T(8,128)(2,1)}, u32[]{:S(2)}) copy-start(bf16[20,20]{1,0:T(8,128)(2,1)} %param.12) | copy-start | bytes 2404
  0.7 13.8 %collective-permute-start = (bf16[3,20,20,2,128]{4,3,2,1,0:T(2,128)(2,1)}, bf16[3,20,20,2,128]{4,3,2,1,0:T(2,128)(2,1)}, u32[]{:S(2)}, u32[]{:S(2)}) collective-permute-start(bf16[3,20,20,2,128]{4,3,2,1,0:T(2,128)(2,1)} %param.11), channel_id=1, source_target_pairs={{0,0},{8,32},{16,64},{24,96},{32,72},{40,104},{48,8},{56,40},{64,1... | collective-permute-start | bytes 1843208 | tf_op jit(solution)/shard_map/ppermute | solution.py:661
  14.5 4.2 %collective-permute-start.2 = (bf16[4,48,1280]{2,1,0:T(8,128)(2,1)}, bf16[4,48,1280]{2,1,0:T(8,128)(2,1)S(1)}, u32[]{:S(2)}, u32[]{:S(2)}) collective-permute-start(bf16[4,48,1280]{2,1,0:T(8,128)(2,1)} %get-tuple-element.49), channel_id=1, source_target_pairs={{0,8},{8,0},{16,24},{24,16},{1,9},{9,1},{17,25},{25,17},{2,10},{10... | collective-permute-start | bytes 1474568 | tf_op jit(solution)/shard_map/ppermute | solution.py:612
  16.9 19.1 %collective-permute-start.4 = (bf16[3,20,20,2,128]{4,3,2,1,0:T(2,128)(2,1)}, bf16[3,20,20,2,128]{4,3,2,1,0:T(2,128)(2,1)}, u32[]{:S(2)}, u32[]{:S(2)}) collective-permute-start(bf16[3,20,20,2,128]{4,3,2,1,0:T(2,128)(2,1)} %collective-permute-done), channel_id=1, source_target_pairs={{32,0},{64,32},{96,64},{0,96},{33,1},{65,33},{97,65},{1,97},{34,2}... | collective-permute-start | bytes 1843208 | tf_op jit(solution)/shard_map/ppermute | solution.py:630
  18.7 17.3 %collective-permute-start.5 = (bf16[3,20,20,2,128]{4,3,2,1,0:T(2,128)(2,1)}, bf16[3,20,20,2,128]{4,3,2,1,0:T(2,128)(2,1)}, u32[]{:S(2)}, u32[]{:S(2)}) collective-permute-start(bf16[3,20,20,2,128]{4,3,2,1,0:T(2,128)(2,1)} %collective-permute-done), channel_id=1, source_target_pairs={{96,0},{0,32},{32,64},{64,96},{97,1},{1,33},{33,65},{65,97},{98,2}... | collective-permute-start | bytes 1843208 | tf_op jit(solution)/shard_map/ppermute | solution.py:630
  19.8 12.7 %collective-permute-start.3 = (bf16[4,48,1280]{2,1,0:T(8,128)(2,1)S(1)}, bf16[4,48,1280]{2,1,0:T(8,128)(2,1)}, u32[]{:S(2)}, u32[]{:S(2)}) collective-permute-start(bf16[4,48,1280]{2,1,0:T(8,128)(2,1)S(1)} %add_convert_fusion.1), channel_id=1, source_target_pairs={{0,16},{8,24},{16,0},{24,8},{1,17},{9,25},{17,1},{25,9},{2,18},{10... | collective-permute-start | bytes 1474568 | tf_op jit(solution)/shard_map/ppermute | solution.py:612
  21.3 11.2 %collective-permute-start.1 = (bf16[4,48,1280]{2,1,0:T(8,128)(2,1)}, bf16[4,48,1280]{2,1,0:T(8,128)(2,1)}, u32[]{:S(2)}, u32[]{:S(2)}) collective-permute-start(bf16[4,48,1280]{2,1,0:T(8,128)(2,1)} %get-tuple-element.47), channel_id=1, source_target_pairs={{0,8},{8,0},{16,24},{24,16},{1,9},{9,1},{17,25},{25,17},{2,10},{10... | collective-permute-start | bytes 1474568 | tf_op jit(solution)/shard_map/ppermute | solution.py:612
  36.0 23.2 %all-to-all-start = ((bf16[8,48,1280]{2,1,0:T(8,128)(2,1)}), bf16[8,48,1280]{2,1,0:T(8,128)(2,1)}, u32[]{:S(2)}, u32[]{:S(2)}) async-start(bf16[8,48,1280]{2,1,0:T(8,128)(2,1)} %to_lines.2), calls=%async_computation | async-start | bytes 1966080 | tf_op jit(solution)/shard_map/all_to_all | solution.py:643
  43.6 15.6 %collective-permute-start.6 = (bf16[3,20,20,2,128]{4,3,2,1,0:T(2,128)(2,1)}, bf16[3,20,20,2,128]{4,3,2,1,0:T(2,128)(2,1)}, u32[]{:S(2)}, u32[]{:S(2)}) collective-permute-start(bf16[3,20,20,2,128]{4,3,2,1,0:T(2,128)(2,1)} %collective-permute-done), channel_id=1, source_target_pairs={{64,0},{96,32},{0,64},{32,96},{65,1},{97,33},{1,65},{33,97},{66,2}... | collective-permute-start | bytes 1843208 | tf_op jit(solution)/shard_map/ppermute | solution.py:630
  64.7 8.1 %collective-permute-start.7 = (bf16[48,1280]{1,0:T(8,128)(2,1)}, bf16[48,1280]{1,0:T(8,128)(2,1)S(1)}, u32[]{:S(2)}, u32[]{:S(2)}) collective-permute-start(bf16[48,1280]{1,0:T(8,128)(2,1)} %bitcast.24), channel_id=1, source_target_pairs={{1,0},{0,1},{3,2},{2,3},{5,4},{4,5},{7,6},{6,7},{9,8},{8,9},{11,10... | collective-permute-start | bytes 368648 | tf_op jit(solution)/shard_map/ppermute | solution.py:635
  67.5 6.0 %collective-permute-start.10 = (bf16[48,1280]{1,0:T(8,128)(2,1)}, bf16[48,1280]{1,0:T(8,128)(2,1)S(1)}, u32[]{:S(2)}, u32[]{:S(2)}) collective-permute-start(bf16[48,1280]{1,0:T(8,128)(2,1)} %bitcast.25), channel_id=1, source_target_pairs={{4,0},{5,1},{6,2},{7,3},{0,4},{1,5},{2,6},{3,7},{12,8},{13,9},{14,... | collective-permute-start | bytes 368648 | tf_op jit(solution)/shard_map/ppermute | solution.py:638
  70.1 6.6 %collective-permute-start.12 = (bf16[48,1280]{1,0:T(8,128)(2,1)}, bf16[48,1280]{1,0:T(8,128)(2,1)S(1)}, u32[]{:S(2)}, u32[]{:S(2)}) collective-permute-start(bf16[48,1280]{1,0:T(8,128)(2,1)} %bitcast.26), channel_id=1, source_target_pairs={{6,0},{7,1},{0,2},{1,3},{2,4},{3,5},{4,6},{5,7},{14,8},{15,9},{8,1... | collective-permute-start | bytes 368648 | tf_op jit(solution)/shard_map/ppermute | solution.py:638
  70.4 7.2 %collective-permute-start.8 = (bf16[48,1280]{1,0:T(8,128)(2,1)}, bf16[48,1280]{1,0:T(8,128)(2,1)S(1)}, u32[]{:S(2)}, u32[]{:S(2)}) collective-permute-start(bf16[48,1280]{1,0:T(8,128)(2,1)} %bitcast.27), channel_id=1, source_target_pairs={{2,0},{3,1},{4,2},{5,3},{6,4},{7,5},{0,6},{1,7},{10,8},{11,9},{12,... | collective-permute-start | bytes 368648 | tf_op jit(solution)/shard_map/ppermute | solution.py:638
  72.8 0.7 copy-start.8
  72.8 6.3 %collective-permute-start.11 = (bf16[48,1280]{1,0:T(8,128)(2,1)S(1)}, bf16[48,1280]{1,0:T(8,128)(2,1)S(1)}, u32[]{:S(2)}, u32[]{:S(2)}) collective-permute-start(bf16[48,1280]{1,0:T(8,128)(2,1)S(1)} %collective-permute-done.7.refs_1_), channel_id=1, source_target_pairs={{4,0},{5,1},{6,2},{7,3},{0,4},{1,5},{2,6},{3,7},{12,8},{13,9},{14,... | collective-permute-start | bytes 368648 | tf_op jit(solution)/shard_map/ppermute | solution.py:638
  72.9 7.4 %collective-permute-start.13 = (bf16[48,1280]{1,0:T(8,128)(2,1)S(1)}, bf16[48,1280]{1,0:T(8,128)(2,1)S(1)}, u32[]{:S(2)}, u32[]{:S(2)}) collective-permute-start(bf16[48,1280]{1,0:T(8,128)(2,1)S(1)} %collective-permute-done.7.refs_1_), channel_id=1, source_target_pairs={{6,0},{7,1},{0,2},{1,3},{2,4},{3,5},{4,6},{5,7},{14,8},{15,9},{8,1... | collective-permute-start | bytes 368648 | tf_op jit(solution)/shard_map/ppermute | solution.py:638
  73.5 6.8 %copy-start.9 = (bf16[48,1280]{1,0:T(8,128)(2,1)}, bf16[48,1280]{1,0:T(8,128)(2,1)S(1)}, u32[]{:S(2)}) copy-start(bf16[48,1280]{1,0:T(8,128)(2,1)S(1)} %collective-permute-done.10.refs_4_) | copy-start | bytes 368644
  73.5 7.7 %collective-permute-start.9 = (bf16[48,1280]{1,0:T(8,128)(2,1)S(1)}, bf16[48,1280]{1,0:T(8,128)(2,1)}, u32[]{:S(2)}, u32[]{:S(2)}) collective-permute-start(bf16[48,1280]{1,0:T(8,128)(2,1)S(1)} %collective-permute-done.7.refs_1_), channel_id=1, source_target_pairs={{2,0},{3,1},{4,2},{5,3},{6,4},{7,5},{0,6},{1,7},{10,8},{11,9},{12,... | collective-permute-start | bytes 368648 | tf_op jit(solution)/shard_map/ppermute | solution.py:638
  76.7 3.6 %copy-start.10 = (bf16[48,1280]{1,0:T(8,128)(2,1)}, bf16[48,1280]{1,0:T(8,128)(2,1)S(1)}, u32[]{:S(2)}) copy-start(bf16[48,1280]{1,0:T(8,128)(2,1)S(1)} %collective-permute-done.12.refs_6_) | copy-start | bytes 368644
  77.6 2.7 %copy-start.11 = (bf16[48,1280]{1,0:T(8,128)(2,1)}, bf16[48,1280]{1,0:T(8,128)(2,1)S(1)}, u32[]{:S(2)}) copy-start(bf16[48,1280]{1,0:T(8,128)(2,1)S(1)} %collective-permute-done.8.refs_2_) | copy-start | bytes 368644
  79.1 1.2 copy-start.12
  80.3 0.6 copy-start.13
  84.4 9.0 %collective-permute-start.14 = (bf16[4,48,1280]{2,1,0:T(8,128)(2,1)}, bf16[4,48,1280]{2,1,0:T(8,128)(2,1)S(1)}, u32[]{:S(2)}, u32[]{:S(2)}) collective-permute-start(bf16[4,48,1280]{2,1,0:T(8,128)(2,1)} %from_line_set.1.i0), channel_id=1, source_target_pairs={{0,16},{8,24},{16,0},{24,8},{1,17},{9,25},{17,1},{25,9},{2,18},{10... | collective-permute-start | bytes 1474568 | tf_op jit(solution)/shard_map/ppermute | solution.py:612
  85.0 13.3 %collective-permute-start.15 = (bf16[4,48,1280]{2,1,0:T(8,128)(2,1)}, bf16[4,48,1280]{2,1,0:T(8,128)(2,1)S(1)}, u32[]{:S(2)}, u32[]{:S(2)}) collective-permute-start(bf16[4,48,1280]{2,1,0:T(8,128)(2,1)} %from_line_set.1.i0), channel_id=1, source_target_pairs={{0,8},{8,0},{16,24},{24,16},{1,9},{9,1},{17,25},{25,17},{2,10},{10... | collective-permute-start | bytes 1474568 | tf_op jit(solution)/shard_map/ppermute | solution.py:612
  93.5 6.3 %copy-start.3 = (bf16[4,48,1280]{2,1,0:T(8,128)(2,1)}, bf16[4,48,1280]{2,1,0:T(8,128)(2,1)S(1)}, u32[]{:S(2)}) copy-start(bf16[4,48,1280]{2,1,0:T(8,128)(2,1)S(1)} %collective-permute-done.14.i1) | copy-start | bytes 1474564
  93.5 6.3 %collective-permute-start.16 = (bf16[4,48,1280]{2,1,0:T(8,128)(2,1)S(1)}, bf16[4,48,1280]{2,1,0:T(8,128)(2,1)S(1)}, u32[]{:S(2)}, u32[]{:S(2)}) collective-permute-start(bf16[4,48,1280]{2,1,0:T(8,128)(2,1)S(1)} %collective-permute-done.14.i1), channel_id=1, source_target_pairs={{0,8},{8,0},{16,24},{24,16},{1,9},{9,1},{17,25},{25,17},{2,10},{10... | collective-permute-start | bytes 1474568 | tf_op jit(solution)/shard_map/ppermute | solution.py:612
  98.3 1.5 copy-start.4
  99.8 0.8 copy-start.5
  100.5 20.0 %copy-start.1 = (bf16[160,20]{1,0:T(8,128)(2,1)S(1)}, bf16[160,20]{1,0:T(8,128)(2,1)}, u32[]{:S(2)}) copy-start(bf16[160,20]{1,0:T(8,128)(2,1)} %constant.24.clone) | copy-start | bytes 19204
  100.6 20.0 %copy-start.7 = (bf16[160,160]{1,0:T(8,128)(2,1)S(1)}, bf16[160,160]{1,0:T(8,128)(2,1)}, u32[]{:S(2)}) copy-start(bf16[160,160]{1,0:T(8,128)(2,1)} %constant.27.clone) | copy-start | bytes 153604
  100.6 20.0 %copy-start.15 = (bf16[20,20]{1,0:T(8,128)(2,1)S(1)}, bf16[20,20]{1,0:T(8,128)(2,1)}, u32[]{:S(2)}) copy-start(bf16[20,20]{1,0:T(8,128)(2,1)} %param.12) | copy-start | bytes 2404
  115.9 2.2 %collective-permute-start.18 = (bf16[4,48,1280]{2,1,0:T(8,128)(2,1)}, bf16[4,48,1280]{2,1,0:T(8,128)(2,1)S(1)}, u32[]{:S(2)}, u32[]{:S(2)}) collective-permute-start(bf16[4,48,1280]{2,1,0:T(8,128)(2,1)} %get-tuple-element.61), channel_id=1, source_target_pairs={{0,8},{8,0},{16,24},{24,16},{1,9},{9,1},{17,25},{25,17},{2,10},{10... | collective-permute-start | bytes 1474568 | tf_op jit(solution)/shard_map/ppermute | solution.py:612
  119.2 12.6 %collective-permute-start.19 = (bf16[4,48,1280]{2,1,0:T(8,128)(2,1)S(1)}, bf16[4,48,1280]{2,1,0:T(8,128)(2,1)}, u32[]{:S(2)}, u32[]{:S(2)}) collective-permute-start(bf16[4,48,1280]{2,1,0:T(8,128)(2,1)S(1)} %add_convert_fusion), channel_id=1, source_target_pairs={{0,16},{8,24},{16,0},{24,8},{1,17},{9,25},{17,1},{25,9},{2,18},{10... | collective-permute-start | bytes 1474568 | tf_op jit(solution)/shard_map/ppermute | solution.py:612
  119.9 12.0 %collective-permute-start.17 = (bf16[4,48,1280]{2,1,0:T(8,128)(2,1)}, bf16[4,48,1280]{2,1,0:T(8,128)(2,1)}, u32[]{:S(2)}, u32[]{:S(2)}) collective-permute-start(bf16[4,48,1280]{2,1,0:T(8,128)(2,1)} %get-tuple-element.59), channel_id=1, source_target_pairs={{0,8},{8,0},{16,24},{24,16},{1,9},{9,1},{17,25},{25,17},{2,10},{10... | collective-permute-start | bytes 1474568 | tf_op jit(solution)/shard_map/ppermute | solution.py:612
  161.6 19.4 %all-to-all-start.2 = ((bf16[8,48,1280]{2,1,0:T(8,128)(2,1)}), bf16[8,48,1280]{2,1,0:T(8,128)(2,1)}, u32[]{:S(2)}, u32[]{:S(2)}) async-start(bf16[8,48,1280]{2,1,0:T(8,128)(2,1)} %get-tuple-element.68), calls=%async_computation.2 | async-start | bytes 1966080 | tf_op jit(solution)/shard_map/all_to_all | solution.py:643
  165.8 8.9 %collective-permute-start.20 = (bf16[2,120,128]{2,1,0:T(8,128)(2,1)}, bf16[2,120,128]{2,1,0:T(8,128)(2,1)}, u32[]{:S(2)}, u32[]{:S(2)}) collective-permute-start(bf16[2,120,128]{2,1,0:T(8,128)(2,1)} %get-tuple-element.69), channel_id=1, source_target_pairs={{0,0},{8,32},{16,64},{24,96},{32,8},{40,40},{48,72},{56,104},{64,1... | collective-permute-start | bytes 184328 | tf_op jit(solution)/shard_map/ppermute | solution.py:652
  171.5 3.3 %collective-permute-start.21 = (bf16[2,120,128]{2,1,0:T(8,128)(2,1)}, bf16[2,120,128]{2,1,0:T(8,128)(2,1)}, u32[]{:S(2)}, u32[]{:S(2)}) collective-permute-start(bf16[2,120,128]{2,1,0:T(8,128)(2,1)} %get-tuple-element.70), channel_id=1, source_target_pairs={{0,8},{8,40},{16,72},{24,104},{32,16},{40,48},{48,80},{56,112},{64... | collective-permute-start | bytes 184328 | tf_op jit(solution)/shard_map/ppermute | solution.py:652
  171.6 5.8 %collective-permute-start.22 = (bf16[2,120,128]{2,1,0:T(8,128)(2,1)}, bf16[2,120,128]{2,1,0:T(8,128)(2,1)}, u32[]{:S(2)}, u32[]{:S(2)}) collective-permute-start(bf16[2,120,128]{2,1,0:T(8,128)(2,1)} %get-tuple-element.71), channel_id=1, source_target_pairs={{0,16},{8,48},{16,80},{24,112},{32,24},{40,56},{48,88},{56,120},{6... | collective-permute-start | bytes 184328 | tf_op jit(solution)/shard_map/ppermute | solution.py:652
  173.4 7.6 %collective-permute-start.23 = (bf16[2,120,128]{2,1,0:T(8,128)(2,1)}, bf16[2,120,128]{2,1,0:T(8,128)(2,1)}, u32[]{:S(2)}, u32[]{:S(2)}) collective-permute-start(bf16[2,120,128]{2,1,0:T(8,128)(2,1)} %get-tuple-element.72), channel_id=1, source_target_pairs={{0,24},{8,56},{16,88},{24,120},{32,0},{40,32},{48,64},{56,96},{64,... | collective-permute-start | bytes 184328 | tf_op jit(solution)/shard_map/ppermute | solution.py:652
  184.1 11.5 %collective-permute-start.24 = (bf16[4,48,1280]{2,1,0:T(8,128)(2,1)}, bf16[4,48,1280]{2,1,0:T(8,128)(2,1)S(1)}, u32[]{:S(2)}, u32[]{:S(2)}) collective-permute-start(bf16[4,48,1280]{2,1,0:T(8,128)(2,1)} %from_lines.1.i0), channel_id=1, source_target_pairs={{0,16},{8,24},{16,0},{24,8},{1,17},{9,25},{17,1},{25,9},{2,18},{10... | collective-permute-start | bytes 1474568 | tf_op jit(solution)/shard_map/ppermute | solution.py:612
  187.4 13.2 %collective-permute-start.25 = (bf16[4,48,1280]{2,1,0:T(8,128)(2,1)}, bf16[4,48,1280]{2,1,0:T(8,128)(2,1)}, u32[]{:S(2)}, u32[]{:S(2)}) collective-permute-start(bf16[4,48,1280]{2,1,0:T(8,128)(2,1)} %from_lines.1.i0), channel_id=1, source_target_pairs={{0,8},{8,0},{16,24},{24,16},{1,9},{9,1},{17,25},{25,17},{2,10},{10... | collective-permute-start | bytes 1474568 | tf_op jit(solution)/shard_map/ppermute | solution.py:612
  195.6 0.8 copy-start.2
  196.3 5.9 %collective-permute-start.26 = (bf16[4,48,1280]{2,1,0:T(8,128)(2,1)S(1)}, bf16[4,48,1280]{2,1,0:T(8,128)(2,1)}, u32[]{:S(2)}, u32[]{:S(2)}) collective-permute-start(bf16[4,48,1280]{2,1,0:T(8,128)(2,1)S(1)} %collective-permute-done.24.i1), channel_id=1, source_target_pairs={{0,8},{8,0},{16,24},{24,16},{1,9},{9,1},{17,25},{25,17},{2,10},{10... | collective-permute-start | bytes 1474568 | tf_op jit(solution)/shard_map/ppermute | solution.py:612

commit v9 on v8

--- a/solution.py
+++ b/solution.py
@@ -354,13 +354,6 @@
         out_ref[:, :, lanes] = dot(table_ref[0], rows).astype(BF).reshape(GY, 48, GL)
 
 
-def unline_kernel(where_ref, modes_ref, table_ref, out_ref):
-    for j in range(GROUPS):
-        lanes = slice(GL * j, GL * (j + 1))
-        rows = modes_ref[:, :, lanes].reshape(GY * 48, GL)
-        out_ref[:, :, lanes] = dot(table_ref[0], rows, 0, 0).astype(BF).reshape(STEPS, ROWS, GL)
-
-
 def unline_set_kernel(where_ref, *refs):
     *modes_refs, table_ref, out_ref, order_ref = refs
     for k in range(GY):
@@ -395,10 +388,6 @@
 def to_lines(where, *parts):
     out = jax.ShapeDtypeStruct((GY, 48, WIDE), BF)
     return line_call(line_kernel, "to_lines", where, parts, out)
-
-
-def from_lines(where, modes):
-    return line_call(unline_kernel, "from_lines", where, (modes,), COEFFS)
 
 
 def from_line_set(where, modes):
@@ -481,9 +470,19 @@
     return pl.multiple_of(block * PAIR, 8)
 
 
+def take_weights(first_ref, rest_ref, held_ref):
+    @pl.when(pl.program_id(0) == 0)
+    def _():
+        held_ref[...] = first_ref[...]
+
+    @pl.when(pl.program_id(0) > 0)
+    def _():
+        held_ref[...] = rest_ref[...]
+
+
 def mix_kernel(
-    where_ref, arrived_ref, w0, w1, w2, w3, out_ref, u0, u1, u2, u3,
-    sum_ref, in_ref, mix_ref,
+    where_ref, arrived_ref, w0, w1, w3, first_ref, rest_ref, out_ref, u0, u1, u2, u3,
+    sum_ref, in_ref, mix_ref, w2,
 ):
     step = pl.program_id(0)
 
@@ -492,6 +491,7 @@
         gather_modes(arrived_ref, sum_ref, in_ref)
         hand_out(where_ref, in_ref, [ref.at[0] for ref in (u0, u1, u2, u3)])
 
+    take_weights(first_ref, rest_ref, w2)
     for k, weight_ref in enumerate((w0, w1, w2, w3)):
         base = set_row(where_ref, k)
 
@@ -514,8 +514,8 @@
 
 
 def back_kernel(
-    where_ref, arrived_ref, w0, w1, w2, w3, s0, s1, s2, s3, out_ref, u0, u1, u2, u3,
-    sum_ref, in_ref, mix_ref,
+    where_ref, arrived_ref, w0, w1, w3, first_ref, rest_ref, s0, s1, s2, s3,
+    out_ref, u0, u1, u2, u3, sum_ref, in_ref, mix_ref, w2,
 ):
     step = pl.program_id(0)
 
@@ -526,6 +526,7 @@
         for spec_ref, ref in zip((s0, s1, s2, s3), (u0, u1, u2, u3)):
             ref[0] = spec_ref[0]
 
+    take_weights(first_ref, rest_ref, w2)
     for k, weight_ref in enumerate((w0, w1, w2, w3)):
         base = set_row(where_ref, k)
         grad = in_ref[pl.ds(base, PAIR), :]
@@ -547,7 +548,8 @@
 
 
 def mode_call(kernel, name, where, arrived, weights, spectra=()):
-    sets, copies = (2, GY) if spectra else (1, 1)
+    sets = 2 if spectra else 1
+    weight = (1, CH, PAIR, 2 * HALF)
 
     def chunk(n):
         return pl.BlockSpec((n, KB * PAIR, 2 * HALF), lambda i, w: (0, 0, 0))
@@ -558,17 +560,20 @@
             num_scalar_prefetch=1,
             grid=(KB,),
             in_specs=[pl.BlockSpec((GY, 48, WIDE), lambda i, w: (0, 0, 0))]
-            + [pl.BlockSpec((1, CH, PAIR, 2 * HALF), lambda i, w: (i, 0, 0, 0))] * 4
+            + [pl.BlockSpec(weight, lambda i, w: (i, 0, 0, 0))] * 3
+            + [pl.BlockSpec(weight, lambda i, w: (0, 0, 0, 0))]
+            + [pl.BlockSpec(weight, lambda i, w: (lax.max(i, 1) - 1, 0, 0, 0))]
             + [chunk(1)] * len(spectra),
-            out_specs=[pl.BlockSpec((copies, 48, WIDE), lambda i, w: (0, 0, 0))]
+            out_specs=[pl.BlockSpec((1, 48, WIDE), lambda i, w: (0, 0, 0))]
             + [chunk(sets)] * 4,
             scratch_shapes=[
                 pltpu.VMEM((48, WIDE), F32),
                 pltpu.VMEM((SETS * PAIR, 2 * HALF), F32),
                 pltpu.VMEM((SETS * PAIR, 2 * HALF), F32),
+                pltpu.VMEM(weight, BF),
             ],
         ),
-        out_shape=[jax.ShapeDtypeStruct((copies, 48, WIDE), BF)]
+        out_shape=[jax.ShapeDtypeStruct((1, 48, WIDE), BF)]
         + [jax.ShapeDtypeStruct((sets, KB * PAIR, 2 * HALF), BF)] * 4,
         compiler_params=ALONE,
         cost_estimate=cost(5),
@@ -625,10 +630,12 @@
 
 
 def gather_weights(weight):
-    held = [weight]
-    for k in range(1, DP):
-        held.append(lax.ppermute(weight, "dp", [((a + k) % DP, a) for a in range(DP)]))
-    return [part.reshape(KB, CH, PAIR, 2 * HALF) for part in held]
+    def fetch(part, k):
+        moved = lax.ppermute(part, "dp", [((a + k) % DP, a) for a in range(DP)])
+        return moved.reshape(-1, CH, PAIR, 2 * HALF)
+
+    own = weight.reshape(KB, CH, PAIR, 2 * HALF)
+    return [own, fetch(weight, 1), fetch(weight, 3), fetch(weight[:1], 2), fetch(weight[1:], 2)]
 
 
 def gather_lines(modes):
@@ -669,9 +676,7 @@
     *pieces, weight = lax.optimization_barrier((*start_columns(where, values), weight))
     parts, bypass = start_slabs(pieces, bypass_columns(values, mixer_of(bypass_weight), bias))
     weights = gather_weights(weight)
-    lines, weights[1], weights[3] = lax.optimization_barrier(
-        (to_lines(where, *parts), weights[1], weights[3])
-    )
+    lines, *weights[1:4] = lax.optimization_barrier((to_lines(where, *parts), *weights[1:4]))
     arrived = exchange_lines(lines)
     modes, *spectra = mode_call(mix_kernel, "mix_modes", where, arrived, weights)
     coeffs = share_slabs(from_line_set(where, gather_lines(modes[0])))
@@ -680,9 +685,10 @@
     parts, bypass = start_slabs(pieces, bypass_columns(grad, mixer, jnp.zeros_like(bias)))
     arrived = exchange_lines(to_lines(where, *parts))
     modes, *pairs = mode_call(back_kernel, "back_modes", where, arrived, weights, spectra)
-    modes, *pairs = lax.optimization_barrier((exchange_lines(modes), *to_owners(pairs)))
-    *coeffs, weight_grad = share_slabs(from_lines(where, modes), outer_sum(pairs))
+    coeffs = share_slabs(from_line_set(where, gather_lines(modes[0])))
     field_grad = end_columns(where, coeffs, bypass)
+    field_grad, *pairs = lax.optimization_barrier((field_grad, *to_owners(pairs)))
+    weight_grad = outer_sum(pairs)
     return (
         activation[None],
         field_grad[None],

time: 213 us -> 216 us (1.014)
  starting transfers between devices: 67.3 us -> 59.2 us
  waiting for transfers between devices: 43.1 us -> 50 us
  local copies, waits for them, and re-layouts: 2.77 us -> 6.49 us
    ppermute x6 -> x12, waiting for transfers between devices: 4.83 us -> 12.3 us  [gather_lines(): held += [lax.ppermute(part, 'gy', pairs) for part in held[:2]]]
    ppermute x4, waiting for transfers between devices: 6.2 us -> 0.01 us  [to_owners(): moved.append(lax.ppermute(chunk, ('dp', 'gx'), pairs))]
    all_to_all x2 -> x1, starting transfers between devices: 11.8 us -> 7.67 us  [exchange_lines(): return lax.all_to_all(parts, 'gy', split_axis=0, concat_axis=0, tiled=True)]
    ppermute x12, starting transfers between devices: 26.3 us -> 22.7 us  [swap(): return lax.ppermute(values, 'gx', [(i, i ^ bit) for i in range(GX)])]
    ppermute x6 -> x12, starting transfers between devices: 8.18 us -> 11.5 us  [gather_lines(): held += [lax.ppermute(part, 'gy', pairs) for part in held[:2]]]
    slice x0 -> x2, local copies, waits for them, and re-layouts: none -> 3.04 us  [the longest x1 1.76 us: gather_weights(): weight[:1]]
    ppermute x1 -> x2, waiting for transfers between devices: 0.01 us -> 2.7 us  [gather_lines(): held = [modes, lax.ppermute(modes, 'gy', [(g ^ 1, g) for g in range(GY)])]]
    all_to_all x2 -> x1, waiting for transfers between devices: 0.01 us -> 2.41 us  [exchange_lines(): return lax.all_to_all(parts, 'gy', split_axis=0, concat_axis=0, tiled=True)]
  transfers between devices with their start and end apart: 29 -> 36, of which waited for: 16 -> 20; matrix products, arithmetic and copies ran while one was open for 2% -> 3% of each run, Pallas kernels for 13% -> 15%
where the time goes in v9:
time: 216 us; the launch traced here: 214 us
  Pallas kernels  73.2 us (34%)
  starting transfers between devices  59.2 us (27%)
  waiting for transfers between devices  50 us (23%)
  blocking collectives  19.6 us (9%)
  local copies, waits for them, and re-layouts  6.49 us (3%)
  other arithmetic  2.93 us (1%)
    ppermute x12, starting transfers between devices, swap(): return lax.ppermute(values, 'gx', [(i, i ^ bit) for i in range(GX)])  22.7 us
    all_to_all x1, blocking collectives, exchange_lines(): return lax.all_to_all(parts, 'gy', split_axis=0, concat_axis=0, tiled=True)  19.6 us
    ppermute x12, waiting for transfers between devices, swap(): return lax.ppermute(values, 'gx', [(i, i ^ bit) for i in range(GX)])  18.4 us
    pallas_call x1, Pallas kernels, middle_columns(): pl.pallas_call(middle_kernel, grid_spec=pltpu.PrefetchScalarGridSpec(num_...  15.4 us
    pallas_call x4, Pallas kernels, line_call(): pl.pallas_call(kernel, grid_spec=pltpu.PrefetchScalarGridSpec(num_scalar_...  13.4 us
    ppermute x4, waiting for transfers between devices, fetch(): moved = lax.ppermute(part, 'dp', [((a + k) % DP, a) for a in range(DP)])  13.3 us
    pallas_call x2, Pallas kernels, bypass_columns(): pl.pallas_call(bypass_kernel, grid=(STEPS,), in_specs=[pl.BlockSpec(memor...  12.4 us
    ppermute x12, waiting for transfers between devices, gather_lines(): held += [lax.ppermute(part, 'gy', pairs) for part in held[:2]]  12.3 us
  transfers between devices with their start and end apart: 36, of which 20 were waited for; matrix products, arithmetic and copies ran while one was open for 3% of the time, Pallas kernels for 15%

profile of v9, /device:TPU:1, one launch (start us, length us, event | category | flops | bytes accessed | tf_op | source)
XLA Modules:
  0.0 214.0 jit_solution(10087204705712437076)
XLA Ops:
  0.7 4.6 %collective-permute-start = (bf16[3,20,20,2,128]{4,3,2,1,0:T(2,128)(2,1)}, bf16[3,20,20,2,128]{4,3,2,1,0:T(2,128)(2,1)}, u32[]{:S(2)}, u32[]{:S(2)}) collective-permute-start(bf16[3,20,20,2,128]{4,3,2,1,0:T(2,128)(2,1)} %param.11), channel_id=1, source_target_pairs={{0,0},{8,32},{16,64},{24,96},{32,72},{40,104},{48,8},{56,40},{64,1... | collective-permute-start | bytes 1843208 | tf_op jit(solution)/shard_map/ppermute | solution.py:668
  6.0 7.6 %start_columns.1 = (bf16[4,48,1280]{2,1,0:T(8,128)(2,1)}, bf16[4,48,1280]{2,1,0:T(8,128)(2,1)}, bf16[4,48,1280]{2,1,0:T(8,128)(2,1)}, bf16[4,48,1280]{2,1,0:T(8,128)(2,1)}) custom-call(s32[3]{0:T(128)} %pad_add_fusion.where_ref, bf16[20,64,2048]{2,1,0:T(8,128)(2,1)} %bitcast.21, bf16[4,24,512]{2,1,0:T(8,128)(2,1)} %constant.25.clone.strip_ref, ...), custom_call_target="tpu_custom_call" | custom-call | bytes 24000000 | tf_op jit(solution)/shard_map/start_columns/pallas_call | solution.py:290
  14.5 2.5 %collective-permute-start.2 = (bf16[4,48,1280]{2,1,0:T(8,128)(2,1)}, bf16[4,48,1280]{2,1,0:T(8,128)(2,1)S(1)}, u32[]{:S(2)}, u32[]{:S(2)}) collective-permute-start(bf16[4,48,1280]{2,1,0:T(8,128)(2,1)} %get-tuple-element.48), channel_id=1, source_target_pairs={{0,8},{8,0},{16,24},{24,16},{1,9},{9,1},{17,25},{25,17},{2,10},{10... | collective-permute-start | bytes 1474568 | tf_op jit(solution)/shard_map/ppermute | solution.py:617
  17.0 1.7 collective-permute-start.4
  18.7 1.1 add_convert_fusion.1
  19.8 1.5 collective-permute-start.3
  21.9 1.8 slice.6
  23.7 2.8 %collective-permute-start.6 = (bf16[1,20,20,2,128]{4,3,2,1,0:T(2,128)(2,1)}, bf16[1,20,20,2,128]{4,3,2,1,0:T(2,128)(2,1)}, u32[]{:S(2)}, u32[]{:S(2)}) collective-permute-start(bf16[1,20,20,2,128]{4,3,2,1,0:T(2,128)(2,1)} %slice.6), channel_id=1, source_target_pairs={{64,0},{96,32},{0,64},{32,96},{65,1},{97,33},{1,65},{33,97},{66,2}... | collective-permute-start | bytes 614408 | tf_op jit(solution)/shard_map/ppermute | solution.py:634
  27.4 6.2 %bypass_columns.2.bypass_ref = bf16[20,64,2048]{2,1,0:T(8,128)(2,1)} custom-call(f32[20]{0:T(128)} %shift_ref.1, bf16[20,64,2048]{2,1,0:T(8,128)(2,1)} %bitcast.22, bf16[160,160]{1,0:T(8,128)(2,1)} %fusion.mixer_ref), custom_call_target="tpu_custom_call" | custom-call | bytes 18000000 | tf_op jit(solution)/shard_map/bypass_columns/pallas_call | solution.py:272
  33.6 3.5 %to_lines.2 = bf16[8,48,1280]{2,1,0:T(8,128)(2,1)} custom-call(s32[3]{0:T(128)} %pad_add_fusion.where_ref, bf16[4,48,1280]{2,1,0:T(8,128)(2,1)} %get-tuple-element.45.a_ref, bf16[4,48,1280]{2,1,0:T(8,128)(2,1)} %collective-permute-done.1.b_ref, bf16[4,48,1280]{2,1,0:T(8,128)(2,1)} %collective-permute-done.3.c_ref, ...), custom_call_target="tpu_custom_call" | custom-call | bytes 9000000 | tf_op jit(solution)/shard_map/to_lines/pallas_call | solution.py:372
  37.1 2.6 %collective-permute-done.6 = bf16[1,20,20,2,128]{4,3,2,1,0:T(2,128)(2,1)} collective-permute-done((bf16[1,20,20,2,128]{4,3,2,1,0:T(2,128)(2,1)}, bf16[1,20,20,2,128]{4,3,2,1,0:T(2,128)(2,1)}, u32[]{:S(2)}, u32[]{:S(2)}) %collective-permute-start.6) | collective-permute-done | bytes 204832 | tf_op jit(solution)/shard_map/ppermute | solution.py:634
  39.7 7.7 %all-to-all-start = ((bf16[8,48,1280]{2,1,0:T(8,128)(2,1)}), bf16[8,48,1280]{2,1,0:T(8,128)(2,1)}, u32[]{:S(2)}, u32[]{:S(2)}) async-start(bf16[8,48,1280]{2,1,0:T(8,128)(2,1)} %to_lines.2), calls=%async_computation | async-start | bytes 1966080 | tf_op jit(solution)/shard_map/all_to_all | solution.py:650
  47.4 1.3 slice.7
  49.2 10.6 %collective-permute-done.7 = bf16[2,20,20,2,128]{4,3,2,1,0:T(2,128)(2,1)} collective-permute-done((bf16[2,20,20,2,128]{4,3,2,1,0:T(2,128)(2,1)S(1)}, bf16[2,20,20,2,128]{4,3,2,1,0:T(2,128)(2,1)}, u32[]{:S(2)}, u32[]{:S(2)}) %collective-permute-start.7) | collective-permute-done | bytes 409632 | tf_op jit(solution)/shard_map/ppermute | solution.py:634
  59.9 2.4 %all-to-all-done.arrived_ref = bf16[8,48,1280]{2,1,0:T(8,128)(2,1)} async-done(((bf16[8,48,1280]{2,1,0:T(8,128)(2,1)}), bf16[8,48,1280]{2,1,0:T(8,128)(2,1)}, u32[]{:S(2)}, u32[]{:S(2)}) %all-to-all-start) | async-done | bytes 983072 | tf_op jit(solution)/shard_map/all_to_all | solution.py:650
  62.3 5.6 %mix_modes.1 = (bf16[1,48,1280]{2,1,0:T(8,128)(2,1)}, bf16[1,120,128]{2,1,0:T(8,128)(2,1)}, bf16[1,120,128]{2,1,0:T(8,128)(2,1)}, bf16[1,120,128]{2,1,0:T(8,128)(2,1)}, bf16[1,120,128]{2,1,0:T(8,128)(2,1)}) custom-call(s32[3]{0:T(128)} %pad_add_fusion.where_ref, bf16[8,48,1280]{2,1,0:T(8,128)(2,1)} %all-to-all-done.arrived_ref, ...), custom_call_target="tpu_custom_call" | custom-call | bytes 15000000 | tf_op jit(solution)/shard_map/mix_modes/pallas_call | solution.py:557
  68.5 2.4 %collective-permute-start.11 = (bf16[48,1280]{1,0:T(8,128)(2,1)}, bf16[48,1280]{1,0:T(8,128)(2,1)S(1)}, u32[]{:S(2)}, u32[]{:S(2)}) collective-permute-start(bf16[48,1280]{1,0:T(8,128)(2,1)} %bitcast.32), channel_id=1, source_target_pairs={{4,0},{5,1},{6,2},{7,3},{0,4},{1,5},{2,6},{3,7},{12,8},{13,9},{14,... | collective-permute-start | bytes 368648 | tf_op jit(solution)/shard_map/ppermute | solution.py:645
  71.6 2.0 collective-permute-start.9
  74.8 1.1 collective-permute-start.14
  76.5 2.5 %collective-permute-done.10.refs_3_ = bf16[48,1280]{1,0:T(8,128)(2,1)S(1)} collective-permute-done((bf16[48,1280]{1,0:T(8,128)(2,1)S(1)}, bf16[48,1280]{1,0:T(8,128)(2,1)S(1)}, u32[]{:S(2)}, u32[]{:S(2)}) %collective-permute-start.10) | collective-permute-done | bytes 122912 | tf_op jit(solution)/shard_map/ppermute | solution.py:645
  78.9 1.5 collective-permute-done.12.refs_5_
  81.1 1.3 collective-permute-done.14.refs_7_
  82.4 3.3 %from_line_set.2.i0 = bf16[4,48,1280]{2,1,0:T(8,128)(2,1)} custom-call(s32[3]{0:T(128)} %pad_add_fusion.where_ref, bf16[48,1280]{1,0:T(8,128)(2,1)} %bitcast.35, bf16[48,1280]{1,0:T(8,128)(2,1)} %copy-done.9, bf16[48,1280]{1,0:T(8,128)(2,1)} %copy-done.15, bf16[48,1280]{1,0:T(8,128)(2,1)} %copy-done.17, bf16[48,1280]{1,0:T(8,128)(2,1)} %copy-done.11, ...), custom_call_target="tpu_custom_call" | custom-call | bytes 9000000 | tf_op jit(solution)/shard_map/from_line_set/pallas_call | solution.py:372
  86.0 3.7 %collective-permute-start.16 = (bf16[4,48,1280]{2,1,0:T(8,128)(2,1)}, bf16[4,48,1280]{2,1,0:T(8,128)(2,1)S(1)}, u32[]{:S(2)}, u32[]{:S(2)}) collective-permute-start(bf16[4,48,1280]{2,1,0:T(8,128)(2,1)} %from_line_set.2.i0), channel_id=1, source_target_pairs={{0,8},{8,0},{16,24},{24,16},{1,9},{9,1},{17,25},{25,17},{2,10},{10... | collective-permute-start | bytes 1474568 | tf_op jit(solution)/shard_map/ppermute | solution.py:617
  89.7 5.5 %collective-permute-done.15.i1 = bf16[4,48,1280]{2,1,0:T(8,128)(2,1)S(1)} collective-permute-done((bf16[4,48,1280]{2,1,0:T(8,128)(2,1)}, bf16[4,48,1280]{2,1,0:T(8,128)(2,1)S(1)}, u32[]{:S(2)}, u32[]{:S(2)}) %collective-permute-start.15) | collective-permute-done | bytes 491552 | tf_op jit(solution)/shard_map/ppermute | solution.py:617
  95.2 4.4 %collective-permute-start.17 = (bf16[4,48,1280]{2,1,0:T(8,128)(2,1)S(1)}, bf16[4,48,1280]{2,1,0:T(8,128)(2,1)S(1)}, u32[]{:S(2)}, u32[]{:S(2)}) collective-permute-start(bf16[4,48,1280]{2,1,0:T(8,128)(2,1)S(1)} %collective-permute-done.15.i1), channel_id=1, source_target_pairs={{0,8},{8,0},{16,24},{24,16},{1,9},{9,1},{17,25},{25,17},{2,10},{10... | collective-permute-start | bytes 1474568 | tf_op jit(solution)/shard_map/ppermute | solution.py:617
  99.5 1.5 collective-permute-done.17.i3
  101.8 15.4 %middle_columns.1 = (bf16[20,64,2048]{2,1,0:T(8,128)(2,1)}, bf16[20,64,2048]{2,1,0:T(8,128)(2,1)}, bf16[4,48,1280]{2,1,0:T(8,128)(2,1)}, bf16[4,48,1280]{2,1,0:T...) custom-call(s32[3]{0:T(128)} %pad_add_fusion.where_ref, bf16[4,48,1280]{2,1,0:T(8,128)(2,1)} %from_line_set.2.i0, ...), custom_call_target="tpu_custom_call" | custom-call | bytes 57000000 | tf_op jit(solution)/shard_map/middle_columns/pallas_call | solution.py:308
  117.7 1.7 collective-permute-done.19
  119.4 1.1 add_convert_fusion
  123.2 6.3 %bypass_columns.3.bypass_ref = bf16[20,64,2048]{2,1,0:T(8,128)(2,1)} custom-call(f32[20]{0:T(128)} %broadcast_1_shift_ref.2.shift_ref, bf16[20,64,2048]{2,1,0:T(8,128)(2,1)} %get-tuple-element.62.source_ref, bf16[160,160]{1,0:T(8,128)(2,1)} %fusion.1.mixer_ref), custom_call_target="tpu_custom_call" | custom-call | bytes 18000000 | tf_op jit(solution)/shard_map/bypass_columns/pallas_call | solution.py:272
  129.4 3.9 %collective-permute-done.20.c_ref = bf16[4,48,1280]{2,1,0:T(8,128)(2,1)} collective-permute-done((bf16[4,48,1280]{2,1,0:T(8,128)(2,1)S(1)}, bf16[4,48,1280]{2,1,0:T(8,128)(2,1)}, u32[]{:S(2)}, u32[]{:S(2)}) %collective-permute-start.20) | collective-permute-done | bytes 491552 | tf_op jit(solution)/shard_map/ppermute | solution.py:617
  133.3 3.5 %to_lines.3 = bf16[8,48,1280]{2,1,0:T(8,128)(2,1)} custom-call(s32[3]{0:T(128)} %pad_add_fusion.where_ref, bf16[4,48,1280]{2,1,0:T(8,128)(2,1)} %get-tuple-element.58.a_ref, bf16[4,48,1280]{2,1,0:T(8,128)(2,1)} %collective-permute-done.18.b_ref, bf16[4,48,1280]{2,1,0:T(8,128)(2,1)} %collective-permute-done.20.c_ref, ...), custom_call_target="tpu_custom_call" | custom-call | bytes 9000000 | tf_op jit(solution)/shard_map/to_lines/pallas_call | solution.py:372
  136.8 19.6 %all_to_all.10.arrived_ref = bf16[8,48,1280]{2,1,0:T(8,128)(2,1)} all-to-all(bf16[8,48,1280]{2,1,0:T(8,128)(2,1)} %to_lines.3), channel_id=1, replica_groups=mesh['dp'=4,'gx'=4,'gy'=8] {'gy'}, dimensions={0} | all-to-all | bytes 1966080 | tf_op jit(solution)/shard_map/all_to_all | solution.py:650
  156.4 6.2 %back_modes.1 = (bf16[1,48,1280]{2,1,0:T(8,128)(2,1)}, bf16[2,120,128]{2,1,0:T(8,128)(2,1)}, bf16[2,120,128]{2,1,0:T(8,128)(2,1)}, bf16[2,120,128]{2,1,0:T(8,128)(2,1)}, bf16[2,120,128]{2,1,0:T(8,128)(2,1)}) custom-call(s32[3]{0:T(128)} %pad_add_fusion.where_ref, bf16[8,48,1280]{2,1,0:T(8,128)(2,1)} %all_to_all.10.arrived_ref, ...), custom_call_target="tpu_custom_call" | custom-call | bytes 15000000 | tf_op jit(solution)/shard_map/back_modes/pallas_call | solution.py:557
  162.8 1.3 collective-permute-start.22
  164.1 1.2 collective-permute-start.24
  165.3 2.7 %collective-permute-done.21.refs_1_ = bf16[48,1280]{1,0:T(8,128)(2,1)S(1)} collective-permute-done((bf16[48,1280]{1,0:T(8,128)(2,1)}, bf16[48,1280]{1,0:T(8,128)(2,1)S(1)}, u32[]{:S(2)}, u32[]{:S(2)}) %collective-permute-start.21) | collective-permute-done | bytes 122912 | tf_op jit(solution)/shard_map/ppermute | solution.py:642
  170.9 2.0 collective-permute-done.23.refs_3_
  172.9 2.2 %collective-permute-done.25.refs_5_ = bf16[48,1280]{1,0:T(8,128)(2,1)S(1)} collective-permute-done((bf16[48,1280]{1,0:T(8,128)(2,1)S(1)}, bf16[48,1280]{1,0:T(8,128)(2,1)S(1)}, u32[]{:S(2)}, u32[]{:S(2)}) %collective-permute-start.25) | collective-permute-done | bytes 122912 | tf_op jit(solution)/shard_map/ppermute | solution.py:645
  176.8 3.3 %from_line_set.3.i0 = bf16[4,48,1280]{2,1,0:T(8,128)(2,1)} custom-call(s32[3]{0:T(128)} %pad_add_fusion.where_ref, bf16[48,1280]{1,0:T(8,128)(2,1)} %bitcast.30, bf16[48,1280]{1,0:T(8,128)(2,1)} %copy-done.8, bf16[48,1280]{1,0:T(8,128)(2,1)} %copy-done.10, bf16[48,1280]{1,0:T(8,128)(2,1)} %copy-done.16, bf16[48,1280]{1,0:T(8,128)(2,1)} %copy-done.12, ...), custom_call_target="tpu_custom_call" | custom-call | bytes 9000000 | tf_op jit(solution)/shard_map/from_line_set/pallas_call | solution.py:372
  180.3 3.5 %collective-permute-start.29 = (bf16[4,48,1280]{2,1,0:T(8,128)(2,1)}, bf16[4,48,1280]{2,1,0:T(8,128)(2,1)}, u32[]{:S(2)}, u32[]{:S(2)}) collective-permute-start(bf16[4,48,1280]{2,1,0:T(8,128)(2,1)} %from_line_set.3.i0), channel_id=1, source_target_pairs={{0,8},{8,0},{16,24},{24,16},{1,9},{9,1},{17,25},{25,17},{2,10},{10... | collective-permute-start | bytes 1474568 | tf_op jit(solution)/shard_map/ppermute | solution.py:617
  183.9 5.8 %collective-permute-done.28.i1 = bf16[4,48,1280]{2,1,0:T(8,128)(2,1)S(1)} collective-permute-done((bf16[4,48,1280]{2,1,0:T(8,128)(2,1)}, bf16[4,48,1280]{2,1,0:T(8,128)(2,1)S(1)}, u32[]{:S(2)}, u32[]{:S(2)}) %collective-permute-start.28) | collective-permute-done | bytes 491552 | tf_op jit(solution)/shard_map/ppermute | solution.py:617
  190.5 4.2 %collective-permute-start.30 = (bf16[4,48,1280]{2,1,0:T(8,128)(2,1)S(1)}, bf16[4,48,1280]{2,1,0:T(8,128)(2,1)}, u32[]{:S(2)}, u32[]{:S(2)}) collective-permute-start(bf16[4,48,1280]{2,1,0:T(8,128)(2,1)S(1)} %collective-permute-done.28.i1), channel_id=1, source_target_pairs={{0,8},{8,0},{16,24},{24,16},{1,9},{9,1},{17,25},{25,17},{2,10},{10... | collective-permute-start | bytes 1474568 | tf_op jit(solution)/shard_map/ppermute | solution.py:617
  194.7 2.2 %collective-permute-start.31 = (bf16[2,120,128]{2,1,0:T(8,128)(2,1)}, bf16[2,120,128]{2,1,0:T(8,128)(2,1)}, u32[]{:S(2)}, u32[]{:S(2)}) collective-permute-start(bf16[2,120,128]{2,1,0:T(8,128)(2,1)} %get-tuple-element.70), channel_id=1, source_target_pairs={{0,0},{8,32},{16,64},{24,96},{32,8},{40,40},{48,72},{56,104},{64,1... | collective-permute-start | bytes 184328 | tf_op jit(solution)/shard_map/ppermute | solution.py:659
  198.2 3.2 %collective-permute-start.34 = (bf16[2,120,128]{2,1,0:T(8,128)(2,1)}, bf16[2,120,128]{2,1,0:T(8,128)(2,1)}, u32[]{:S(2)}, u32[]{:S(2)}) collective-permute-start(bf16[2,120,128]{2,1,0:T(8,128)(2,1)} %get-tuple-element.73), channel_id=1, source_target_pairs={{0,24},{8,56},{16,88},{24,120},{32,0},{40,32},{48,64},{56,96},{64,... | collective-permute-start | bytes 184328 | tf_op jit(solution)/shard_map/ppermute | solution.py:659
  201.4 9.4 %end_columns.1 = bf16[20,64,2048]{2,1,0:T(8,128)(2,1)} custom-call(s32[3]{0:T(128)} %pad_add_fusion.where_ref, bf16[4,48,1280]{2,1,0:T(8,128)(2,1)} %from_line_set.3.i0, bf16[4,48,1280]{2,1,0:T(8,128)(2,1)} %copy-done.2, bf16[4,48,1280]{2,1,0:T(8,128)(2,1)} %collective-permute-done.29.i2, bf16[4,48,1280]{2,1,0:T(8,128)(2,1)} %collective-permute-done.30.i3, ...), custom_call_target="tpu_custom_call" | custom-call | bytes 30000000 | tf_op jit(solution)/shard_map/end_columns/pallas_call | solution.py:326
  210.8 3.1 %outer_sum.1 = f32[3,20,40,128]{3,2,1,0:T(8,128)} custom-call(bf16[2,120,128]{2,1,0:T(8,128)(2,1)} %collective-permute-done.31.p0, bf16[2,120,128]{2,1,0:T(8,128)(2,1)} %collective-permute-done.32.p1, bf16[2,120,128]{2,1,0:T(8,128)(2,1)} %collective-permute-done.33.p2, bf16[2,120,128]{2,1,0:T(8,128)(2,1)} %collective-permute-done.34.p3), custom_call_target="tpu_custom_call" | custom-call | bytes 9000000 | tf_op jit(solution)/shard_map/outer_sum/pallas_call | solution.py:607
  (89 shorter events, 19.0 us)
Async XLA Ops:
  0.6 25.9 %copy-start = (bf16[160,20]{1,0:T(8,128)(2,1)S(1)}, bf16[160,20]{1,0:T(8,128)(2,1)}, u32[]{:S(2)}) copy-start(bf16[160,20]{1,0:T(8,128)(2,1)} %constant.24.clone) | copy-start | bytes 19204
  0.6 25.9 %copy-start.6 = (bf16[160,160]{1,0:T(8,128)(2,1)S(1)}, bf16[160,160]{1,0:T(8,128)(2,1)}, u32[]{:S(2)}) copy-start(bf16[160,160]{1,0:T(8,128)(2,1)} %constant.27.clone) | copy-start | bytes 153604
  0.7 25.8 %copy-start.20 = (bf16[20,20]{1,0:T(8,128)(2,1)S(1)}, bf16[20,20]{1,0:T(8,128)(2,1)}, u32[]{:S(2)}) copy-start(bf16[20,20]{1,0:T(8,128)(2,1)} %param.12) | copy-start | bytes 2404
  0.7 13.8 %collective-permute-start = (bf16[3,20,20,2,128]{4,3,2,1,0:T(2,128)(2,1)}, bf16[3,20,20,2,128]{4,3,2,1,0:T(2,128)(2,1)}, u32[]{:S(2)}, u32[]{:S(2)}) collective-permute-start(bf16[3,20,20,2,128]{4,3,2,1,0:T(2,128)(2,1)} %param.11), channel_id=1, source_target_pairs={{0,0},{8,32},{16,64},{24,96},{32,72},{40,104},{48,8},{56,40},{64,1... | collective-permute-start | bytes 1843208 | tf_op jit(solution)/shard_map/ppermute | solution.py:668
  14.5 4.2 %collective-permute-start.2 = (bf16[4,48,1280]{2,1,0:T(8,128)(2,1)}, bf16[4,48,1280]{2,1,0:T(8,128)(2,1)S(1)}, u32[]{:S(2)}, u32[]{:S(2)}) collective-permute-start(bf16[4,48,1280]{2,1,0:T(8,128)(2,1)} %get-tuple-element.48), channel_id=1, source_target_pairs={{0,8},{8,0},{16,24},{24,16},{1,9},{9,1},{17,25},{25,17},{2,10},{10... | collective-permute-start | bytes 1474568 | tf_op jit(solution)/shard_map/ppermute | solution.py:617
  17.0 22.7 %collective-permute-start.4 = (bf16[3,20,20,2,128]{4,3,2,1,0:T(2,128)(2,1)}, bf16[3,20,20,2,128]{4,3,2,1,0:T(2,128)(2,1)}, u32[]{:S(2)}, u32[]{:S(2)}) collective-permute-start(bf16[3,20,20,2,128]{4,3,2,1,0:T(2,128)(2,1)} %collective-permute-done), channel_id=1, source_target_pairs={{32,0},{64,32},{96,64},{0,96},{33,1},{65,33},{97,65},{1,97},{34,2}... | collective-permute-start | bytes 1843208 | tf_op jit(solution)/shard_map/ppermute | solution.py:634
  18.7 21.0 %collective-permute-start.5 = (bf16[3,20,20,2,128]{4,3,2,1,0:T(2,128)(2,1)}, bf16[3,20,20,2,128]{4,3,2,1,0:T(2,128)(2,1)}, u32[]{:S(2)}, u32[]{:S(2)}) collective-permute-start(bf16[3,20,20,2,128]{4,3,2,1,0:T(2,128)(2,1)} %collective-permute-done), channel_id=1, source_target_pairs={{96,0},{0,32},{32,64},{64,96},{97,1},{1,33},{33,65},{65,97},{98,2}... | collective-permute-start | bytes 1843208 | tf_op jit(solution)/shard_map/ppermute | solution.py:634
  19.8 13.8 %collective-permute-start.3 = (bf16[4,48,1280]{2,1,0:T(8,128)(2,1)S(1)}, bf16[4,48,1280]{2,1,0:T(8,128)(2,1)}, u32[]{:S(2)}, u32[]{:S(2)}) collective-permute-start(bf16[4,48,1280]{2,1,0:T(8,128)(2,1)S(1)} %add_convert_fusion.1), channel_id=1, source_target_pairs={{0,16},{8,24},{16,0},{24,8},{1,17},{9,25},{17,1},{25,9},{2,18},{10... | collective-permute-start | bytes 1474568 | tf_op jit(solution)/shard_map/ppermute | solution.py:617
  21.3 12.3 %collective-permute-start.1 = (bf16[4,48,1280]{2,1,0:T(8,128)(2,1)}, bf16[4,48,1280]{2,1,0:T(8,128)(2,1)}, u32[]{:S(2)}, u32[]{:S(2)}) collective-permute-start(bf16[4,48,1280]{2,1,0:T(8,128)(2,1)} %get-tuple-element.46), channel_id=1, source_target_pairs={{0,8},{8,0},{16,24},{24,16},{1,9},{9,1},{17,25},{25,17},{2,10},{10... | collective-permute-start | bytes 1474568 | tf_op jit(solution)/shard_map/ppermute | solution.py:617
  23.7 16.0 %collective-permute-start.6 = (bf16[1,20,20,2,128]{4,3,2,1,0:T(2,128)(2,1)}, bf16[1,20,20,2,128]{4,3,2,1,0:T(2,128)(2,1)}, u32[]{:S(2)}, u32[]{:S(2)}) collective-permute-start(bf16[1,20,20,2,128]{4,3,2,1,0:T(2,128)(2,1)} %slice.6), channel_id=1, source_target_pairs={{64,0},{96,32},{0,64},{32,96},{65,1},{97,33},{1,65},{33,97},{66,2}... | collective-permute-start | bytes 614408 | tf_op jit(solution)/shard_map/ppermute | solution.py:634
  39.7 22.6 %all-to-all-start = ((bf16[8,48,1280]{2,1,0:T(8,128)(2,1)}), bf16[8,48,1280]{2,1,0:T(8,128)(2,1)}, u32[]{:S(2)}, u32[]{:S(2)}) async-start(bf16[8,48,1280]{2,1,0:T(8,128)(2,1)} %to_lines.2), calls=%async_computation | async-start | bytes 1966080 | tf_op jit(solution)/shard_map/all_to_all | solution.py:650
  48.7 11.2 %collective-permute-start.7 = (bf16[2,20,20,2,128]{4,3,2,1,0:T(2,128)(2,1)S(1)}, bf16[2,20,20,2,128]{4,3,2,1,0:T(2,128)(2,1)}, u32[]{:S(2)}, u32[]{:S(2)}) collective-permute-start(bf16[2,20,20,2,128]{4,3,2,1,0:T(2,128)(2,1)S(1)} %slice.7), channel_id=1, source_target_pairs={{64,0},{96,32},{0,64},{32,96},{65,1},{97,33},{1,65},{33,97},{66,2}... | collective-permute-start | bytes 1228808 | tf_op jit(solution)/shard_map/ppermute | solution.py:634
  67.9 5.7 %collective-permute-start.8 = (bf16[48,1280]{1,0:T(8,128)(2,1)}, bf16[48,1280]{1,0:T(8,128)(2,1)S(1)}, u32[]{:S(2)}, u32[]{:S(2)}) collective-permute-start(bf16[48,1280]{1,0:T(8,128)(2,1)} %bitcast.31), channel_id=1, source_target_pairs={{1,0},{0,1},{3,2},{2,3},{5,4},{4,5},{7,6},{6,7},{9,8},{8,9},{11,10... | collective-permute-start | bytes 368648 | tf_op jit(solution)/shard_map/ppermute | solution.py:642
  68.5 6.4 %collective-permute-start.11 = (bf16[48,1280]{1,0:T(8,128)(2,1)}, bf16[48,1280]{1,0:T(8,128)(2,1)S(1)}, u32[]{:S(2)}, u32[]{:S(2)}) collective-permute-start(bf16[48,1280]{1,0:T(8,128)(2,1)} %bitcast.32), channel_id=1, source_target_pairs={{4,0},{5,1},{6,2},{7,3},{0,4},{1,5},{2,6},{3,7},{12,8},{13,9},{14,... | collective-permute-start | bytes 368648 | tf_op jit(solution)/shard_map/ppermute | solution.py:645
  70.9 5.5 %collective-permute-start.13 = (bf16[48,1280]{1,0:T(8,128)(2,1)}, bf16[48,1280]{1,0:T(8,128)(2,1)S(1)}, u32[]{:S(2)}, u32[]{:S(2)}) collective-permute-start(bf16[48,1280]{1,0:T(8,128)(2,1)} %bitcast.33), channel_id=1, source_target_pairs={{6,0},{7,1},{0,2},{1,3},{2,4},{3,5},{4,6},{5,7},{14,8},{15,9},{8,1... | collective-permute-start | bytes 368648 | tf_op jit(solution)/shard_map/ppermute | solution.py:645
  71.6 4.9 %collective-permute-start.9 = (bf16[48,1280]{1,0:T(8,128)(2,1)}, bf16[48,1280]{1,0:T(8,128)(2,1)S(1)}, u32[]{:S(2)}, u32[]{:S(2)}) collective-permute-start(bf16[48,1280]{1,0:T(8,128)(2,1)} %bitcast.34), channel_id=1, source_target_pairs={{2,0},{3,1},{4,2},{5,3},{6,4},{7,5},{0,6},{1,7},{10,8},{11,9},{12,... | collective-permute-start | bytes 368648 | tf_op jit(solution)/shard_map/ppermute | solution.py:645
  73.6 5.3 %collective-permute-start.10 = (bf16[48,1280]{1,0:T(8,128)(2,1)S(1)}, bf16[48,1280]{1,0:T(8,128)(2,1)S(1)}, u32[]{:S(2)}, u32[]{:S(2)}) collective-permute-start(bf16[48,1280]{1,0:T(8,128)(2,1)S(1)} %collective-permute-done.8.refs_1_), channel_id=1, source_target_pairs={{2,0},{3,1},{4,2},{5,3},{6,4},{7,5},{0,6},{1,7},{10,8},{11,9},{12,... | collective-permute-start | bytes 368648 | tf_op jit(solution)/shard_map/ppermute | solution.py:645
  74.3 6.2 %collective-permute-start.12 = (bf16[48,1280]{1,0:T(8,128)(2,1)S(1)}, bf16[48,1280]{1,0:T(8,128)(2,1)S(1)}, u32[]{:S(2)}, u32[]{:S(2)}) collective-permute-start(bf16[48,1280]{1,0:T(8,128)(2,1)S(1)} %collective-permute-done.8.refs_1_), channel_id=1, source_target_pairs={{4,0},{5,1},{6,2},{7,3},{0,4},{1,5},{2,6},{3,7},{12,8},{13,9},{14,... | collective-permute-start | bytes 368648 | tf_op jit(solution)/shard_map/ppermute | solution.py:645
  74.8 5.6 %copy-start.11 = (bf16[48,1280]{1,0:T(8,128)(2,1)}, bf16[48,1280]{1,0:T(8,128)(2,1)S(1)}, u32[]{:S(2)}) copy-start(bf16[48,1280]{1,0:T(8,128)(2,1)S(1)} %collective-permute-done.11.refs_4_) | copy-start | bytes 368644
  74.8 7.6 %collective-permute-start.14 = (bf16[48,1280]{1,0:T(8,128)(2,1)S(1)}, bf16[48,1280]{1,0:T(8,128)(2,1)}, u32[]{:S(2)}, u32[]{:S(2)}) collective-permute-start(bf16[48,1280]{1,0:T(8,128)(2,1)S(1)} %collective-permute-done.8.refs_1_), channel_id=1, source_target_pairs={{6,0},{7,1},{0,2},{1,3},{2,4},{3,5},{4,6},{5,7},{14,8},{15,9},{8,1... | collective-permute-start | bytes 368648 | tf_op jit(solution)/shard_map/ppermute | solution.py:645
  76.4 4.1 %copy-start.13 = (bf16[48,1280]{1,0:T(8,128)(2,1)}, bf16[48,1280]{1,0:T(8,128)(2,1)S(1)}, u32[]{:S(2)}) copy-start(bf16[48,1280]{1,0:T(8,128)(2,1)S(1)} %collective-permute-done.13.refs_6_) | copy-start | bytes 368644
  85.7 9.5 %collective-permute-start.15 = (bf16[4,48,1280]{2,1,0:T(8,128)(2,1)}, bf16[4,48,1280]{2,1,0:T(8,128)(2,1)S(1)}, u32[]{:S(2)}, u32[]{:S(2)}) collective-permute-start(bf16[4,48,1280]{2,1,0:T(8,128)(2,1)} %from_line_set.2.i0), channel_id=1, source_target_pairs={{0,16},{8,24},{16,0},{24,8},{1,17},{9,25},{17,1},{25,9},{2,18},{10... | collective-permute-start | bytes 1474568 | tf_op jit(solution)/shard_map/ppermute | solution.py:617
  86.0 13.5 %collective-permute-start.16 = (bf16[4,48,1280]{2,1,0:T(8,128)(2,1)}, bf16[4,48,1280]{2,1,0:T(8,128)(2,1)S(1)}, u32[]{:S(2)}, u32[]{:S(2)}) collective-permute-start(bf16[4,48,1280]{2,1,0:T(8,128)(2,1)} %from_line_set.2.i0), channel_id=1, source_target_pairs={{0,8},{8,0},{16,24},{24,16},{1,9},{9,1},{17,25},{25,17},{2,10},{10... | collective-permute-start | bytes 1474568 | tf_op jit(solution)/shard_map/ppermute | solution.py:617
  95.2 5.8 %copy-start.3 = (bf16[4,48,1280]{2,1,0:T(8,128)(2,1)}, bf16[4,48,1280]{2,1,0:T(8,128)(2,1)S(1)}, u32[]{:S(2)}) copy-start(bf16[4,48,1280]{2,1,0:T(8,128)(2,1)S(1)} %collective-permute-done.15.i1) | copy-start | bytes 1474564
  95.2 5.8 %collective-permute-start.17 = (bf16[4,48,1280]{2,1,0:T(8,128)(2,1)S(1)}, bf16[4,48,1280]{2,1,0:T(8,128)(2,1)S(1)}, u32[]{:S(2)}, u32[]{:S(2)}) collective-permute-start(bf16[4,48,1280]{2,1,0:T(8,128)(2,1)S(1)} %collective-permute-done.15.i1), channel_id=1, source_target_pairs={{0,8},{8,0},{16,24},{24,16},{1,9},{9,1},{17,25},{25,17},{2,10},{10... | collective-permute-start | bytes 1474568 | tf_op jit(solution)/shard_map/ppermute | solution.py:617
  101.8 20.0 %copy-start.1 = (bf16[160,20]{1,0:T(8,128)(2,1)S(1)}, bf16[160,20]{1,0:T(8,128)(2,1)}, u32[]{:S(2)}) copy-start(bf16[160,20]{1,0:T(8,128)(2,1)} %constant.24.clone) | copy-start | bytes 19204
  101.8 20.0 %copy-start.7 = (bf16[160,160]{1,0:T(8,128)(2,1)S(1)}, bf16[160,160]{1,0:T(8,128)(2,1)}, u32[]{:S(2)}) copy-start(bf16[160,160]{1,0:T(8,128)(2,1)} %constant.27.clone) | copy-start | bytes 153604
  101.8 20.0 %copy-start.21 = (bf16[20,20]{1,0:T(8,128)(2,1)S(1)}, bf16[20,20]{1,0:T(8,128)(2,1)}, u32[]{:S(2)}) copy-start(bf16[20,20]{1,0:T(8,128)(2,1)} %param.12) | copy-start | bytes 2404
  117.2 2.2 %collective-permute-start.19 = (bf16[4,48,1280]{2,1,0:T(8,128)(2,1)}, bf16[4,48,1280]{2,1,0:T(8,128)(2,1)S(1)}, u32[]{:S(2)}, u32[]{:S(2)}) collective-permute-start(bf16[4,48,1280]{2,1,0:T(8,128)(2,1)} %get-tuple-element.61), channel_id=1, source_target_pairs={{0,8},{8,0},{16,24},{24,16},{1,9},{9,1},{17,25},{25,17},{2,10},{10... | collective-permute-start | bytes 1474568 | tf_op jit(solution)/shard_map/ppermute | solution.py:617
  120.5 12.8 %collective-permute-start.20 = (bf16[4,48,1280]{2,1,0:T(8,128)(2,1)S(1)}, bf16[4,48,1280]{2,1,0:T(8,128)(2,1)}, u32[]{:S(2)}, u32[]{:S(2)}) collective-permute-start(bf16[4,48,1280]{2,1,0:T(8,128)(2,1)S(1)} %add_convert_fusion), channel_id=1, source_target_pairs={{0,16},{8,24},{16,0},{24,8},{1,17},{9,25},{17,1},{25,9},{2,18},{10... | collective-permute-start | bytes 1474568 | tf_op jit(solution)/shard_map/ppermute | solution.py:617
  121.1 12.2 %collective-permute-start.18 = (bf16[4,48,1280]{2,1,0:T(8,128)(2,1)}, bf16[4,48,1280]{2,1,0:T(8,128)(2,1)}, u32[]{:S(2)}, u32[]{:S(2)}) collective-permute-start(bf16[4,48,1280]{2,1,0:T(8,128)(2,1)} %get-tuple-element.59), channel_id=1, source_target_pairs={{0,8},{8,0},{16,24},{24,16},{1,9},{9,1},{17,25},{25,17},{2,10},{10... | collective-permute-start | bytes 1474568 | tf_op jit(solution)/shard_map/ppermute | solution.py:617
  162.5 5.5 %collective-permute-start.21 = (bf16[48,1280]{1,0:T(8,128)(2,1)}, bf16[48,1280]{1,0:T(8,128)(2,1)S(1)}, u32[]{:S(2)}, u32[]{:S(2)}) collective-permute-start(bf16[48,1280]{1,0:T(8,128)(2,1)} %bitcast.26), channel_id=1, source_target_pairs={{1,0},{0,1},{3,2},{2,3},{5,4},{4,5},{7,6},{6,7},{9,8},{8,9},{11,10... | collective-permute-start | bytes 368648 | tf_op jit(solution)/shard_map/ppermute | solution.py:642
  162.8 6.4 %collective-permute-start.22 = (bf16[48,1280]{1,0:T(8,128)(2,1)}, bf16[48,1280]{1,0:T(8,128)(2,1)S(1)}, u32[]{:S(2)}, u32[]{:S(2)}) collective-permute-start(bf16[48,1280]{1,0:T(8,128)(2,1)} %bitcast.27), channel_id=1, source_target_pairs={{2,0},{3,1},{4,2},{5,3},{6,4},{7,5},{0,6},{1,7},{10,8},{11,9},{12,... | collective-permute-start | bytes 368648 | tf_op jit(solution)/shard_map/ppermute | solution.py:645
  164.1 5.7 %collective-permute-start.24 = (bf16[48,1280]{1,0:T(8,128)(2,1)}, bf16[48,1280]{1,0:T(8,128)(2,1)S(1)}, u32[]{:S(2)}, u32[]{:S(2)}) collective-permute-start(bf16[48,1280]{1,0:T(8,128)(2,1)} %bitcast.28), channel_id=1, source_target_pairs={{4,0},{5,1},{6,2},{7,3},{0,4},{1,5},{2,6},{3,7},{12,8},{13,9},{14,... | collective-permute-start | bytes 368648 | tf_op jit(solution)/shard_map/ppermute | solution.py:645
  165.3 5.6 %collective-permute-start.26 = (bf16[48,1280]{1,0:T(8,128)(2,1)}, bf16[48,1280]{1,0:T(8,128)(2,1)S(1)}, u32[]{:S(2)}, u32[]{:S(2)}) collective-permute-start(bf16[48,1280]{1,0:T(8,128)(2,1)} %bitcast.29), channel_id=1, source_target_pairs={{6,0},{7,1},{0,2},{1,3},{2,4},{3,5},{4,6},{5,7},{14,8},{15,9},{8,1... | collective-permute-start | bytes 368648 | tf_op jit(solution)/shard_map/ppermute | solution.py:645
  168.0 4.9 %collective-permute-start.23 = (bf16[48,1280]{1,0:T(8,128)(2,1)S(1)}, bf16[48,1280]{1,0:T(8,128)(2,1)S(1)}, u32[]{:S(2)}, u32[]{:S(2)}) collective-permute-start(bf16[48,1280]{1,0:T(8,128)(2,1)S(1)} %collective-permute-done.21.refs_1_), channel_id=1, source_target_pairs={{2,0},{3,1},{4,2},{5,3},{6,4},{7,5},{0,6},{1,7},{10,8},{11,9},{12,... | collective-permute-start | bytes 368648 | tf_op jit(solution)/shard_map/ppermute | solution.py:645
  168.6 6.5 %collective-permute-start.25 = (bf16[48,1280]{1,0:T(8,128)(2,1)S(1)}, bf16[48,1280]{1,0:T(8,128)(2,1)S(1)}, u32[]{:S(2)}, u32[]{:S(2)}) collective-permute-start(bf16[48,1280]{1,0:T(8,128)(2,1)S(1)} %collective-permute-done.21.refs_1_), channel_id=1, source_target_pairs={{4,0},{5,1},{6,2},{7,3},{0,4},{1,5},{2,6},{3,7},{12,8},{13,9},{14,... | collective-permute-start | bytes 368648 | tf_op jit(solution)/shard_map/ppermute | solution.py:645
  169.3 5.8 %copy-start.10 = (bf16[48,1280]{1,0:T(8,128)(2,1)}, bf16[48,1280]{1,0:T(8,128)(2,1)S(1)}, u32[]{:S(2)}) copy-start(bf16[48,1280]{1,0:T(8,128)(2,1)S(1)} %collective-permute-done.22.refs_2_) | copy-start | bytes 368644
  169.3 7.5 %collective-permute-start.27 = (bf16[48,1280]{1,0:T(8,128)(2,1)S(1)}, bf16[48,1280]{1,0:T(8,128)(2,1)}, u32[]{:S(2)}, u32[]{:S(2)}) collective-permute-start(bf16[48,1280]{1,0:T(8,128)(2,1)S(1)} %collective-permute-done.21.refs_1_), channel_id=1, source_target_pairs={{6,0},{7,1},{0,2},{1,3},{2,4},{3,5},{4,6},{5,7},{14,8},{15,9},{8,1... | collective-permute-start | bytes 368648 | tf_op jit(solution)/shard_map/ppermute | solution.py:645
  169.9 5.2 %copy-start.12 = (bf16[48,1280]{1,0:T(8,128)(2,1)}, bf16[48,1280]{1,0:T(8,128)(2,1)S(1)}, u32[]{:S(2)}) copy-start(bf16[48,1280]{1,0:T(8,128)(2,1)S(1)} %collective-permute-done.24.refs_4_) | copy-start | bytes 368644
  170.9 4.2 %copy-start.14 = (bf16[48,1280]{1,0:T(8,128)(2,1)}, bf16[48,1280]{1,0:T(8,128)(2,1)S(1)}, u32[]{:S(2)}) copy-start(bf16[48,1280]{1,0:T(8,128)(2,1)S(1)} %collective-permute-done.26.refs_6_) | copy-start | bytes 368644
  180.0 9.7 %collective-permute-start.28 = (bf16[4,48,1280]{2,1,0:T(8,128)(2,1)}, bf16[4,48,1280]{2,1,0:T(8,128)(2,1)S(1)}, u32[]{:S(2)}, u32[]{:S(2)}) collective-permute-start(bf16[4,48,1280]{2,1,0:T(8,128)(2,1)} %from_line_set.3.i0), channel_id=1, source_target_pairs={{0,16},{8,24},{16,0},{24,8},{1,17},{9,25},{17,1},{25,9},{2,18},{10... | collective-permute-start | bytes 1474568 | tf_op jit(solution)/shard_map/ppermute | solution.py:617
  180.3 17.8 %collective-permute-start.29 = (bf16[4,48,1280]{2,1,0:T(8,128)(2,1)}, bf16[4,48,1280]{2,1,0:T(8,128)(2,1)}, u32[]{:S(2)}, u32[]{:S(2)}) collective-permute-start(bf16[4,48,1280]{2,1,0:T(8,128)(2,1)} %from_line_set.3.i0), channel_id=1, source_target_pairs={{0,8},{8,0},{16,24},{24,16},{1,9},{9,1},{17,25},{25,17},{2,10},{10... | collective-permute-start | bytes 1474568 | tf_op jit(solution)/shard_map/ppermute | solution.py:617
  190.5 10.9 %collective-permute-start.30 = (bf16[4,48,1280]{2,1,0:T(8,128)(2,1)S(1)}, bf16[4,48,1280]{2,1,0:T(8,128)(2,1)}, u32[]{:S(2)}, u32[]{:S(2)}) collective-permute-start(bf16[4,48,1280]{2,1,0:T(8,128)(2,1)S(1)} %collective-permute-done.28.i1), channel_id=1, source_target_pairs={{0,8},{8,0},{16,24},{24,16},{1,9},{9,1},{17,25},{25,17},{2,10},{10... | collective-permute-start | bytes 1474568 | tf_op jit(solution)/shard_map/ppermute | solution.py:617
  194.7 16.1 %collective-permute-start.31 = (bf16[2,120,128]{2,1,0:T(8,128)(2,1)}, bf16[2,120,128]{2,1,0:T(8,128)(2,1)}, u32[]{:S(2)}, u32[]{:S(2)}) collective-permute-start(bf16[2,120,128]{2,1,0:T(8,128)(2,1)} %get-tuple-element.70), channel_id=1, source_target_pairs={{0,0},{8,32},{16,64},{24,96},{32,8},{40,40},{48,72},{56,104},{64,1... | collective-permute-start | bytes 184328 | tf_op jit(solution)/shard_map/ppermute | solution.py:659
  196.9 14.0 %collective-permute-start.32 = (bf16[2,120,128]{2,1,0:T(8,128)(2,1)}, bf16[2,120,128]{2,1,0:T(8,128)(2,1)}, u32[]{:S(2)}, u32[]{:S(2)}) collective-permute-start(bf16[2,120,128]{2,1,0:T(8,128)(2,1)} %get-tuple-element.71), channel_id=1, source_target_pairs={{0,8},{8,40},{16,72},{24,104},{32,16},{40,48},{48,80},{56,112},{64... | collective-permute-start | bytes 184328 | tf_op jit(solution)/shard_map/ppermute | solution.py:659
  197.2 13.7 %collective-permute-start.33 = (bf16[2,120,128]{2,1,0:T(8,128)(2,1)}, bf16[2,120,128]{2,1,0:T(8,128)(2,1)}, u32[]{:S(2)}, u32[]{:S(2)}) collective-permute-start(bf16[2,120,128]{2,1,0:T(8,128)(2,1)} %get-tuple-element.72), channel_id=1, source_target_pairs={{0,16},{8,48},{16,80},{24,112},{32,24},{40,56},{48,88},{56,120},{6... | collective-permute-start | bytes 184328 | tf_op jit(solution)/shard_map/ppermute | solution.py:659
  198.2 12.7 %collective-permute-start.34 = (bf16[2,120,128]{2,1,0:T(8,128)(2,1)}, bf16[2,120,128]{2,1,0:T(8,128)(2,1)}, u32[]{:S(2)}, u32[]{:S(2)}) collective-permute-start(bf16[2,120,128]{2,1,0:T(8,128)(2,1)} %get-tuple-element.73), channel_id=1, source_target_pairs={{0,24},{8,56},{16,88},{24,120},{32,0},{40,32},{48,64},{56,96},{64,... | collective-permute-start | bytes 184328 | tf_op jit(solution)/shard_map/ppermute | solution.py:659
  (10 other events, 14.7 us)

commit v10 on v8

--- a/solution.py
+++ b/solution.py
@@ -406,7 +406,7 @@
     return line_call(unline_set_kernel, "from_line_set", where, modes, COEFFS, [order])
 
 
-UNROLL = 4
+UNROLL = 10
 SETS = GX * KB
 PAIR = 2 * CH
 HALF = KX

time: 213 us -> 213 us (level)
  no operation moved by 1% of the time
where the time goes in v10:
time: 213 us; the launch traced here: 211 us
  Pallas kernels  72.7 us (34%)
  starting transfers between devices  67.3 us (32%)
  waiting for transfers between devices  43.1 us (20%)
  blocking collectives  19.9 us (9%)
  other arithmetic  2.85 us (1%)
  local copies, waits for them, and re-layouts  2.77 us (1%)
    ppermute x12, starting transfers between devices, swap(): return lax.ppermute(values, 'gx', [(i, i ^ bit) for i in range(GX)])  26.3 us
    all_to_all x1, blocking collectives, exchange_lines(): return lax.all_to_all(parts, 'gy', split_axis=0, concat_axis=0, tiled=True)  19.9 us
    ppermute x12, waiting for transfers between devices, swap(): return lax.ppermute(values, 'gx', [(i, i ^ bit) for i in range(GX)])  18.3 us
    pallas_call x1, Pallas kernels, middle_columns(): pl.pallas_call(middle_kernel, grid_spec=pltpu.PrefetchScalarGridSpec(num_...  15.4 us
    pallas_call x4, Pallas kernels, line_call(): pl.pallas_call(kernel, grid_spec=pltpu.PrefetchScalarGridSpec(num_scalar_...  13.3 us
    ppermute x3, waiting for transfers between devices, gather_weights(): lax.ppermute(weight, 'dp', [((a + k) % DP, a) for a in range(DP)])  12.8 us
    pallas_call x2, Pallas kernels, bypass_columns(): pl.pallas_call(bypass_kernel, grid=(STEPS,), in_specs=[pl.BlockSpec(memor...  12.5 us
    all_to_all x2, starting transfers between devices, exchange_lines(): return lax.all_to_all(parts, 'gy', split_axis=0, concat_axis=0, tiled=True)  11.8 us
  transfers between devices with their start and end apart: 29, of which 16 were waited for; matrix products, arithmetic and copies ran while one was open for 2% of the time, Pallas kernels for 13%

profile of v10, /device:TPU:1, one launch (start us, length us, event | category | flops | bytes accessed | tf_op | source)
XLA Modules:
  0.0 211.2 jit_solution(9526988556795885160)
XLA Ops:
  0.7 4.6 %collective-permute-start = (bf16[3,20,20,2,128]{4,3,2,1,0:T(2,128)(2,1)}, bf16[3,20,20,2,128]{4,3,2,1,0:T(2,128)(2,1)}, u32[]{:S(2)}, u32[]{:S(2)}) collective-permute-start(bf16[3,20,20,2,128]{4,3,2,1,0:T(2,128)(2,1)} %param.11), channel_id=1, source_target_pairs={{0,0},{8,32},{16,64},{24,96},{32,72},{40,104},{48,8},{56,40},{64,1... | collective-permute-start | bytes 1843208 | tf_op jit(solution)/shard_map/ppermute | solution.py:661
  5.9 7.6 %start_columns.1 = (bf16[4,48,1280]{2,1,0:T(8,128)(2,1)}, bf16[4,48,1280]{2,1,0:T(8,128)(2,1)}, bf16[4,48,1280]{2,1,0:T(8,128)(2,1)}, bf16[4,48,1280]{2,1,0:T(8,128)(2,1)}) custom-call(s32[3]{0:T(128)} %pad_add_fusion.where_ref, bf16[20,64,2048]{2,1,0:T(8,128)(2,1)} %bitcast.19, bf16[4,24,512]{2,1,0:T(8,128)(2,1)} %constant.25.clone.strip_ref, ...), custom_call_target="tpu_custom_call" | custom-call | bytes 24000000 | tf_op jit(solution)/shard_map/start_columns/pallas_call | solution.py:290
  13.5 1.0 collective-permute-done
  14.5 2.4 %collective-permute-start.2 = (bf16[4,48,1280]{2,1,0:T(8,128)(2,1)}, bf16[4,48,1280]{2,1,0:T(8,128)(2,1)S(1)}, u32[]{:S(2)}, u32[]{:S(2)}) collective-permute-start(bf16[4,48,1280]{2,1,0:T(8,128)(2,1)} %get-tuple-element.49), channel_id=1, source_target_pairs={{0,8},{8,0},{16,24},{24,16},{1,9},{9,1},{17,25},{25,17},{2,10},{10... | collective-permute-start | bytes 1474568 | tf_op jit(solution)/shard_map/ppermute | solution.py:612
  16.9 1.8 collective-permute-start.4
  18.7 1.1 add_convert_fusion.1
  19.8 1.5 collective-permute-start.3
  22.9 6.2 %bypass_columns.2.bypass_ref = bf16[20,64,2048]{2,1,0:T(8,128)(2,1)} custom-call(f32[20]{0:T(128)} %shift_ref.1, bf16[20,64,2048]{2,1,0:T(8,128)(2,1)} %bitcast.20, bf16[160,160]{1,0:T(8,128)(2,1)} %fusion.mixer_ref), custom_call_target="tpu_custom_call" | custom-call | bytes 18000000 | tf_op jit(solution)/shard_map/bypass_columns/pallas_call | solution.py:272
  29.1 3.5 %collective-permute-done.3.c_ref = bf16[4,48,1280]{2,1,0:T(8,128)(2,1)} collective-permute-done((bf16[4,48,1280]{2,1,0:T(8,128)(2,1)S(1)}, bf16[4,48,1280]{2,1,0:T(8,128)(2,1)}, u32[]{:S(2)}, u32[]{:S(2)}) %collective-permute-start.3) | collective-permute-done | bytes 491552 | tf_op jit(solution)/shard_map/ppermute | solution.py:612
  32.5 3.5 %to_lines.2 = bf16[8,48,1280]{2,1,0:T(8,128)(2,1)} custom-call(s32[3]{0:T(128)} %pad_add_fusion.where_ref, bf16[4,48,1280]{2,1,0:T(8,128)(2,1)} %get-tuple-element.46.a_ref, bf16[4,48,1280]{2,1,0:T(8,128)(2,1)} %collective-permute-done.1.b_ref, bf16[4,48,1280]{2,1,0:T(8,128)(2,1)} %collective-permute-done.3.c_ref, ...), custom_call_target="tpu_custom_call" | custom-call | bytes 9000000 | tf_op jit(solution)/shard_map/to_lines/pallas_call | solution.py:379
  36.0 7.6 %all-to-all-start = ((bf16[8,48,1280]{2,1,0:T(8,128)(2,1)}), bf16[8,48,1280]{2,1,0:T(8,128)(2,1)}, u32[]{:S(2)}, u32[]{:S(2)}) async-start(bf16[8,48,1280]{2,1,0:T(8,128)(2,1)} %to_lines.2), calls=%async_computation | async-start | bytes 1966080 | tf_op jit(solution)/shard_map/all_to_all | solution.py:643
  43.6 2.9 %collective-permute-start.6 = (bf16[3,20,20,2,128]{4,3,2,1,0:T(2,128)(2,1)}, bf16[3,20,20,2,128]{4,3,2,1,0:T(2,128)(2,1)}, u32[]{:S(2)}, u32[]{:S(2)}) collective-permute-start(bf16[3,20,20,2,128]{4,3,2,1,0:T(2,128)(2,1)} %collective-permute-done), channel_id=1, source_target_pairs={{64,0},{96,32},{0,64},{32,96},{65,1},{97,33},{1,65},{33,97},{66,2}... | collective-permute-start | bytes 1843208 | tf_op jit(solution)/shard_map/ppermute | solution.py:630
  46.4 12.8 %collective-permute-done.6 = bf16[3,20,20,2,128]{4,3,2,1,0:T(2,128)(2,1)} collective-permute-done((bf16[3,20,20,2,128]{4,3,2,1,0:T(2,128)(2,1)}, bf16[3,20,20,2,128]{4,3,2,1,0:T(2,128)(2,1)}, u32[]{:S(2)}, u32[]{:S(2)}) %collective-permute-start.6) | collective-permute-done | bytes 614432 | tf_op jit(solution)/shard_map/ppermute | solution.py:630
  59.2 5.4 %mix_modes.1 = (bf16[1,48,1280]{2,1,0:T(8,128)(2,1)}, bf16[1,120,128]{2,1,0:T(8,128)(2,1)}, bf16[1,120,128]{2,1,0:T(8,128)(2,1)}, bf16[1,120,128]{2,1,0:T(8,128)(2,1)}, bf16[1,120,128]{2,1,0:T(8,128)(2,1)}) custom-call(s32[3]{0:T(128)} %pad_add_fusion.where_ref, bf16[8,48,1280]{2,1,0:T(8,128)(2,1)} %all-to-all-done.arrived_ref, ...), custom_call_target="tpu_custom_call" | custom-call | bytes 15000000 | tf_op jit(solution)/shard_map/mix_modes/pallas_call | solution.py:555
  64.6 2.8 %collective-permute-start.7 = (bf16[48,1280]{1,0:T(8,128)(2,1)}, bf16[48,1280]{1,0:T(8,128)(2,1)S(1)}, u32[]{:S(2)}, u32[]{:S(2)}) collective-permute-start(bf16[48,1280]{1,0:T(8,128)(2,1)} %bitcast.24), channel_id=1, source_target_pairs={{1,0},{0,1},{3,2},{2,3},{5,4},{4,5},{7,6},{6,7},{9,8},{8,9},{11,10... | collective-permute-start | bytes 368648 | tf_op jit(solution)/shard_map/ppermute | solution.py:635
  67.3 2.7 %collective-permute-start.10 = (bf16[48,1280]{1,0:T(8,128)(2,1)}, bf16[48,1280]{1,0:T(8,128)(2,1)S(1)}, u32[]{:S(2)}, u32[]{:S(2)}) collective-permute-start(bf16[48,1280]{1,0:T(8,128)(2,1)} %bitcast.25), channel_id=1, source_target_pairs={{4,0},{5,1},{6,2},{7,3},{0,4},{1,5},{2,6},{3,7},{12,8},{13,9},{14,... | collective-permute-start | bytes 368648 | tf_op jit(solution)/shard_map/ppermute | solution.py:638
  70.3 2.4 %collective-permute-start.8 = (bf16[48,1280]{1,0:T(8,128)(2,1)}, bf16[48,1280]{1,0:T(8,128)(2,1)S(1)}, u32[]{:S(2)}, u32[]{:S(2)}) collective-permute-start(bf16[48,1280]{1,0:T(8,128)(2,1)} %bitcast.27), channel_id=1, source_target_pairs={{2,0},{3,1},{4,2},{5,3},{6,4},{7,5},{0,6},{1,7},{10,8},{11,9},{12,... | collective-permute-start | bytes 368648 | tf_op jit(solution)/shard_map/ppermute | solution.py:638
  73.4 2.2 %collective-permute-start.9 = (bf16[48,1280]{1,0:T(8,128)(2,1)S(1)}, bf16[48,1280]{1,0:T(8,128)(2,1)}, u32[]{:S(2)}, u32[]{:S(2)}) collective-permute-start(bf16[48,1280]{1,0:T(8,128)(2,1)S(1)} %collective-permute-done.7.refs_1_), channel_id=1, source_target_pairs={{2,0},{3,1},{4,2},{5,3},{6,4},{7,5},{0,6},{1,7},{10,8},{11,9},{12,... | collective-permute-start | bytes 368648 | tf_op jit(solution)/shard_map/ppermute | solution.py:638
  75.5 1.1 collective-permute-done.12.refs_6_
  77.5 1.5 collective-permute-done.11.refs_5_
  79.0 1.2 collective-permute-done.13.refs_7_
  81.0 3.3 %from_line_set.1.i0 = bf16[4,48,1280]{2,1,0:T(8,128)(2,1)} custom-call(s32[3]{0:T(128)} %pad_add_fusion.where_ref, bf16[48,1280]{1,0:T(8,128)(2,1)} %bitcast.28, bf16[48,1280]{1,0:T(8,128)(2,1)} %copy-done.8, bf16[48,1280]{1,0:T(8,128)(2,1)} %copy-done.11, bf16[48,1280]{1,0:T(8,128)(2,1)} %collective-permute-done.9.refs_3_, bf16[48,1280]{1,0:T(8,128)(2,1)} %copy-done.9, ...), custom_call_target="tpu_custom_call" | custom-call | bytes 9000000 | tf_op jit(solution)/shard_map/from_line_set/pallas_call | solution.py:379
  84.9 4.1 %collective-permute-start.15 = (bf16[4,48,1280]{2,1,0:T(8,128)(2,1)}, bf16[4,48,1280]{2,1,0:T(8,128)(2,1)S(1)}, u32[]{:S(2)}, u32[]{:S(2)}) collective-permute-start(bf16[4,48,1280]{2,1,0:T(8,128)(2,1)} %from_line_set.1.i0), channel_id=1, source_target_pairs={{0,8},{8,0},{16,24},{24,16},{1,9},{9,1},{17,25},{25,17},{2,10},{10... | collective-permute-start | bytes 1474568 | tf_op jit(solution)/shard_map/ppermute | solution.py:612
  89.0 4.4 %collective-permute-done.14.i1 = bf16[4,48,1280]{2,1,0:T(8,128)(2,1)S(1)} collective-permute-done((bf16[4,48,1280]{2,1,0:T(8,128)(2,1)}, bf16[4,48,1280]{2,1,0:T(8,128)(2,1)S(1)}, u32[]{:S(2)}, u32[]{:S(2)}) %collective-permute-start.14) | collective-permute-done | bytes 491552 | tf_op jit(solution)/shard_map/ppermute | solution.py:612
  93.3 4.8 %collective-permute-start.16 = (bf16[4,48,1280]{2,1,0:T(8,128)(2,1)S(1)}, bf16[4,48,1280]{2,1,0:T(8,128)(2,1)S(1)}, u32[]{:S(2)}, u32[]{:S(2)}) collective-permute-start(bf16[4,48,1280]{2,1,0:T(8,128)(2,1)S(1)} %collective-permute-done.14.i1), channel_id=1, source_target_pairs={{0,8},{8,0},{16,24},{24,16},{1,9},{9,1},{17,25},{25,17},{2,10},{10... | collective-permute-start | bytes 1474568 | tf_op jit(solution)/shard_map/ppermute | solution.py:612
  98.2 1.5 collective-permute-done.16.i3
  100.4 15.4 %middle_columns.1 = (bf16[20,64,2048]{2,1,0:T(8,128)(2,1)}, bf16[20,64,2048]{2,1,0:T(8,128)(2,1)}, bf16[4,48,1280]{2,1,0:T(8,128)(2,1)}, bf16[4,48,1280]{2,1,0:T...) custom-call(s32[3]{0:T(128)} %pad_add_fusion.where_ref, bf16[4,48,1280]{2,1,0:T(8,128)(2,1)} %from_line_set.1.i0, ...), custom_call_target="tpu_custom_call" | custom-call | bytes 57000000 | tf_op jit(solution)/shard_map/middle_columns/pallas_call | solution.py:308
  116.3 1.7 collective-permute-done.18
  118.0 1.1 add_convert_fusion
  121.9 6.3 %bypass_columns.3.bypass_ref = bf16[20,64,2048]{2,1,0:T(8,128)(2,1)} custom-call(f32[20]{0:T(128)} %broadcast_1_shift_ref.2.shift_ref, bf16[20,64,2048]{2,1,0:T(8,128)(2,1)} %get-tuple-element.62.source_ref, bf16[160,160]{1,0:T(8,128)(2,1)} %fusion.1.mixer_ref), custom_call_target="tpu_custom_call" | custom-call | bytes 18000000 | tf_op jit(solution)/shard_map/bypass_columns/pallas_call | solution.py:272
  128.1 3.6 %collective-permute-done.19.c_ref = bf16[4,48,1280]{2,1,0:T(8,128)(2,1)} collective-permute-done((bf16[4,48,1280]{2,1,0:T(8,128)(2,1)S(1)}, bf16[4,48,1280]{2,1,0:T(8,128)(2,1)}, u32[]{:S(2)}, u32[]{:S(2)}) %collective-permute-start.19) | collective-permute-done | bytes 491552 | tf_op jit(solution)/shard_map/ppermute | solution.py:612
  131.8 3.5 %to_lines.3 = bf16[8,48,1280]{2,1,0:T(8,128)(2,1)} custom-call(s32[3]{0:T(128)} %pad_add_fusion.where_ref, bf16[4,48,1280]{2,1,0:T(8,128)(2,1)} %get-tuple-element.58.a_ref, bf16[4,48,1280]{2,1,0:T(8,128)(2,1)} %collective-permute-done.17.b_ref, bf16[4,48,1280]{2,1,0:T(8,128)(2,1)} %collective-permute-done.19.c_ref, ...), custom_call_target="tpu_custom_call" | custom-call | bytes 9000000 | tf_op jit(solution)/shard_map/to_lines/pallas_call | solution.py:379
  135.2 19.9 %all_to_all.15.arrived_ref = bf16[8,48,1280]{2,1,0:T(8,128)(2,1)} all-to-all(bf16[8,48,1280]{2,1,0:T(8,128)(2,1)} %to_lines.3), channel_id=1, replica_groups=mesh['dp'=4,'gx'=4,'gy'=8] {'gy'}, dimensions={0} | all-to-all | bytes 1966080 | tf_op jit(solution)/shard_map/all_to_all | solution.py:643
  155.1 6.1 %back_modes.1 = (bf16[8,48,1280]{2,1,0:T(8,128)(2,1)}, bf16[2,120,128]{2,1,0:T(8,128)(2,1)}, bf16[2,120,128]{2,1,0:T(8,128)(2,1)}, bf16[2,120,128]{2,1,0:T(8,128)(2,1)}, bf16[2,120,128]{2,1,0:T(8,128)(2,1)}) custom-call(s32[3]{0:T(128)} %pad_add_fusion.where_ref, bf16[8,48,1280]{2,1,0:T(8,128)(2,1)} %all_to_all.15.arrived_ref, ...), custom_call_target="tpu_custom_call" | custom-call | bytes 15000000 | tf_op jit(solution)/shard_map/back_modes/pallas_call | solution.py:555
  161.2 4.3 %all-to-all-start.2 = ((bf16[8,48,1280]{2,1,0:T(8,128)(2,1)}), bf16[8,48,1280]{2,1,0:T(8,128)(2,1)}, u32[]{:S(2)}, u32[]{:S(2)}) async-start(bf16[8,48,1280]{2,1,0:T(8,128)(2,1)} %get-tuple-element.68), calls=%async_computation.2 | async-start | bytes 1966080 | tf_op jit(solution)/shard_map/all_to_all | solution.py:643
  165.5 5.6 %collective-permute-start.20 = (bf16[2,120,128]{2,1,0:T(8,128)(2,1)}, bf16[2,120,128]{2,1,0:T(8,128)(2,1)}, u32[]{:S(2)}, u32[]{:S(2)}) collective-permute-start(bf16[2,120,128]{2,1,0:T(8,128)(2,1)} %get-tuple-element.69), channel_id=1, source_target_pairs={{0,0},{8,32},{16,64},{24,96},{32,8},{40,40},{48,72},{56,104},{64,1... | collective-permute-start | bytes 184328 | tf_op jit(solution)/shard_map/ppermute | solution.py:652
  171.2 1.8 collective-permute-start.22
  173.0 1.4 collective-permute-start.23
  174.3 2.6 %collective-permute-done.22.p2 = bf16[2,120,128]{2,1,0:T(8,128)(2,1)} collective-permute-done((bf16[2,120,128]{2,1,0:T(8,128)(2,1)}, bf16[2,120,128]{2,1,0:T(8,128)(2,1)}, u32[]{:S(2)}, u32[]{:S(2)}) %collective-permute-start.22) | collective-permute-done | bytes 61472 | tf_op jit(solution)/shard_map/ppermute | solution.py:652
  177.0 3.6 %collective-permute-done.23.p3 = bf16[2,120,128]{2,1,0:T(8,128)(2,1)} collective-permute-done((bf16[2,120,128]{2,1,0:T(8,128)(2,1)}, bf16[2,120,128]{2,1,0:T(8,128)(2,1)}, u32[]{:S(2)}, u32[]{:S(2)}) %collective-permute-start.23) | collective-permute-done | bytes 61472 | tf_op jit(solution)/shard_map/ppermute | solution.py:652
  180.5 3.1 %from_lines.1.i0 = bf16[4,48,1280]{2,1,0:T(8,128)(2,1)} custom-call(s32[3]{0:T(128)} %pad_add_fusion.where_ref, bf16[8,48,1280]{2,1,0:T(8,128)(2,1)} %all-to-all-done.2.modes_ref, bf16[8,384,192]{2,1,0:T(8,128)(2,1)} %constant.28.clone.table_ref.refs_8_), custom_call_target="tpu_custom_call" | custom-call | bytes 9000000 | tf_op jit(solution)/shard_map/from_lines/pallas_call | solution.py:379
  183.7 3.4 %collective-permute-start.24 = (bf16[4,48,1280]{2,1,0:T(8,128)(2,1)}, bf16[4,48,1280]{2,1,0:T(8,128)(2,1)S(1)}, u32[]{:S(2)}, u32[]{:S(2)}) collective-permute-start(bf16[4,48,1280]{2,1,0:T(8,128)(2,1)} %from_lines.1.i0), channel_id=1, source_target_pairs={{0,16},{8,24},{16,0},{24,8},{1,17},{9,25},{17,1},{25,9},{2,18},{10... | collective-permute-start | bytes 1474568 | tf_op jit(solution)/shard_map/ppermute | solution.py:612
  187.0 3.0 %collective-permute-start.25 = (bf16[4,48,1280]{2,1,0:T(8,128)(2,1)}, bf16[4,48,1280]{2,1,0:T(8,128)(2,1)}, u32[]{:S(2)}, u32[]{:S(2)}) collective-permute-start(bf16[4,48,1280]{2,1,0:T(8,128)(2,1)} %from_lines.1.i0), channel_id=1, source_target_pairs={{0,8},{8,0},{16,24},{24,16},{1,9},{9,1},{17,25},{25,17},{2,10},{10... | collective-permute-start | bytes 1474568 | tf_op jit(solution)/shard_map/ppermute | solution.py:612
  190.0 3.1 %outer_sum.1 = f32[3,20,40,128]{3,2,1,0:T(8,128)} custom-call(bf16[2,120,128]{2,1,0:T(8,128)(2,1)} %collective-permute-done.20.p0, bf16[2,120,128]{2,1,0:T(8,128)(2,1)} %collective-permute-done.21.p1, bf16[2,120,128]{2,1,0:T(8,128)(2,1)} %collective-permute-done.22.p2, bf16[2,120,128]{2,1,0:T(8,128)(2,1)} %collective-permute-done.23.p3), custom_call_target="tpu_custom_call" | custom-call | bytes 9000000 | tf_op jit(solution)/shard_map/outer_sum/pallas_call | solution.py:602
  193.1 2.0 collective-permute-done.24.i1
  196.0 4.2 %collective-permute-start.26 = (bf16[4,48,1280]{2,1,0:T(8,128)(2,1)S(1)}, bf16[4,48,1280]{2,1,0:T(8,128)(2,1)}, u32[]{:S(2)}, u32[]{:S(2)}) collective-permute-start(bf16[4,48,1280]{2,1,0:T(8,128)(2,1)S(1)} %collective-permute-done.24.i1), channel_id=1, source_target_pairs={{0,8},{8,0},{16,24},{24,16},{1,9},{9,1},{17,25},{25,17},{2,10},{10... | collective-permute-start | bytes 1474568 | tf_op jit(solution)/shard_map/ppermute | solution.py:612
  200.2 1.6 collective-permute-done.26.i3
  201.8 9.4 %end_columns.1 = bf16[20,64,2048]{2,1,0:T(8,128)(2,1)} custom-call(s32[3]{0:T(128)} %pad_add_fusion.where_ref, bf16[4,48,1280]{2,1,0:T(8,128)(2,1)} %from_lines.1.i0, bf16[4,48,1280]{2,1,0:T(8,128)(2,1)} %copy-done.2, bf16[4,48,1280]{2,1,0:T(8,128)(2,1)} %collective-permute-done.25.i2, bf16[4,48,1280]{2,1,0:T(8,128)(2,1)} %collective-permute-done.26.i3, ...), custom_call_target="tpu_custom_call" | custom-call | bytes 30000000 | tf_op jit(solution)/shard_map/end_columns/pallas_call | solution.py:326
  (61 shorter events, 10.3 us)
Async XLA Ops:
  0.6 21.3 %copy-start = (bf16[160,20]{1,0:T(8,128)(2,1)S(1)}, bf16[160,20]{1,0:T(8,128)(2,1)}, u32[]{:S(2)}) copy-start(bf16[160,20]{1,0:T(8,128)(2,1)} %constant.24.clone) | copy-start | bytes 19204
  0.6 21.3 %copy-start.6 = (bf16[160,160]{1,0:T(8,128)(2,1)S(1)}, bf16[160,160]{1,0:T(8,128)(2,1)}, u32[]{:S(2)}) copy-start(bf16[160,160]{1,0:T(8,128)(2,1)} %constant.27.clone) | copy-start | bytes 153604
  0.7 21.3 %copy-start.14 = (bf16[20,20]{1,0:T(8,128)(2,1)S(1)}, bf16[20,20]{1,0:T(8,128)(2,1)}, u32[]{:S(2)}) copy-start(bf16[20,20]{1,0:T(8,128)(2,1)} %param.12) | copy-start | bytes 2404
  0.7 13.8 %collective-permute-start = (bf16[3,20,20,2,128]{4,3,2,1,0:T(2,128)(2,1)}, bf16[3,20,20,2,128]{4,3,2,1,0:T(2,128)(2,1)}, u32[]{:S(2)}, u32[]{:S(2)}) collective-permute-start(bf16[3,20,20,2,128]{4,3,2,1,0:T(2,128)(2,1)} %param.11), channel_id=1, source_target_pairs={{0,0},{8,32},{16,64},{24,96},{32,72},{40,104},{48,8},{56,40},{64,1... | collective-permute-start | bytes 1843208 | tf_op jit(solution)/shard_map/ppermute | solution.py:661
  14.5 4.2 %collective-permute-start.2 = (bf16[4,48,1280]{2,1,0:T(8,128)(2,1)}, bf16[4,48,1280]{2,1,0:T(8,128)(2,1)S(1)}, u32[]{:S(2)}, u32[]{:S(2)}) collective-permute-start(bf16[4,48,1280]{2,1,0:T(8,128)(2,1)} %get-tuple-element.49), channel_id=1, source_target_pairs={{0,8},{8,0},{16,24},{24,16},{1,9},{9,1},{17,25},{25,17},{2,10},{10... | collective-permute-start | bytes 1474568 | tf_op jit(solution)/shard_map/ppermute | solution.py:612
  16.9 19.1 %collective-permute-start.4 = (bf16[3,20,20,2,128]{4,3,2,1,0:T(2,128)(2,1)}, bf16[3,20,20,2,128]{4,3,2,1,0:T(2,128)(2,1)}, u32[]{:S(2)}, u32[]{:S(2)}) collective-permute-start(bf16[3,20,20,2,128]{4,3,2,1,0:T(2,128)(2,1)} %collective-permute-done), channel_id=1, source_target_pairs={{32,0},{64,32},{96,64},{0,96},{33,1},{65,33},{97,65},{1,97},{34,2}... | collective-permute-start | bytes 1843208 | tf_op jit(solution)/shard_map/ppermute | solution.py:630
  18.7 17.3 %collective-permute-start.5 = (bf16[3,20,20,2,128]{4,3,2,1,0:T(2,128)(2,1)}, bf16[3,20,20,2,128]{4,3,2,1,0:T(2,128)(2,1)}, u32[]{:S(2)}, u32[]{:S(2)}) collective-permute-start(bf16[3,20,20,2,128]{4,3,2,1,0:T(2,128)(2,1)} %collective-permute-done), channel_id=1, source_target_pairs={{96,0},{0,32},{32,64},{64,96},{97,1},{1,33},{33,65},{65,97},{98,2}... | collective-permute-start | bytes 1843208 | tf_op jit(solution)/shard_map/ppermute | solution.py:630
  19.8 12.7 %collective-permute-start.3 = (bf16[4,48,1280]{2,1,0:T(8,128)(2,1)S(1)}, bf16[4,48,1280]{2,1,0:T(8,128)(2,1)}, u32[]{:S(2)}, u32[]{:S(2)}) collective-permute-start(bf16[4,48,1280]{2,1,0:T(8,128)(2,1)S(1)} %add_convert_fusion.1), channel_id=1, source_target_pairs={{0,16},{8,24},{16,0},{24,8},{1,17},{9,25},{17,1},{25,9},{2,18},{10... | collective-permute-start | bytes 1474568 | tf_op jit(solution)/shard_map/ppermute | solution.py:612
  21.3 11.2 %collective-permute-start.1 = (bf16[4,48,1280]{2,1,0:T(8,128)(2,1)}, bf16[4,48,1280]{2,1,0:T(8,128)(2,1)}, u32[]{:S(2)}, u32[]{:S(2)}) collective-permute-start(bf16[4,48,1280]{2,1,0:T(8,128)(2,1)} %get-tuple-element.47), channel_id=1, source_target_pairs={{0,8},{8,0},{16,24},{24,16},{1,9},{9,1},{17,25},{25,17},{2,10},{10... | collective-permute-start | bytes 1474568 | tf_op jit(solution)/shard_map/ppermute | solution.py:612
  36.0 23.2 %all-to-all-start = ((bf16[8,48,1280]{2,1,0:T(8,128)(2,1)}), bf16[8,48,1280]{2,1,0:T(8,128)(2,1)}, u32[]{:S(2)}, u32[]{:S(2)}) async-start(bf16[8,48,1280]{2,1,0:T(8,128)(2,1)} %to_lines.2), calls=%async_computation | async-start | bytes 1966080 | tf_op jit(solution)/shard_map/all_to_all | solution.py:643
  43.6 15.6 %collective-permute-start.6 = (bf16[3,20,20,2,128]{4,3,2,1,0:T(2,128)(2,1)}, bf16[3,20,20,2,128]{4,3,2,1,0:T(2,128)(2,1)}, u32[]{:S(2)}, u32[]{:S(2)}) collective-permute-start(bf16[3,20,20,2,128]{4,3,2,1,0:T(2,128)(2,1)} %collective-permute-done), channel_id=1, source_target_pairs={{64,0},{96,32},{0,64},{32,96},{65,1},{97,33},{1,65},{33,97},{66,2}... | collective-permute-start | bytes 1843208 | tf_op jit(solution)/shard_map/ppermute | solution.py:630
  64.6 8.1 %collective-permute-start.7 = (bf16[48,1280]{1,0:T(8,128)(2,1)}, bf16[48,1280]{1,0:T(8,128)(2,1)S(1)}, u32[]{:S(2)}, u32[]{:S(2)}) collective-permute-start(bf16[48,1280]{1,0:T(8,128)(2,1)} %bitcast.24), channel_id=1, source_target_pairs={{1,0},{0,1},{3,2},{2,3},{5,4},{4,5},{7,6},{6,7},{9,8},{8,9},{11,10... | collective-permute-start | bytes 368648 | tf_op jit(solution)/shard_map/ppermute | solution.py:635
  67.3 6.0 %collective-permute-start.10 = (bf16[48,1280]{1,0:T(8,128)(2,1)}, bf16[48,1280]{1,0:T(8,128)(2,1)S(1)}, u32[]{:S(2)}, u32[]{:S(2)}) collective-permute-start(bf16[48,1280]{1,0:T(8,128)(2,1)} %bitcast.25), channel_id=1, source_target_pairs={{4,0},{5,1},{6,2},{7,3},{0,4},{1,5},{2,6},{3,7},{12,8},{13,9},{14,... | collective-permute-start | bytes 368648 | tf_op jit(solution)/shard_map/ppermute | solution.py:638
  70.0 6.6 %collective-permute-start.12 = (bf16[48,1280]{1,0:T(8,128)(2,1)}, bf16[48,1280]{1,0:T(8,128)(2,1)S(1)}, u32[]{:S(2)}, u32[]{:S(2)}) collective-permute-start(bf16[48,1280]{1,0:T(8,128)(2,1)} %bitcast.26), channel_id=1, source_target_pairs={{6,0},{7,1},{0,2},{1,3},{2,4},{3,5},{4,6},{5,7},{14,8},{15,9},{8,1... | collective-permute-start | bytes 368648 | tf_op jit(solution)/shard_map/ppermute | solution.py:638
  70.3 7.2 %collective-permute-start.8 = (bf16[48,1280]{1,0:T(8,128)(2,1)}, bf16[48,1280]{1,0:T(8,128)(2,1)S(1)}, u32[]{:S(2)}, u32[]{:S(2)}) collective-permute-start(bf16[48,1280]{1,0:T(8,128)(2,1)} %bitcast.27), channel_id=1, source_target_pairs={{2,0},{3,1},{4,2},{5,3},{6,4},{7,5},{0,6},{1,7},{10,8},{11,9},{12,... | collective-permute-start | bytes 368648 | tf_op jit(solution)/shard_map/ppermute | solution.py:638
  72.7 0.7 copy-start.8
  72.7 6.3 %collective-permute-start.11 = (bf16[48,1280]{1,0:T(8,128)(2,1)S(1)}, bf16[48,1280]{1,0:T(8,128)(2,1)S(1)}, u32[]{:S(2)}, u32[]{:S(2)}) collective-permute-start(bf16[48,1280]{1,0:T(8,128)(2,1)S(1)} %collective-permute-done.7.refs_1_), channel_id=1, source_target_pairs={{4,0},{5,1},{6,2},{7,3},{0,4},{1,5},{2,6},{3,7},{12,8},{13,9},{14,... | collective-permute-start | bytes 368648 | tf_op jit(solution)/shard_map/ppermute | solution.py:638
  72.8 7.4 %collective-permute-start.13 = (bf16[48,1280]{1,0:T(8,128)(2,1)S(1)}, bf16[48,1280]{1,0:T(8,128)(2,1)S(1)}, u32[]{:S(2)}, u32[]{:S(2)}) collective-permute-start(bf16[48,1280]{1,0:T(8,128)(2,1)S(1)} %collective-permute-done.7.refs_1_), channel_id=1, source_target_pairs={{6,0},{7,1},{0,2},{1,3},{2,4},{3,5},{4,6},{5,7},{14,8},{15,9},{8,1... | collective-permute-start | bytes 368648 | tf_op jit(solution)/shard_map/ppermute | solution.py:638
  73.4 6.8 %copy-start.9 = (bf16[48,1280]{1,0:T(8,128)(2,1)}, bf16[48,1280]{1,0:T(8,128)(2,1)S(1)}, u32[]{:S(2)}) copy-start(bf16[48,1280]{1,0:T(8,128)(2,1)S(1)} %collective-permute-done.10.refs_4_) | copy-start | bytes 368644
  73.4 7.7 %collective-permute-start.9 = (bf16[48,1280]{1,0:T(8,128)(2,1)S(1)}, bf16[48,1280]{1,0:T(8,128)(2,1)}, u32[]{:S(2)}, u32[]{:S(2)}) collective-permute-start(bf16[48,1280]{1,0:T(8,128)(2,1)S(1)} %collective-permute-done.7.refs_1_), channel_id=1, source_target_pairs={{2,0},{3,1},{4,2},{5,3},{6,4},{7,5},{0,6},{1,7},{10,8},{11,9},{12,... | collective-permute-start | bytes 368648 | tf_op jit(solution)/shard_map/ppermute | solution.py:638
  76.6 3.6 %copy-start.10 = (bf16[48,1280]{1,0:T(8,128)(2,1)}, bf16[48,1280]{1,0:T(8,128)(2,1)S(1)}, u32[]{:S(2)}) copy-start(bf16[48,1280]{1,0:T(8,128)(2,1)S(1)} %collective-permute-done.12.refs_6_) | copy-start | bytes 368644
  77.5 2.7 %copy-start.11 = (bf16[48,1280]{1,0:T(8,128)(2,1)}, bf16[48,1280]{1,0:T(8,128)(2,1)S(1)}, u32[]{:S(2)}) copy-start(bf16[48,1280]{1,0:T(8,128)(2,1)S(1)} %collective-permute-done.8.refs_2_) | copy-start | bytes 368644
  79.0 1.2 copy-start.12
  80.2 0.6 copy-start.13
  84.3 9.0 %collective-permute-start.14 = (bf16[4,48,1280]{2,1,0:T(8,128)(2,1)}, bf16[4,48,1280]{2,1,0:T(8,128)(2,1)S(1)}, u32[]{:S(2)}, u32[]{:S(2)}) collective-permute-start(bf16[4,48,1280]{2,1,0:T(8,128)(2,1)} %from_line_set.1.i0), channel_id=1, source_target_pairs={{0,16},{8,24},{16,0},{24,8},{1,17},{9,25},{17,1},{25,9},{2,18},{10... | collective-permute-start | bytes 1474568 | tf_op jit(solution)/shard_map/ppermute | solution.py:612
  84.9 13.3 %collective-permute-start.15 = (bf16[4,48,1280]{2,1,0:T(8,128)(2,1)}, bf16[4,48,1280]{2,1,0:T(8,128)(2,1)S(1)}, u32[]{:S(2)}, u32[]{:S(2)}) collective-permute-start(bf16[4,48,1280]{2,1,0:T(8,128)(2,1)} %from_line_set.1.i0), channel_id=1, source_target_pairs={{0,8},{8,0},{16,24},{24,16},{1,9},{9,1},{17,25},{25,17},{2,10},{10... | collective-permute-start | bytes 1474568 | tf_op jit(solution)/shard_map/ppermute | solution.py:612
  93.3 6.3 %copy-start.3 = (bf16[4,48,1280]{2,1,0:T(8,128)(2,1)}, bf16[4,48,1280]{2,1,0:T(8,128)(2,1)S(1)}, u32[]{:S(2)}) copy-start(bf16[4,48,1280]{2,1,0:T(8,128)(2,1)S(1)} %collective-permute-done.14.i1) | copy-start | bytes 1474564
  93.3 6.3 %collective-permute-start.16 = (bf16[4,48,1280]{2,1,0:T(8,128)(2,1)S(1)}, bf16[4,48,1280]{2,1,0:T(8,128)(2,1)S(1)}, u32[]{:S(2)}, u32[]{:S(2)}) collective-permute-start(bf16[4,48,1280]{2,1,0:T(8,128)(2,1)S(1)} %collective-permute-done.14.i1), channel_id=1, source_target_pairs={{0,8},{8,0},{16,24},{24,16},{1,9},{9,1},{17,25},{25,17},{2,10},{10... | collective-permute-start | bytes 1474568 | tf_op jit(solution)/shard_map/ppermute | solution.py:612
  98.2 1.5 copy-start.4
  99.6 0.8 copy-start.5
  100.4 20.0 %copy-start.1 = (bf16[160,20]{1,0:T(8,128)(2,1)S(1)}, bf16[160,20]{1,0:T(8,128)(2,1)}, u32[]{:S(2)}) copy-start(bf16[160,20]{1,0:T(8,128)(2,1)} %constant.24.clone) | copy-start | bytes 19204
  100.4 20.0 %copy-start.7 = (bf16[160,160]{1,0:T(8,128)(2,1)S(1)}, bf16[160,160]{1,0:T(8,128)(2,1)}, u32[]{:S(2)}) copy-start(bf16[160,160]{1,0:T(8,128)(2,1)} %constant.27.clone) | copy-start | bytes 153604
  100.4 20.0 %copy-start.15 = (bf16[20,20]{1,0:T(8,128)(2,1)S(1)}, bf16[20,20]{1,0:T(8,128)(2,1)}, u32[]{:S(2)}) copy-start(bf16[20,20]{1,0:T(8,128)(2,1)} %param.12) | copy-start | bytes 2404
  115.8 2.2 %collective-permute-start.18 = (bf16[4,48,1280]{2,1,0:T(8,128)(2,1)}, bf16[4,48,1280]{2,1,0:T(8,128)(2,1)S(1)}, u32[]{:S(2)}, u32[]{:S(2)}) collective-permute-start(bf16[4,48,1280]{2,1,0:T(8,128)(2,1)} %get-tuple-element.61), channel_id=1, source_target_pairs={{0,8},{8,0},{16,24},{24,16},{1,9},{9,1},{17,25},{25,17},{2,10},{10... | collective-permute-start | bytes 1474568 | tf_op jit(solution)/shard_map/ppermute | solution.py:612
  119.1 12.6 %collective-permute-start.19 = (bf16[4,48,1280]{2,1,0:T(8,128)(2,1)S(1)}, bf16[4,48,1280]{2,1,0:T(8,128)(2,1)}, u32[]{:S(2)}, u32[]{:S(2)}) collective-permute-start(bf16[4,48,1280]{2,1,0:T(8,128)(2,1)S(1)} %add_convert_fusion), channel_id=1, source_target_pairs={{0,16},{8,24},{16,0},{24,8},{1,17},{9,25},{17,1},{25,9},{2,18},{10... | collective-permute-start | bytes 1474568 | tf_op jit(solution)/shard_map/ppermute | solution.py:612
  119.8 12.0 %collective-permute-start.17 = (bf16[4,48,1280]{2,1,0:T(8,128)(2,1)}, bf16[4,48,1280]{2,1,0:T(8,128)(2,1)}, u32[]{:S(2)}, u32[]{:S(2)}) collective-permute-start(bf16[4,48,1280]{2,1,0:T(8,128)(2,1)} %get-tuple-element.59), channel_id=1, source_target_pairs={{0,8},{8,0},{16,24},{24,16},{1,9},{9,1},{17,25},{25,17},{2,10},{10... | collective-permute-start | bytes 1474568 | tf_op jit(solution)/shard_map/ppermute | solution.py:612
  161.2 19.4 %all-to-all-start.2 = ((bf16[8,48,1280]{2,1,0:T(8,128)(2,1)}), bf16[8,48,1280]{2,1,0:T(8,128)(2,1)}, u32[]{:S(2)}, u32[]{:S(2)}) async-start(bf16[8,48,1280]{2,1,0:T(8,128)(2,1)} %get-tuple-element.68), calls=%async_computation.2 | async-start | bytes 1966080 | tf_op jit(solution)/shard_map/all_to_all | solution.py:643
  165.5 8.9 %collective-permute-start.20 = (bf16[2,120,128]{2,1,0:T(8,128)(2,1)}, bf16[2,120,128]{2,1,0:T(8,128)(2,1)}, u32[]{:S(2)}, u32[]{:S(2)}) collective-permute-start(bf16[2,120,128]{2,1,0:T(8,128)(2,1)} %get-tuple-element.69), channel_id=1, source_target_pairs={{0,0},{8,32},{16,64},{24,96},{32,8},{40,40},{48,72},{56,104},{64,1... | collective-permute-start | bytes 184328 | tf_op jit(solution)/shard_map/ppermute | solution.py:652
  171.1 3.2 %collective-permute-start.21 = (bf16[2,120,128]{2,1,0:T(8,128)(2,1)}, bf16[2,120,128]{2,1,0:T(8,128)(2,1)}, u32[]{:S(2)}, u32[]{:S(2)}) collective-permute-start(bf16[2,120,128]{2,1,0:T(8,128)(2,1)} %get-tuple-element.70), channel_id=1, source_target_pairs={{0,8},{8,40},{16,72},{24,104},{32,16},{40,48},{48,80},{56,112},{64... | collective-permute-start | bytes 184328 | tf_op jit(solution)/shard_map/ppermute | solution.py:652
  171.2 5.8 %collective-permute-start.22 = (bf16[2,120,128]{2,1,0:T(8,128)(2,1)}, bf16[2,120,128]{2,1,0:T(8,128)(2,1)}, u32[]{:S(2)}, u32[]{:S(2)}) collective-permute-start(bf16[2,120,128]{2,1,0:T(8,128)(2,1)} %get-tuple-element.71), channel_id=1, source_target_pairs={{0,16},{8,48},{16,80},{24,112},{32,24},{40,56},{48,88},{56,120},{6... | collective-permute-start | bytes 184328 | tf_op jit(solution)/shard_map/ppermute | solution.py:652
  173.0 7.6 %collective-permute-start.23 = (bf16[2,120,128]{2,1,0:T(8,128)(2,1)}, bf16[2,120,128]{2,1,0:T(8,128)(2,1)}, u32[]{:S(2)}, u32[]{:S(2)}) collective-permute-start(bf16[2,120,128]{2,1,0:T(8,128)(2,1)} %get-tuple-element.72), channel_id=1, source_target_pairs={{0,24},{8,56},{16,88},{24,120},{32,0},{40,32},{48,64},{56,96},{64,... | collective-permute-start | bytes 184328 | tf_op jit(solution)/shard_map/ppermute | solution.py:652
  183.7 11.5 %collective-permute-start.24 = (bf16[4,48,1280]{2,1,0:T(8,128)(2,1)}, bf16[4,48,1280]{2,1,0:T(8,128)(2,1)S(1)}, u32[]{:S(2)}, u32[]{:S(2)}) collective-permute-start(bf16[4,48,1280]{2,1,0:T(8,128)(2,1)} %from_lines.1.i0), channel_id=1, source_target_pairs={{0,16},{8,24},{16,0},{24,8},{1,17},{9,25},{17,1},{25,9},{2,18},{10... | collective-permute-start | bytes 1474568 | tf_op jit(solution)/shard_map/ppermute | solution.py:612
  187.0 13.2 %collective-permute-start.25 = (bf16[4,48,1280]{2,1,0:T(8,128)(2,1)}, bf16[4,48,1280]{2,1,0:T(8,128)(2,1)}, u32[]{:S(2)}, u32[]{:S(2)}) collective-permute-start(bf16[4,48,1280]{2,1,0:T(8,128)(2,1)} %from_lines.1.i0), channel_id=1, source_target_pairs={{0,8},{8,0},{16,24},{24,16},{1,9},{9,1},{17,25},{25,17},{2,10},{10... | collective-permute-start | bytes 1474568 | tf_op jit(solution)/shard_map/ppermute | solution.py:612
  195.2 0.8 copy-start.2
  196.0 5.9 %collective-permute-start.26 = (bf16[4,48,1280]{2,1,0:T(8,128)(2,1)S(1)}, bf16[4,48,1280]{2,1,0:T(8,128)(2,1)}, u32[]{:S(2)}, u32[]{:S(2)}) collective-permute-start(bf16[4,48,1280]{2,1,0:T(8,128)(2,1)S(1)} %collective-permute-done.24.i1), channel_id=1, source_target_pairs={{0,8},{8,0},{16,24},{24,16},{1,9},{9,1},{17,25},{25,17},{2,10},{10... | collective-permute-start | bytes 1474568 | tf_op jit(solution)/shard_map/ppermute | solution.py:612

commit v11 on v10

--- a/solution.py
+++ b/solution.py
@@ -680,7 +680,8 @@
     parts, bypass = start_slabs(pieces, bypass_columns(grad, mixer, jnp.zeros_like(bias)))
     arrived = exchange_lines(to_lines(where, *parts))
     modes, *pairs = mode_call(back_kernel, "back_modes", where, arrived, weights, spectra)
-    modes, *pairs = lax.optimization_barrier((exchange_lines(modes), *to_owners(pairs)))
+    pairs = to_owners(pairs)
+    modes, *pairs[:2] = lax.optimization_barrier((exchange_lines(modes), *pairs[:2]))
     *coeffs, weight_grad = share_slabs(from_lines(where, modes), outer_sum(pairs))
     field_grad = end_columns(where, coeffs, bypass)
     return (

time: 213 us -> 215 us (level)
  waiting for transfers between devices: 43.1 us -> 48.1 us
  starting transfers between devices: 67.3 us -> 64 us
    ppermute x12, starting transfers between devices: 26.3 us -> 18.6 us  [swap(): return lax.ppermute(values, 'gx', [(i, i ^ bit) for i in range(GX)])]
    all_to_all x2, waiting for transfers between devices: 0.01 us -> 5.74 us  [exchange_lines(): return lax.all_to_all(parts, 'gy', split_axis=0, concat_axis=0, tiled=True)]
    ppermute x4, starting transfers between devices: 8.86 us -> 13.3 us  [to_owners(): moved.append(lax.ppermute(chunk, ('dp', 'gx'), pairs))]
  transfers between devices with their start and end apart: 29 -> 29, of which waited for: 16 -> 17; matrix products, arithmetic and copies ran while one was open for 2% -> 2% of each run, Pallas kernels for 13% -> 12%
where the time goes in v11:
time: 215 us; the launch traced here: 214 us
  Pallas kernels  72.8 us (34%)
  starting transfers between devices  64 us (30%)
  waiting for transfers between devices  48.1 us (22%)
  blocking collectives  19.9 us (9%)
  local copies, waits for them, and re-layouts  3.43 us (2%)
  other arithmetic  2.88 us (1%)
    all_to_all x1, blocking collectives, exchange_lines(): return lax.all_to_all(parts, 'gy', split_axis=0, concat_axis=0, tiled=True)  19.9 us
    ppermute x12, starting transfers between devices, swap(): return lax.ppermute(values, 'gx', [(i, i ^ bit) for i in range(GX)])  18.6 us
    ppermute x12, waiting for transfers between devices, swap(): return lax.ppermute(values, 'gx', [(i, i ^ bit) for i in range(GX)])  16.3 us
    pallas_call x1, Pallas kernels, middle_columns(): pl.pallas_call(middle_kernel, grid_spec=pltpu.PrefetchScalarGridSpec(num_...  15.4 us
    pallas_call x4, Pallas kernels, line_call(): pl.pallas_call(kernel, grid_spec=pltpu.PrefetchScalarGridSpec(num_scalar_...  13.3 us
    ppermute x4, starting transfers between devices, to_owners(): moved.append(lax.ppermute(chunk, ('dp', 'gx'), pairs))  13.3 us
    ppermute x3, waiting for transfers between devices, gather_weights(): lax.ppermute(weight, 'dp', [((a + k) % DP, a) for a in range(DP)])  12.8 us
    pallas_call x2, Pallas kernels, bypass_columns(): pl.pallas_call(bypass_kernel, grid=(STEPS,), in_specs=[pl.BlockSpec(memor...  12.4 us
  transfers between devices with their start and end apart: 29, of which 17 were waited for; matrix products, arithmetic and copies ran while one was open for 2% of the time, Pallas kernels for 12%

profile of v11, /device:TPU:1, one launch (start us, length us, event | category | flops | bytes accessed | tf_op | source)
XLA Modules:
  0.0 213.7 jit_solution(6845372434598956229)
XLA Ops:
  0.7 4.6 %collective-permute-start = (bf16[3,20,20,2,128]{4,3,2,1,0:T(2,128)(2,1)}, bf16[3,20,20,2,128]{4,3,2,1,0:T(2,128)(2,1)}, u32[]{:S(2)}, u32[]{:S(2)}) collective-permute-start(bf16[3,20,20,2,128]{4,3,2,1,0:T(2,128)(2,1)} %param.11), channel_id=1, source_target_pairs={{0,0},{8,32},{16,64},{24,96},{32,72},{40,104},{48,8},{56,40},{64,1... | collective-permute-start | bytes 1843208 | tf_op jit(solution)/shard_map/ppermute | solution.py:661
  5.9 7.6 %start_columns.1 = (bf16[4,48,1280]{2,1,0:T(8,128)(2,1)}, bf16[4,48,1280]{2,1,0:T(8,128)(2,1)}, bf16[4,48,1280]{2,1,0:T(8,128)(2,1)}, bf16[4,48,1280]{2,1,0:T(8,128)(2,1)}) custom-call(s32[3]{0:T(128)} %pad_add_fusion.where_ref, bf16[20,64,2048]{2,1,0:T(8,128)(2,1)} %bitcast.19, bf16[4,24,512]{2,1,0:T(8,128)(2,1)} %constant.25.clone.strip_ref, ...), custom_call_target="tpu_custom_call" | custom-call | bytes 24000000 | tf_op jit(solution)/shard_map/start_columns/pallas_call | solution.py:290
  13.5 0.9 collective-permute-done
  14.5 2.5 %collective-permute-start.2 = (bf16[4,48,1280]{2,1,0:T(8,128)(2,1)}, bf16[4,48,1280]{2,1,0:T(8,128)(2,1)S(1)}, u32[]{:S(2)}, u32[]{:S(2)}) collective-permute-start(bf16[4,48,1280]{2,1,0:T(8,128)(2,1)} %get-tuple-element.47), channel_id=1, source_target_pairs={{0,8},{8,0},{16,24},{24,16},{1,9},{9,1},{17,25},{25,17},{2,10},{10... | collective-permute-start | bytes 1474568 | tf_op jit(solution)/shard_map/ppermute | solution.py:612
  16.9 1.7 collective-permute-start.4
  18.7 1.1 add_convert_fusion.1
  19.8 1.5 collective-permute-start.3
  22.9 6.2 %bypass_columns.2.bypass_ref = bf16[20,64,2048]{2,1,0:T(8,128)(2,1)} custom-call(f32[20]{0:T(128)} %shift_ref.1, bf16[20,64,2048]{2,1,0:T(8,128)(2,1)} %bitcast.20, bf16[160,160]{1,0:T(8,128)(2,1)} %fusion.mixer_ref), custom_call_target="tpu_custom_call" | custom-call | bytes 18000000 | tf_op jit(solution)/shard_map/bypass_columns/pallas_call | solution.py:272
  29.1 3.4 %collective-permute-done.3.c_ref = bf16[4,48,1280]{2,1,0:T(8,128)(2,1)} collective-permute-done((bf16[4,48,1280]{2,1,0:T(8,128)(2,1)S(1)}, bf16[4,48,1280]{2,1,0:T(8,128)(2,1)}, u32[]{:S(2)}, u32[]{:S(2)}) %collective-permute-start.3) | collective-permute-done | bytes 491552 | tf_op jit(solution)/shard_map/ppermute | solution.py:612
  32.4 3.5 %to_lines.2 = bf16[8,48,1280]{2,1,0:T(8,128)(2,1)} custom-call(s32[3]{0:T(128)} %pad_add_fusion.where_ref, bf16[4,48,1280]{2,1,0:T(8,128)(2,1)} %get-tuple-element.44.a_ref, bf16[4,48,1280]{2,1,0:T(8,128)(2,1)} %collective-permute-done.1.b_ref, bf16[4,48,1280]{2,1,0:T(8,128)(2,1)} %collective-permute-done.3.c_ref, ...), custom_call_target="tpu_custom_call" | custom-call | bytes 9000000 | tf_op jit(solution)/shard_map/to_lines/pallas_call | solution.py:379
  35.9 7.7 %all-to-all-start = ((bf16[8,48,1280]{2,1,0:T(8,128)(2,1)}), bf16[8,48,1280]{2,1,0:T(8,128)(2,1)}, u32[]{:S(2)}, u32[]{:S(2)}) async-start(bf16[8,48,1280]{2,1,0:T(8,128)(2,1)} %to_lines.2), calls=%async_computation | async-start | bytes 1966080 | tf_op jit(solution)/shard_map/all_to_all | solution.py:643
  43.6 2.8 %collective-permute-start.6 = (bf16[3,20,20,2,128]{4,3,2,1,0:T(2,128)(2,1)}, bf16[3,20,20,2,128]{4,3,2,1,0:T(2,128)(2,1)}, u32[]{:S(2)}, u32[]{:S(2)}) collective-permute-start(bf16[3,20,20,2,128]{4,3,2,1,0:T(2,128)(2,1)} %collective-permute-done), channel_id=1, source_target_pairs={{64,0},{96,32},{0,64},{32,96},{65,1},{97,33},{1,65},{33,97},{66,2}... | collective-permute-start | bytes 1843208 | tf_op jit(solution)/shard_map/ppermute | solution.py:630
  46.4 12.8 %collective-permute-done.6 = bf16[3,20,20,2,128]{4,3,2,1,0:T(2,128)(2,1)} collective-permute-done((bf16[3,20,20,2,128]{4,3,2,1,0:T(2,128)(2,1)}, bf16[3,20,20,2,128]{4,3,2,1,0:T(2,128)(2,1)}, u32[]{:S(2)}, u32[]{:S(2)}) %collective-permute-start.6) | collective-permute-done | bytes 614432 | tf_op jit(solution)/shard_map/ppermute | solution.py:630
  59.2 5.4 %mix_modes.1 = (bf16[1,48,1280]{2,1,0:T(8,128)(2,1)}, bf16[1,120,128]{2,1,0:T(8,128)(2,1)}, bf16[1,120,128]{2,1,0:T(8,128)(2,1)}, bf16[1,120,128]{2,1,0:T(8,128)(2,1)}, bf16[1,120,128]{2,1,0:T(8,128)(2,1)}) custom-call(s32[3]{0:T(128)} %pad_add_fusion.where_ref, bf16[8,48,1280]{2,1,0:T(8,128)(2,1)} %all-to-all-done.arrived_ref, ...), custom_call_target="tpu_custom_call" | custom-call | bytes 15000000 | tf_op jit(solution)/shard_map/mix_modes/pallas_call | solution.py:555
  64.6 2.8 %collective-permute-start.7 = (bf16[48,1280]{1,0:T(8,128)(2,1)}, bf16[48,1280]{1,0:T(8,128)(2,1)S(1)}, u32[]{:S(2)}, u32[]{:S(2)}) collective-permute-start(bf16[48,1280]{1,0:T(8,128)(2,1)} %bitcast.24), channel_id=1, source_target_pairs={{1,0},{0,1},{3,2},{2,3},{5,4},{4,5},{7,6},{6,7},{9,8},{8,9},{11,10... | collective-permute-start | bytes 368648 | tf_op jit(solution)/shard_map/ppermute | solution.py:635
  67.4 2.7 %collective-permute-start.10 = (bf16[48,1280]{1,0:T(8,128)(2,1)}, bf16[48,1280]{1,0:T(8,128)(2,1)S(1)}, u32[]{:S(2)}, u32[]{:S(2)}) collective-permute-start(bf16[48,1280]{1,0:T(8,128)(2,1)} %bitcast.25), channel_id=1, source_target_pairs={{4,0},{5,1},{6,2},{7,3},{0,4},{1,5},{2,6},{3,7},{12,8},{13,9},{14,... | collective-permute-start | bytes 368648 | tf_op jit(solution)/shard_map/ppermute | solution.py:638
  70.4 2.4 %collective-permute-start.8 = (bf16[48,1280]{1,0:T(8,128)(2,1)}, bf16[48,1280]{1,0:T(8,128)(2,1)S(1)}, u32[]{:S(2)}, u32[]{:S(2)}) collective-permute-start(bf16[48,1280]{1,0:T(8,128)(2,1)} %bitcast.27), channel_id=1, source_target_pairs={{2,0},{3,1},{4,2},{5,3},{6,4},{7,5},{0,6},{1,7},{10,8},{11,9},{12,... | collective-permute-start | bytes 368648 | tf_op jit(solution)/shard_map/ppermute | solution.py:638
  73.4 2.2 %collective-permute-start.9 = (bf16[48,1280]{1,0:T(8,128)(2,1)S(1)}, bf16[48,1280]{1,0:T(8,128)(2,1)}, u32[]{:S(2)}, u32[]{:S(2)}) collective-permute-start(bf16[48,1280]{1,0:T(8,128)(2,1)S(1)} %collective-permute-done.7.refs_1_), channel_id=1, source_target_pairs={{2,0},{3,1},{4,2},{5,3},{6,4},{7,5},{0,6},{1,7},{10,8},{11,9},{12,... | collective-permute-start | bytes 368648 | tf_op jit(solution)/shard_map/ppermute | solution.py:638
  75.6 1.1 collective-permute-done.12.refs_6_
  76.6 0.9 collective-permute-done.8.refs_2_
  77.6 1.5 collective-permute-done.11.refs_5_
  79.0 1.2 collective-permute-done.13.refs_7_
  81.1 3.3 %from_line_set.1.i0 = bf16[4,48,1280]{2,1,0:T(8,128)(2,1)} custom-call(s32[3]{0:T(128)} %pad_add_fusion.where_ref, bf16[48,1280]{1,0:T(8,128)(2,1)} %bitcast.28, bf16[48,1280]{1,0:T(8,128)(2,1)} %copy-done.8, bf16[48,1280]{1,0:T(8,128)(2,1)} %copy-done.11, bf16[48,1280]{1,0:T(8,128)(2,1)} %collective-permute-done.9.refs_3_, bf16[48,1280]{1,0:T(8,128)(2,1)} %copy-done.9, ...), custom_call_target="tpu_custom_call" | custom-call | bytes 9000000 | tf_op jit(solution)/shard_map/from_line_set/pallas_call | solution.py:379
  84.9 4.1 %collective-permute-start.15 = (bf16[4,48,1280]{2,1,0:T(8,128)(2,1)}, bf16[4,48,1280]{2,1,0:T(8,128)(2,1)S(1)}, u32[]{:S(2)}, u32[]{:S(2)}) collective-permute-start(bf16[4,48,1280]{2,1,0:T(8,128)(2,1)} %from_line_set.1.i0), channel_id=1, source_target_pairs={{0,8},{8,0},{16,24},{24,16},{1,9},{9,1},{17,25},{25,17},{2,10},{10... | collective-permute-start | bytes 1474568 | tf_op jit(solution)/shard_map/ppermute | solution.py:612
  89.0 4.4 %collective-permute-done.14.i1 = bf16[4,48,1280]{2,1,0:T(8,128)(2,1)S(1)} collective-permute-done((bf16[4,48,1280]{2,1,0:T(8,128)(2,1)}, bf16[4,48,1280]{2,1,0:T(8,128)(2,1)S(1)}, u32[]{:S(2)}, u32[]{:S(2)}) %collective-permute-start.14) | collective-permute-done | bytes 491552 | tf_op jit(solution)/shard_map/ppermute | solution.py:612
  93.4 4.8 %collective-permute-start.16 = (bf16[4,48,1280]{2,1,0:T(8,128)(2,1)S(1)}, bf16[4,48,1280]{2,1,0:T(8,128)(2,1)S(1)}, u32[]{:S(2)}, u32[]{:S(2)}) collective-permute-start(bf16[4,48,1280]{2,1,0:T(8,128)(2,1)S(1)} %collective-permute-done.14.i1), channel_id=1, source_target_pairs={{0,8},{8,0},{16,24},{24,16},{1,9},{9,1},{17,25},{25,17},{2,10},{10... | collective-permute-start | bytes 1474568 | tf_op jit(solution)/shard_map/ppermute | solution.py:612
  98.2 1.5 collective-permute-done.16.i3
  100.5 15.4 %middle_columns.1 = (bf16[20,64,2048]{2,1,0:T(8,128)(2,1)}, bf16[20,64,2048]{2,1,0:T(8,128)(2,1)}, bf16[4,48,1280]{2,1,0:T(8,128)(2,1)}, bf16[4,48,1280]{2,1,0:T...) custom-call(s32[3]{0:T(128)} %pad_add_fusion.where_ref, bf16[4,48,1280]{2,1,0:T(8,128)(2,1)} %from_line_set.1.i0, ...), custom_call_target="tpu_custom_call" | custom-call | bytes 57000000 | tf_op jit(solution)/shard_map/middle_columns/pallas_call | solution.py:308
  116.3 1.7 collective-permute-done.18
  118.0 1.1 add_convert_fusion
  121.9 6.3 %bypass_columns.3.bypass_ref = bf16[20,64,2048]{2,1,0:T(8,128)(2,1)} custom-call(f32[20]{0:T(128)} %broadcast_1_shift_ref.2.shift_ref, bf16[20,64,2048]{2,1,0:T(8,128)(2,1)} %get-tuple-element.60.source_ref, bf16[160,160]{1,0:T(8,128)(2,1)} %fusion.1.mixer_ref), custom_call_target="tpu_custom_call" | custom-call | bytes 18000000 | tf_op jit(solution)/shard_map/bypass_columns/pallas_call | solution.py:272
  128.2 3.7 %collective-permute-done.19.c_ref = bf16[4,48,1280]{2,1,0:T(8,128)(2,1)} collective-permute-done((bf16[4,48,1280]{2,1,0:T(8,128)(2,1)S(1)}, bf16[4,48,1280]{2,1,0:T(8,128)(2,1)}, u32[]{:S(2)}, u32[]{:S(2)}) %collective-permute-start.19) | collective-permute-done | bytes 491552 | tf_op jit(solution)/shard_map/ppermute | solution.py:612
  131.8 3.5 %to_lines.3 = bf16[8,48,1280]{2,1,0:T(8,128)(2,1)} custom-call(s32[3]{0:T(128)} %pad_add_fusion.where_ref, bf16[4,48,1280]{2,1,0:T(8,128)(2,1)} %get-tuple-element.56.a_ref, bf16[4,48,1280]{2,1,0:T(8,128)(2,1)} %collective-permute-done.17.b_ref, bf16[4,48,1280]{2,1,0:T(8,128)(2,1)} %collective-permute-done.19.c_ref, ...), custom_call_target="tpu_custom_call" | custom-call | bytes 9000000 | tf_op jit(solution)/shard_map/to_lines/pallas_call | solution.py:379
  135.3 19.9 %all_to_all.15.arrived_ref = bf16[8,48,1280]{2,1,0:T(8,128)(2,1)} all-to-all(bf16[8,48,1280]{2,1,0:T(8,128)(2,1)} %to_lines.3), channel_id=1, replica_groups=mesh['dp'=4,'gx'=4,'gy'=8] {'gy'}, dimensions={0} | all-to-all | bytes 1966080 | tf_op jit(solution)/shard_map/all_to_all | solution.py:643
  155.2 6.1 %back_modes.1 = (bf16[8,48,1280]{2,1,0:T(8,128)(2,1)}, bf16[2,120,128]{2,1,0:T(8,128)(2,1)}, bf16[2,120,128]{2,1,0:T(8,128)(2,1)}, bf16[2,120,128]{2,1,0:T(8,128)(2,1)}, bf16[2,120,128]{2,1,0:T(8,128)(2,1)}) custom-call(s32[3]{0:T(128)} %pad_add_fusion.where_ref, bf16[8,48,1280]{2,1,0:T(8,128)(2,1)} %all_to_all.15.arrived_ref, ...), custom_call_target="tpu_custom_call" | custom-call | bytes 15000000 | tf_op jit(solution)/shard_map/back_modes/pallas_call | solution.py:555
  161.3 4.3 %all-to-all-start.2 = ((bf16[8,48,1280]{2,1,0:T(8,128)(2,1)}), bf16[8,48,1280]{2,1,0:T(8,128)(2,1)}, u32[]{:S(2)}, u32[]{:S(2)}) async-start(bf16[8,48,1280]{2,1,0:T(8,128)(2,1)} %get-tuple-element.66), calls=%async_computation.2 | async-start | bytes 1966080 | tf_op jit(solution)/shard_map/all_to_all | solution.py:643
  165.5 5.6 %collective-permute-start.20 = (bf16[2,120,128]{2,1,0:T(8,128)(2,1)}, bf16[2,120,128]{2,1,0:T(8,128)(2,1)}, u32[]{:S(2)}, u32[]{:S(2)}) collective-permute-start(bf16[2,120,128]{2,1,0:T(8,128)(2,1)} %get-tuple-element.67), channel_id=1, source_target_pairs={{0,0},{8,32},{16,64},{24,96},{32,8},{40,40},{48,72},{56,104},{64,1... | collective-permute-start | bytes 184328 | tf_op jit(solution)/shard_map/ppermute | solution.py:652
  171.2 2.4 %collective-permute-done.20.p0 = bf16[2,120,128]{2,1,0:T(8,128)(2,1)} collective-permute-done((bf16[2,120,128]{2,1,0:T(8,128)(2,1)}, bf16[2,120,128]{2,1,0:T(8,128)(2,1)}, u32[]{:S(2)}, u32[]{:S(2)}) %collective-permute-start.20) | collective-permute-done | bytes 61472 | tf_op jit(solution)/shard_map/ppermute | solution.py:652
  173.6 5.7 %all-to-all-done.2.modes_ref = bf16[8,48,1280]{2,1,0:T(8,128)(2,1)} async-done(((bf16[8,48,1280]{2,1,0:T(8,128)(2,1)}), bf16[8,48,1280]{2,1,0:T(8,128)(2,1)}, u32[]{:S(2)}, u32[]{:S(2)}) %all-to-all-start.2) | async-done | bytes 983072 | tf_op jit(solution)/shard_map/all_to_all | solution.py:643
  179.4 3.1 %from_lines.1.i0 = bf16[4,48,1280]{2,1,0:T(8,128)(2,1)} custom-call(s32[3]{0:T(128)} %pad_add_fusion.where_ref, bf16[8,48,1280]{2,1,0:T(8,128)(2,1)} %all-to-all-done.2.modes_ref, bf16[8,384,192]{2,1,0:T(8,128)(2,1)} %constant.28.clone.table_ref.refs_8_), custom_call_target="tpu_custom_call" | custom-call | bytes 9000000 | tf_op jit(solution)/shard_map/from_lines/pallas_call | solution.py:379
  182.5 1.1 collective-permute-start.22
  183.6 7.6 %collective-permute-start.23 = (bf16[2,120,128]{2,1,0:T(8,128)(2,1)}, bf16[2,120,128]{2,1,0:T(8,128)(2,1)S(1)}, u32[]{:S(2)}, u32[]{:S(2)}) collective-permute-start(bf16[2,120,128]{2,1,0:T(8,128)(2,1)} %get-tuple-element.72), channel_id=1, source_target_pairs={{0,16},{8,48},{16,80},{24,112},{32,24},{40,56},{48,88},{56,120},{6... | collective-permute-start | bytes 184328 | tf_op jit(solution)/shard_map/ppermute | solution.py:652
  191.4 2.0 collective-permute-done.23.p2
  193.4 3.2 %collective-permute-done.24.p3 = bf16[2,120,128]{2,1,0:T(8,128)(2,1)S(1)} collective-permute-done((bf16[2,120,128]{2,1,0:T(8,128)(2,1)}, bf16[2,120,128]{2,1,0:T(8,128)(2,1)S(1)}, u32[]{:S(2)}, u32[]{:S(2)}) %collective-permute-start.24) | collective-permute-done | bytes 61472 | tf_op jit(solution)/shard_map/ppermute | solution.py:652
  197.2 3.1 %outer_sum.1 = f32[3,20,40,128]{3,2,1,0:T(8,128)} custom-call(bf16[2,120,128]{2,1,0:T(8,128)(2,1)} %collective-permute-done.20.p0, bf16[2,120,128]{2,1,0:T(8,128)(2,1)} %collective-permute-done.21.p1, bf16[2,120,128]{2,1,0:T(8,128)(2,1)} %copy-done.14, bf16[2,120,128]{2,1,0:T(8,128)(2,1)} %copy-done.15), custom_call_target="tpu_custom_call" | custom-call | bytes 9000000 | tf_op jit(solution)/shard_map/outer_sum/pallas_call | solution.py:602
  201.1 1.5 collective-permute-start.26
  202.7 1.6 collective-permute-done.26.i3
  204.3 9.4 %end_columns.1 = bf16[20,64,2048]{2,1,0:T(8,128)(2,1)} custom-call(s32[3]{0:T(128)} %pad_add_fusion.where_ref, bf16[4,48,1280]{2,1,0:T(8,128)(2,1)} %from_lines.1.i0, bf16[4,48,1280]{2,1,0:T(8,128)(2,1)} %copy-done.2, bf16[4,48,1280]{2,1,0:T(8,128)(2,1)} %collective-permute-done.25.i2, bf16[4,48,1280]{2,1,0:T(8,128)(2,1)} %collective-permute-done.26.i3, ...), custom_call_target="tpu_custom_call" | custom-call | bytes 30000000 | tf_op jit(solution)/shard_map/end_columns/pallas_call | solution.py:326
  (65 shorter events, 10.3 us)
Async XLA Ops:
  0.6 21.3 %copy-start = (bf16[160,20]{1,0:T(8,128)(2,1)S(1)}, bf16[160,20]{1,0:T(8,128)(2,1)}, u32[]{:S(2)}) copy-start(bf16[160,20]{1,0:T(8,128)(2,1)} %constant.24.clone) | copy-start | bytes 19204
  0.6 21.3 %copy-start.6 = (bf16[160,160]{1,0:T(8,128)(2,1)S(1)}, bf16[160,160]{1,0:T(8,128)(2,1)}, u32[]{:S(2)}) copy-start(bf16[160,160]{1,0:T(8,128)(2,1)} %constant.27.clone) | copy-start | bytes 153604
  0.7 21.3 %copy-start.16 = (bf16[20,20]{1,0:T(8,128)(2,1)S(1)}, bf16[20,20]{1,0:T(8,128)(2,1)}, u32[]{:S(2)}) copy-start(bf16[20,20]{1,0:T(8,128)(2,1)} %param.12) | copy-start | bytes 2404
  0.7 13.8 %collective-permute-start = (bf16[3,20,20,2,128]{4,3,2,1,0:T(2,128)(2,1)}, bf16[3,20,20,2,128]{4,3,2,1,0:T(2,128)(2,1)}, u32[]{:S(2)}, u32[]{:S(2)}) collective-permute-start(bf16[3,20,20,2,128]{4,3,2,1,0:T(2,128)(2,1)} %param.11), channel_id=1, source_target_pairs={{0,0},{8,32},{16,64},{24,96},{32,72},{40,104},{48,8},{56,40},{64,1... | collective-permute-start | bytes 1843208 | tf_op jit(solution)/shard_map/ppermute | solution.py:661
  14.5 4.2 %collective-permute-start.2 = (bf16[4,48,1280]{2,1,0:T(8,128)(2,1)}, bf16[4,48,1280]{2,1,0:T(8,128)(2,1)S(1)}, u32[]{:S(2)}, u32[]{:S(2)}) collective-permute-start(bf16[4,48,1280]{2,1,0:T(8,128)(2,1)} %get-tuple-element.47), channel_id=1, source_target_pairs={{0,8},{8,0},{16,24},{24,16},{1,9},{9,1},{17,25},{25,17},{2,10},{10... | collective-permute-start | bytes 1474568 | tf_op jit(solution)/shard_map/ppermute | solution.py:612
  16.9 19.0 %collective-permute-start.4 = (bf16[3,20,20,2,128]{4,3,2,1,0:T(2,128)(2,1)}, bf16[3,20,20,2,128]{4,3,2,1,0:T(2,128)(2,1)}, u32[]{:S(2)}, u32[]{:S(2)}) collective-permute-start(bf16[3,20,20,2,128]{4,3,2,1,0:T(2,128)(2,1)} %collective-permute-done), channel_id=1, source_target_pairs={{32,0},{64,32},{96,64},{0,96},{33,1},{65,33},{97,65},{1,97},{34,2}... | collective-permute-start | bytes 1843208 | tf_op jit(solution)/shard_map/ppermute | solution.py:630
  18.7 17.2 %collective-permute-start.5 = (bf16[3,20,20,2,128]{4,3,2,1,0:T(2,128)(2,1)}, bf16[3,20,20,2,128]{4,3,2,1,0:T(2,128)(2,1)}, u32[]{:S(2)}, u32[]{:S(2)}) collective-permute-start(bf16[3,20,20,2,128]{4,3,2,1,0:T(2,128)(2,1)} %collective-permute-done), channel_id=1, source_target_pairs={{96,0},{0,32},{32,64},{64,96},{97,1},{1,33},{33,65},{65,97},{98,2}... | collective-permute-start | bytes 1843208 | tf_op jit(solution)/shard_map/ppermute | solution.py:630
  19.8 12.6 %collective-permute-start.3 = (bf16[4,48,1280]{2,1,0:T(8,128)(2,1)S(1)}, bf16[4,48,1280]{2,1,0:T(8,128)(2,1)}, u32[]{:S(2)}, u32[]{:S(2)}) collective-permute-start(bf16[4,48,1280]{2,1,0:T(8,128)(2,1)S(1)} %add_convert_fusion.1), channel_id=1, source_target_pairs={{0,16},{8,24},{16,0},{24,8},{1,17},{9,25},{17,1},{25,9},{2,18},{10... | collective-permute-start | bytes 1474568 | tf_op jit(solution)/shard_map/ppermute | solution.py:612
  21.3 11.2 %collective-permute-start.1 = (bf16[4,48,1280]{2,1,0:T(8,128)(2,1)}, bf16[4,48,1280]{2,1,0:T(8,128)(2,1)}, u32[]{:S(2)}, u32[]{:S(2)}) collective-permute-start(bf16[4,48,1280]{2,1,0:T(8,128)(2,1)} %get-tuple-element.45), channel_id=1, source_target_pairs={{0,8},{8,0},{16,24},{24,16},{1,9},{9,1},{17,25},{25,17},{2,10},{10... | collective-permute-start | bytes 1474568 | tf_op jit(solution)/shard_map/ppermute | solution.py:612
  35.9 23.3 %all-to-all-start = ((bf16[8,48,1280]{2,1,0:T(8,128)(2,1)}), bf16[8,48,1280]{2,1,0:T(8,128)(2,1)}, u32[]{:S(2)}, u32[]{:S(2)}) async-start(bf16[8,48,1280]{2,1,0:T(8,128)(2,1)} %to_lines.2), calls=%async_computation | async-start | bytes 1966080 | tf_op jit(solution)/shard_map/all_to_all | solution.py:643
  43.6 15.6 %collective-permute-start.6 = (bf16[3,20,20,2,128]{4,3,2,1,0:T(2,128)(2,1)}, bf16[3,20,20,2,128]{4,3,2,1,0:T(2,128)(2,1)}, u32[]{:S(2)}, u32[]{:S(2)}) collective-permute-start(bf16[3,20,20,2,128]{4,3,2,1,0:T(2,128)(2,1)} %collective-permute-done), channel_id=1, source_target_pairs={{64,0},{96,32},{0,64},{32,96},{65,1},{97,33},{1,65},{33,97},{66,2}... | collective-permute-start | bytes 1843208 | tf_op jit(solution)/shard_map/ppermute | solution.py:630
  64.6 8.1 %collective-permute-start.7 = (bf16[48,1280]{1,0:T(8,128)(2,1)}, bf16[48,1280]{1,0:T(8,128)(2,1)S(1)}, u32[]{:S(2)}, u32[]{:S(2)}) collective-permute-start(bf16[48,1280]{1,0:T(8,128)(2,1)} %bitcast.24), channel_id=1, source_target_pairs={{1,0},{0,1},{3,2},{2,3},{5,4},{4,5},{7,6},{6,7},{9,8},{8,9},{11,10... | collective-permute-start | bytes 368648 | tf_op jit(solution)/shard_map/ppermute | solution.py:635
  67.4 6.0 %collective-permute-start.10 = (bf16[48,1280]{1,0:T(8,128)(2,1)}, bf16[48,1280]{1,0:T(8,128)(2,1)S(1)}, u32[]{:S(2)}, u32[]{:S(2)}) collective-permute-start(bf16[48,1280]{1,0:T(8,128)(2,1)} %bitcast.25), channel_id=1, source_target_pairs={{4,0},{5,1},{6,2},{7,3},{0,4},{1,5},{2,6},{3,7},{12,8},{13,9},{14,... | collective-permute-start | bytes 368648 | tf_op jit(solution)/shard_map/ppermute | solution.py:638
  70.1 6.6 %collective-permute-start.12 = (bf16[48,1280]{1,0:T(8,128)(2,1)}, bf16[48,1280]{1,0:T(8,128)(2,1)S(1)}, u32[]{:S(2)}, u32[]{:S(2)}) collective-permute-start(bf16[48,1280]{1,0:T(8,128)(2,1)} %bitcast.26), channel_id=1, source_target_pairs={{6,0},{7,1},{0,2},{1,3},{2,4},{3,5},{4,6},{5,7},{14,8},{15,9},{8,1... | collective-permute-start | bytes 368648 | tf_op jit(solution)/shard_map/ppermute | solution.py:638
  70.4 7.2 %collective-permute-start.8 = (bf16[48,1280]{1,0:T(8,128)(2,1)}, bf16[48,1280]{1,0:T(8,128)(2,1)S(1)}, u32[]{:S(2)}, u32[]{:S(2)}) collective-permute-start(bf16[48,1280]{1,0:T(8,128)(2,1)} %bitcast.27), channel_id=1, source_target_pairs={{2,0},{3,1},{4,2},{5,3},{6,4},{7,5},{0,6},{1,7},{10,8},{11,9},{12,... | collective-permute-start | bytes 368648 | tf_op jit(solution)/shard_map/ppermute | solution.py:638
  72.8 0.7 copy-start.8
  72.8 6.3 %collective-permute-start.11 = (bf16[48,1280]{1,0:T(8,128)(2,1)S(1)}, bf16[48,1280]{1,0:T(8,128)(2,1)S(1)}, u32[]{:S(2)}, u32[]{:S(2)}) collective-permute-start(bf16[48,1280]{1,0:T(8,128)(2,1)S(1)} %collective-permute-done.7.refs_1_), channel_id=1, source_target_pairs={{4,0},{5,1},{6,2},{7,3},{0,4},{1,5},{2,6},{3,7},{12,8},{13,9},{14,... | collective-permute-start | bytes 368648 | tf_op jit(solution)/shard_map/ppermute | solution.py:638
  72.8 7.4 %collective-permute-start.13 = (bf16[48,1280]{1,0:T(8,128)(2,1)S(1)}, bf16[48,1280]{1,0:T(8,128)(2,1)S(1)}, u32[]{:S(2)}, u32[]{:S(2)}) collective-permute-start(bf16[48,1280]{1,0:T(8,128)(2,1)S(1)} %collective-permute-done.7.refs_1_), channel_id=1, source_target_pairs={{6,0},{7,1},{0,2},{1,3},{2,4},{3,5},{4,6},{5,7},{14,8},{15,9},{8,1... | collective-permute-start | bytes 368648 | tf_op jit(solution)/shard_map/ppermute | solution.py:638
  73.4 6.8 %copy-start.9 = (bf16[48,1280]{1,0:T(8,128)(2,1)}, bf16[48,1280]{1,0:T(8,128)(2,1)S(1)}, u32[]{:S(2)}) copy-start(bf16[48,1280]{1,0:T(8,128)(2,1)S(1)} %collective-permute-done.10.refs_4_) | copy-start | bytes 368644
  73.4 7.7 %collective-permute-start.9 = (bf16[48,1280]{1,0:T(8,128)(2,1)S(1)}, bf16[48,1280]{1,0:T(8,128)(2,1)}, u32[]{:S(2)}, u32[]{:S(2)}) collective-permute-start(bf16[48,1280]{1,0:T(8,128)(2,1)S(1)} %collective-permute-done.7.refs_1_), channel_id=1, source_target_pairs={{2,0},{3,1},{4,2},{5,3},{6,4},{7,5},{0,6},{1,7},{10,8},{11,9},{12,... | collective-permute-start | bytes 368648 | tf_op jit(solution)/shard_map/ppermute | solution.py:638
  76.6 3.6 %copy-start.10 = (bf16[48,1280]{1,0:T(8,128)(2,1)}, bf16[48,1280]{1,0:T(8,128)(2,1)S(1)}, u32[]{:S(2)}) copy-start(bf16[48,1280]{1,0:T(8,128)(2,1)S(1)} %collective-permute-done.12.refs_6_) | copy-start | bytes 368644
  77.6 2.7 %copy-start.11 = (bf16[48,1280]{1,0:T(8,128)(2,1)}, bf16[48,1280]{1,0:T(8,128)(2,1)S(1)}, u32[]{:S(2)}) copy-start(bf16[48,1280]{1,0:T(8,128)(2,1)S(1)} %collective-permute-done.8.refs_2_) | copy-start | bytes 368644
  79.0 1.2 copy-start.12
  80.3 0.7 copy-start.13
  84.3 9.0 %collective-permute-start.14 = (bf16[4,48,1280]{2,1,0:T(8,128)(2,1)}, bf16[4,48,1280]{2,1,0:T(8,128)(2,1)S(1)}, u32[]{:S(2)}, u32[]{:S(2)}) collective-permute-start(bf16[4,48,1280]{2,1,0:T(8,128)(2,1)} %from_line_set.1.i0), channel_id=1, source_target_pairs={{0,16},{8,24},{16,0},{24,8},{1,17},{9,25},{17,1},{25,9},{2,18},{10... | collective-permute-start | bytes 1474568 | tf_op jit(solution)/shard_map/ppermute | solution.py:612
  84.9 13.3 %collective-permute-start.15 = (bf16[4,48,1280]{2,1,0:T(8,128)(2,1)}, bf16[4,48,1280]{2,1,0:T(8,128)(2,1)S(1)}, u32[]{:S(2)}, u32[]{:S(2)}) collective-permute-start(bf16[4,48,1280]{2,1,0:T(8,128)(2,1)} %from_line_set.1.i0), channel_id=1, source_target_pairs={{0,8},{8,0},{16,24},{24,16},{1,9},{9,1},{17,25},{25,17},{2,10},{10... | collective-permute-start | bytes 1474568 | tf_op jit(solution)/shard_map/ppermute | solution.py:612
  93.4 6.3 %copy-start.3 = (bf16[4,48,1280]{2,1,0:T(8,128)(2,1)}, bf16[4,48,1280]{2,1,0:T(8,128)(2,1)S(1)}, u32[]{:S(2)}) copy-start(bf16[4,48,1280]{2,1,0:T(8,128)(2,1)S(1)} %collective-permute-done.14.i1) | copy-start | bytes 1474564
  93.4 6.3 %collective-permute-start.16 = (bf16[4,48,1280]{2,1,0:T(8,128)(2,1)S(1)}, bf16[4,48,1280]{2,1,0:T(8,128)(2,1)S(1)}, u32[]{:S(2)}, u32[]{:S(2)}) collective-permute-start(bf16[4,48,1280]{2,1,0:T(8,128)(2,1)S(1)} %collective-permute-done.14.i1), channel_id=1, source_target_pairs={{0,8},{8,0},{16,24},{24,16},{1,9},{9,1},{17,25},{25,17},{2,10},{10... | collective-permute-start | bytes 1474568 | tf_op jit(solution)/shard_map/ppermute | solution.py:612
  98.2 1.5 copy-start.4
  99.7 0.8 copy-start.5
  100.5 20.0 %copy-start.1 = (bf16[160,20]{1,0:T(8,128)(2,1)S(1)}, bf16[160,20]{1,0:T(8,128)(2,1)}, u32[]{:S(2)}) copy-start(bf16[160,20]{1,0:T(8,128)(2,1)} %constant.24.clone) | copy-start | bytes 19204
  100.5 20.0 %copy-start.7 = (bf16[160,160]{1,0:T(8,128)(2,1)S(1)}, bf16[160,160]{1,0:T(8,128)(2,1)}, u32[]{:S(2)}) copy-start(bf16[160,160]{1,0:T(8,128)(2,1)} %constant.27.clone) | copy-start | bytes 153604
  100.5 20.0 %copy-start.17 = (bf16[20,20]{1,0:T(8,128)(2,1)S(1)}, bf16[20,20]{1,0:T(8,128)(2,1)}, u32[]{:S(2)}) copy-start(bf16[20,20]{1,0:T(8,128)(2,1)} %param.12) | copy-start | bytes 2404
  115.9 2.2 %collective-permute-start.18 = (bf16[4,48,1280]{2,1,0:T(8,128)(2,1)}, bf16[4,48,1280]{2,1,0:T(8,128)(2,1)S(1)}, u32[]{:S(2)}, u32[]{:S(2)}) collective-permute-start(bf16[4,48,1280]{2,1,0:T(8,128)(2,1)} %get-tuple-element.59), channel_id=1, source_target_pairs={{0,8},{8,0},{16,24},{24,16},{1,9},{9,1},{17,25},{25,17},{2,10},{10... | collective-permute-start | bytes 1474568 | tf_op jit(solution)/shard_map/ppermute | solution.py:612
  119.2 12.6 %collective-permute-start.19 = (bf16[4,48,1280]{2,1,0:T(8,128)(2,1)S(1)}, bf16[4,48,1280]{2,1,0:T(8,128)(2,1)}, u32[]{:S(2)}, u32[]{:S(2)}) collective-permute-start(bf16[4,48,1280]{2,1,0:T(8,128)(2,1)S(1)} %add_convert_fusion), channel_id=1, source_target_pairs={{0,16},{8,24},{16,0},{24,8},{1,17},{9,25},{17,1},{25,9},{2,18},{10... | collective-permute-start | bytes 1474568 | tf_op jit(solution)/shard_map/ppermute | solution.py:612
  119.8 12.0 %collective-permute-start.17 = (bf16[4,48,1280]{2,1,0:T(8,128)(2,1)}, bf16[4,48,1280]{2,1,0:T(8,128)(2,1)}, u32[]{:S(2)}, u32[]{:S(2)}) collective-permute-start(bf16[4,48,1280]{2,1,0:T(8,128)(2,1)} %get-tuple-element.57), channel_id=1, source_target_pairs={{0,8},{8,0},{16,24},{24,16},{1,9},{9,1},{17,25},{25,17},{2,10},{10... | collective-permute-start | bytes 1474568 | tf_op jit(solution)/shard_map/ppermute | solution.py:612
  161.3 18.1 %all-to-all-start.2 = ((bf16[8,48,1280]{2,1,0:T(8,128)(2,1)}), bf16[8,48,1280]{2,1,0:T(8,128)(2,1)}, u32[]{:S(2)}, u32[]{:S(2)}) async-start(bf16[8,48,1280]{2,1,0:T(8,128)(2,1)} %get-tuple-element.66), calls=%async_computation.2 | async-start | bytes 1966080 | tf_op jit(solution)/shard_map/all_to_all | solution.py:643
  165.5 8.1 %collective-permute-start.20 = (bf16[2,120,128]{2,1,0:T(8,128)(2,1)}, bf16[2,120,128]{2,1,0:T(8,128)(2,1)}, u32[]{:S(2)}, u32[]{:S(2)}) collective-permute-start(bf16[2,120,128]{2,1,0:T(8,128)(2,1)} %get-tuple-element.67), channel_id=1, source_target_pairs={{0,0},{8,32},{16,64},{24,96},{32,8},{40,40},{48,72},{56,104},{64,1... | collective-permute-start | bytes 184328 | tf_op jit(solution)/shard_map/ppermute | solution.py:652
  171.1 2.5 %collective-permute-start.21 = (bf16[2,120,128]{2,1,0:T(8,128)(2,1)}, bf16[2,120,128]{2,1,0:T(8,128)(2,1)}, u32[]{:S(2)}, u32[]{:S(2)}) collective-permute-start(bf16[2,120,128]{2,1,0:T(8,128)(2,1)} %get-tuple-element.68), channel_id=1, source_target_pairs={{0,8},{8,40},{16,72},{24,104},{32,16},{40,48},{48,80},{56,112},{64... | collective-permute-start | bytes 184328 | tf_op jit(solution)/shard_map/ppermute | solution.py:652
  182.5 17.8 %collective-permute-start.22 = (bf16[4,48,1280]{2,1,0:T(8,128)(2,1)}, bf16[4,48,1280]{2,1,0:T(8,128)(2,1)S(1)}, u32[]{:S(2)}, u32[]{:S(2)}) collective-permute-start(bf16[4,48,1280]{2,1,0:T(8,128)(2,1)} %from_lines.1.i0), channel_id=1, source_target_pairs={{0,16},{8,24},{16,0},{24,8},{1,17},{9,25},{17,1},{25,9},{2,18},{10... | collective-permute-start | bytes 1474568 | tf_op jit(solution)/shard_map/ppermute | solution.py:612
  183.6 9.9 %collective-permute-start.23 = (bf16[2,120,128]{2,1,0:T(8,128)(2,1)}, bf16[2,120,128]{2,1,0:T(8,128)(2,1)S(1)}, u32[]{:S(2)}, u32[]{:S(2)}) collective-permute-start(bf16[2,120,128]{2,1,0:T(8,128)(2,1)} %get-tuple-element.72), channel_id=1, source_target_pairs={{0,16},{8,48},{16,80},{24,112},{32,24},{40,56},{48,88},{56,120},{6... | collective-permute-start | bytes 184328 | tf_op jit(solution)/shard_map/ppermute | solution.py:652
  191.2 5.4 %collective-permute-start.24 = (bf16[2,120,128]{2,1,0:T(8,128)(2,1)}, bf16[2,120,128]{2,1,0:T(8,128)(2,1)S(1)}, u32[]{:S(2)}, u32[]{:S(2)}) collective-permute-start(bf16[2,120,128]{2,1,0:T(8,128)(2,1)} %get-tuple-element.73), channel_id=1, source_target_pairs={{0,24},{8,56},{16,88},{24,120},{32,0},{40,32},{48,64},{56,96},{64,... | collective-permute-start | bytes 184328 | tf_op jit(solution)/shard_map/ppermute | solution.py:652
  191.2 11.5 %collective-permute-start.25 = (bf16[4,48,1280]{2,1,0:T(8,128)(2,1)}, bf16[4,48,1280]{2,1,0:T(8,128)(2,1)}, u32[]{:S(2)}, u32[]{:S(2)}) collective-permute-start(bf16[4,48,1280]{2,1,0:T(8,128)(2,1)} %from_lines.1.i0), channel_id=1, source_target_pairs={{0,8},{8,0},{16,24},{24,16},{1,9},{9,1},{17,25},{25,17},{2,10},{10... | collective-permute-start | bytes 1474568 | tf_op jit(solution)/shard_map/ppermute | solution.py:612
  193.4 3.2 %copy-start.14 = (bf16[2,120,128]{2,1,0:T(8,128)(2,1)}, bf16[2,120,128]{2,1,0:T(8,128)(2,1)S(1)}, u32[]{:S(2)}) copy-start(bf16[2,120,128]{2,1,0:T(8,128)(2,1)S(1)} %collective-permute-done.23.p2) | copy-start | bytes 184324
  196.6 0.6 copy-start.15
  200.3 0.8 copy-start.2
  201.1 3.1 %collective-permute-start.26 = (bf16[4,48,1280]{2,1,0:T(8,128)(2,1)S(1)}, bf16[4,48,1280]{2,1,0:T(8,128)(2,1)}, u32[]{:S(2)}, u32[]{:S(2)}) collective-permute-start(bf16[4,48,1280]{2,1,0:T(8,128)(2,1)S(1)} %collective-permute-done.22.i1), channel_id=1, source_target_pairs={{0,8},{8,0},{16,24},{24,16},{1,9},{9,1},{17,25},{25,17},{2,10},{10... | collective-permute-start | bytes 1474568 | tf_op jit(solution)/shard_map/ppermute | solution.py:612

commit v12 on v10

--- a/solution.py
+++ b/solution.py
@@ -315,7 +315,7 @@
             scratch_shapes=BLOCKS + [TOTAL],
         ),
         out_shape=[COLUMNS, COLUMNS] + [COEFFS] * 4,
-        compiler_params=PARAMS,
+        compiler_params=ALONE,
         cost_estimate=cost(19),
         name="middle_columns",
     )(where, *coeffs_in, bypass, upstream, jnp.asarray(DEPTH), jnp.asarray(WIDTH))
@@ -406,7 +406,7 @@
     return line_call(unline_set_kernel, "from_line_set", where, modes, COEFFS, [order])
 
 
-UNROLL = 10
+UNROLL = 20
 SETS = GX * KB
 PAIR = 2 * CH
 HALF = KX

time: 213 us -> 214 us (level)
  no operation moved by 1% of the time
where the time goes in v12:
time: 214 us; the launch traced here: 212 us
  Pallas kernels  72.5 us (34%)
  starting transfers between devices  67.4 us (31%)
  waiting for transfers between devices  42.1 us (20%)
  blocking collectives  19.9 us (9%)
  local copies, waits for them, and re-layouts  3.54 us (2%)
  other arithmetic  2.9 us (1%)
  matrix products  2.78 us (1%)
    ppermute x12, starting transfers between devices, swap(): return lax.ppermute(values, 'gx', [(i, i ^ bit) for i in range(GX)])  26.4 us
    all_to_all x1, blocking collectives, exchange_lines(): return lax.all_to_all(parts, 'gy', split_axis=0, concat_axis=0, tiled=True)  19.9 us
    ppermute x12, waiting for transfers between devices, swap(): return lax.ppermute(values, 'gx', [(i, i ^ bit) for i in range(GX)])  17.3 us
    pallas_call x1, Pallas kernels, middle_columns(): pl.pallas_call(middle_kernel, grid_spec=pltpu.PrefetchScalarGridSpec(num_...  15.3 us
    pallas_call x4, Pallas kernels, line_call(): pl.pallas_call(kernel, grid_spec=pltpu.PrefetchScalarGridSpec(num_scalar_...  13.3 us
    ppermute x3, waiting for transfers between devices, gather_weights(): lax.ppermute(weight, 'dp', [((a + k) % DP, a) for a in range(DP)])  12.8 us
    pallas_call x2, Pallas kernels, bypass_columns(): pl.pallas_call(bypass_kernel, grid=(STEPS,), in_specs=[pl.BlockSpec(memor...  12.4 us
    all_to_all x2, starting transfers between devices, exchange_lines(): return lax.all_to_all(parts, 'gy', split_axis=0, concat_axis=0, tiled=True)  11.8 us
  transfers between devices with their start and end apart: 29, of which 16 were waited for; matrix products, arithmetic and copies ran while one was open for 2% of the time, Pallas kernels for 13%

profile of v12, /device:TPU:1, one launch (start us, length us, event | category | flops | bytes accessed | tf_op | source)
XLA Modules:
  0.0 211.8 jit_solution(10793308554995760639)
XLA Ops:
  0.7 4.6 %collective-permute-start = (bf16[3,20,20,2,128]{4,3,2,1,0:T(2,128)(2,1)}, bf16[3,20,20,2,128]{4,3,2,1,0:T(2,128)(2,1)}, u32[]{:S(2)}, u32[]{:S(2)}) collective-permute-start(bf16[3,20,20,2,128]{4,3,2,1,0:T(2,128)(2,1)} %param.11), channel_id=1, source_target_pairs={{0,0},{8,32},{16,64},{24,96},{32,72},{40,104},{48,8},{56,40},{64,1... | collective-permute-start | bytes 1843208 | tf_op jit(solution)/shard_map/ppermute | solution.py:661
  5.9 7.6 %start_columns.1 = (bf16[4,48,1280]{2,1,0:T(8,128)(2,1)}, bf16[4,48,1280]{2,1,0:T(8,128)(2,1)}, bf16[4,48,1280]{2,1,0:T(8,128)(2,1)}, bf16[4,48,1280]{2,1,0:T(8,128)(2,1)}) custom-call(s32[3]{0:T(128)} %pad_add_fusion.where_ref, bf16[20,64,2048]{2,1,0:T(8,128)(2,1)} %bitcast.19, bf16[4,24,512]{2,1,0:T(8,128)(2,1)} %constant.25.clone.strip_ref, ...), custom_call_target="tpu_custom_call" | custom-call | bytes 24000000 | tf_op jit(solution)/shard_map/start_columns/pallas_call | solution.py:290
  14.5 2.4 %collective-permute-start.2 = (bf16[4,48,1280]{2,1,0:T(8,128)(2,1)}, bf16[4,48,1280]{2,1,0:T(8,128)(2,1)S(1)}, u32[]{:S(2)}, u32[]{:S(2)}) collective-permute-start(bf16[4,48,1280]{2,1,0:T(8,128)(2,1)} %get-tuple-element.49), channel_id=1, source_target_pairs={{0,8},{8,0},{16,24},{24,16},{1,9},{9,1},{17,25},{25,17},{2,10},{10... | collective-permute-start | bytes 1474568 | tf_op jit(solution)/shard_map/ppermute | solution.py:612
  16.9 1.8 collective-permute-start.4
  18.7 1.1 add_convert_fusion.1
  19.8 1.5 collective-permute-start.3
  22.9 6.2 %bypass_columns.2.bypass_ref = bf16[20,64,2048]{2,1,0:T(8,128)(2,1)} custom-call(f32[20]{0:T(128)} %shift_ref.1, bf16[20,64,2048]{2,1,0:T(8,128)(2,1)} %bitcast.20, bf16[160,160]{1,0:T(8,128)(2,1)} %fusion.mixer_ref), custom_call_target="tpu_custom_call" | custom-call | bytes 18000000 | tf_op jit(solution)/shard_map/bypass_columns/pallas_call | solution.py:272
  29.1 3.4 %collective-permute-done.3.c_ref = bf16[4,48,1280]{2,1,0:T(8,128)(2,1)} collective-permute-done((bf16[4,48,1280]{2,1,0:T(8,128)(2,1)S(1)}, bf16[4,48,1280]{2,1,0:T(8,128)(2,1)}, u32[]{:S(2)}, u32[]{:S(2)}) %collective-permute-start.3) | collective-permute-done | bytes 491552 | tf_op jit(solution)/shard_map/ppermute | solution.py:612
  32.5 3.5 %to_lines.2 = bf16[8,48,1280]{2,1,0:T(8,128)(2,1)} custom-call(s32[3]{0:T(128)} %pad_add_fusion.where_ref, bf16[4,48,1280]{2,1,0:T(8,128)(2,1)} %get-tuple-element.46.a_ref, bf16[4,48,1280]{2,1,0:T(8,128)(2,1)} %collective-permute-done.1.b_ref, bf16[4,48,1280]{2,1,0:T(8,128)(2,1)} %collective-permute-done.3.c_ref, ...), custom_call_target="tpu_custom_call" | custom-call | bytes 9000000 | tf_op jit(solution)/shard_map/to_lines/pallas_call | solution.py:379
  36.0 7.6 %all-to-all-start = ((bf16[8,48,1280]{2,1,0:T(8,128)(2,1)}), bf16[8,48,1280]{2,1,0:T(8,128)(2,1)}, u32[]{:S(2)}, u32[]{:S(2)}) async-start(bf16[8,48,1280]{2,1,0:T(8,128)(2,1)} %to_lines.2), calls=%async_computation | async-start | bytes 1966080 | tf_op jit(solution)/shard_map/all_to_all | solution.py:643
  43.6 2.9 %collective-permute-start.6 = (bf16[3,20,20,2,128]{4,3,2,1,0:T(2,128)(2,1)}, bf16[3,20,20,2,128]{4,3,2,1,0:T(2,128)(2,1)}, u32[]{:S(2)}, u32[]{:S(2)}) collective-permute-start(bf16[3,20,20,2,128]{4,3,2,1,0:T(2,128)(2,1)} %collective-permute-done), channel_id=1, source_target_pairs={{64,0},{96,32},{0,64},{32,96},{65,1},{97,33},{1,65},{33,97},{66,2}... | collective-permute-start | bytes 1843208 | tf_op jit(solution)/shard_map/ppermute | solution.py:630
  46.4 12.8 %collective-permute-done.6 = bf16[3,20,20,2,128]{4,3,2,1,0:T(2,128)(2,1)} collective-permute-done((bf16[3,20,20,2,128]{4,3,2,1,0:T(2,128)(2,1)}, bf16[3,20,20,2,128]{4,3,2,1,0:T(2,128)(2,1)}, u32[]{:S(2)}, u32[]{:S(2)}) %collective-permute-start.6) | collective-permute-done | bytes 614432 | tf_op jit(solution)/shard_map/ppermute | solution.py:630
  59.2 5.4 %mix_modes.1 = (bf16[1,48,1280]{2,1,0:T(8,128)(2,1)}, bf16[1,120,128]{2,1,0:T(8,128)(2,1)}, bf16[1,120,128]{2,1,0:T(8,128)(2,1)}, bf16[1,120,128]{2,1,0:T(8,128)(2,1)}, bf16[1,120,128]{2,1,0:T(8,128)(2,1)}) custom-call(s32[3]{0:T(128)} %pad_add_fusion.where_ref, bf16[8,48,1280]{2,1,0:T(8,128)(2,1)} %all-to-all-done.arrived_ref, ...), custom_call_target="tpu_custom_call" | custom-call | bytes 15000000 | tf_op jit(solution)/shard_map/mix_modes/pallas_call | solution.py:555
  64.6 2.8 %collective-permute-start.7 = (bf16[48,1280]{1,0:T(8,128)(2,1)}, bf16[48,1280]{1,0:T(8,128)(2,1)S(1)}, u32[]{:S(2)}, u32[]{:S(2)}) collective-permute-start(bf16[48,1280]{1,0:T(8,128)(2,1)} %bitcast.24), channel_id=1, source_target_pairs={{1,0},{0,1},{3,2},{2,3},{5,4},{4,5},{7,6},{6,7},{9,8},{8,9},{11,10... | collective-permute-start | bytes 368648 | tf_op jit(solution)/shard_map/ppermute | solution.py:635
  67.4 2.7 %collective-permute-start.10 = (bf16[48,1280]{1,0:T(8,128)(2,1)}, bf16[48,1280]{1,0:T(8,128)(2,1)S(1)}, u32[]{:S(2)}, u32[]{:S(2)}) collective-permute-start(bf16[48,1280]{1,0:T(8,128)(2,1)} %bitcast.25), channel_id=1, source_target_pairs={{4,0},{5,1},{6,2},{7,3},{0,4},{1,5},{2,6},{3,7},{12,8},{13,9},{14,... | collective-permute-start | bytes 368648 | tf_op jit(solution)/shard_map/ppermute | solution.py:638
  70.3 2.4 %collective-permute-start.8 = (bf16[48,1280]{1,0:T(8,128)(2,1)}, bf16[48,1280]{1,0:T(8,128)(2,1)S(1)}, u32[]{:S(2)}, u32[]{:S(2)}) collective-permute-start(bf16[48,1280]{1,0:T(8,128)(2,1)} %bitcast.27), channel_id=1, source_target_pairs={{2,0},{3,1},{4,2},{5,3},{6,4},{7,5},{0,6},{1,7},{10,8},{11,9},{12,... | collective-permute-start | bytes 368648 | tf_op jit(solution)/shard_map/ppermute | solution.py:638
  73.4 2.2 %collective-permute-start.9 = (bf16[48,1280]{1,0:T(8,128)(2,1)S(1)}, bf16[48,1280]{1,0:T(8,128)(2,1)}, u32[]{:S(2)}, u32[]{:S(2)}) collective-permute-start(bf16[48,1280]{1,0:T(8,128)(2,1)S(1)} %collective-permute-done.7.refs_1_), channel_id=1, source_target_pairs={{2,0},{3,1},{4,2},{5,3},{6,4},{7,5},{0,6},{1,7},{10,8},{11,9},{12,... | collective-permute-start | bytes 368648 | tf_op jit(solution)/shard_map/ppermute | solution.py:638
  75.6 1.1 collective-permute-done.12.refs_6_
  77.5 1.5 collective-permute-done.11.refs_5_
  79.0 1.2 collective-permute-done.13.refs_7_
  81.1 3.3 %from_line_set.1.i0 = bf16[4,48,1280]{2,1,0:T(8,128)(2,1)} custom-call(s32[3]{0:T(128)} %pad_add_fusion.where_ref, bf16[48,1280]{1,0:T(8,128)(2,1)} %bitcast.28, bf16[48,1280]{1,0:T(8,128)(2,1)} %copy-done.6, bf16[48,1280]{1,0:T(8,128)(2,1)} %copy-done.9, bf16[48,1280]{1,0:T(8,128)(2,1)} %collective-permute-done.9.refs_3_, bf16[48,1280]{1,0:T(8,128)(2,1)} %copy-done.7, ...), custom_call_target="tpu_custom_call" | custom-call | bytes 9000000 | tf_op jit(solution)/shard_map/from_line_set/pallas_call | solution.py:379
  84.9 4.1 %collective-permute-start.15 = (bf16[4,48,1280]{2,1,0:T(8,128)(2,1)}, bf16[4,48,1280]{2,1,0:T(8,128)(2,1)S(1)}, u32[]{:S(2)}, u32[]{:S(2)}) collective-permute-start(bf16[4,48,1280]{2,1,0:T(8,128)(2,1)} %from_line_set.1.i0), channel_id=1, source_target_pairs={{0,8},{8,0},{16,24},{24,16},{1,9},{9,1},{17,25},{25,17},{2,10},{10... | collective-permute-start | bytes 1474568 | tf_op jit(solution)/shard_map/ppermute | solution.py:612
  89.0 4.3 %collective-permute-done.14.i1 = bf16[4,48,1280]{2,1,0:T(8,128)(2,1)S(1)} collective-permute-done((bf16[4,48,1280]{2,1,0:T(8,128)(2,1)}, bf16[4,48,1280]{2,1,0:T(8,128)(2,1)S(1)}, u32[]{:S(2)}, u32[]{:S(2)}) %collective-permute-start.14) | collective-permute-done | bytes 491552 | tf_op jit(solution)/shard_map/ppermute | solution.py:612
  94.1 4.8 %collective-permute-start.16 = (bf16[4,48,1280]{2,1,0:T(8,128)(2,1)S(1)}, bf16[4,48,1280]{2,1,0:T(8,128)(2,1)S(1)}, u32[]{:S(2)}, u32[]{:S(2)}) collective-permute-start(bf16[4,48,1280]{2,1,0:T(8,128)(2,1)S(1)} %collective-permute-done.14.i1), channel_id=1, source_target_pairs={{0,8},{8,0},{16,24},{24,16},{1,9},{9,1},{17,25},{25,17},{2,10},{10... | collective-permute-start | bytes 1474568 | tf_op jit(solution)/shard_map/ppermute | solution.py:612
  98.9 1.5 collective-permute-done.16.i3
  101.2 15.3 %middle_columns.1 = (bf16[20,64,2048]{2,1,0:T(8,128)(2,1)}, bf16[20,64,2048]{2,1,0:T(8,128)(2,1)}, bf16[4,48,1280]{2,1,0:T(8,128)(2,1)}, bf16[4,48,1280]{2,1,0:T...) custom-call(s32[3]{0:T(128)} %pad_add_fusion.where_ref, bf16[4,48,1280]{2,1,0:T(8,128)(2,1)} %from_line_set.1.i0, ...), custom_call_target="tpu_custom_call" | custom-call | bytes 57000000 | tf_op jit(solution)/shard_map/middle_columns/pallas_call | solution.py:308
  116.9 1.7 collective-permute-done.18
  118.6 1.1 add_convert_fusion
  121.1 1.9 fusion.1.mixer_ref
  123.5 6.2 %bypass_columns.3.bypass_ref = bf16[20,64,2048]{2,1,0:T(8,128)(2,1)} custom-call(f32[20]{0:T(128)} %broadcast_1_shift_ref.2.shift_ref, bf16[20,64,2048]{2,1,0:T(8,128)(2,1)} %get-tuple-element.62.source_ref, bf16[160,160]{1,0:T(8,128)(2,1)} %fusion.1.mixer_ref), custom_call_target="tpu_custom_call" | custom-call | bytes 18000000 | tf_op jit(solution)/shard_map/bypass_columns/pallas_call | solution.py:272
  129.7 2.7 %collective-permute-done.19.c_ref = bf16[4,48,1280]{2,1,0:T(8,128)(2,1)} collective-permute-done((bf16[4,48,1280]{2,1,0:T(8,128)(2,1)S(1)}, bf16[4,48,1280]{2,1,0:T(8,128)(2,1)}, u32[]{:S(2)}, u32[]{:S(2)}) %collective-permute-start.19) | collective-permute-done | bytes 491552 | tf_op jit(solution)/shard_map/ppermute | solution.py:612
  132.4 3.5 %to_lines.3 = bf16[8,48,1280]{2,1,0:T(8,128)(2,1)} custom-call(s32[3]{0:T(128)} %pad_add_fusion.where_ref, bf16[4,48,1280]{2,1,0:T(8,128)(2,1)} %get-tuple-element.58.a_ref, bf16[4,48,1280]{2,1,0:T(8,128)(2,1)} %collective-permute-done.17.b_ref, bf16[4,48,1280]{2,1,0:T(8,128)(2,1)} %collective-permute-done.19.c_ref, ...), custom_call_target="tpu_custom_call" | custom-call | bytes 9000000 | tf_op jit(solution)/shard_map/to_lines/pallas_call | solution.py:379
  135.9 19.9 %all_to_all.15.arrived_ref = bf16[8,48,1280]{2,1,0:T(8,128)(2,1)} all-to-all(bf16[8,48,1280]{2,1,0:T(8,128)(2,1)} %to_lines.3), channel_id=1, replica_groups=mesh['dp'=4,'gx'=4,'gy'=8] {'gy'}, dimensions={0} | all-to-all | bytes 1966080 | tf_op jit(solution)/shard_map/all_to_all | solution.py:643
  155.8 6.0 %back_modes.1 = (bf16[8,48,1280]{2,1,0:T(8,128)(2,1)}, bf16[2,120,128]{2,1,0:T(8,128)(2,1)}, bf16[2,120,128]{2,1,0:T(8,128)(2,1)}, bf16[2,120,128]{2,1,0:T(8,128)(2,1)}, bf16[2,120,128]{2,1,0:T(8,128)(2,1)}) custom-call(s32[3]{0:T(128)} %pad_add_fusion.where_ref, bf16[8,48,1280]{2,1,0:T(8,128)(2,1)} %all_to_all.15.arrived_ref, ...), custom_call_target="tpu_custom_call" | custom-call | bytes 15000000 | tf_op jit(solution)/shard_map/back_modes/pallas_call | solution.py:555
  161.7 4.2 %all-to-all-start.2 = ((bf16[8,48,1280]{2,1,0:T(8,128)(2,1)}), bf16[8,48,1280]{2,1,0:T(8,128)(2,1)}, u32[]{:S(2)}, u32[]{:S(2)}) async-start(bf16[8,48,1280]{2,1,0:T(8,128)(2,1)} %get-tuple-element.68), calls=%async_computation.2 | async-start | bytes 1966080 | tf_op jit(solution)/shard_map/all_to_all | solution.py:643
  166.0 5.6 %collective-permute-start.20 = (bf16[2,120,128]{2,1,0:T(8,128)(2,1)}, bf16[2,120,128]{2,1,0:T(8,128)(2,1)}, u32[]{:S(2)}, u32[]{:S(2)}) collective-permute-start(bf16[2,120,128]{2,1,0:T(8,128)(2,1)} %get-tuple-element.69), channel_id=1, source_target_pairs={{0,0},{8,32},{16,64},{24,96},{32,8},{40,40},{48,72},{56,104},{64,1... | collective-permute-start | bytes 184328 | tf_op jit(solution)/shard_map/ppermute | solution.py:652
  171.7 1.8 collective-permute-start.22
  173.5 1.3 collective-permute-start.23
  174.9 2.6 %collective-permute-done.22.p2 = bf16[2,120,128]{2,1,0:T(8,128)(2,1)} collective-permute-done((bf16[2,120,128]{2,1,0:T(8,128)(2,1)}, bf16[2,120,128]{2,1,0:T(8,128)(2,1)}, u32[]{:S(2)}, u32[]{:S(2)}) %collective-permute-start.22) | collective-permute-done | bytes 61472 | tf_op jit(solution)/shard_map/ppermute | solution.py:652
  177.5 3.6 %collective-permute-done.23.p3 = bf16[2,120,128]{2,1,0:T(8,128)(2,1)} collective-permute-done((bf16[2,120,128]{2,1,0:T(8,128)(2,1)}, bf16[2,120,128]{2,1,0:T(8,128)(2,1)}, u32[]{:S(2)}, u32[]{:S(2)}) %collective-permute-start.23) | collective-permute-done | bytes 61472 | tf_op jit(solution)/shard_map/ppermute | solution.py:652
  181.1 3.1 %from_lines.1.i0 = bf16[4,48,1280]{2,1,0:T(8,128)(2,1)} custom-call(s32[3]{0:T(128)} %pad_add_fusion.where_ref, bf16[8,48,1280]{2,1,0:T(8,128)(2,1)} %all-to-all-done.2.modes_ref, bf16[8,384,192]{2,1,0:T(8,128)(2,1)} %constant.28.clone.table_ref.refs_8_), custom_call_target="tpu_custom_call" | custom-call | bytes 9000000 | tf_op jit(solution)/shard_map/from_lines/pallas_call | solution.py:379
  184.2 3.4 %collective-permute-start.24 = (bf16[4,48,1280]{2,1,0:T(8,128)(2,1)}, bf16[4,48,1280]{2,1,0:T(8,128)(2,1)S(1)}, u32[]{:S(2)}, u32[]{:S(2)}) collective-permute-start(bf16[4,48,1280]{2,1,0:T(8,128)(2,1)} %from_lines.1.i0), channel_id=1, source_target_pairs={{0,16},{8,24},{16,0},{24,8},{1,17},{9,25},{17,1},{25,9},{2,18},{10... | collective-permute-start | bytes 1474568 | tf_op jit(solution)/shard_map/ppermute | solution.py:612
  187.6 3.0 %collective-permute-start.25 = (bf16[4,48,1280]{2,1,0:T(8,128)(2,1)}, bf16[4,48,1280]{2,1,0:T(8,128)(2,1)}, u32[]{:S(2)}, u32[]{:S(2)}) collective-permute-start(bf16[4,48,1280]{2,1,0:T(8,128)(2,1)} %from_lines.1.i0), channel_id=1, source_target_pairs={{0,8},{8,0},{16,24},{24,16},{1,9},{9,1},{17,25},{25,17},{2,10},{10... | collective-permute-start | bytes 1474568 | tf_op jit(solution)/shard_map/ppermute | solution.py:612
  190.5 3.1 %outer_sum.1 = f32[3,20,40,128]{3,2,1,0:T(8,128)} custom-call(bf16[2,120,128]{2,1,0:T(8,128)(2,1)} %collective-permute-done.20.p0, bf16[2,120,128]{2,1,0:T(8,128)(2,1)} %collective-permute-done.21.p1, bf16[2,120,128]{2,1,0:T(8,128)(2,1)} %collective-permute-done.22.p2, bf16[2,120,128]{2,1,0:T(8,128)(2,1)} %collective-permute-done.23.p3), custom_call_target="tpu_custom_call" | custom-call | bytes 9000000 | tf_op jit(solution)/shard_map/outer_sum/pallas_call | solution.py:602
  193.7 2.0 collective-permute-done.24.i1
  196.5 4.2 %collective-permute-start.26 = (bf16[4,48,1280]{2,1,0:T(8,128)(2,1)S(1)}, bf16[4,48,1280]{2,1,0:T(8,128)(2,1)}, u32[]{:S(2)}, u32[]{:S(2)}) collective-permute-start(bf16[4,48,1280]{2,1,0:T(8,128)(2,1)S(1)} %collective-permute-done.24.i1), channel_id=1, source_target_pairs={{0,8},{8,0},{16,24},{24,16},{1,9},{9,1},{17,25},{25,17},{2,10},{10... | collective-permute-start | bytes 1474568 | tf_op jit(solution)/shard_map/ppermute | solution.py:612
  200.8 1.6 collective-permute-done.26.i3
  202.4 9.4 %end_columns.1 = bf16[20,64,2048]{2,1,0:T(8,128)(2,1)} custom-call(s32[3]{0:T(128)} %pad_add_fusion.where_ref, bf16[4,48,1280]{2,1,0:T(8,128)(2,1)} %from_lines.1.i0, bf16[4,48,1280]{2,1,0:T(8,128)(2,1)} %copy-done.1, bf16[4,48,1280]{2,1,0:T(8,128)(2,1)} %collective-permute-done.25.i2, bf16[4,48,1280]{2,1,0:T(8,128)(2,1)} %collective-permute-done.26.i3, ...), custom_call_target="tpu_custom_call" | custom-call | bytes 30000000 | tf_op jit(solution)/shard_map/end_columns/pallas_call | solution.py:326
  (55 shorter events, 11.2 us)
Async XLA Ops:
  0.6 21.3 %copy-start = (bf16[160,20]{1,0:T(8,128)(2,1)S(1)}, bf16[160,20]{1,0:T(8,128)(2,1)}, u32[]{:S(2)}) copy-start(bf16[160,20]{1,0:T(8,128)(2,1)} %constant.24.clone) | copy-start | bytes 19204
  0.6 21.3 %copy-start.5 = (bf16[160,160]{1,0:T(8,128)(2,1)S(1)}, bf16[160,160]{1,0:T(8,128)(2,1)}, u32[]{:S(2)}) copy-start(bf16[160,160]{1,0:T(8,128)(2,1)} %constant.27.clone) | copy-start | bytes 153604
  0.7 21.3 %copy-start.12 = (bf16[20,20]{1,0:T(8,128)(2,1)S(1)}, bf16[20,20]{1,0:T(8,128)(2,1)}, u32[]{:S(2)}) copy-start(bf16[20,20]{1,0:T(8,128)(2,1)} %param.12) | copy-start | bytes 2404
  0.7 13.8 %collective-permute-start = (bf16[3,20,20,2,128]{4,3,2,1,0:T(2,128)(2,1)}, bf16[3,20,20,2,128]{4,3,2,1,0:T(2,128)(2,1)}, u32[]{:S(2)}, u32[]{:S(2)}) collective-permute-start(bf16[3,20,20,2,128]{4,3,2,1,0:T(2,128)(2,1)} %param.11), channel_id=1, source_target_pairs={{0,0},{8,32},{16,64},{24,96},{32,72},{40,104},{48,8},{56,40},{64,1... | collective-permute-start | bytes 1843208 | tf_op jit(solution)/shard_map/ppermute | solution.py:661
  14.5 4.2 %collective-permute-start.2 = (bf16[4,48,1280]{2,1,0:T(8,128)(2,1)}, bf16[4,48,1280]{2,1,0:T(8,128)(2,1)S(1)}, u32[]{:S(2)}, u32[]{:S(2)}) collective-permute-start(bf16[4,48,1280]{2,1,0:T(8,128)(2,1)} %get-tuple-element.49), channel_id=1, source_target_pairs={{0,8},{8,0},{16,24},{24,16},{1,9},{9,1},{17,25},{25,17},{2,10},{10... | collective-permute-start | bytes 1474568 | tf_op jit(solution)/shard_map/ppermute | solution.py:612
  16.9 19.0 %collective-permute-start.4 = (bf16[3,20,20,2,128]{4,3,2,1,0:T(2,128)(2,1)}, bf16[3,20,20,2,128]{4,3,2,1,0:T(2,128)(2,1)}, u32[]{:S(2)}, u32[]{:S(2)}) collective-permute-start(bf16[3,20,20,2,128]{4,3,2,1,0:T(2,128)(2,1)} %collective-permute-done), channel_id=1, source_target_pairs={{32,0},{64,32},{96,64},{0,96},{33,1},{65,33},{97,65},{1,97},{34,2}... | collective-permute-start | bytes 1843208 | tf_op jit(solution)/shard_map/ppermute | solution.py:630
  18.7 17.3 %collective-permute-start.5 = (bf16[3,20,20,2,128]{4,3,2,1,0:T(2,128)(2,1)}, bf16[3,20,20,2,128]{4,3,2,1,0:T(2,128)(2,1)}, u32[]{:S(2)}, u32[]{:S(2)}) collective-permute-start(bf16[3,20,20,2,128]{4,3,2,1,0:T(2,128)(2,1)} %collective-permute-done), channel_id=1, source_target_pairs={{96,0},{0,32},{32,64},{64,96},{97,1},{1,33},{33,65},{65,97},{98,2}... | collective-permute-start | bytes 1843208 | tf_op jit(solution)/shard_map/ppermute | solution.py:630
  19.8 12.7 %collective-permute-start.3 = (bf16[4,48,1280]{2,1,0:T(8,128)(2,1)S(1)}, bf16[4,48,1280]{2,1,0:T(8,128)(2,1)}, u32[]{:S(2)}, u32[]{:S(2)}) collective-permute-start(bf16[4,48,1280]{2,1,0:T(8,128)(2,1)S(1)} %add_convert_fusion.1), channel_id=1, source_target_pairs={{0,16},{8,24},{16,0},{24,8},{1,17},{9,25},{17,1},{25,9},{2,18},{10... | collective-permute-start | bytes 1474568 | tf_op jit(solution)/shard_map/ppermute | solution.py:612
  21.3 11.2 %collective-permute-start.1 = (bf16[4,48,1280]{2,1,0:T(8,128)(2,1)}, bf16[4,48,1280]{2,1,0:T(8,128)(2,1)}, u32[]{:S(2)}, u32[]{:S(2)}) collective-permute-start(bf16[4,48,1280]{2,1,0:T(8,128)(2,1)} %get-tuple-element.47), channel_id=1, source_target_pairs={{0,8},{8,0},{16,24},{24,16},{1,9},{9,1},{17,25},{25,17},{2,10},{10... | collective-permute-start | bytes 1474568 | tf_op jit(solution)/shard_map/ppermute | solution.py:612
  36.0 23.2 %all-to-all-start = ((bf16[8,48,1280]{2,1,0:T(8,128)(2,1)}), bf16[8,48,1280]{2,1,0:T(8,128)(2,1)}, u32[]{:S(2)}, u32[]{:S(2)}) async-start(bf16[8,48,1280]{2,1,0:T(8,128)(2,1)} %to_lines.2), calls=%async_computation | async-start | bytes 1966080 | tf_op jit(solution)/shard_map/all_to_all | solution.py:643
  43.6 15.6 %collective-permute-start.6 = (bf16[3,20,20,2,128]{4,3,2,1,0:T(2,128)(2,1)}, bf16[3,20,20,2,128]{4,3,2,1,0:T(2,128)(2,1)}, u32[]{:S(2)}, u32[]{:S(2)}) collective-permute-start(bf16[3,20,20,2,128]{4,3,2,1,0:T(2,128)(2,1)} %collective-permute-done), channel_id=1, source_target_pairs={{64,0},{96,32},{0,64},{32,96},{65,1},{97,33},{1,65},{33,97},{66,2}... | collective-permute-start | bytes 1843208 | tf_op jit(solution)/shard_map/ppermute | solution.py:630
  64.6 8.1 %collective-permute-start.7 = (bf16[48,1280]{1,0:T(8,128)(2,1)}, bf16[48,1280]{1,0:T(8,128)(2,1)S(1)}, u32[]{:S(2)}, u32[]{:S(2)}) collective-permute-start(bf16[48,1280]{1,0:T(8,128)(2,1)} %bitcast.24), channel_id=1, source_target_pairs={{1,0},{0,1},{3,2},{2,3},{5,4},{4,5},{7,6},{6,7},{9,8},{8,9},{11,10... | collective-permute-start | bytes 368648 | tf_op jit(solution)/shard_map/ppermute | solution.py:635
  67.4 6.0 %collective-permute-start.10 = (bf16[48,1280]{1,0:T(8,128)(2,1)}, bf16[48,1280]{1,0:T(8,128)(2,1)S(1)}, u32[]{:S(2)}, u32[]{:S(2)}) collective-permute-start(bf16[48,1280]{1,0:T(8,128)(2,1)} %bitcast.25), channel_id=1, source_target_pairs={{4,0},{5,1},{6,2},{7,3},{0,4},{1,5},{2,6},{3,7},{12,8},{13,9},{14,... | collective-permute-start | bytes 368648 | tf_op jit(solution)/shard_map/ppermute | solution.py:638
  70.0 6.6 %collective-permute-start.12 = (bf16[48,1280]{1,0:T(8,128)(2,1)}, bf16[48,1280]{1,0:T(8,128)(2,1)S(1)}, u32[]{:S(2)}, u32[]{:S(2)}) collective-permute-start(bf16[48,1280]{1,0:T(8,128)(2,1)} %bitcast.26), channel_id=1, source_target_pairs={{6,0},{7,1},{0,2},{1,3},{2,4},{3,5},{4,6},{5,7},{14,8},{15,9},{8,1... | collective-permute-start | bytes 368648 | tf_op jit(solution)/shard_map/ppermute | solution.py:638
  70.3 7.2 %collective-permute-start.8 = (bf16[48,1280]{1,0:T(8,128)(2,1)}, bf16[48,1280]{1,0:T(8,128)(2,1)S(1)}, u32[]{:S(2)}, u32[]{:S(2)}) collective-permute-start(bf16[48,1280]{1,0:T(8,128)(2,1)} %bitcast.27), channel_id=1, source_target_pairs={{2,0},{3,1},{4,2},{5,3},{6,4},{7,5},{0,6},{1,7},{10,8},{11,9},{12,... | collective-permute-start | bytes 368648 | tf_op jit(solution)/shard_map/ppermute | solution.py:638
  72.7 0.7 copy-start.6
  72.7 6.3 %collective-permute-start.11 = (bf16[48,1280]{1,0:T(8,128)(2,1)S(1)}, bf16[48,1280]{1,0:T(8,128)(2,1)S(1)}, u32[]{:S(2)}, u32[]{:S(2)}) collective-permute-start(bf16[48,1280]{1,0:T(8,128)(2,1)S(1)} %collective-permute-done.7.refs_1_), channel_id=1, source_target_pairs={{4,0},{5,1},{6,2},{7,3},{0,4},{1,5},{2,6},{3,7},{12,8},{13,9},{14,... | collective-permute-start | bytes 368648 | tf_op jit(solution)/shard_map/ppermute | solution.py:638
  72.8 7.4 %collective-permute-start.13 = (bf16[48,1280]{1,0:T(8,128)(2,1)S(1)}, bf16[48,1280]{1,0:T(8,128)(2,1)S(1)}, u32[]{:S(2)}, u32[]{:S(2)}) collective-permute-start(bf16[48,1280]{1,0:T(8,128)(2,1)S(1)} %collective-permute-done.7.refs_1_), channel_id=1, source_target_pairs={{6,0},{7,1},{0,2},{1,3},{2,4},{3,5},{4,6},{5,7},{14,8},{15,9},{8,1... | collective-permute-start | bytes 368648 | tf_op jit(solution)/shard_map/ppermute | solution.py:638
  73.4 6.8 %copy-start.7 = (bf16[48,1280]{1,0:T(8,128)(2,1)}, bf16[48,1280]{1,0:T(8,128)(2,1)S(1)}, u32[]{:S(2)}) copy-start(bf16[48,1280]{1,0:T(8,128)(2,1)S(1)} %collective-permute-done.10.refs_4_) | copy-start | bytes 368644
  73.4 7.7 %collective-permute-start.9 = (bf16[48,1280]{1,0:T(8,128)(2,1)S(1)}, bf16[48,1280]{1,0:T(8,128)(2,1)}, u32[]{:S(2)}, u32[]{:S(2)}) collective-permute-start(bf16[48,1280]{1,0:T(8,128)(2,1)S(1)} %collective-permute-done.7.refs_1_), channel_id=1, source_target_pairs={{2,0},{3,1},{4,2},{5,3},{6,4},{7,5},{0,6},{1,7},{10,8},{11,9},{12,... | collective-permute-start | bytes 368648 | tf_op jit(solution)/shard_map/ppermute | solution.py:638
  76.6 3.6 %copy-start.8 = (bf16[48,1280]{1,0:T(8,128)(2,1)}, bf16[48,1280]{1,0:T(8,128)(2,1)S(1)}, u32[]{:S(2)}) copy-start(bf16[48,1280]{1,0:T(8,128)(2,1)S(1)} %collective-permute-done.12.refs_6_) | copy-start | bytes 368644
  77.5 2.7 %copy-start.9 = (bf16[48,1280]{1,0:T(8,128)(2,1)}, bf16[48,1280]{1,0:T(8,128)(2,1)S(1)}, u32[]{:S(2)}) copy-start(bf16[48,1280]{1,0:T(8,128)(2,1)S(1)} %collective-permute-done.8.refs_2_) | copy-start | bytes 368644
  79.0 1.2 copy-start.10
  80.2 0.6 copy-start.11
  84.3 9.0 %collective-permute-start.14 = (bf16[4,48,1280]{2,1,0:T(8,128)(2,1)}, bf16[4,48,1280]{2,1,0:T(8,128)(2,1)S(1)}, u32[]{:S(2)}, u32[]{:S(2)}) collective-permute-start(bf16[4,48,1280]{2,1,0:T(8,128)(2,1)} %from_line_set.1.i0), channel_id=1, source_target_pairs={{0,16},{8,24},{16,0},{24,8},{1,17},{9,25},{17,1},{25,9},{2,18},{10... | collective-permute-start | bytes 1474568 | tf_op jit(solution)/shard_map/ppermute | solution.py:612
  84.9 14.0 %collective-permute-start.15 = (bf16[4,48,1280]{2,1,0:T(8,128)(2,1)}, bf16[4,48,1280]{2,1,0:T(8,128)(2,1)S(1)}, u32[]{:S(2)}, u32[]{:S(2)}) collective-permute-start(bf16[4,48,1280]{2,1,0:T(8,128)(2,1)} %from_line_set.1.i0), channel_id=1, source_target_pairs={{0,8},{8,0},{16,24},{24,16},{1,9},{9,1},{17,25},{25,17},{2,10},{10... | collective-permute-start | bytes 1474568 | tf_op jit(solution)/shard_map/ppermute | solution.py:612
  93.3 0.8 copy-start.2
  94.1 6.3 %collective-permute-start.16 = (bf16[4,48,1280]{2,1,0:T(8,128)(2,1)S(1)}, bf16[4,48,1280]{2,1,0:T(8,128)(2,1)S(1)}, u32[]{:S(2)}, u32[]{:S(2)}) collective-permute-start(bf16[4,48,1280]{2,1,0:T(8,128)(2,1)S(1)} %collective-permute-done.14.i1), channel_id=1, source_target_pairs={{0,8},{8,0},{16,24},{24,16},{1,9},{9,1},{17,25},{25,17},{2,10},{10... | collective-permute-start | bytes 1474568 | tf_op jit(solution)/shard_map/ppermute | solution.py:612
  98.9 1.5 copy-start.3
  100.4 0.8 copy-start.4
  116.5 2.2 %collective-permute-start.18 = (bf16[4,48,1280]{2,1,0:T(8,128)(2,1)}, bf16[4,48,1280]{2,1,0:T(8,128)(2,1)S(1)}, u32[]{:S(2)}, u32[]{:S(2)}) collective-permute-start(bf16[4,48,1280]{2,1,0:T(8,128)(2,1)} %get-tuple-element.61), channel_id=1, source_target_pairs={{0,8},{8,0},{16,24},{24,16},{1,9},{9,1},{17,25},{25,17},{2,10},{10... | collective-permute-start | bytes 1474568 | tf_op jit(solution)/shard_map/ppermute | solution.py:612
  119.8 12.6 %collective-permute-start.19 = (bf16[4,48,1280]{2,1,0:T(8,128)(2,1)S(1)}, bf16[4,48,1280]{2,1,0:T(8,128)(2,1)}, u32[]{:S(2)}, u32[]{:S(2)}) collective-permute-start(bf16[4,48,1280]{2,1,0:T(8,128)(2,1)S(1)} %add_convert_fusion), channel_id=1, source_target_pairs={{0,16},{8,24},{16,0},{24,8},{1,17},{9,25},{17,1},{25,9},{2,18},{10... | collective-permute-start | bytes 1474568 | tf_op jit(solution)/shard_map/ppermute | solution.py:612
  120.5 11.9 %collective-permute-start.17 = (bf16[4,48,1280]{2,1,0:T(8,128)(2,1)}, bf16[4,48,1280]{2,1,0:T(8,128)(2,1)}, u32[]{:S(2)}, u32[]{:S(2)}) collective-permute-start(bf16[4,48,1280]{2,1,0:T(8,128)(2,1)} %get-tuple-element.59), channel_id=1, source_target_pairs={{0,8},{8,0},{16,24},{24,16},{1,9},{9,1},{17,25},{25,17},{2,10},{10... | collective-permute-start | bytes 1474568 | tf_op jit(solution)/shard_map/ppermute | solution.py:612
  161.7 19.3 %all-to-all-start.2 = ((bf16[8,48,1280]{2,1,0:T(8,128)(2,1)}), bf16[8,48,1280]{2,1,0:T(8,128)(2,1)}, u32[]{:S(2)}, u32[]{:S(2)}) async-start(bf16[8,48,1280]{2,1,0:T(8,128)(2,1)} %get-tuple-element.68), calls=%async_computation.2 | async-start | bytes 1966080 | tf_op jit(solution)/shard_map/all_to_all | solution.py:643
  166.0 8.9 %collective-permute-start.20 = (bf16[2,120,128]{2,1,0:T(8,128)(2,1)}, bf16[2,120,128]{2,1,0:T(8,128)(2,1)}, u32[]{:S(2)}, u32[]{:S(2)}) collective-permute-start(bf16[2,120,128]{2,1,0:T(8,128)(2,1)} %get-tuple-element.69), channel_id=1, source_target_pairs={{0,0},{8,32},{16,64},{24,96},{32,8},{40,40},{48,72},{56,104},{64,1... | collective-permute-start | bytes 184328 | tf_op jit(solution)/shard_map/ppermute | solution.py:652
  171.6 3.2 %collective-permute-start.21 = (bf16[2,120,128]{2,1,0:T(8,128)(2,1)}, bf16[2,120,128]{2,1,0:T(8,128)(2,1)}, u32[]{:S(2)}, u32[]{:S(2)}) collective-permute-start(bf16[2,120,128]{2,1,0:T(8,128)(2,1)} %get-tuple-element.70), channel_id=1, source_target_pairs={{0,8},{8,40},{16,72},{24,104},{32,16},{40,48},{48,80},{56,112},{64... | collective-permute-start | bytes 184328 | tf_op jit(solution)/shard_map/ppermute | solution.py:652
  171.7 5.8 %collective-permute-start.22 = (bf16[2,120,128]{2,1,0:T(8,128)(2,1)}, bf16[2,120,128]{2,1,0:T(8,128)(2,1)}, u32[]{:S(2)}, u32[]{:S(2)}) collective-permute-start(bf16[2,120,128]{2,1,0:T(8,128)(2,1)} %get-tuple-element.71), channel_id=1, source_target_pairs={{0,16},{8,48},{16,80},{24,112},{32,24},{40,56},{48,88},{56,120},{6... | collective-permute-start | bytes 184328 | tf_op jit(solution)/shard_map/ppermute | solution.py:652
  173.5 7.5 %collective-permute-start.23 = (bf16[2,120,128]{2,1,0:T(8,128)(2,1)}, bf16[2,120,128]{2,1,0:T(8,128)(2,1)}, u32[]{:S(2)}, u32[]{:S(2)}) collective-permute-start(bf16[2,120,128]{2,1,0:T(8,128)(2,1)} %get-tuple-element.72), channel_id=1, source_target_pairs={{0,24},{8,56},{16,88},{24,120},{32,0},{40,32},{48,64},{56,96},{64,... | collective-permute-start | bytes 184328 | tf_op jit(solution)/shard_map/ppermute | solution.py:652
  184.2 11.5 %collective-permute-start.24 = (bf16[4,48,1280]{2,1,0:T(8,128)(2,1)}, bf16[4,48,1280]{2,1,0:T(8,128)(2,1)S(1)}, u32[]{:S(2)}, u32[]{:S(2)}) collective-permute-start(bf16[4,48,1280]{2,1,0:T(8,128)(2,1)} %from_lines.1.i0), channel_id=1, source_target_pairs={{0,16},{8,24},{16,0},{24,8},{1,17},{9,25},{17,1},{25,9},{2,18},{10... | collective-permute-start | bytes 1474568 | tf_op jit(solution)/shard_map/ppermute | solution.py:612
  187.6 13.2 %collective-permute-start.25 = (bf16[4,48,1280]{2,1,0:T(8,128)(2,1)}, bf16[4,48,1280]{2,1,0:T(8,128)(2,1)}, u32[]{:S(2)}, u32[]{:S(2)}) collective-permute-start(bf16[4,48,1280]{2,1,0:T(8,128)(2,1)} %from_lines.1.i0), channel_id=1, source_target_pairs={{0,8},{8,0},{16,24},{24,16},{1,9},{9,1},{17,25},{25,17},{2,10},{10... | collective-permute-start | bytes 1474568 | tf_op jit(solution)/shard_map/ppermute | solution.py:612
  195.7 0.8 copy-start.1
  196.5 5.9 %collective-permute-start.26 = (bf16[4,48,1280]{2,1,0:T(8,128)(2,1)S(1)}, bf16[4,48,1280]{2,1,0:T(8,128)(2,1)}, u32[]{:S(2)}, u32[]{:S(2)}) collective-permute-start(bf16[4,48,1280]{2,1,0:T(8,128)(2,1)S(1)} %collective-permute-done.24.i1), channel_id=1, source_target_pairs={{0,8},{8,0},{16,24},{24,16},{1,9},{9,1},{17,25},{25,17},{2,10},{10... | collective-permute-start | bytes 1474568 | tf_op jit(solution)/shard_map/ppermute | solution.py:612
